TPU v7x, 32 devices: a whole 2x2x4 slice. The times are simulated.
32 devices in a mesh: group: 4 (over y, x), row: 8 (over z, core).
Axes of the slice: x: 2, y: 2, z: 4, core: 2. Of those that a mesh axis runs over, the one named last changes fastest.
Arguments:
- snapshots: bfloat16 [1024, 8192], P(('group', 'row')), may hold values from -6 to 6
- bnd_index: int32 [16, 1024], replicated, may hold values from 0 to 8191
- recovery: bfloat16 [512, 512, 1024], P(('group', 'row')), may hold values from -0.1875 to 0.1875
- block_se: int32 [512], P(('group', 'row')), may hold values from 0 to 3
- connect: int32 [16384, 24], P(('group', 'row')), may hold values from 0 to 8703, as said below
- stress_mat: bfloat16 [16384, 6, 24], P(('group', 'row')), may hold values from -1.25 to 1.25
Outputs:
- stresses: bfloat16 [16384, 6, 1024], P(('group', 'row'))
Inputs may be any that keep to these rules, and one draw needn't show every extreme that they name: `connect`: among one device's elements, the first 8192 entries of its connectivity, read element by element, name each of rows 256 to 8447 once.
All inputs are finite; a program needn't handle non-finite values.
Results may differ from a plain program's by a relative error of at most 0.0049.
Values may be sent and summed in bfloat16 or wider, within the bound.
No kernel may reach another device: no remote copies, remote signals or barrier semaphores. Data moves between devices by JAX's collectives and lax.ppermute only.
A program may use at most 128 MiB of HBM per device.

v0:
```python
import math

import jax
import jax.numpy as jnp
from jax import lax
from jax.sharding import PartitionSpec as P

HW = 256
NC = 6
NDOF = 24


def extended_2(cells, sides, width):
    for axis, dim in sides:
        count = lax.axis_size(axis)
        ends = count - 1
        head = lax.slice_in_dim(cells, 0, width, axis=dim)
        tail = lax.slice_in_dim(cells, cells.shape[dim] - width, cells.shape[dim], axis=dim)
        cells = jnp.concatenate(
            [
                lax.ppermute(tail, axis, [(i, (i + 1) % count) for i in range(ends)]),
                cells,
                lax.ppermute(head, axis, [((i + 1) % count, i) for i in range(ends)]),
            ],
            axis=dim,
        )
    return cells


def body(snapshots, bnd_index, recovery, block_se, connect, stress_mat):
    picked = jnp.take(snapshots, bnd_index, axis=1)
    widened = lax.all_gather(picked, "row", axis=0, tiled=True)
    arrived = lax.all_to_all(widened, "group", split_axis=1, concat_axis=0, tiled=True)
    bvals = jnp.transpose(arrived, (1, 0, 2))

    def one_block(entry):
        matrix, which = entry
        sliced = lax.dynamic_index_in_dim(bvals, which, 0, keepdims=False)
        result = lax.dot_general(
            matrix, sliced, (((1,), (1,)), ((), ())), preferred_element_type=jnp.float32
        )
        return result.astype(jnp.bfloat16)

    interior = lax.map(one_block, (recovery, block_se))
    interior = interior.reshape(interior.shape[0] * interior.shape[1], interior.shape[2])
    extended = extended_2(interior, (("row", 0),), HW)
    elem_count = connect.shape[0]
    elem_block = math.gcd(elem_count, 128)

    def one_part(entry):
        link_rows, mat_rows = entry
        values = jnp.take(extended, link_rows, axis=0)
        result = jnp.einsum("eck,ekt->ect", mat_rows, values, preferred_element_type=jnp.float32)
        return result.astype(jnp.bfloat16)

    links = connect.reshape(elem_count // elem_block, elem_block, NDOF)
    mats = stress_mat.reshape(elem_count // elem_block, elem_block, NC, NDOF)
    stresses = lax.map(one_part, (links, mats))
    return stresses.reshape(elem_count, NC, extended.shape[1])


def solution(mesh):
    in_specs = (
        P(("group", "row"), None),
        P(),
        P(("group", "row"), None, None),
        P(("group", "row")),
        P(("group", "row"), None),
        P(("group", "row"), None, None),
    )
    out_specs = P(("group", "row"), None, None)
    return jax.shard_map(body, mesh=mesh, in_specs=in_specs, out_specs=out_specs, check_vma=False)
```

profile of v0, /device:TPU:11, one launch (start us, length us, event | category | flops | bytes accessed | tf_op | source)
XLA Modules:
  0.0 551.9 jit_solution(11753239106156816748)
XLA Ops:
  6.5 0.8 fusion.25
  7.4 0.9 compare_and_fusion.1
  8.2 1.9 copy.25
  10.2 57.9 %gather_fusion.1 = bf16[16384,32]{1,0:T(8,128)(2,1)} fusion(bf16[32,8192]{0,1:T(8,128)(2,1)S(1)} %copy.25, s32[16384]{0:T(1024)S(1)} %broadcast_clamp_fusion.1), kind=kCustom, calls=%fused_computation.1 | custom fusion | bytes 2162688 | tf_op jit(solution)/shard_map/jit(_take)/gather | solution.py:31
  68.1 4.0 copy.26
  72.1 1.1 select_bitcast_fusion
  73.2 81.3 %all-gather.2.cloned.1.call-done = bf16[256,16,1024]{2,1,0:T(8,128)(2,1)} async-done(((bf16[32,16,1024]{2,1,0:T(8,128)(2,1)}), bf16[256,16,1024]{2,1,0:T(8,128)(2,1)}) %all-gather.2.cloned.1.call-update) | async-done | bytes 8388624 | tf_op jit(solution)/shard_map/all_gather | solution.py:32
  154.5 11.3 %copy.27 = bf16[256,16,1024]{2,0,1:T(8,128)(2,1)} copy(bf16[256,16,1024]{2,1,0:T(8,128)(2,1)} %all-gather.2.cloned.1.call-done) | data formatting | bytes 16777216 | tf_op jit(solution)/shard_map/all_gather | solution.py:32
  165.8 5.7 %all-to-all-start = ((bf16[256,16,1024]{2,0,1:T(8,128)(2,1)}), bf16[256,16,1024]{2,0,1:T(8,128)(2,1)}, u32[]{:S(2)}, u32[]{:S(2)}) async-start(bf16[256,16,1024]{2,0,1:T(8,128)(2,1)} %copy.27), calls=%async_computation | async-start | bytes 16777216 | tf_op jit(solution)/shard_map/all_to_all | solution.py:33
  171.5 91.9 %all-to-all-done = bf16[256,16,1024]{2,0,1:T(8,128)(2,1)} async-done(((bf16[256,16,1024]{2,0,1:T(8,128)(2,1)}), bf16[256,16,1024]{2,0,1:T(8,128)(2,1)}, u32[]{:S(2)}, u32[]{:S(2)}) %all-to-all-start) | async-done | bytes 8388640 | tf_op jit(solution)/shard_map/all_to_all | solution.py:33
  263.5 8.0 %copy.28 = bf16[4,256,4,1024]{3,1,0,2:T(8,128)(2,1)} copy(bf16[4,256,4,1024]{3,1,2,0:T(8,128)(2,1)} %bitcast.14) | data formatting | bytes 16777216 | tf_op jit(solution)/shard_map/all_to_all | solution.py:33
  271.4 111.2 %while.20 = (s32[]{:T(128)}, bf16[16,512,1024]{2,1,0:T(8,128)(2,1)}, bf16[16,512,1024]{2,1,0:T(8,128)(2,1)}, s32[16]{0:T(128)S(1)}, bf16[4,1024,1024]{2,1,0:T(8,128)(2,1)}, /*index=5*/s32[]{:T(128)}, s32[]{:T(128)}, s32[]{:T(128)}) while((s32[]{:T(128)}, bf16[16,512,1024]{2,1,0:T(8,128)(2,1)}, bf16[16,512,1024]{2,1,0:T(8,128)(2,1)}, ...), condition=%wide.region_1.2_spmd, body=%wide.region_0.1_spmd.sunk | while | flops 1074266112 | bytes 4195463 | solution.py:44
  274.2 4.2 fusion.34
  281.1 4.2 fusion.34
  288.0 4.2 fusion.34
  295.0 4.2 fusion.34
  301.9 4.2 fusion.34
  308.8 4.2 fusion.34
  315.8 4.2 fusion.34
  322.7 4.3 fusion.34
  329.7 4.2 fusion.34
  336.6 4.2 fusion.34
  343.6 4.2 fusion.34
  350.5 4.3 fusion.34
  357.6 4.2 fusion.34
  364.5 4.2 fusion.34
  371.4 4.2 fusion.34
  378.3 4.2 fusion.34
  382.6 1.3 fusion.26
  383.8 5.3 collective-permute-start
  389.1 2.1 collective-permute-start.1
  391.2 0.8 copy.23
  392.2 3.1 collective-permute-done
  395.2 4.4 collective-permute-done.1
  399.6 22.7 %pad_maximum_fusion = bf16[8704,1024]{1,0:T(8,128)(2,1)} fusion(bf16[256,1024]{1,0:T(8,128)(2,1)S(1)} %collective-permute-done.1, bf16[8192,1024]{1,0:T(8,128)(2,1)} %bitcast.67, bf16[256,1024]{1,0:T(8,128)(2,1)S(1)} %collective-permute-done), kind=kLoop, calls=%fused_computation.25 | loop fusion | flops 53477376 | bytes 35651584 | tf_op jit(solution)/shard_map/concatenate | solution.py:19
  422.4 122.7 %while.21 = (s32[]{:T(128)}, bf16[4,128,6,1024]{3,1,0,2:T(8,128)(2,1)}, bf16[4,128,6,24]{3,2,1,0:T(8,128)(2,1)S(1)}, s32[4,128,24]{2,1,0:T(8,128)S(1)}, bf16[8704,1024]{1,0:T(8,128)(2,1)}, /*index=5*/s32[]{:T(128)}) while((s32[]{:T(128)}, bf16[4,128,6,1024]{3,1,0,2:T(8,128)(2,1)}, bf16[4,128,6,24]{3,2,1,0:T(8,128)(2,1)S(1)}, ...), condition=%wide.region_3.4_spmd, body=%wide.region_2.3_spmd.sunk | while | flops 41711616 | bytes 23973456 | solution.py:58
  422.5 24.3 %gather_fusion = bf16[3072,1024]{1,0:T(8,128)(2,1)} fusion(bf16[8704,1024]{1,0:T(8,128)(2,1)} %get-tuple-element.185, s32[3072]{0:T(1024)S(1)} %broadcast_clamp_fusion.3), kind=kCustom, calls=%fused_computation.clone.1 | custom fusion | bytes 12595200 | tf_op jit(solution)/shard_map/while/body/eval_jaxpr/jit(_take)/gather | solution.py:52
  446.8 4.2 convert_bitcast_fusion.2
  451.0 2.0 copy_dynamic-update-slice_fusion.2
  453.2 24.3 %gather_fusion = bf16[3072,1024]{1,0:T(8,128)(2,1)} fusion(bf16[8704,1024]{1,0:T(8,128)(2,1)} %get-tuple-element.185, s32[3072]{0:T(1024)S(1)} %broadcast_clamp_fusion.3), kind=kCustom, calls=%fused_computation.clone.1 | custom fusion | bytes 12595200 | tf_op jit(solution)/shard_map/while/body/eval_jaxpr/jit(_take)/gather | solution.py:52
  477.5 4.2 convert_bitcast_fusion.2
  481.7 2.0 copy_dynamic-update-slice_fusion.2
  483.8 24.3 %gather_fusion = bf16[3072,1024]{1,0:T(8,128)(2,1)} fusion(bf16[8704,1024]{1,0:T(8,128)(2,1)} %get-tuple-element.185, s32[3072]{0:T(1024)S(1)} %broadcast_clamp_fusion.3), kind=kCustom, calls=%fused_computation.clone.1 | custom fusion | bytes 12595200 | tf_op jit(solution)/shard_map/while/body/eval_jaxpr/jit(_take)/gather | solution.py:52
  508.1 4.2 convert_bitcast_fusion.2
  512.4 2.0 copy_dynamic-update-slice_fusion.2
  514.5 24.3 %gather_fusion = bf16[3072,1024]{1,0:T(8,128)(2,1)} fusion(bf16[8704,1024]{1,0:T(8,128)(2,1)} %get-tuple-element.185, s32[3072]{0:T(1024)S(1)} %broadcast_clamp_fusion.3), kind=kCustom, calls=%fused_computation.clone.1 | custom fusion | bytes 12595200 | tf_op jit(solution)/shard_map/while/body/eval_jaxpr/jit(_take)/gather | solution.py:52
  538.8 4.2 convert_bitcast_fusion.2
  543.0 2.0 copy_dynamic-update-slice_fusion.2
  (45 shorter events, 11.3 us)
Async XLA Ops:
  6.5 148.0 %all-gather.2.cloned.1.call-start = ((), (), s32[]{:S(2)}) async-start(), calls=%async_computation.1 | async-start | bytes 9437184 | tf_op jit(solution)/shard_map/all_gather | solution.py:32
  165.8 97.6 %all-to-all-start = ((bf16[256,16,1024]{2,0,1:T(8,128)(2,1)}), bf16[256,16,1024]{2,0,1:T(8,128)(2,1)}, u32[]{:S(2)}, u32[]{:S(2)}) async-start(bf16[256,16,1024]{2,0,1:T(8,128)(2,1)} %copy.27), calls=%async_computation | async-start | bytes 16777216 | tf_op jit(solution)/shard_map/all_to_all | solution.py:33
  263.5 8.0 %copy-start.2 = (s32[16]{0:T(128)S(1)}, s32[16]{0:T(128)}, u32[]{:S(2)}) copy-start(s32[16]{0:T(128)} %param.13) | copy-start | bytes 196
  271.4 119.8 %copy-start = (bf16[512,6,24]{0,2,1:T(8,128)(2,1)S(1)}, bf16[512,6,24]{0,2,1:T(8,128)(2,1)}, u32[]{:S(2)}) copy-start(bf16[512,6,24]{0,2,1:T(8,128)(2,1)} %param.15) | copy-start | bytes 442372
  271.4 120.6 %copy-start.1 = (s32[512,24]{0,1:T(8,128)S(1)}, s32[512,24]{0,1:T(8,128)}, u32[]{:S(2)}) copy-start(s32[512,24]{0,1:T(8,128)} %param.14) | copy-start | bytes 147460
  383.8 11.4 %collective-permute-start = (bf16[256,1024]{1,0:T(8,128)(2,1)S(1)}, bf16[256,1024]{1,0:T(8,128)(2,1)S(1)}, u32[]{:S(2)}, u32[]{:S(2)}) collective-permute-start(bf16[256,1024]{1,0:T(8,128)(2,1)S(1)} %get-tuple-element.81), channel_id=1, source_target_pairs={{0,1},{1,2},{2,3},{3,4},{4,5},{5,6},{6,7},{8,9},{9,10},{10,11},{11... | collective-permute-start | bytes 1572872 | tf_op jit(solution)/shard_map/ppermute | solution.py:21
  389.1 10.5 %collective-permute-start.1 = (bf16[256,1024]{1,0:T(8,128)(2,1)S(1)}, bf16[256,1024]{1,0:T(8,128)(2,1)S(1)}, u32[]{:S(2)}, u32[]{:S(2)}) collective-permute-start(bf16[256,1024]{1,0:T(8,128)(2,1)S(1)} %get-tuple-element.82), channel_id=1, source_target_pairs={{1,0},{2,1},{3,2},{4,3},{5,4},{6,5},{7,6},{9,8},{10,9},{11,10},{12... | collective-permute-start | bytes 1572872 | tf_op jit(solution)/shard_map/ppermute | solution.py:23
Sparse Core Ops, SparseCore 0:
  73.3 81.1 all-gather.1
where the time goes:
time: 554 us; the launch traced here: 552 us
  local copies, waits for them, and re-layouts  201 us (36%)
  waiting for transfers between devices  181 us (33%)
  matrix products  84.3 us (15%)
  loops' own time  33.3 us (6%)
  other arithmetic  25.7 us (5%)
  between operations  13.5 us (2%)
  starting transfers between devices  13.1 us (2%)
    gather x4, local copies, waits for them, and re-layouts, one_part(): values = jnp.take(extended, link_rows, axis=0)  97.1 us
    all_to_all x1, waiting for transfers between devices, body(): lax.all_to_all(widened, 'group', split_axis=1, concat_axis=0, tiled=True)  91.9 us
    all_gather x1, waiting for transfers between devices, body(): widened = lax.all_gather(picked, 'row', axis=0, tiled=True)  81.3 us
    dot_general x16, matrix products, one_block(): lax.dot_general(matrix, sliced, (((1,), (1,)), ((), ())), preferred_eleme...  67.4 us
    gather x2, local copies, waits for them, and re-layouts, body(): picked = jnp.take(snapshots, bnd_index, axis=1)  61.9 us
    another operation x1, loops' own time, body(): interior = lax.map(one_block, (recovery, block_se))  33.2 us
    concatenate x1, other arithmetic, extended_2(): jnp.concatenate([lax.ppermute(tail, axis, [(i, (i + 1) % count) for i in...  22.7 us
    dot_general x4, matrix products, one_part(): jnp.einsum('eck,ekt->ect', mat_rows, values, preferred_element_type=jnp.f...  16.9 us
  transfers between devices with their start and end apart: 4, of which 4 were waited for; matrix products, arithmetic and copies ran while one was open for 0% of the time, Pallas kernels for 0%

commit v1 on v0

v1 whole, which is shorter than its diff:
```python
import functools

import jax
import jax.numpy as jnp
from jax import lax
from jax.experimental import pallas as pl
from jax.experimental.pallas import tpu as pltpu
from jax.sharding import PartitionSpec as P

HW = 256
SUB = 8
LANES = 128


def combine_kernel(
    conn, tags_ref, s_ref, rec_ref, head_ref, tail_ref, w_ref, tbl, gat,
    *, nfill, blk, nlt, nse, nc, ndof, inner
):
    step = pl.program_id(0)
    rows = SUB * ndof
    out_rows = SUB * nc

    def fill(src, base, count):
        def one(i, carry):
            at = pl.multiple_of(i * 16, 16)
            for j in range(nlt):
                part = src[pl.ds(at, 16), j * LANES:(j + 1) * LANES].astype(jnp.float32)
                tbl[pl.ds((base + at) * nlt + j, 16, stride=nlt), :] = part
            return carry

        lax.fori_loop(0, count // 16, one, 0, unroll=2)

    @pl.when(step < nfill)
    def _():
        fill(rec_ref.at[0], HW + step * blk, blk)

    @pl.when(step == 0)
    def _():
        fill(head_ref, 0, HW)
        fill(tail_ref, HW + nfill * blk, HW)

    @pl.when(step >= nfill)
    def _():
        spread = (
            lax.broadcasted_iota(jnp.int32, (ndof, rows), 1) % ndof
            == lax.broadcasted_iota(jnp.int32, (ndof, rows), 0)
        ).astype(jnp.bfloat16)
        own = (
            lax.broadcasted_iota(jnp.int32, (out_rows, rows), 1) // ndof
            == lax.broadcasted_iota(jnp.int32, (out_rows, rows), 0) // nc
        )

        def one(i, carry):
            first = ((step - nfill) * inner + i) * rows
            for q in range(rows):
                at = pl.multiple_of(conn[first + q] * nlt, nlt)
                gat[pl.ds(q, nlt, stride=rows), :] = tbl[pl.ds(at, nlt), :]
            at = pl.multiple_of(i * out_rows, out_rows)
            wide = jnp.dot(s_ref[pl.ds(at, out_rows), :], spread, preferred_element_type=jnp.float32)
            wide = jnp.where(own, wide, 0.0)
            tag = jnp.broadcast_to(tags_ref[i], (out_rows, rows))
            parts = [jnp.where(tag == se, wide, 0.0).astype(jnp.bfloat16) for se in range(nse)]
            lhs = jnp.concatenate(parts, axis=0)
            for j in range(0, nlt, 2):
                rhs = jnp.concatenate(
                    [gat[(j + d) * rows:(j + d + 1) * rows, :].astype(jnp.bfloat16) for d in range(2)], axis=1
                )
                res = jnp.dot(lhs, rhs, preferred_element_type=jnp.float32).astype(jnp.bfloat16)
                for se in range(nse):
                    col = (se * nlt + j) * LANES
                    w_ref[pl.ds(at, out_rows), col:col + 2 * LANES] = res[se * out_rows:(se + 1) * out_rows]
            return carry

        lax.fori_loop(0, inner, one, 0)


def combine(conn, tags, smat, recovery, head, tail, nse):
    nblk, blk, nb = recovery.shape
    nel = conn.shape[0]
    ndof = conn.shape[1]
    nc = smat.shape[1]
    nlt = nb // LANES
    inner = 4
    rows = SUB * ndof
    steps = nel // (SUB * inner)
    kern = functools.partial(
        combine_kernel, nfill=nblk, blk=blk, nlt=nlt, nse=nse, nc=nc, ndof=ndof, inner=inner
    )
    later = lambda i: jnp.maximum(i - nblk, 0)
    return pl.pallas_call(
        kern,
        out_shape=jax.ShapeDtypeStruct((nel * nc, nse * nb), jnp.bfloat16),
        grid_spec=pltpu.PrefetchScalarGridSpec(
            num_scalar_prefetch=1,
            grid=(nblk + steps,),
            in_specs=[
                pl.BlockSpec((inner, 1, rows), lambda i, c: (later(i), 0, 0)),
                pl.BlockSpec((SUB * inner * nc, ndof), lambda i, c: (later(i), 0)),
                pl.BlockSpec((1, blk, nb), lambda i, c: (jnp.minimum(i, nblk - 1), 0, 0)),
                pl.BlockSpec((HW, nb), lambda i, c: (0, 0)),
                pl.BlockSpec((HW, nb), lambda i, c: (0, 0)),
            ],
            out_specs=pl.BlockSpec((SUB * inner * nc, nse * nb), lambda i, c: (later(i), 0)),
            scratch_shapes=[
                pltpu.VMEM(((nblk * blk + 2 * HW) * nlt, LANES), jnp.float32),
                pltpu.VMEM((rows * nlt, LANES), jnp.float32),
            ],
        ),
        compiler_params=pltpu.CompilerParams(
            dimension_semantics=("arbitrary",), vmem_limit_bytes=60 << 20
        ),
        name="combine",
    )(conn.reshape(-1), tags.reshape(-1, 1, rows), smat.reshape(nel * nc, ndof), recovery, head, tail)


def pick_kernel(idx, *refs, nsrc, tper, chunk):
    srcs = refs[:nsrc]
    o_ref, tbl, buf = refs[nsrc:]
    step = pl.program_id(0)
    nd = tbl.shape[0]

    @pl.when(step == 0)
    def _():
        def one(i, carry):
            at = pl.multiple_of(i * LANES, LANES)
            parts = [s[:, pl.ds(at, LANES)].astype(jnp.float32) for s in srcs]
            short = LANES - nsrc * tper
            if short:
                parts.append(jnp.zeros((short, LANES), jnp.float32))
            tbl[pl.ds(at, LANES), :] = jnp.concatenate(parts, axis=0).T
            return carry

        lax.fori_loop(0, nd // LANES, one, 0)

    def some(i, carry):
        at = pl.multiple_of(i * 64, 64)
        for q in range(64):
            buf[pl.ds(at + q, 1), :] = tbl[pl.ds(idx[step * chunk + at + q], 1), :]
        return carry

    lax.fori_loop(0, chunk // 64, some, 0)
    o_ref[...] = buf[...].astype(jnp.bfloat16)


def pick(idx, srcs):
    tper, nd = srcs[0].shape
    n = idx.shape[0]
    chunk = 1024
    return pl.pallas_call(
        functools.partial(pick_kernel, nsrc=len(srcs), tper=tper, chunk=chunk),
        out_shape=jax.ShapeDtypeStruct((n, LANES), jnp.bfloat16),
        grid_spec=pltpu.PrefetchScalarGridSpec(
            num_scalar_prefetch=1,
            grid=(n // chunk,),
            in_specs=[pl.BlockSpec((tper, nd), lambda i, c: (0, 0)) for _ in srcs],
            out_specs=pl.BlockSpec((chunk, LANES), lambda i, c: (i, 0)),
            scratch_shapes=[pltpu.VMEM((nd, LANES), jnp.float32), pltpu.VMEM((chunk, LANES), jnp.float32)],
        ),
        compiler_params=pltpu.CompilerParams(
            dimension_semantics=("arbitrary",), vmem_limit_bytes=40 << 20
        ),
        name="pick",
    )(idx, *srcs)


def product_kernel(w_ref, b_hbm, o_ref, bt, sem, *, nchunk, ngroup, tper):
    @pl.when(pl.program_id(0) == 0)
    def _():
        copies = [
            pltpu.make_async_copy(b_hbm.at[r], bt.at[:, r * LANES:(r + 1) * LANES], sem.at[r])
            for r in range(nchunk)
        ]
        for c in copies:
            c.start()
        for c in copies:
            c.wait()

    res = jnp.dot(w_ref[...], bt[...], preferred_element_type=jnp.float32)
    per = LANES // tper
    lane = lax.broadcasted_iota(jnp.int32, (res.shape[0], LANES), 1) // tper
    for g in range(ngroup):
        for h in range(nchunk // per):
            tile = None
            for j in range(per):
                src = (h * per + j) * LANES
                moved = pltpu.roll(res[:, src:src + LANES], ((j - g) * tper) % LANES, 1)
                tile = moved if tile is None else jnp.where(lane == j, moved, tile)
            col = (g * (nchunk // per) + h) * LANES
            o_ref[:, col:col + LANES] = tile.astype(jnp.bfloat16)


def product(w, chunks, ngroup, tper, snap):
    m, k = w.shape
    nchunk = chunks.shape[0]
    mb = 256
    return pl.pallas_call(
        functools.partial(product_kernel, nchunk=nchunk, ngroup=ngroup, tper=tper),
        out_shape=jax.ShapeDtypeStruct((m, snap), jnp.bfloat16),
        grid=(m // mb,),
        in_specs=[pl.BlockSpec((mb, k), lambda i: (i, 0)), pl.BlockSpec(memory_space=pl.ANY)],
        out_specs=pl.BlockSpec((mb, snap), lambda i: (i, 0)),
        scratch_shapes=[
            pltpu.VMEM((k, nchunk * LANES), jnp.bfloat16),
            pltpu.SemaphoreType.DMA((nchunk,)),
        ],
        compiler_params=pltpu.CompilerParams(
            dimension_semantics=("arbitrary",), vmem_limit_bytes=56 << 20
        ),
        name="product",
    )(w, chunks)


def body(snapshots, bnd_index, recovery, block_se, connect, stress_mat):
    ngroup = lax.axis_size("group")
    nrow = lax.axis_size("row")
    nse = bnd_index.shape[0] // ngroup
    nblk, blk, nb = recovery.shape
    tper = snapshots.shape[0]
    snap = tper * ngroup * nrow
    group = lax.axis_index("group")

    gathered = lax.all_gather(snapshots, "group", axis=0, tiled=False)
    idx = lax.dynamic_slice_in_dim(bnd_index, group * nse, nse, 0).reshape(-1)
    picked = pick(idx, [gathered[g] for g in range(ngroup)])
    chunks = lax.all_gather(picked, "row", axis=0, tiled=False)

    ends = nrow - 1
    up = [(i, i + 1) for i in range(ends)]
    down = [(i + 1, i) for i in range(ends)]
    head = lax.ppermute(recovery[nblk - 1, blk - HW:], "row", up)
    tail = lax.ppermute(recovery[0, :HW], "row", down)
    se_f = block_se.astype(jnp.float32)
    ends_se = jnp.stack([se_f[-1:], se_f[:1]])
    head_se = lax.ppermute(se_f[-1:], "row", up)
    tail_se = lax.ppermute(se_f[:1], "row", down)
    se_all = jnp.concatenate([head_se, se_f, tail_se]).astype(jnp.int32)
    where = (connect + (blk - HW)) // blk
    tags = jnp.zeros_like(connect)
    for b in range(nblk + 2):
        tags = jnp.where(where == b, se_all[b], tags)
    w = combine(connect, tags, stress_mat, recovery, head, tail, nse)
    out = product(w, chunks, ngroup, tper, snap)
    return out.reshape(connect.shape[0], stress_mat.shape[1], snap)


def solution(mesh):
    in_specs = (
        P(("group", "row"), None),
        P(),
        P(("group", "row"), None, None),
        P(("group", "row")),
        P(("group", "row"), None),
        P(("group", "row"), None, None),
    )
    out_specs = P(("group", "row"), None, None)
    return jax.shard_map(body, mesh=mesh, in_specs=in_specs, out_specs=out_specs, check_vma=False)
```

time: 554 us -> 242 us (0.44)
  local copies, waits for them, and re-layouts: 201 us -> 30.5 us
  waiting for transfers between devices: 181 us -> 51.6 us
  Pallas kernels: 0 us -> 122 us
  matrix products: 84.3 us -> 0 us
  loops' own time: 33.3 us -> 0 us
  other arithmetic: 25.7 us -> 12.4 us
    gather x6 -> x0, local copies, waits for them, and re-layouts: 159 us -> none  [the longest x4 97.1 us: one_part(): values = jnp.take(extended, link_rows, axis=0)]
    pallas_call x0 -> x3, Pallas kernels: none -> 122 us  [the longest x1 72.9 us: combine(): pl.pallas_call(kern, out_shape=jax.ShapeDtypeStruct((nel * nc, nse * nb),...]
    all_to_all x1 -> x0, waiting for transfers between devices: 91.9 us -> none  [body(): lax.all_to_all(widened, 'group', split_axis=1, concat_axis=0, tiled=True)]
    dot_general x20 -> x0, matrix products: 84.3 us -> none  [the longest x16 67.4 us: one_block(): lax.dot_general(matrix, sliced, (((1,), (1,)), ((), ())), preferred_eleme...]
    all_gather x1 -> x2, waiting for transfers between devices: 81.3 us -> 38.3 us  [the longest x1 38.3 us: body(): gathered = lax.all_gather(snapshots, 'group', axis=0, tiled=False)]
    another operation x2 -> x0, loops' own time: 33.3 us -> none  [the longest x1 33.2 us: body(): interior = lax.map(one_block, (recovery, block_se))]
    reshape x0 -> x5, local copies, waits for them, and re-layouts: none -> 23.5 us  [the longest x2 20.6 us: body(): return out.reshape(connect.shape[0], stress_mat.shape[1], snap)]
    concatenate x1 -> x0, other arithmetic: 22.7 us -> none  [extended_2(): jnp.concatenate([lax.ppermute(tail, axis, [(i, (i + 1) % count) for i in...]
  transfers between devices with their start and end apart: 4 -> 6, of which waited for: 4 -> 2; matrix products, arithmetic and copies ran while one was open for 0% -> 8% of each run, Pallas kernels for 0% -> 30%
where the time goes in v1:
time: 242 us; the launch traced here: 240 us
  Pallas kernels  122 us (50%)
  waiting for transfers between devices  51.6 us (21%)
  local copies, waits for them, and re-layouts  30.5 us (13%)
  between operations  13.5 us (6%)
  other arithmetic  12.4 us (5%)
  starting transfers between devices  9.98 us (4%)
    pallas_call x1, Pallas kernels, combine(): pl.pallas_call(kern, out_shape=jax.ShapeDtypeStruct((nel * nc, nse * nb),...  72.9 us
    all_gather x1, waiting for transfers between devices, body(): gathered = lax.all_gather(snapshots, 'group', axis=0, tiled=False)  38.3 us
    pallas_call x1, Pallas kernels, product(): pl.pallas_call(functools.partial(product_kernel, nchunk=nchunk, ngroup=ng...  36.8 us
    reshape x2, local copies, waits for them, and re-layouts, body(): return out.reshape(connect.shape[0], stress_mat.shape[1], snap)  20.6 us
    ppermute x1, waiting for transfers between devices, body(): head_se = lax.ppermute(se_f[-1:], 'row', up)  12.6 us
    pallas_call x1, Pallas kernels, pick(): pl.pallas_call(functools.partial(pick_kernel, nsrc=len(srcs), tper=tper,...  11.8 us
    select_n x1, other arithmetic, body(): tags = jnp.where(where == b, se_all[b], tags)  11.1 us
  transfers between devices with their start and end apart: 6, of which 2 were waited for; matrix products, arithmetic and copies ran while one was open for 8% of the time, Pallas kernels for 30%

profile of v1, /device:TPU:11, one launch (start us, length us, event | category | flops | bytes accessed | tf_op | source)
XLA Modules:
  0.0 239.5 jit_solution(97992843576158078)
XLA Ops:
  6.5 0.0 copy-start
  6.5 0.0 copy-start.6
  6.5 0.0 copy-start.4
  6.5 0.0 copy-start.5
  6.5 0.0 all-gather.5.cloned.1.call-start
  6.6 0.7 all-gather.5.cloned.1.call-update
  7.3 0.0 all-gather.7.cloned.1.call-start
  7.3 0.1 copy-done
  7.4 38.3 %all-gather.5.cloned.1.call-done = bf16[128,8192]{1,0:T(8,128)(2,1)} async-done(((bf16[32,8192]{1,0:T(8,128)(2,1)}), bf16[128,8192]{1,0:T(8,128)(2,1)}) %all-gather.5.cloned.1.call-update) | async-done | bytes 2097168 | tf_op jit(solution)/shard_map/all_gather | solution.py:222
  45.7 1.7 fusion.2
  47.4 11.8 %pick.1 = bf16[4096,128]{1,0:T(8,128)(2,1)} custom-call(s32[4096]{0:T(1024)S(1)} %bitcast.28, bf16[32,8192]{1,0:T(8,128)(2,1)S(1)} %get-tuple-element.10.refs_0_, bf16[32,8192]{1,0:T(8,128)(2,1)S(1)} %get-tuple-element.9.refs_1_, bf16[32,8192]{1,0:T(8,128)(2,1)S(1)} %get-tuple-element.8.refs_2_, bf16[32,8192]{1,0:T(8,128)(2,1)S(1)} %get-tuple-element.7.refs_3_), custom_call_target="tpu_custom_call" | custom-call | tf_op jit(solution)/shard_map/pick/pallas_call | solution.py:149
  59.2 0.0 all-gather.7.cloned.1.call-update
  59.3 1.3 slice_bitcast_fusion
  60.5 2.6 %collective-permute-start.3 = (bf16[256,1024]{1,0:T(8,128)(2,1)S(1)}, bf16[256,1024]{1,0:T(8,128)(2,1)S(1)}, u32[]{:S(2)}, u32[]{:S(2)}) collective-permute-start(bf16[256,1024]{1,0:T(8,128)(2,1)S(1)} %get-tuple-element.5), channel_id=1, source_target_pairs={{1,0},{2,1},{3,2},{4,3},{5,4},{6,5},{7,6},{9,8},{10,9},{11,10},{12... | collective-permute-start | bytes 1572872 | tf_op jit(solution)/shard_map/ppermute | solution.py:231
  63.1 3.0 %collective-permute-start.2 = (bf16[256,1024]{1,0:T(8,128)(2,1)S(1)}, bf16[256,1024]{1,0:T(8,128)(2,1)S(1)}, u32[]{:S(2)}, u32[]{:S(2)}) collective-permute-start(bf16[256,1024]{1,0:T(8,128)(2,1)S(1)} %get-tuple-element.6), channel_id=1, source_target_pairs={{0,1},{1,2},{2,3},{3,4},{4,5},{5,6},{6,7},{8,9},{9,10},{10,11},{11... | collective-permute-start | bytes 1572872 | tf_op jit(solution)/shard_map/ppermute | solution.py:230
  66.1 0.0 copy-done.6
  66.2 0.6 fusion.4
  66.8 2.4 %collective-permute-start = (f32[1]{0:T(128)}, f32[1]{0:T(128)}, u32[]{:S(2)}, u32[]{:S(2)}) collective-permute-start(f32[1]{0:T(128)} %get-tuple-element.29), channel_id=1, source_target_pairs={{0,1},{1,2},{2,3},{3,4},{4,5},{5,6},{6,7},{8,9},{9,10},{10,11},{11... | collective-permute-start | bytes 20 | tf_op jit(solution)/shard_map/ppermute | solution.py:234
  69.2 1.9 collective-permute-start.1
  71.1 0.0 copy-done.4
  71.1 0.1 copy.10
  71.2 0.8 reshape.15.conn
  72.0 0.0 copy-done.5
  72.0 0.8 copy.12
  72.8 1.3 reshape.17.s_ref
  74.1 12.6 %collective-permute-done = f32[1]{0:T(128)} collective-permute-done((f32[1]{0:T(128)}, f32[1]{0:T(128)}, u32[]{:S(2)}, u32[]{:S(2)}) %collective-permute-start) | collective-permute-done | bytes 36 | tf_op jit(solution)/shard_map/ppermute | solution.py:234
  86.7 0.0 collective-permute-done.1
  86.7 1.3 maximum_convert_fusion
  87.9 0.7 fusion.3
  88.7 11.1 %select_select_fusion = s32[512,24]{0,1:T(8,128)S(1)} fusion(s32[512,24]{0,1:T(8,128)S(1)} %copy-done.4, s32[]{:T(128)} %bitcast.17, s32[]{:T(128)} %bitcast.16, s32[]{:T(128)} %bitcast.15, s32[]{:T(128)} %bitcast.14, s32[]{:T(128)} %bitcast.13, s32[]{:T(128)} %bitcast.12, s32[]{:T(128)} %bitcast.11, s32[]{:T(128)} %bitcast.10, s32[]{:T(128)} %bitcast.9, ...), kind=kLoop, calls=%fused_computation.7 | loop fusion | flops 638976 | bytes 98376 | tf_op jit(solution)/shard_map/jit(_where)/select_n | solution.py:240
  99.8 0.1 copy.11
  99.9 0.9 reshape.30.tags_ref
  100.8 0.0 collective-permute-done.3.tail_ref
  100.8 0.0 copy-start.2
  100.8 0.0 collective-permute-done.2.head_ref
  100.8 0.8 copy-done.2
  101.6 0.0 copy-start.3
  101.6 0.8 copy-done.3
  102.4 72.9 %combine.1.w_ref = bf16[3072,4096]{1,0:T(8,128)(2,1)} custom-call(s32[12288]{0:T(1024)} %reshape.15.conn, s32[64,1,192]{2,1,0:T(1,128)} %reshape.30.tags_ref, bf16[3072,24]{1,0:T(8,128)(2,1)} %reshape.17.s_ref, bf16[16,512,1024]{2,1,0:T(8,128)(2,1)} %rec_ref.1, bf16[256,1024]{1,0:T(8,128)(2,1)} %copy-done.3, bf16[256,1024]{1,0:T(8,128)(2,1)} %copy-done.2), custom_call_target="tpu_custom_call" | custom-call | tf_op jit(solution)/shard_map/combine/pallas_call | solution.py:90
  175.3 0.0 all-gather.7.cloned.1.call-done
  175.3 36.8 %product.1 = bf16[3072,1024]{1,0:T(8,128)(2,1)} custom-call(bf16[3072,4096]{1,0:T(8,128)(2,1)} %combine.1.w_ref, bf16[8,4096,128]{2,1,0:T(8,128)(2,1)} %bitcast.29), custom_call_target="tpu_custom_call" | custom-call | tf_op jit(solution)/shard_map/product/pallas_call | solution.py:196
  212.1 0.0 copy-start.1
  212.1 11.0 %reshape.19 = bf16[512,6,1024]{2,1,0:T(8,128)(2,1)} reshape(bf16[3072,1024]{1,0:T(8,128)(2,1)} %product.1) | data formatting | bytes 12582912 | tf_op jit(solution)/shard_map/reshape | solution.py:243
  223.1 9.6 %copy.14 = bf16[512,6,1024]{2,0,1:T(8,128)(2,1)} copy(bf16[512,6,1024]{2,1,0:T(8,128)(2,1)} %reshape.19) | data formatting | bytes 12582912 | tf_op jit(solution)/shard_map/reshape | solution.py:243
  232.7 0.0 copy-done.1
  (3 shorter events, 0.0 us)
Async XLA Ops:
  6.5 0.8 copy-start
  6.5 59.6 %copy-start.6 = (s32[16]{0:T(128)S(1)}, s32[16]{0:T(128)}, u32[]{:S(2)}) copy-start(s32[16]{0:T(128)} %param.9) | copy-start | bytes 196
  6.5 64.5 %copy-start.4 = (s32[512,24]{0,1:T(8,128)S(1)}, s32[512,24]{0,1:T(8,128)}, u32[]{:S(2)}) copy-start(s32[512,24]{0,1:T(8,128)} %param.10) | copy-start | bytes 147460
  6.5 65.5 %copy-start.5 = (bf16[512,6,24]{0,2,1:T(8,128)(2,1)S(1)}, bf16[512,6,24]{0,2,1:T(8,128)(2,1)}, u32[]{:S(2)}) copy-start(bf16[512,6,24]{0,2,1:T(8,128)(2,1)} %param.11) | copy-start | bytes 442372
  6.5 39.2 %all-gather.5.cloned.1.call-start = ((), (), s32[]{:S(2)}) async-start(), calls=%async_computation | async-start | bytes 2621440 | tf_op jit(solution)/shard_map/all_gather | solution.py:222
  7.3 168.0 %all-gather.7.cloned.1.call-start = ((), (), s32[]{:S(2)}) async-start(), calls=%async_computation.1 | async-start | bytes 9437184 | tf_op jit(solution)/shard_map/all_gather | solution.py:225
  60.5 40.3 %collective-permute-start.3 = (bf16[256,1024]{1,0:T(8,128)(2,1)S(1)}, bf16[256,1024]{1,0:T(8,128)(2,1)S(1)}, u32[]{:S(2)}, u32[]{:S(2)}) collective-permute-start(bf16[256,1024]{1,0:T(8,128)(2,1)S(1)} %get-tuple-element.5), channel_id=1, source_target_pairs={{1,0},{2,1},{3,2},{4,3},{5,4},{6,5},{7,6},{9,8},{10,9},{11,10},{12... | collective-permute-start | bytes 1572872 | tf_op jit(solution)/shard_map/ppermute | solution.py:231
  63.1 37.7 %collective-permute-start.2 = (bf16[256,1024]{1,0:T(8,128)(2,1)S(1)}, bf16[256,1024]{1,0:T(8,128)(2,1)S(1)}, u32[]{:S(2)}, u32[]{:S(2)}) collective-permute-start(bf16[256,1024]{1,0:T(8,128)(2,1)S(1)} %get-tuple-element.6), channel_id=1, source_target_pairs={{0,1},{1,2},{2,3},{3,4},{4,5},{5,6},{6,7},{8,9},{9,10},{10,11},{11... | collective-permute-start | bytes 1572872 | tf_op jit(solution)/shard_map/ppermute | solution.py:230
  66.8 19.9 %collective-permute-start = (f32[1]{0:T(128)}, f32[1]{0:T(128)}, u32[]{:S(2)}, u32[]{:S(2)}) collective-permute-start(f32[1]{0:T(128)} %get-tuple-element.29), channel_id=1, source_target_pairs={{0,1},{1,2},{2,3},{3,4},{4,5},{5,6},{6,7},{8,9},{9,10},{10,11},{11... | collective-permute-start | bytes 20 | tf_op jit(solution)/shard_map/ppermute | solution.py:234
  69.2 17.5 %collective-permute-start.1 = (f32[1]{0:T(128)}, f32[1]{0:T(128)}, u32[]{:S(2)}, u32[]{:S(2)}) collective-permute-start(f32[1]{0:T(128)} %get-tuple-element.30), channel_id=1, source_target_pairs={{1,0},{2,1},{3,2},{4,3},{5,4},{6,5},{7,6},{9,8},{10,9},{11,10},{12... | collective-permute-start | bytes 20 | tf_op jit(solution)/shard_map/ppermute | solution.py:235
  100.8 0.8 copy-start.2
  101.6 0.8 copy-start.3
  212.1 20.6 %copy-start.1 = (s32[16,1024]{1,0:T(8,128)S(1)}, s32[16,1024]{1,0:T(8,128)}, u32[]{:S(2)}) copy-start(s32[16,1024]{1,0:T(8,128)} %param.7) | copy-start | bytes 196612
Sparse Core Ops, SparseCore 0:
  9.2 36.4 all-gather.4
  59.4 83.4 all-gather.6

commit v2 on v1

v2 whole, which is shorter than its diff:
```python
import functools

import jax
import jax.numpy as jnp
from jax import lax
from jax.experimental import pallas as pl
from jax.experimental.pallas import tpu as pltpu
from jax.sharding import PartitionSpec as P

HW = 256
SUB = 8
LANES = 128


def combine_kernel(conn, se, grow_ref, s_ref, rec_ref, head_ref, tail_ref, w_ref, tbl, g0, g1,
    *, nfill, blk, nlt, nse, nc, ndof, inner, ts, gs,
):
    step = pl.program_id(0)
    rows = SUB * ndof
    out_rows = SUB * nc
    steps = pl.num_programs(0) - nfill

    def fill(src, base, count):
        def one(i, carry):
            at = pl.multiple_of(i * 16, 16)
            for j in range(nlt):
                part = src[pl.ds(at, 16), j * LANES:(j + 1) * LANES].astype(jnp.float32)
                tbl[pl.ds((base + at) * ts + j, 16, stride=ts), :] = part
            return carry
        lax.fori_loop(0, count // 16, one, 0, unroll=2)

    def gather(group, dst):
        first = group * rows
        for q in range(rows):
            dst[pl.ds(q, nlt, stride=gs), :] = tbl[pl.ds(conn[first + q] * ts, nlt), :]

    def matmul(i, src):
        own = (
            lax.broadcasted_iota(jnp.int32, (SUB, rows), 1) % SUB
            == lax.broadcasted_iota(jnp.int32, (SUB, rows), 0)
        )
        where = (grow_ref[i] + (blk - HW)) // blk
        tag = jnp.zeros((1, rows), jnp.int32)
        for b in range(nfill + 2):
            tag = jnp.where(where == b, se[b], tag)
        tag = jnp.where(own, jnp.broadcast_to(tag, (SUB, rows)), -1)
        parts = []
        smat = s_ref[i].astype(jnp.float32)
        for s in range(nse):
            hit = tag == s
            for c in range(nc):
                parts.append(jnp.where(hit, jnp.broadcast_to(smat[c:c + 1], (SUB, rows)), 0.0))
        lhs = jnp.concatenate(parts, axis=0).astype(jnp.bfloat16)
        at = pl.multiple_of(i * SUB, SUB)
        for j in range(0, nlt, 2):
            rhs = jnp.concatenate(
                [src[(j + d) * gs:(j + d) * gs + rows, :].astype(jnp.bfloat16) for d in range(2)], axis=1)
            res = jnp.dot(lhs, rhs, preferred_element_type=jnp.float32).astype(jnp.bfloat16)
            for s in range(nse):
                col = (s * nlt + j) * LANES
                for c in range(nc):
                    w_ref[c, pl.ds(at, SUB), col:col + 2 * LANES] = res[(s * nc + c) * SUB:(s * nc + c + 1) * SUB]

    @pl.when(step < nfill)
    def _():
        fill(rec_ref.at[0], HW + step * blk, blk)

    @pl.when(step == 0)
    def _():
        fill(head_ref, 0, HW)
        fill(tail_ref, HW + nfill * blk, HW)

    @pl.when(step >= nfill)
    def _():
        base = (step - nfill) * inner
        last = steps * inner - 1

        @pl.when(step == nfill)
        def _():
            gather(0, g0)

        def two(i, carry):
            n = base + 2 * i
            gather(n + 1, g1)
            matmul(2 * i, g0)
            gather(jnp.minimum(n + 2, last), g0)
            matmul(2 * i + 1, g1)
            return carry
        lax.fori_loop(0, inner // 2, two, 0)

def combine(conn, se, grow, smat, recovery, head, tail, nse, inner=4):
    nblk, blk, nb = recovery.shape
    ngrp, _, rows = grow.shape
    nel = ngrp * SUB
    ndof = rows // SUB
    nc = smat.shape[1]
    nlt = nb // LANES
    steps = ngrp // inner
    ts = nlt + 1
    gs = rows + 1
    kern = functools.partial(
        combine_kernel, nfill=nblk, blk=blk, nlt=nlt, nse=nse, nc=nc, ndof=ndof, inner=inner, ts=ts, gs=gs
    )
    later = lambda i: jnp.maximum(i - nblk, 0)
    return pl.pallas_call(
        kern,
        out_shape=jax.ShapeDtypeStruct((nc, nel, nse * nb), jnp.bfloat16),
        grid_spec=pltpu.PrefetchScalarGridSpec(
            num_scalar_prefetch=2,
            grid=(nblk + steps,),
            in_specs=[
                pl.BlockSpec((inner, 1, rows), lambda i, c, s: (later(i), 0, 0)),
                pl.BlockSpec((inner, nc, rows), lambda i, c, s: (later(i), 0, 0)),
                pl.BlockSpec((1, blk, nb), lambda i, c, s: (jnp.minimum(i, nblk - 1), 0, 0)),
                pl.BlockSpec((HW, nb), lambda i, c, s: (0, 0)),
                pl.BlockSpec((HW, nb), lambda i, c, s: (0, 0)),
            ],
            out_specs=pl.BlockSpec((nc, SUB * inner, nse * nb), lambda i, c, s: (0, later(i), 0)),
            scratch_shapes=[
                pltpu.VMEM(((nblk * blk + 2 * HW) * ts, LANES), jnp.float32),
                pltpu.VMEM((gs * nlt, LANES), jnp.float32),
                pltpu.VMEM((gs * nlt, LANES), jnp.float32),
            ],
        ),
        compiler_params=pltpu.CompilerParams(dimension_semantics=("arbitrary",), vmem_limit_bytes=60 << 20),
        name="combine",
    )(conn, se, grow, smat, recovery, head, tail)


def pick_near_kernel(idx, *refs, nsrc, half, parts, chunk):
    srcs = refs[:nsrc]
    o_ref, tbl = refs[nsrc:nsrc + 2]
    bufs = refs[nsrc + 2:]
    step = pl.program_id(0)
    nd = tbl.shape[0]
    total = chunk * pl.num_programs(0)

    @pl.when(step == 0)
    def _():
        def one(i, carry):
            at = pl.multiple_of(i * LANES, LANES)
            rows = jnp.concatenate([s[:, pl.ds(at, LANES)].astype(jnp.float32) for s in srcs] * parts, axis=0)
            tbl[pl.ds(at, LANES), :] = rows.T
            return carry

        lax.fori_loop(0, nd // LANES, one, 0, unroll=2)

    def some(i, carry):
        at = pl.multiple_of(i * 64, 64)
        for p in range(parts):
            for q in range(64):
                k = idx[p * total + step * chunk + at + q]
                bufs[p][pl.ds(at + q, 1), :] = tbl[pl.ds(k, 1), :]
        return carry

    lax.fori_loop(0, chunk // 64, some, 0)
    piece = lax.broadcasted_iota(jnp.int32, (chunk, LANES), 1) // (LANES // parts)
    out = bufs[0][...]
    for p in range(1, parts):
        out = jnp.where(piece == p, bufs[p][...], out)
    o_ref[...] = out.astype(jnp.bfloat16)


def pick_near(idx, srcs):
    half, nd = srcs[0].shape
    parts = LANES // (half * len(srcs))
    n = idx.shape[0] // parts
    chunk = min(n, 1024)
    return pl.pallas_call(
        functools.partial(pick_near_kernel, nsrc=len(srcs), half=half, parts=parts, chunk=chunk),
        out_shape=jax.ShapeDtypeStruct((n, LANES), jnp.bfloat16),
        grid_spec=pltpu.PrefetchScalarGridSpec(
            num_scalar_prefetch=1,
            grid=(n // chunk,),
            in_specs=[pl.BlockSpec((half, nd), lambda i, c: (0, 0)) for _ in srcs],
            out_specs=pl.BlockSpec((chunk, LANES), lambda i, c: (i, 0)),
            scratch_shapes=[pltpu.VMEM((nd, LANES), jnp.float32)]
            + [pltpu.VMEM((chunk, LANES), jnp.float32) for _ in range(parts)],
        ),
        compiler_params=pltpu.CompilerParams(
            dimension_semantics=("arbitrary",), vmem_limit_bytes=40 << 20
        ),
        name="pick_near",
    )(idx, *srcs)


def pick_far_kernel(idx, src, *refs, nout, order, half, chunk, per_out):
    outs = refs[:nout]
    tbl, buf = refs[nout:]
    step = pl.program_id(0)
    nd = tbl.shape[0]

    @pl.when(step == 0)
    def _():
        def one(i, carry):
            at = pl.multiple_of(i * LANES, LANES)
            rows = jnp.concatenate([src[r, :, pl.ds(at, LANES)].astype(jnp.float32) for r in order], axis=0)
            tbl[pl.ds(at, LANES), :] = rows.T
            return carry

        lax.fori_loop(0, nd // LANES, one, 0, unroll=2)

    def some(i, carry):
        at = pl.multiple_of(i * 64, 64)
        for q in range(64):
            buf[pl.ds(at + q, 1), :] = tbl[pl.ds(idx[step * chunk + at + q], 1), :]
        return carry

    lax.fori_loop(0, chunk // 64, some, 0)
    for s in range(nout):
        @pl.when(step // per_out == s)
        def _():
            outs[s][...] = buf[...].astype(jnp.bfloat16)


def pick_far(idx, src, order):
    nrow, half, nd = src.shape
    nout, n = idx.shape
    chunk = min(n, 1024)
    per_out = n // chunk

    def place(s):
        return lambda i, c: (jnp.clip(i - s * per_out, 0, per_out - 1), 0)

    return pl.pallas_call(
        functools.partial(
            pick_far_kernel, nout=nout, order=order, half=half, chunk=chunk, per_out=per_out
        ),
        out_shape=[jax.ShapeDtypeStruct((n, LANES), jnp.bfloat16) for _ in range(nout)],
        grid_spec=pltpu.PrefetchScalarGridSpec(
            num_scalar_prefetch=1,
            grid=(nout * per_out,),
            in_specs=[pl.BlockSpec((nrow, half, nd), lambda i, c: (0, 0, 0))],
            out_specs=[pl.BlockSpec((chunk, LANES), place(s)) for s in range(nout)],
            scratch_shapes=[pltpu.VMEM((nd, LANES), jnp.float32), pltpu.VMEM((chunk, LANES), jnp.float32)],
        ),
        compiler_params=pltpu.CompilerParams(
            dimension_semantics=("arbitrary",), vmem_limit_bytes=40 << 20
        ),
        name="pick_far",
    )(idx.reshape(-1), src)


def product_kernel(
    where, w_ref, *refs, ngroup, nrow, tper, half, parts
):
    mine = refs[:ngroup]
    theirs = refs[ngroup:2 * ngroup]
    near_hbm, o_ref, bt, near, sem = refs[2 * ngroup:]
    group = where[0]
    core = where[1]
    nh = tper * nrow // LANES
    per = LANES // tper
    npair = ngroup * half // tper
    rows = bt.shape[0] // 2
    nk = bt.shape[0] // parts

    @pl.when(pl.program_id(0) == 0)
    def _():
        last = pltpu.make_async_copy(near_hbm, near, sem.at[2 * ngroup])
        last.start()
        copies = []
        for s in range(ngroup):
            cols = slice(s * LANES, (s + 1) * LANES)
            for d, ref in ((0, mine[s]), (1, theirs[s])):
                at = pl.multiple_of(jnp.where(core == d, 0, 1) * rows, rows)
                copies.append(pltpu.make_async_copy(ref, bt.at[pl.ds(at, rows), cols], sem.at[2 * s + d]))
        for c in copies:
            c.start()
        last.wait()
        step_rows = min(nk, 256)
        lane = lax.broadcasted_iota(jnp.int32, (step_rows, LANES), 1) // tper

        def arrange(i, carry):
            at = pl.multiple_of(i * step_rows, step_rows)
            for h in range(nh):
                got = [near[h * per + j, pl.ds(at, step_rows), :].astype(jnp.float32) for j in range(per)]
                for p in range(npair):
                    for kp in range(parts):
                        tile = None
                        for j in range(per):
                            shift = (tper * j - (kp * (LANES // parts) + tper * p)) % LANES
                            moved = pltpu.roll(got[j], shift, 1) if shift else got[j]
                            tile = moved if tile is None else jnp.where(lane == j, moved, tile)
                        col = (ngroup + h * npair + p) * LANES
                        bt[pl.ds(kp * nk + at, step_rows), col:col + LANES] = tile.astype(jnp.bfloat16)
            return carry

        lax.fori_loop(0, nk // step_rows, arrange, 0)
        for c in copies:
            c.wait()

    res = jnp.dot(w_ref[...], bt[...], preferred_element_type=jnp.float32)
    slot = (lax.broadcasted_iota(jnp.int32, (res.shape[0], LANES), 1) // half) % 2
    for s in range(ngroup):
        far = res[:, s * LANES:(s + 1) * LANES]
        for h in range(nh):
            first = pltpu.roll(far, LANES - half * h, 1) if h else far
            at = (ngroup + h * npair + s // 2) * LANES
            second = res[:, at:at + LANES]
            if s % 2 == 0:
                second = pltpu.roll(second, half, 1)
            tile = jnp.where(slot == 0, first, second).astype(jnp.bfloat16)
            col = pl.multiple_of(((group ^ s) * nh + h) * LANES, LANES)
            o_ref[:, pl.ds(col, LANES)] = tile


def product(where, w, mine, theirs, near, tper, snap):
    m, k = w.shape
    ngroup = len(mine)
    nrow, nk, _ = near.shape
    mb = 256
    return pl.pallas_call(
        functools.partial(
            product_kernel, ngroup=ngroup, nrow=nrow, tper=tper, half=tper // 2, parts=k // nk
        ),
        out_shape=jax.ShapeDtypeStruct((m, snap), jnp.bfloat16),
        grid_spec=pltpu.PrefetchScalarGridSpec(
            num_scalar_prefetch=1,
            grid=(m // mb,),
            in_specs=[pl.BlockSpec((mb, k), lambda i, c: (i, 0))]
            + [pl.BlockSpec(memory_space=pl.ANY)] * (2 * ngroup + 1),
            out_specs=pl.BlockSpec((mb, snap), lambda i, c: (i, 0)),
            scratch_shapes=[
                pltpu.VMEM((k, snap), jnp.bfloat16),
                pltpu.VMEM(near.shape, jnp.bfloat16),
                pltpu.SemaphoreType.DMA((2 * ngroup + 1,)),
            ],
        ),
        compiler_params=pltpu.CompilerParams(
            dimension_semantics=("arbitrary",), vmem_limit_bytes=56 << 20
        ),
        name="product",
    )(where, w, *mine, *theirs, near)


def body(snapshots, bnd_index, recovery, block_se, connect, stress_mat):
    ngroup = lax.axis_size("group")
    nrow = lax.axis_size("row")
    nse = bnd_index.shape[0] // ngroup
    nblk, blk, nb = recovery.shape
    nel, nc, ndof = stress_mat.shape
    tper = snapshots.shape[0]
    half = tper // 2
    snap = tper * ngroup * nrow
    group = lax.axis_index("group")
    core = lax.axis_index("row") % 2
    swap = lambda s: [(i, i ^ s) for i in range(ngroup)]
    other = [(i, i ^ 1) for i in range(nrow)]

    top = snapshots[:half]
    bottom = snapshots[half:]
    along_row = lax.all_gather(top, "row", axis=0, tiled=False)
    along_group = [bottom] + [lax.ppermute(bottom, "group", swap(s)) for s in range(1, ngroup)]

    own_idx = lax.dynamic_slice_in_dim(bnd_index, group * nse, nse, 0).reshape(-1)
    near = lax.all_gather(pick_near(own_idx, along_group), "row", axis=0, tiled=False)

    rows = nse * nb // 2
    far_idx = jnp.stack([
        lax.dynamic_slice_in_dim(
            lax.dynamic_slice_in_dim(bnd_index, (group ^ s) * nse, nse, 0).reshape(-1), core * rows, rows, 0
        )
        for s in range(ngroup)
    ])
    per = LANES // tper
    order = [per * h + j for j in range(per) for h in range(nrow // per)]
    far = pick_far(far_idx, along_row, order)
    mine = [far[0]] + [lax.ppermute(far[s], "group", swap(s)) for s in range(1, ngroup)]
    theirs = [lax.ppermute(x, "row", other) for x in mine]

    ends = nrow - 1
    up = [(i, i + 1) for i in range(ends)]
    down = [(i + 1, i) for i in range(ends)]
    head = lax.ppermute(recovery[nblk - 1, blk - HW:], "row", up)
    tail = lax.ppermute(recovery[0, :HW], "row", down)
    head_se = lax.ppermute(block_se[-1:], "row", up)
    tail_se = lax.ppermute(block_se[:1], "row", down)
    se_all = jnp.concatenate([head_se, block_se, tail_se])

    ngrp = nel // SUB
    conn = connect.T.reshape(ndof, ngrp, SUB).transpose(1, 0, 2).reshape(ngrp, 1, ndof * SUB)
    smat = stress_mat.transpose(1, 2, 0).reshape(nc, ndof, ngrp, SUB).transpose(2, 0, 1, 3)
    smat = smat.reshape(ngrp, nc, ndof * SUB)
    flat, far0 = lax.optimization_barrier((conn.reshape(-1), far[0]))
    mine[0] = far0
    w = combine(flat, se_all, conn, smat, recovery, head, tail, nse)
    where = jnp.stack([group, core]).astype(jnp.int32)
    out = product(where, w.reshape(nc * nel, nse * nb), mine, theirs, near, tper, snap)
    return out.reshape(nc, nel, snap).transpose(1, 0, 2)


def solution(mesh):
    in_specs = (
        P(("group", "row"), None),
        P(),
        P(("group", "row"), None, None),
        P(("group", "row")),
        P(("group", "row"), None),
        P(("group", "row"), None, None),
    )
    out_specs = P(("group", "row"), None, None)
    return jax.shard_map(body, mesh=mesh, in_specs=in_specs, out_specs=out_specs, check_vma=False)
```

time: 242 us -> 179 us (0.74)
  waiting for transfers between devices: 51.6 us -> 18.6 us
  Pallas kernels: 122 us -> 101 us
  local copies, waits for them, and re-layouts: 30.5 us -> 13.5 us
  starting transfers between devices: 9.98 us -> 26.5 us
  other arithmetic: 12.4 us -> 3.18 us
    all_gather x2, waiting for transfers between devices: 38.3 us -> 3.32 us  [the longest x1 3.29 us: body(): along_row = lax.all_gather(top, 'row', axis=0, tiled=False)]
    reshape x5 -> x3, local copies, waits for them, and re-layouts: 23.5 us -> 1.67 us  [the longest x1 0.95 us: body(): smat = smat.reshape(ngrp, nc, ndof * SUB)]
    pallas_call x3 -> x4, Pallas kernels: 122 us -> 101 us  [the longest x1 40.9 us: combine(): pl.pallas_call(kern, out_shape=jax.ShapeDtypeStruct((nc, nel, nse * nb),...]
    ppermute x2 -> x12, starting transfers between devices: 4.32 us -> 22 us  [the longest x4 9.52 us: body(): theirs = [lax.ppermute(x, 'row', other) for x in mine]]
    select_n x1 -> x0, other arithmetic: 11.1 us -> none  [body(): tags = jnp.where(where == b, se_all[b], tags)]
    transpose x0 -> x5, local copies, waits for them, and re-layouts: none -> 3.17 us  [the longest x2 1.81 us: body(): stress_mat.transpose(1, 2, 0).reshape(nc, ndof, ngrp, SUB)]
    ppermute x2 -> x12, waiting for transfers between devices: 12.6 us -> 15.2 us  [the longest x3 11.2 us: body(): lax.ppermute(bottom, 'group', swap(s))]
    concatenate x0 -> x1, other arithmetic: none -> 2.56 us  [body(): se_all = jnp.concatenate([head_se, block_se, tail_se])]
  transfers between devices with their start and end apart: 6 -> 16, of which waited for: 2 -> 6; matrix products, arithmetic and copies ran while one was open for 8% -> 8% of each run, Pallas kernels for 30% -> 35%
where the time goes in v2:
time: 179 us; the launch traced here: 177 us
  Pallas kernels  101 us (56%)
  starting transfers between devices  26.5 us (15%)
  waiting for transfers between devices  18.6 us (10%)
  between operations  13.7 us (8%)
  local copies, waits for them, and re-layouts  13.5 us (8%)
  other arithmetic  3.18 us (2%)
    pallas_call x1, Pallas kernels, combine(): pl.pallas_call(kern, out_shape=jax.ShapeDtypeStruct((nc, nel, nse * nb),...  40.9 us
    pallas_call x1, Pallas kernels, product(): pl.pallas_call(functools.partial(product_kernel, ngroup=ngroup, nrow=nrow...  40 us
    pallas_call x1, Pallas kernels, pick_far(): pl.pallas_call(functools.partial(pick_far_kernel, nout=nout, order=order,...  12.1 us
    ppermute x3, waiting for transfers between devices, body(): lax.ppermute(bottom, 'group', swap(s))  11.2 us
    ppermute x4, starting transfers between devices, body(): theirs = [lax.ppermute(x, 'row', other) for x in mine]  9.52 us
    pallas_call x1, Pallas kernels, pick_near(): pl.pallas_call(functools.partial(pick_near_kernel, nsrc=len(srcs), half=h...  8.39 us
    ppermute x1, starting transfers between devices, body(): head_se = lax.ppermute(block_se[-1:], 'row', up)  3.6 us
  transfers between devices with their start and end apart: 16, of which 6 were waited for; matrix products, arithmetic and copies ran while one was open for 8% of the time, Pallas kernels for 35%

profile of v2, /device:TPU:11, one launch (start us, length us, event | category | flops | bytes accessed | tf_op | source)
XLA Modules:
  0.0 176.7 jit_solution(5892567808926661354)
XLA Ops:
  6.5 1.8 %fusion = (bf16[16,8192]{1,0:T(8,128)(2,1)S(1)}, bf16[16,8192]{1,0:T(8,128)(2,1)}) fusion(bf16[32,8192]{1,0:T(8,128)(2,1)} %param.6), kind=kLoop, calls=%fused_computation.13 | loop fusion | bytes 1048576 | tf_op jit(solution)/shard_map/slice | solution.py:352
  8.3 0.0 all-gather.5.cloned.1.call-update
  8.3 0.0 all-gather.7.cloned.1.call-start
  8.4 1.3 collective-permute-start.13
  9.7 0.2 collective-permute-start.12
  9.9 1.2 collective-permute-start.11
  11.1 0.8 dynamic-slice_bitcast_fusion.3
  12.0 4.6 %collective-permute-done.13.refs_3_ = bf16[16,8192]{1,0:T(8,128)(2,1)S(1)} collective-permute-done((bf16[16,8192]{1,0:T(8,128)(2,1)S(1)}, bf16[16,8192]{1,0:T(8,128)(2,1)S(1)}, u32[]{:S(2)}, u32[]{:S(2)}) %collective-permute-start.13) | collective-permute-done | bytes 262176 | tf_op jit(solution)/shard_map/ppermute | solution.py:354
  16.6 6.6 %collective-permute-done.12.refs_2_ = bf16[16,8192]{1,0:T(8,128)(2,1)S(1)} collective-permute-done((bf16[16,8192]{1,0:T(8,128)(2,1)S(1)}, bf16[16,8192]{1,0:T(8,128)(2,1)S(1)}, u32[]{:S(2)}, u32[]{:S(2)}) %collective-permute-start.12) | collective-permute-done | bytes 262176 | tf_op jit(solution)/shard_map/ppermute | solution.py:354
  23.2 0.0 collective-permute-done.11.refs_1_
  23.2 8.4 %pick_near.1 = bf16[2048,128]{1,0:T(8,128)(2,1)} custom-call(s32[4096]{0:T(1024)S(1)} %bitcast.49, bf16[16,8192]{1,0:T(8,128)(2,1)S(1)} %get-tuple-element.19.refs_0_, bf16[16,8192]{1,0:T(8,128)(2,1)S(1)} %collective-permute-done.11.refs_1_, bf16[16,8192]{1,0:T(8,128)(2,1)S(1)} %collective-permute-done.12.refs_2_, ...), custom_call_target="tpu_custom_call" | custom-call | tf_op jit(solution)/shard_map/pick_near/pallas_call | solution.py:169
  31.6 0.0 all-gather.7.cloned.1.call-update
  31.6 2.1 %slice_bitcast_fusion = (bf16[256,1024]{1,0:T(8,128)(2,1)S(1)}, bf16[256,1024]{1,0:T(8,128)(2,1)}) fusion(bf16[16,512,1024]{2,1,0:T(8,128)(2,1)} %rec_ref.1), kind=kLoop, calls=%fused_computation | loop fusion | bytes 2097152 | tf_op jit(solution)/shard_map/squeeze | solution.py:376
  33.7 2.5 %collective-permute-start.3 = (bf16[256,1024]{1,0:T(8,128)(2,1)S(1)}, bf16[256,1024]{1,0:T(8,128)(2,1)S(1)}, u32[]{:S(2)}, u32[]{:S(2)}) collective-permute-start(bf16[256,1024]{1,0:T(8,128)(2,1)S(1)} %get-tuple-element.17), channel_id=1, source_target_pairs={{1,0},{2,1},{3,2},{4,3},{5,4},{6,5},{7,6},{9,8},{10,9},{11,10},{12... | collective-permute-start | bytes 1572872 | tf_op jit(solution)/shard_map/ppermute | solution.py:376
  36.3 3.3 %all-gather.5.cloned.1.call-done = bf16[128,8192]{1,0:T(8,128)(2,1)} async-done(((bf16[16,8192]{1,0:T(8,128)(2,1)}), bf16[128,8192]{1,0:T(8,128)(2,1)}) %all-gather.5.cloned.1.call-update) | async-done | bytes 2097168 | tf_op jit(solution)/shard_map/all_gather | solution.py:353
  39.6 1.6 copy-done
  41.2 12.1 %pick_far.1 = (bf16[2048,128]{1,0:T(8,128)(2,1)S(1)}, bf16[2048,128]{1,0:T(8,128)(2,1)S(1)}, bf16[2048,128]{1,0:T(8,128)(2,1)S(1)}, bf16[2048,128]{1,0:T(8,128)(2,1)S(1)}) custom-call(s32[8192]{0:T(1024)S(1)} %bitcast.48, bf16[8,16,8192]{2,1,0:T(8,128)(2,1)S(1)} %bitcast.47), custom_call_target="tpu_custom_call" | custom-call | tf_op jit(solution)/shard_map/pick_far/pallas_call | solution.py:225
  53.3 0.3 collective-permute-start.4
  53.7 1.2 collective-permute-start.5
  54.9 1.2 collective-permute-start.6
  56.1 1.4 fusion.1
  57.4 3.6 %collective-permute-start = (s32[1]{0:T(128)}, s32[1]{0:T(128)}, u32[]{:S(2)}, u32[]{:S(2)}) collective-permute-start(s32[1]{0:T(128)} %get-tuple-element.25), channel_id=1, source_target_pairs={{0,1},{1,2},{2,3},{3,4},{4,5},{5,6},{6,7},{8,9},{9,10},{10,11},{11... | collective-permute-start | bytes 20 | tf_op jit(solution)/shard_map/ppermute | solution.py:377
  61.1 0.9 collective-permute-done
  62.0 3.5 %collective-permute-start.1 = (s32[1]{0:T(128)}, s32[1]{0:T(128)}, u32[]{:S(2)}, u32[]{:S(2)}) collective-permute-start(s32[1]{0:T(128)} %get-tuple-element.26), channel_id=1, source_target_pairs={{1,0},{2,1},{3,2},{4,3},{5,4},{6,5},{7,6},{9,8},{10,9},{11,10},{12... | collective-permute-start | bytes 20 | tf_op jit(solution)/shard_map/ppermute | solution.py:378
  65.5 2.4 %collective-permute-done.1 = s32[1]{0:T(128)} collective-permute-done((s32[1]{0:T(128)}, s32[1]{0:T(128)}, u32[]{:S(2)}, u32[]{:S(2)}) %collective-permute-start.1) | collective-permute-done | bytes 36 | tf_op jit(solution)/shard_map/ppermute | solution.py:378
  67.9 1.9 %collective-permute-start.2 = (bf16[256,1024]{1,0:T(8,128)(2,1)}, bf16[256,1024]{1,0:T(8,128)(2,1)}, u32[]{:S(2)}, u32[]{:S(2)}) collective-permute-start(bf16[256,1024]{1,0:T(8,128)(2,1)} %get-tuple-element.18), channel_id=1, source_target_pairs={{0,1},{1,2},{2,3},{3,4},{4,5},{5,6},{6,7},{8,9},{9,10},{10,11},{11... | collective-permute-start | bytes 1572872 | tf_op jit(solution)/shard_map/ppermute | solution.py:375
  69.8 0.0 collective-permute-done.3.tail_ref
  69.8 0.6 collective-permute-start.7
  70.4 0.1 collective-permute-start.8
  70.5 0.0 collective-permute-done.5.refs_2_
  70.5 7.8 %collective-permute-start.9 = (bf16[2048,128]{1,0:T(8,128)(2,1)S(1)}, bf16[2048,128]{1,0:T(8,128)(2,1)}, u32[]{:S(2)}, u32[]{:S(2)}) collective-permute-start(bf16[2048,128]{1,0:T(8,128)(2,1)S(1)} %collective-permute-done.5.refs_2_), channel_id=1, source_target_pairs={{0,1},{1,0},{2,3},{3,2},{4,5},{5,4},{6,7},{7,6},{8,9},{9,8},{10,11... | collective-permute-start | bytes 1572872 | tf_op jit(solution)/shard_map/ppermute | solution.py:370
  78.3 0.6 collective-permute-done.6.refs_3_
  78.9 1.1 collective-permute-start.10
  80.0 0.9 copy.9
  80.9 0.2 copy.11
  81.1 0.3 copy.10
  81.4 0.7 copy.14.grow_ref
  82.1 0.9 reshape_reshape.3.conn
  83.0 1.3 copy.12
  84.3 0.5 copy.13
  84.8 1.0 copy.15.s_ref
  85.8 0.6 pad_add_fusion.where
  86.4 2.6 %pad_add_fusion.1.se = s32[18]{0:T(128)} fusion(s32[1]{0:T(128)} %collective-permute-done.1, s32[16]{0:T(128)} %param.9, s32[1]{0:T(128)} %collective-permute-done), kind=kLoop, calls=%fused_computation.12 | loop fusion | flops 36 | bytes 144 | tf_op jit(solution)/shard_map/concatenate | solution.py:379
  88.9 0.0 collective-permute-done.2.head_ref
  88.9 40.9 %combine.1 = bf16[6,512,4096]{2,1,0:T(8,128)(2,1)} custom-call(s32[12288]{0:T(1024)} %reshape_reshape.3.conn, s32[18]{0:T(128)} %pad_add_fusion.1.se, s32[64,1,192]{2,1,0:T(1,128)} %copy.14.grow_ref, bf16[64,6,192]{2,1,0:T(8,128)(2,1)} %copy.15.s_ref, bf16[16,512,1024]{2,1,0:T(8,128)(2,1)} %rec_ref.1, bf16[256,1024]{1,0:T(8,128)(2,1)} %collective-permute-done.2.head_ref, ...), custom_call_target="tpu_custom_call" | custom-call | tf_op jit(solution)/shard_map/combine/pallas_call | solution.py:105
  129.8 0.0 collective-permute-done.7.refs_4_
  129.9 0.0 all-gather.7.cloned.1.call-done
  129.9 40.0 %product.1 = bf16[3072,1024]{1,0:T(8,128)(2,1)} custom-call(s32[2]{0:T(128)} %pad_add_fusion.where, bf16[3072,4096]{1,0:T(8,128)(2,1)} %bitcast.51, bf16[2048,128]{1,0:T(8,128)(2,1)} %copy-done.1, bf16[2048,128]{1,0:T(8,128)(2,1)} %copy-done.3, bf16[2048,128]{1,0:T(8,128)(2,1)} %copy-done.4, bf16[2048,128]{1,0:T(8,128)(2,1)} %collective-permute-done.6.refs_3_, ...), custom_call_target="tpu_custom_call" | custom-call | tf_op jit(solution)/shard_map/product/pallas_call | solution.py:313
  (23 shorter events, 0.1 us)
Async XLA Ops:
  6.5 33.1 %all-gather.5.cloned.1.call-start = ((), (), s32[]{:S(2)}) async-start(), calls=%async_computation | async-start | bytes 2359296 | tf_op jit(solution)/shard_map/all_gather | solution.py:353
  8.3 121.6 %all-gather.7.cloned.1.call-start = ((), (), s32[]{:S(2)}) async-start(), calls=%async_computation.1 | async-start | bytes 4718592 | tf_op jit(solution)/shard_map/all_gather | solution.py:357
  8.4 8.2 %collective-permute-start.13 = (bf16[16,8192]{1,0:T(8,128)(2,1)S(1)}, bf16[16,8192]{1,0:T(8,128)(2,1)S(1)}, u32[]{:S(2)}, u32[]{:S(2)}) collective-permute-start(bf16[16,8192]{1,0:T(8,128)(2,1)S(1)} %get-tuple-element.19.refs_0_), channel_id=1, source_target_pairs={{0,24},{8,16},{16,8},{24,0},{1,25},{9,17},{17,9},{25,1},{2,26},{10... | collective-permute-start | bytes 786440 | tf_op jit(solution)/shard_map/ppermute | solution.py:354
  9.7 13.5 %collective-permute-start.12 = (bf16[16,8192]{1,0:T(8,128)(2,1)S(1)}, bf16[16,8192]{1,0:T(8,128)(2,1)S(1)}, u32[]{:S(2)}, u32[]{:S(2)}) collective-permute-start(bf16[16,8192]{1,0:T(8,128)(2,1)S(1)} %get-tuple-element.19.refs_0_), channel_id=1, source_target_pairs={{0,16},{8,24},{16,0},{24,8},{1,17},{9,25},{17,1},{25,9},{2,18},{10... | collective-permute-start | bytes 786440 | tf_op jit(solution)/shard_map/ppermute | solution.py:354
  9.9 13.3 %collective-permute-start.11 = (bf16[16,8192]{1,0:T(8,128)(2,1)S(1)}, bf16[16,8192]{1,0:T(8,128)(2,1)S(1)}, u32[]{:S(2)}, u32[]{:S(2)}) collective-permute-start(bf16[16,8192]{1,0:T(8,128)(2,1)S(1)} %get-tuple-element.19.refs_0_), channel_id=1, source_target_pairs={{0,8},{8,0},{16,24},{24,16},{1,9},{9,1},{17,25},{25,17},{2,10},{10... | collective-permute-start | bytes 786440 | tf_op jit(solution)/shard_map/ppermute | solution.py:354
  33.7 36.1 %collective-permute-start.3 = (bf16[256,1024]{1,0:T(8,128)(2,1)S(1)}, bf16[256,1024]{1,0:T(8,128)(2,1)S(1)}, u32[]{:S(2)}, u32[]{:S(2)}) collective-permute-start(bf16[256,1024]{1,0:T(8,128)(2,1)S(1)} %get-tuple-element.17), channel_id=1, source_target_pairs={{1,0},{2,1},{3,2},{4,3},{5,4},{6,5},{7,6},{9,8},{10,9},{11,10},{12... | collective-permute-start | bytes 1572872 | tf_op jit(solution)/shard_map/ppermute | solution.py:376
  39.6 1.6 copy-start
  53.3 76.5 %copy-start.1 = (bf16[2048,128]{1,0:T(8,128)(2,1)}, bf16[2048,128]{1,0:T(8,128)(2,1)S(1)}, u32[]{:S(2)}) copy-start(bf16[2048,128]{1,0:T(8,128)(2,1)S(1)} %get-tuple-element.13.refs_0_) | copy-start | bytes 1572868
  53.3 17.1 %collective-permute-start.4 = (bf16[2048,128]{1,0:T(8,128)(2,1)S(1)}, bf16[2048,128]{1,0:T(8,128)(2,1)S(1)}, u32[]{:S(2)}, u32[]{:S(2)}) collective-permute-start(bf16[2048,128]{1,0:T(8,128)(2,1)S(1)} %get-tuple-element.14), channel_id=1, source_target_pairs={{0,8},{8,0},{16,24},{24,16},{1,9},{9,1},{17,25},{25,17},{2,10},{10... | collective-permute-start | bytes 1572872 | tf_op jit(solution)/shard_map/ppermute | solution.py:369
  53.7 16.8 %collective-permute-start.5 = (bf16[2048,128]{1,0:T(8,128)(2,1)S(1)}, bf16[2048,128]{1,0:T(8,128)(2,1)S(1)}, u32[]{:S(2)}, u32[]{:S(2)}) collective-permute-start(bf16[2048,128]{1,0:T(8,128)(2,1)S(1)} %get-tuple-element.15), channel_id=1, source_target_pairs={{0,16},{8,24},{16,0},{24,8},{1,17},{9,25},{17,1},{25,9},{2,18},{10... | collective-permute-start | bytes 1572872 | tf_op jit(solution)/shard_map/ppermute | solution.py:369
  54.9 24.0 %collective-permute-start.6 = (bf16[2048,128]{1,0:T(8,128)(2,1)S(1)}, bf16[2048,128]{1,0:T(8,128)(2,1)}, u32[]{:S(2)}, u32[]{:S(2)}) collective-permute-start(bf16[2048,128]{1,0:T(8,128)(2,1)S(1)} %get-tuple-element.16), channel_id=1, source_target_pairs={{0,24},{8,16},{16,8},{24,0},{1,25},{9,17},{17,9},{25,1},{2,26},{10... | collective-permute-start | bytes 1572872 | tf_op jit(solution)/shard_map/ppermute | solution.py:369
  57.4 4.5 %collective-permute-start = (s32[1]{0:T(128)}, s32[1]{0:T(128)}, u32[]{:S(2)}, u32[]{:S(2)}) collective-permute-start(s32[1]{0:T(128)} %get-tuple-element.25), channel_id=1, source_target_pairs={{0,1},{1,2},{2,3},{3,4},{4,5},{5,6},{6,7},{8,9},{9,10},{10,11},{11... | collective-permute-start | bytes 20 | tf_op jit(solution)/shard_map/ppermute | solution.py:377
  62.0 5.9 %collective-permute-start.1 = (s32[1]{0:T(128)}, s32[1]{0:T(128)}, u32[]{:S(2)}, u32[]{:S(2)}) collective-permute-start(s32[1]{0:T(128)} %get-tuple-element.26), channel_id=1, source_target_pairs={{1,0},{2,1},{3,2},{4,3},{5,4},{6,5},{7,6},{9,8},{10,9},{11,10},{12... | collective-permute-start | bytes 20 | tf_op jit(solution)/shard_map/ppermute | solution.py:378
  67.9 21.1 %collective-permute-start.2 = (bf16[256,1024]{1,0:T(8,128)(2,1)}, bf16[256,1024]{1,0:T(8,128)(2,1)}, u32[]{:S(2)}, u32[]{:S(2)}) collective-permute-start(bf16[256,1024]{1,0:T(8,128)(2,1)} %get-tuple-element.18), channel_id=1, source_target_pairs={{0,1},{1,2},{2,3},{3,4},{4,5},{5,6},{6,7},{8,9},{9,10},{10,11},{11... | collective-permute-start | bytes 1572872 | tf_op jit(solution)/shard_map/ppermute | solution.py:375
  69.8 19.1 %copy-start.2 = (bf16[256,1024]{1,0:T(8,128)(2,1)}, bf16[256,1024]{1,0:T(8,128)(2,1)S(1)}, u32[]{:S(2)}) copy-start(bf16[256,1024]{1,0:T(8,128)(2,1)S(1)} %collective-permute-done.3.tail_ref) | copy-start | bytes 1572868
  69.8 60.0 %collective-permute-start.7 = (bf16[2048,128]{1,0:T(8,128)(2,1)S(1)}, bf16[2048,128]{1,0:T(8,128)(2,1)}, u32[]{:S(2)}, u32[]{:S(2)}) collective-permute-start(bf16[2048,128]{1,0:T(8,128)(2,1)S(1)} %get-tuple-element.13.refs_0_), channel_id=1, source_target_pairs={{0,1},{1,0},{2,3},{3,2},{4,5},{5,4},{6,7},{7,6},{8,9},{9,8},{10,11... | collective-permute-start | bytes 1572872 | tf_op jit(solution)/shard_map/ppermute | solution.py:370
  70.4 59.4 %copy-start.3 = (bf16[2048,128]{1,0:T(8,128)(2,1)}, bf16[2048,128]{1,0:T(8,128)(2,1)S(1)}, u32[]{:S(2)}) copy-start(bf16[2048,128]{1,0:T(8,128)(2,1)S(1)} %collective-permute-done.4.refs_1_) | copy-start | bytes 1572868
  70.4 59.4 %collective-permute-start.8 = (bf16[2048,128]{1,0:T(8,128)(2,1)S(1)}, bf16[2048,128]{1,0:T(8,128)(2,1)}, u32[]{:S(2)}, u32[]{:S(2)}) collective-permute-start(bf16[2048,128]{1,0:T(8,128)(2,1)S(1)} %collective-permute-done.4.refs_1_), channel_id=1, source_target_pairs={{0,1},{1,0},{2,3},{3,2},{4,5},{5,4},{6,7},{7,6},{8,9},{9,8},{10,11... | collective-permute-start | bytes 1572872 | tf_op jit(solution)/shard_map/ppermute | solution.py:370
  70.5 59.3 %copy-start.4 = (bf16[2048,128]{1,0:T(8,128)(2,1)}, bf16[2048,128]{1,0:T(8,128)(2,1)S(1)}, u32[]{:S(2)}) copy-start(bf16[2048,128]{1,0:T(8,128)(2,1)S(1)} %collective-permute-done.5.refs_2_) | copy-start | bytes 1572868
  70.5 59.4 %collective-permute-start.9 = (bf16[2048,128]{1,0:T(8,128)(2,1)S(1)}, bf16[2048,128]{1,0:T(8,128)(2,1)}, u32[]{:S(2)}, u32[]{:S(2)}) collective-permute-start(bf16[2048,128]{1,0:T(8,128)(2,1)S(1)} %collective-permute-done.5.refs_2_), channel_id=1, source_target_pairs={{0,1},{1,0},{2,3},{3,2},{4,5},{5,4},{6,7},{7,6},{8,9},{9,8},{10,11... | collective-permute-start | bytes 1572872 | tf_op jit(solution)/shard_map/ppermute | solution.py:370
  78.9 50.9 %collective-permute-start.10 = (bf16[2048,128]{1,0:T(8,128)(2,1)}, bf16[2048,128]{1,0:T(8,128)(2,1)}, u32[]{:S(2)}, u32[]{:S(2)}) collective-permute-start(bf16[2048,128]{1,0:T(8,128)(2,1)} %collective-permute-done.6.refs_3_), channel_id=1, source_target_pairs={{0,1},{1,0},{2,3},{3,2},{4,5},{5,4},{6,7},{7,6},{8,9},{9,8},{10,11... | collective-permute-start | bytes 1572872 | tf_op jit(solution)/shard_map/ppermute | solution.py:370
Sparse Core Ops, SparseCore 0:
  9.0 30.6 all-gather.4
  41.2 49.8 all-gather.6

commit v3 on v2

--- a/solution.py
+++ b/solution.py
@@ -12,7 +12,7 @@
 LANES = 128
 
 
-def combine_kernel(conn, se, grow_ref, s_ref, rec_ref, head_ref, tail_ref, w_ref, tbl, g0, g1,
+def combine_kernel(conn, se, grow_ref, s_ref, rec_ref, head_ref, tail_ref, w_ref, tbl, g0, g1, g2, g3,
     *, nfill, blk, nlt, nse, nc, ndof, inner, ts, gs,
 ):
     step = pl.program_id(0)
@@ -27,39 +27,47 @@
                 part = src[pl.ds(at, 16), j * LANES:(j + 1) * LANES].astype(jnp.float32)
                 tbl[pl.ds((base + at) * ts + j, 16, stride=ts), :] = part
             return carry
-        lax.fori_loop(0, count // 16, one, 0, unroll=2)
+        lax.fori_loop(0, count // 16, one, 0, unroll=4)
 
     def gather(group, dst):
         first = group * rows
         for q in range(rows):
             dst[pl.ds(q, nlt, stride=gs), :] = tbl[pl.ds(conn[first + q] * ts, nlt), :]
 
-    def matmul(i, src):
-        own = (
-            lax.broadcasted_iota(jnp.int32, (SUB, rows), 1) % SUB
-            == lax.broadcasted_iota(jnp.int32, (SUB, rows), 0)
-        )
+    own = (
+        lax.broadcasted_iota(jnp.int32, (SUB, rows), 1) % SUB
+        == lax.broadcasted_iota(jnp.int32, (SUB, rows), 0)
+    )
+
+    def left(i):
         where = (grow_ref[i] + (blk - HW)) // blk
         tag = jnp.zeros((1, rows), jnp.int32)
         for b in range(nfill + 2):
             tag = jnp.where(where == b, se[b], tag)
         tag = jnp.where(own, jnp.broadcast_to(tag, (SUB, rows)), -1)
+        smat = s_ref[i].astype(jnp.float32)
         parts = []
-        smat = s_ref[i].astype(jnp.float32)
         for s in range(nse):
             hit = tag == s
             for c in range(nc):
                 parts.append(jnp.where(hit, jnp.broadcast_to(smat[c:c + 1], (SUB, rows)), 0.0))
-        lhs = jnp.concatenate(parts, axis=0).astype(jnp.bfloat16)
-        at = pl.multiple_of(i * SUB, SUB)
+        return jnp.concatenate(parts, axis=0).astype(jnp.bfloat16)
+
+    def matmul(i, srcs):
+        lhs = [left(i), left(i + 1)]
+        at = pl.multiple_of(i * SUB, 2 * SUB)
         for j in range(0, nlt, 2):
-            rhs = jnp.concatenate(
-                [src[(j + d) * gs:(j + d) * gs + rows, :].astype(jnp.bfloat16) for d in range(2)], axis=1)
-            res = jnp.dot(lhs, rhs, preferred_element_type=jnp.float32).astype(jnp.bfloat16)
+            res = []
+            for l, src in zip(lhs, srcs):
+                rhs = jnp.concatenate(
+                    [src[(j + d) * gs:(j + d) * gs + rows, :].astype(jnp.bfloat16) for d in range(2)], axis=1)
+                res.append(jnp.dot(l, rhs, preferred_element_type=jnp.float32))
             for s in range(nse):
                 col = (s * nlt + j) * LANES
                 for c in range(nc):
-                    w_ref[c, pl.ds(at, SUB), col:col + 2 * LANES] = res[(s * nc + c) * SUB:(s * nc + c + 1) * SUB]
+                    r0 = (s * nc + c) * SUB
+                    both = jnp.concatenate([r[r0:r0 + SUB] for r in res], axis=0)
+                    w_ref[c, pl.ds(at, 2 * SUB), col:col + 2 * LANES] = both.astype(jnp.bfloat16)
 
     @pl.when(step < nfill)
     def _():
@@ -78,15 +86,19 @@
         @pl.when(step == nfill)
         def _():
             gather(0, g0)
-
-        def two(i, carry):
-            n = base + 2 * i
-            gather(n + 1, g1)
-            matmul(2 * i, g0)
-            gather(jnp.minimum(n + 2, last), g0)
-            matmul(2 * i + 1, g1)
+            gather(1, g1)
+
+        def four(i, carry):
+            n = base + 4 * i
+            gather(n + 2, g2)
+            gather(n + 3, g3)
+            matmul(4 * i, (g0, g1))
+            gather(jnp.minimum(n + 4, last), g0)
+            gather(jnp.minimum(n + 5, last), g1)
+            matmul(4 * i + 2, (g2, g3))
             return carry
-        lax.fori_loop(0, inner // 2, two, 0)
+        lax.fori_loop(0, inner // 4, four, 0)
+
 
 def combine(conn, se, grow, smat, recovery, head, tail, nse, inner=4):
     nblk, blk, nb = recovery.shape
@@ -118,11 +130,10 @@
             out_specs=pl.BlockSpec((nc, SUB * inner, nse * nb), lambda i, c, s: (0, later(i), 0)),
             scratch_shapes=[
                 pltpu.VMEM(((nblk * blk + 2 * HW) * ts, LANES), jnp.float32),
-                pltpu.VMEM((gs * nlt, LANES), jnp.float32),
-                pltpu.VMEM((gs * nlt, LANES), jnp.float32),
-            ],
+            ] + [pltpu.VMEM((gs * nlt, LANES), jnp.float32)] * 4,
         ),
         compiler_params=pltpu.CompilerParams(dimension_semantics=("arbitrary",), vmem_limit_bytes=60 << 20),
+        cost_estimate=pl.CostEstimate(flops=30 * 10**9, bytes_accessed=120 << 20, transcendentals=0),
         name="combine",
     )(conn, se, grow, smat, recovery, head, tail)
 
@@ -241,33 +252,15 @@
     )(idx.reshape(-1), src)
 
 
-def product_kernel(
-    where, w_ref, *refs, ngroup, nrow, tper, half, parts
-):
-    mine = refs[:ngroup]
-    theirs = refs[ngroup:2 * ngroup]
-    near_hbm, o_ref, bt, near, sem = refs[2 * ngroup:]
-    group = where[0]
-    core = where[1]
-    nh = tper * nrow // LANES
+def product_near_kernel(w_ref, near_hbm, o_ref, bt, near, sem, *, tper, nh, npair, parts):
     per = LANES // tper
-    npair = ngroup * half // tper
-    rows = bt.shape[0] // 2
     nk = bt.shape[0] // parts
 
     @pl.when(pl.program_id(0) == 0)
     def _():
-        last = pltpu.make_async_copy(near_hbm, near, sem.at[2 * ngroup])
-        last.start()
-        copies = []
-        for s in range(ngroup):
-            cols = slice(s * LANES, (s + 1) * LANES)
-            for d, ref in ((0, mine[s]), (1, theirs[s])):
-                at = pl.multiple_of(jnp.where(core == d, 0, 1) * rows, rows)
-                copies.append(pltpu.make_async_copy(ref, bt.at[pl.ds(at, rows), cols], sem.at[2 * s + d]))
-        for c in copies:
-            c.start()
-        last.wait()
+        copy = pltpu.make_async_copy(near_hbm, near, sem.at[0])
+        copy.start()
+        copy.wait()
         step_rows = min(nk, 256)
         lane = lax.broadcasted_iota(jnp.int32, (step_rows, LANES), 1) // tper
 
@@ -282,11 +275,60 @@
                             shift = (tper * j - (kp * (LANES // parts) + tper * p)) % LANES
                             moved = pltpu.roll(got[j], shift, 1) if shift else got[j]
                             tile = moved if tile is None else jnp.where(lane == j, moved, tile)
-                        col = (ngroup + h * npair + p) * LANES
+                        col = (h * npair + p) * LANES
                         bt[pl.ds(kp * nk + at, step_rows), col:col + LANES] = tile.astype(jnp.bfloat16)
             return carry
 
         lax.fori_loop(0, nk // step_rows, arrange, 0)
+
+    o_ref[...] = jnp.dot(w_ref[...], bt[...], preferred_element_type=jnp.float32).astype(jnp.bfloat16)
+
+
+def product_near(w, near, ngroup, tper):
+    m, k = w.shape
+    nrow, nk, _ = near.shape
+    nh = tper * nrow // LANES
+    npair = ngroup // 2
+    cols = nh * npair * LANES
+    mb = 512
+    return pl.pallas_call(
+        functools.partial(product_near_kernel, tper=tper, nh=nh, npair=npair, parts=k // nk),
+        out_shape=jax.ShapeDtypeStruct((m, cols), jnp.bfloat16),
+        grid=(m // mb,),
+        in_specs=[pl.BlockSpec((mb, k), lambda i: (i, 0)), pl.BlockSpec(memory_space=pl.ANY)],
+        out_specs=pl.BlockSpec((mb, cols), lambda i: (i, 0)),
+        scratch_shapes=[
+            pltpu.VMEM((k, cols), jnp.bfloat16),
+            pltpu.VMEM(near.shape, jnp.bfloat16),
+            pltpu.SemaphoreType.DMA((1,)),
+        ],
+        compiler_params=pltpu.CompilerParams(
+            dimension_semantics=("arbitrary",), vmem_limit_bytes=56 << 20
+        ),
+        cost_estimate=pl.CostEstimate(flops=2 * m * k * cols, bytes_accessed=40 << 20, transcendentals=0),
+        name="product_near",
+    )(w, near)
+
+
+def product_far_kernel(where, w_ref, near_ref, *refs, ngroup, nh, half):
+    mine = refs[:ngroup]
+    theirs = refs[ngroup:2 * ngroup]
+    o_ref, bt, sem = refs[2 * ngroup:]
+    group = where[0]
+    core = where[1]
+    npair = ngroup // 2
+    rows = bt.shape[0] // 2
+
+    @pl.when(pl.program_id(0) == 0)
+    def _():
+        copies = []
+        for s in range(ngroup):
+            cols = slice(s * LANES, (s + 1) * LANES)
+            for d, ref in ((0, mine[s]), (1, theirs[s])):
+                at = pl.multiple_of(jnp.where(core == d, 0, 1) * rows, rows)
+                copies.append(pltpu.make_async_copy(ref, bt.at[pl.ds(at, rows), cols], sem.at[2 * s + d]))
+        for c in copies:
+            c.start()
         for c in copies:
             c.wait()
 
@@ -296,8 +338,8 @@
         far = res[:, s * LANES:(s + 1) * LANES]
         for h in range(nh):
             first = pltpu.roll(far, LANES - half * h, 1) if h else far
-            at = (ngroup + h * npair + s // 2) * LANES
-            second = res[:, at:at + LANES]
+            at = (h * npair + s // 2) * LANES
+            second = near_ref[:, at:at + LANES].astype(jnp.float32)
             if s % 2 == 0:
                 second = pltpu.roll(second, half, 1)
             tile = jnp.where(slot == 0, first, second).astype(jnp.bfloat16)
@@ -305,33 +347,31 @@
             o_ref[:, pl.ds(col, LANES)] = tile
 
 
-def product(where, w, mine, theirs, near, tper, snap):
+def product_far(where, w, near, mine, theirs, half, snap):
     m, k = w.shape
     ngroup = len(mine)
-    nrow, nk, _ = near.shape
-    mb = 256
+    cols = near.shape[1]
+    mb = 512
     return pl.pallas_call(
-        functools.partial(
-            product_kernel, ngroup=ngroup, nrow=nrow, tper=tper, half=tper // 2, parts=k // nk
-        ),
+        functools.partial(product_far_kernel, ngroup=ngroup, nh=snap // (ngroup * LANES), half=half),
         out_shape=jax.ShapeDtypeStruct((m, snap), jnp.bfloat16),
         grid_spec=pltpu.PrefetchScalarGridSpec(
             num_scalar_prefetch=1,
             grid=(m // mb,),
-            in_specs=[pl.BlockSpec((mb, k), lambda i, c: (i, 0))]
-            + [pl.BlockSpec(memory_space=pl.ANY)] * (2 * ngroup + 1),
+            in_specs=[pl.BlockSpec((mb, k), lambda i, c: (i, 0)), pl.BlockSpec((mb, cols), lambda i, c: (i, 0))]
+            + [pl.BlockSpec(memory_space=pl.ANY)] * (2 * ngroup),
             out_specs=pl.BlockSpec((mb, snap), lambda i, c: (i, 0)),
             scratch_shapes=[
-                pltpu.VMEM((k, snap), jnp.bfloat16),
-                pltpu.VMEM(near.shape, jnp.bfloat16),
-                pltpu.SemaphoreType.DMA((2 * ngroup + 1,)),
+                pltpu.VMEM((k, ngroup * LANES), jnp.bfloat16),
+                pltpu.SemaphoreType.DMA((2 * ngroup,)),
             ],
         ),
         compiler_params=pltpu.CompilerParams(
             dimension_semantics=("arbitrary",), vmem_limit_bytes=56 << 20
         ),
-        name="product",
-    )(where, w, *mine, *theirs, near)
+        cost_estimate=pl.CostEstimate(flops=2 * m * k * cols, bytes_accessed=40 << 20, transcendentals=0),
+        name="product_far",
+    )(where, w, near, *mine, *theirs)
 
 
 def body(snapshots, bnd_index, recovery, block_se, connect, stress_mat):
@@ -353,22 +393,6 @@
     along_row = lax.all_gather(top, "row", axis=0, tiled=False)
     along_group = [bottom] + [lax.ppermute(bottom, "group", swap(s)) for s in range(1, ngroup)]
 
-    own_idx = lax.dynamic_slice_in_dim(bnd_index, group * nse, nse, 0).reshape(-1)
-    near = lax.all_gather(pick_near(own_idx, along_group), "row", axis=0, tiled=False)
-
-    rows = nse * nb // 2
-    far_idx = jnp.stack([
-        lax.dynamic_slice_in_dim(
-            lax.dynamic_slice_in_dim(bnd_index, (group ^ s) * nse, nse, 0).reshape(-1), core * rows, rows, 0
-        )
-        for s in range(ngroup)
-    ])
-    per = LANES // tper
-    order = [per * h + j for j in range(per) for h in range(nrow // per)]
-    far = pick_far(far_idx, along_row, order)
-    mine = [far[0]] + [lax.ppermute(far[s], "group", swap(s)) for s in range(1, ngroup)]
-    theirs = [lax.ppermute(x, "row", other) for x in mine]
-
     ends = nrow - 1
     up = [(i, i + 1) for i in range(ends)]
     down = [(i + 1, i) for i in range(ends)]
@@ -382,11 +406,34 @@
     conn = connect.T.reshape(ndof, ngrp, SUB).transpose(1, 0, 2).reshape(ngrp, 1, ndof * SUB)
     smat = stress_mat.transpose(1, 2, 0).reshape(nc, ndof, ngrp, SUB).transpose(2, 0, 1, 3)
     smat = smat.reshape(ngrp, nc, ndof * SUB)
-    flat, far0 = lax.optimization_barrier((conn.reshape(-1), far[0]))
-    mine[0] = far0
+    flat = conn.reshape(-1)
+    where = jnp.stack([group, core]).astype(jnp.int32)
+
+    own_idx = lax.dynamic_slice_in_dim(bnd_index, group * nse, nse, 0).reshape(-1)
+    rows = nse * nb // 2
+    far_idx = jnp.stack([
+        lax.dynamic_slice_in_dim(
+            lax.dynamic_slice_in_dim(bnd_index, (group ^ s) * nse, nse, 0).reshape(-1), core * rows, rows, 0
+        )
+        for s in range(ngroup)
+    ]).reshape(-1)
+
+    own_idx, far_idx, flat, conn, smat, se_all, head, tail, where = lax.optimization_barrier(
+        (own_idx, far_idx, flat, conn, smat, se_all, head, tail, where)
+    )
+    near = lax.all_gather(pick_near(own_idx, along_group), "row", axis=0, tiled=False)
+    per = LANES // tper
+    order = [per * h + j for j in range(per) for h in range(nrow // per)]
+    far = pick_far(far_idx.reshape(ngroup, rows), along_row, order)
+    mine = [far[0]] + [lax.ppermute(far[s], "group", swap(s)) for s in range(1, ngroup)]
+
+    flat, mine[0] = lax.optimization_barrier((flat, mine[0]))
     w = combine(flat, se_all, conn, smat, recovery, head, tail, nse)
-    where = jnp.stack([group, core]).astype(jnp.int32)
-    out = product(where, w.reshape(nc * nel, nse * nb), mine, theirs, near, tper, snap)
+    *mine, w = lax.optimization_barrier((*mine, w))
+    theirs = [lax.ppermute(x, "row", other) for x in mine]
+    w = w.reshape(nc * nel, nse * nb)
+    out = product_near(w, near, ngroup, tper)
+    out = product_far(where, w, out, mine, theirs, half, snap)
     return out.reshape(nc, nel, snap).transpose(1, 0, 2)
 
 

time: 179 us -> 173 us (0.966)
  starting transfers between devices: 26.5 us -> 18.1 us
  Pallas kernels: 101 us -> 106 us
    ppermute x1, waiting for transfers between devices: 2.42 us -> 17.1 us  [body(): tail_se = lax.ppermute(block_se[:1], 'row', down)]
    ppermute x3, waiting for transfers between devices: 11.2 us -> 1.73 us  [body(): lax.ppermute(bottom, 'group', swap(s))]
    ppermute x4, starting transfers between devices: 9.52 us -> 1.8 us  [body(): theirs = [lax.ppermute(x, 'row', other) for x in mine]]
    pallas_call x1 -> x2, Pallas kernels: 40 us -> 46.6 us  [the longest x1 23.7 us: product_near(): pl.pallas_call(functools.partial(product_near_kernel, tper=tper, nh=nh, n...]
    all_gather x1, waiting for transfers between devices: 3.29 us -> 0.01 us  [body(): along_row = lax.all_gather(top, 'row', axis=0, tiled=False)]
    pallas_call x1, Pallas kernels: 40.9 us -> 38.6 us  [combine(): pl.pallas_call(kern, out_shape=jax.ShapeDtypeStruct((nc, nel, nse * nb),...]
  transfers between devices with their start and end apart: 16 -> 16, of which waited for: 6 -> 2; matrix products, arithmetic and copies ran while one was open for 8% -> 6% of each run, Pallas kernels for 35% -> 48%
where the time goes in v3:
time: 173 us; the launch traced here: 172 us
  Pallas kernels  106 us (61%)
  waiting for transfers between devices  18.9 us (11%)
  starting transfers between devices  18.1 us (10%)
  between operations  13.8 us (8%)
  local copies, waits for them, and re-layouts  12.8 us (7%)
  other arithmetic  2.36 us (1%)
    pallas_call x1, Pallas kernels, combine(): pl.pallas_call(kern, out_shape=jax.ShapeDtypeStruct((nc, nel, nse * nb),...  38.6 us
    pallas_call x1, Pallas kernels, product_near(): pl.pallas_call(functools.partial(product_near_kernel, tper=tper, nh=nh, n...  23.7 us
    pallas_call x1, Pallas kernels, product_far(): pl.pallas_call(functools.partial(product_far_kernel, ngroup=ngroup, nh=sn...  23 us
    ppermute x1, waiting for transfers between devices, body(): tail_se = lax.ppermute(block_se[:1], 'row', down)  17.1 us
    pallas_call x1, Pallas kernels, pick_far(): pl.pallas_call(functools.partial(pick_far_kernel, nout=nout, order=order,...  12.1 us
    pallas_call x1, Pallas kernels, pick_near(): pl.pallas_call(functools.partial(pick_near_kernel, nsrc=len(srcs), half=h...  8.37 us
    ppermute x1, starting transfers between devices, body(): head_se = lax.ppermute(block_se[-1:], 'row', up)  4.31 us
    ppermute x1, starting transfers between devices, body(): head = lax.ppermute(recovery[nblk - 1, blk - HW:], 'row', up)  3.64 us
  transfers between devices with their start and end apart: 16, of which 2 were waited for; matrix products, arithmetic and copies ran while one was open for 6% of the time, Pallas kernels for 48%

profile of v3, /device:TPU:11, one launch (start us, length us, event | category | flops | bytes accessed | tf_op | source)
XLA Modules:
  0.0 171.7 jit_solution(3183836893848587430)
XLA Ops:
  6.5 1.8 %fusion = (bf16[16,8192]{1,0:T(8,128)(2,1)S(1)}, bf16[16,8192]{1,0:T(8,128)(2,1)}) fusion(bf16[32,8192]{1,0:T(8,128)(2,1)} %param.6), kind=kLoop, calls=%fused_computation.13 | loop fusion | bytes 1048576 | tf_op jit(solution)/shard_map/slice | solution.py:392
  8.4 0.0 all-gather.5.cloned.1.call-update
  8.4 0.0 all-gather.7.cloned.1.call-start
  8.4 1.3 collective-permute-start.9
  9.7 0.2 collective-permute-start.8
  9.9 1.3 fusion.1
  11.2 4.3 %collective-permute-start = (s32[1]{0:T(128)}, s32[1]{0:T(128)}, u32[]{:S(2)}, u32[]{:S(2)}) collective-permute-start(s32[1]{0:T(128)} %get-tuple-element.53), channel_id=1, source_target_pairs={{0,1},{1,2},{2,3},{3,4},{4,5},{5,6},{6,7},{8,9},{9,10},{10,11},{11... | collective-permute-start | bytes 20 | tf_op jit(solution)/shard_map/ppermute | solution.py:401
  15.6 1.3 slice_bitcast_fusion
  16.8 1.9 %collective-permute-start.3 = (bf16[256,1024]{1,0:T(8,128)(2,1)S(1)}, bf16[256,1024]{1,0:T(8,128)(2,1)}, u32[]{:S(2)}, u32[]{:S(2)}) collective-permute-start(bf16[256,1024]{1,0:T(8,128)(2,1)S(1)} %get-tuple-element.45), channel_id=1, source_target_pairs={{1,0},{2,1},{3,2},{4,3},{5,4},{6,5},{7,6},{9,8},{10,9},{11,10},{12... | collective-permute-start | bytes 1572872 | tf_op jit(solution)/shard_map/ppermute | solution.py:400
  18.8 3.6 %collective-permute-start.2 = (bf16[256,1024]{1,0:T(8,128)(2,1)S(1)}, bf16[256,1024]{1,0:T(8,128)(2,1)}, u32[]{:S(2)}, u32[]{:S(2)}) collective-permute-start(bf16[256,1024]{1,0:T(8,128)(2,1)S(1)} %get-tuple-element.46), channel_id=1, source_target_pairs={{0,1},{1,2},{2,3},{3,4},{4,5},{5,6},{6,7},{8,9},{9,10},{10,11},{11... | collective-permute-start | bytes 1572872 | tf_op jit(solution)/shard_map/ppermute | solution.py:399
  22.5 0.9 dynamic-slice_bitcast_fusion.2
  23.4 1.9 %collective-permute-start.1 = (s32[1]{0:T(128)}, s32[1]{0:T(128)}, u32[]{:S(2)}, u32[]{:S(2)}) collective-permute-start(s32[1]{0:T(128)} %get-tuple-element.54), channel_id=1, source_target_pairs={{1,0},{2,1},{3,2},{4,3},{5,4},{6,5},{7,6},{9,8},{10,9},{11,10},{12... | collective-permute-start | bytes 20 | tf_op jit(solution)/shard_map/ppermute | solution.py:402
  25.4 17.1 %collective-permute-done.1 = s32[1]{0:T(128)} collective-permute-done((s32[1]{0:T(128)}, s32[1]{0:T(128)}, u32[]{:S(2)}, u32[]{:S(2)}) %collective-permute-start.1) | collective-permute-done | bytes 36 | tf_op jit(solution)/shard_map/ppermute | solution.py:402
  42.5 0.3 collective-permute-start.7
  42.8 0.9 copy.9
  43.7 0.2 copy.11
  43.9 0.3 copy.10
  44.2 0.9 reshape_reshape.3.conn
  45.1 0.4 copy.12
  45.5 0.5 copy.13
  46.0 0.6 pad_add_fusion.1.where
  46.6 1.7 pad_add_fusion.se
  48.4 0.0 collective-permute-done.3.tail_ref
  48.4 0.0 collective-permute-done.2.head_ref
  48.4 0.0 collective-permute-done.9.refs_3_
  48.4 1.7 %collective-permute-done.7.refs_1_ = bf16[16,8192]{1,0:T(8,128)(2,1)S(1)} collective-permute-done((bf16[16,8192]{1,0:T(8,128)(2,1)S(1)}, bf16[16,8192]{1,0:T(8,128)(2,1)S(1)}, u32[]{:S(2)}, u32[]{:S(2)}) %collective-permute-start.7) | collective-permute-done | bytes 262176 | tf_op jit(solution)/shard_map/ppermute | solution.py:394
  50.1 8.4 %pick_near.1 = bf16[2048,128]{1,0:T(8,128)(2,1)} custom-call(s32[4096]{0:T(1024)S(1)} %bitcast.50, bf16[16,8192]{1,0:T(8,128)(2,1)S(1)} %get-tuple-element.47.refs_0_, bf16[16,8192]{1,0:T(8,128)(2,1)S(1)} %collective-permute-done.7.refs_1_, bf16[16,8192]{1,0:T(8,128)(2,1)S(1)} %collective-permute-done.8.refs_2_, ...), custom_call_target="tpu_custom_call" | custom-call | tf_op jit(solution)/shard_map/pick_near/pallas_call | solution.py:180
  58.5 0.0 all-gather.7.cloned.1.call-update
  58.5 0.7 copy.14.grow_ref
  59.2 1.0 copy.15.s_ref
  60.2 1.6 copy-done
  61.8 12.1 %pick_far.1 = (bf16[2048,128]{1,0:T(8,128)(2,1)S(1)}, bf16[2048,128]{1,0:T(8,128)(2,1)S(1)}, bf16[2048,128]{1,0:T(8,128)(2,1)S(1)}, bf16[2048,128]{1,0:T(8,128)(2,1)S(1)}) custom-call(s32[8192]{0:T(1024)S(1)} %bitcast.48, bf16[8,16,8192]{2,1,0:T(8,128)(2,1)S(1)} %bitcast.47), custom_call_target="tpu_custom_call" | custom-call | tf_op jit(solution)/shard_map/pick_far/pallas_call | solution.py:236
  73.9 0.3 collective-permute-start.4
  74.2 1.2 collective-permute-start.5
  75.4 1.2 collective-permute-start.6
  76.6 38.6 %combine.1 = bf16[6,512,4096]{2,1,0:T(8,128)(2,1)} custom-call(s32[12288]{0:T(1024)} %reshape_reshape.3.conn, s32[18]{0:T(128)} %pad_add_fusion.se, s32[64,1,192]{2,1,0:T(1,128)} %copy.14.grow_ref, bf16[64,6,192]{2,1,0:T(8,128)(2,1)} %copy.15.s_ref, bf16[16,512,1024]{2,1,0:T(8,128)(2,1)} %rec_ref.1, bf16[256,1024]{1,0:T(8,128)(2,1)} %collective-permute-done.2.head_ref, ...), custom_call_target="tpu_custom_call" | custom-call | flops 30000001024 | bytes 125829120 | tf_op jit(solution)/shard_map/combine/pallas_call | solution.py:117
  115.2 0.0 collective-permute-done.4.refs_1_
  115.2 0.0 collective-permute-done.5.refs_2_
  115.2 0.0 collective-permute-done.6.refs_3_
  115.3 1.2 collective-permute-start.10
  116.5 0.1 collective-permute-start.11
  116.6 0.4 collective-permute-start.12
  117.0 0.1 collective-permute-start.13
  117.1 23.7 %product_near.1.near_ref = bf16[3072,512]{1,0:T(8,128)(2,1)} custom-call(bf16[3072,4096]{1,0:T(8,128)(2,1)} %bitcast.64, bf16[8,2048,128]{2,1,0:T(8,128)(2,1)} %bitcast.63), custom_call_target="tpu_custom_call" | custom-call | flops 12884901888 | bytes 41943040 | tf_op jit(solution)/shard_map/product_near/pallas_call | solution.py:294
  140.8 0.0 collective-permute-done.11.refs_5_
  140.8 0.8 copy-done.7
  141.7 0.2 copy-done.8
  141.8 23.0 %product_far.1 = bf16[3072,1024]{1,0:T(8,128)(2,1)} custom-call(s32[2]{0:T(128)} %pad_add_fusion.1.where, bf16[3072,4096]{1,0:T(8,128)(2,1)} %bitcast.65, bf16[3072,512]{1,0:T(8,128)(2,1)} %product_near.1.near_ref, bf16[2048,128]{1,0:T(8,128)(2,1)} %copy-done.1, bf16[2048,128]{1,0:T(8,128)(2,1)} %copy-done.4, bf16[2048,128]{1,0:T(8,128)(2,1)} %copy-done.5, ...), custom_call_target="tpu_custom_call" | custom-call | flops 12884901888 | bytes 41943040 | tf_op jit(solution)/shard_map/product_far/pallas_call | solution.py:355
  (32 shorter events, 0.1 us)
Async XLA Ops:
  6.5 40.1 %copy-start.3 = (s32[16]{0:T(128)S(1)}, s32[16]{0:T(128)}, u32[]{:S(2)}) copy-start(s32[16]{0:T(128)} %param.9) | copy-start | bytes 196
  6.5 38.6 %copy-start.2 = (bf16[512,6,24]{0,2,1:T(8,128)(2,1)S(1)}, bf16[512,6,24]{0,2,1:T(8,128)(2,1)}, u32[]{:S(2)}) copy-start(bf16[512,6,24]{0,2,1:T(8,128)(2,1)} %param.11) | copy-start | bytes 442372
  6.5 53.6 %all-gather.5.cloned.1.call-start = ((), (), s32[]{:S(2)}) async-start(), calls=%async_computation | async-start | bytes 2359296 | tf_op jit(solution)/shard_map/all_gather | solution.py:393
  8.4 108.7 %all-gather.7.cloned.1.call-start = ((), (), s32[]{:S(2)}) async-start(), calls=%async_computation.1 | async-start | bytes 4718592 | tf_op jit(solution)/shard_map/all_gather | solution.py:424
  8.4 39.9 %collective-permute-start.9 = (bf16[16,8192]{1,0:T(8,128)(2,1)S(1)}, bf16[16,8192]{1,0:T(8,128)(2,1)S(1)}, u32[]{:S(2)}, u32[]{:S(2)}) collective-permute-start(bf16[16,8192]{1,0:T(8,128)(2,1)S(1)} %get-tuple-element.47.refs_0_), channel_id=1, source_target_pairs={{0,24},{8,16},{16,8},{24,0},{1,25},{9,17},{17,9},{25,1},{2,26},{10... | collective-permute-start | bytes 786440 | tf_op jit(solution)/shard_map/ppermute | solution.py:394
  9.7 38.7 %collective-permute-start.8 = (bf16[16,8192]{1,0:T(8,128)(2,1)S(1)}, bf16[16,8192]{1,0:T(8,128)(2,1)S(1)}, u32[]{:S(2)}, u32[]{:S(2)}) collective-permute-start(bf16[16,8192]{1,0:T(8,128)(2,1)S(1)} %get-tuple-element.47.refs_0_), channel_id=1, source_target_pairs={{0,16},{8,24},{16,0},{24,8},{1,17},{9,25},{17,1},{25,9},{2,18},{10... | collective-permute-start | bytes 786440 | tf_op jit(solution)/shard_map/ppermute | solution.py:394
  11.2 12.2 %collective-permute-start = (s32[1]{0:T(128)}, s32[1]{0:T(128)}, u32[]{:S(2)}, u32[]{:S(2)}) collective-permute-start(s32[1]{0:T(128)} %get-tuple-element.53), channel_id=1, source_target_pairs={{0,1},{1,2},{2,3},{3,4},{4,5},{5,6},{6,7},{8,9},{9,10},{10,11},{11... | collective-permute-start | bytes 20 | tf_op jit(solution)/shard_map/ppermute | solution.py:401
  16.8 31.5 %collective-permute-start.3 = (bf16[256,1024]{1,0:T(8,128)(2,1)S(1)}, bf16[256,1024]{1,0:T(8,128)(2,1)}, u32[]{:S(2)}, u32[]{:S(2)}) collective-permute-start(bf16[256,1024]{1,0:T(8,128)(2,1)S(1)} %get-tuple-element.45), channel_id=1, source_target_pairs={{1,0},{2,1},{3,2},{4,3},{5,4},{6,5},{7,6},{9,8},{10,9},{11,10},{12... | collective-permute-start | bytes 1572872 | tf_op jit(solution)/shard_map/ppermute | solution.py:400
  18.8 29.6 %collective-permute-start.2 = (bf16[256,1024]{1,0:T(8,128)(2,1)S(1)}, bf16[256,1024]{1,0:T(8,128)(2,1)}, u32[]{:S(2)}, u32[]{:S(2)}) collective-permute-start(bf16[256,1024]{1,0:T(8,128)(2,1)S(1)} %get-tuple-element.46), channel_id=1, source_target_pairs={{0,1},{1,2},{2,3},{3,4},{4,5},{5,6},{6,7},{8,9},{9,10},{10,11},{11... | collective-permute-start | bytes 1572872 | tf_op jit(solution)/shard_map/ppermute | solution.py:399
  23.4 19.0 %collective-permute-start.1 = (s32[1]{0:T(128)}, s32[1]{0:T(128)}, u32[]{:S(2)}, u32[]{:S(2)}) collective-permute-start(s32[1]{0:T(128)} %get-tuple-element.54), channel_id=1, source_target_pairs={{1,0},{2,1},{3,2},{4,3},{5,4},{6,5},{7,6},{9,8},{10,9},{11,10},{12... | collective-permute-start | bytes 20 | tf_op jit(solution)/shard_map/ppermute | solution.py:402
  42.5 7.6 %collective-permute-start.7 = (bf16[16,8192]{1,0:T(8,128)(2,1)S(1)}, bf16[16,8192]{1,0:T(8,128)(2,1)S(1)}, u32[]{:S(2)}, u32[]{:S(2)}) collective-permute-start(bf16[16,8192]{1,0:T(8,128)(2,1)S(1)} %get-tuple-element.47.refs_0_), channel_id=1, source_target_pairs={{0,8},{8,0},{16,24},{24,16},{1,9},{9,1},{17,25},{25,17},{2,10},{10... | collective-permute-start | bytes 786440 | tf_op jit(solution)/shard_map/ppermute | solution.py:394
  60.2 1.6 copy-start
  73.9 41.4 %copy-start.1 = (bf16[2048,128]{1,0:T(8,128)(2,1)}, bf16[2048,128]{1,0:T(8,128)(2,1)S(1)}, u32[]{:S(2)}) copy-start(bf16[2048,128]{1,0:T(8,128)(2,1)S(1)} %get-tuple-element.41.refs_0_) | copy-start | bytes 1572868
  73.9 41.3 %collective-permute-start.4 = (bf16[2048,128]{1,0:T(8,128)(2,1)S(1)}, bf16[2048,128]{1,0:T(8,128)(2,1)S(1)}, u32[]{:S(2)}, u32[]{:S(2)}) collective-permute-start(bf16[2048,128]{1,0:T(8,128)(2,1)S(1)} %get-tuple-element.30), channel_id=1, source_target_pairs={{0,8},{8,0},{16,24},{24,16},{1,9},{9,1},{17,25},{25,17},{2,10},{10... | collective-permute-start | bytes 1572872 | tf_op jit(solution)/shard_map/ppermute | solution.py:428
  74.2 41.0 %collective-permute-start.5 = (bf16[2048,128]{1,0:T(8,128)(2,1)S(1)}, bf16[2048,128]{1,0:T(8,128)(2,1)S(1)}, u32[]{:S(2)}, u32[]{:S(2)}) collective-permute-start(bf16[2048,128]{1,0:T(8,128)(2,1)S(1)} %get-tuple-element.31), channel_id=1, source_target_pairs={{0,16},{8,24},{16,0},{24,8},{1,17},{9,25},{17,1},{25,9},{2,18},{10... | collective-permute-start | bytes 1572872 | tf_op jit(solution)/shard_map/ppermute | solution.py:428
  75.4 39.8 %collective-permute-start.6 = (bf16[2048,128]{1,0:T(8,128)(2,1)S(1)}, bf16[2048,128]{1,0:T(8,128)(2,1)S(1)}, u32[]{:S(2)}, u32[]{:S(2)}) collective-permute-start(bf16[2048,128]{1,0:T(8,128)(2,1)S(1)} %get-tuple-element.32), channel_id=1, source_target_pairs={{0,24},{8,16},{16,8},{24,0},{1,25},{9,17},{17,9},{25,1},{2,26},{10... | collective-permute-start | bytes 1572872 | tf_op jit(solution)/shard_map/ppermute | solution.py:428
  115.2 25.5 %copy-start.4 = (bf16[2048,128]{1,0:T(8,128)(2,1)}, bf16[2048,128]{1,0:T(8,128)(2,1)S(1)}, u32[]{:S(2)}) copy-start(bf16[2048,128]{1,0:T(8,128)(2,1)S(1)} %collective-permute-done.4.refs_1_) | copy-start | bytes 1572868
  115.2 25.5 %copy-start.5 = (bf16[2048,128]{1,0:T(8,128)(2,1)}, bf16[2048,128]{1,0:T(8,128)(2,1)S(1)}, u32[]{:S(2)}) copy-start(bf16[2048,128]{1,0:T(8,128)(2,1)S(1)} %collective-permute-done.5.refs_2_) | copy-start | bytes 1572868
  115.3 25.5 %copy-start.6 = (bf16[2048,128]{1,0:T(8,128)(2,1)}, bf16[2048,128]{1,0:T(8,128)(2,1)S(1)}, u32[]{:S(2)}) copy-start(bf16[2048,128]{1,0:T(8,128)(2,1)S(1)} %collective-permute-done.6.refs_3_) | copy-start | bytes 1572868
  115.3 25.5 %collective-permute-start.10 = (bf16[2048,128]{1,0:T(8,128)(2,1)S(1)}, bf16[2048,128]{1,0:T(8,128)(2,1)S(1)}, u32[]{:S(2)}, u32[]{:S(2)}) collective-permute-start(bf16[2048,128]{1,0:T(8,128)(2,1)S(1)} %get-tuple-element.41.refs_0_), channel_id=1, source_target_pairs={{0,1},{1,0},{2,3},{3,2},{4,5},{5,4},{6,7},{7,6},{8,9},{9,8},{10,11... | collective-permute-start | bytes 1572872 | tf_op jit(solution)/shard_map/ppermute | solution.py:433
  116.5 24.3 %collective-permute-start.11 = (bf16[2048,128]{1,0:T(8,128)(2,1)S(1)}, bf16[2048,128]{1,0:T(8,128)(2,1)S(1)}, u32[]{:S(2)}, u32[]{:S(2)}) collective-permute-start(bf16[2048,128]{1,0:T(8,128)(2,1)S(1)} %collective-permute-done.4.refs_1_), channel_id=1, source_target_pairs={{0,1},{1,0},{2,3},{3,2},{4,5},{5,4},{6,7},{7,6},{8,9},{9,8},{10,11... | collective-permute-start | bytes 1572872 | tf_op jit(solution)/shard_map/ppermute | solution.py:433
  116.6 24.3 %collective-permute-start.12 = (bf16[2048,128]{1,0:T(8,128)(2,1)S(1)}, bf16[2048,128]{1,0:T(8,128)(2,1)}, u32[]{:S(2)}, u32[]{:S(2)}) collective-permute-start(bf16[2048,128]{1,0:T(8,128)(2,1)S(1)} %collective-permute-done.5.refs_2_), channel_id=1, source_target_pairs={{0,1},{1,0},{2,3},{3,2},{4,5},{5,4},{6,7},{7,6},{8,9},{9,8},{10,11... | collective-permute-start | bytes 1572872 | tf_op jit(solution)/shard_map/ppermute | solution.py:433
  117.0 23.9 %collective-permute-start.13 = (bf16[2048,128]{1,0:T(8,128)(2,1)S(1)}, bf16[2048,128]{1,0:T(8,128)(2,1)}, u32[]{:S(2)}, u32[]{:S(2)}) collective-permute-start(bf16[2048,128]{1,0:T(8,128)(2,1)S(1)} %collective-permute-done.6.refs_3_), channel_id=1, source_target_pairs={{0,1},{1,0},{2,3},{3,2},{4,5},{5,4},{6,7},{7,6},{8,9},{9,8},{10,11... | collective-permute-start | bytes 1572872 | tf_op jit(solution)/shard_map/ppermute | solution.py:433
  140.8 0.9 copy-start.7
  140.8 1.0 copy-start.8
Sparse Core Ops, SparseCore 0:
  9.0 36.2 all-gather.4
  58.6 44.7 all-gather.6

commit v4 on v3

--- a/solution.py
+++ b/solution.py
@@ -100,13 +100,14 @@
         lax.fori_loop(0, inner // 4, four, 0)
 
 
-def combine(conn, se, grow, smat, recovery, head, tail, nse, inner=4):
+def combine(conn, se, grow, smat, recovery, head, tail, nse, part, inner=4):
     nblk, blk, nb = recovery.shape
     ngrp, _, rows = grow.shape
     nel = ngrp * SUB
     ndof = rows // SUB
     nc = smat.shape[1]
-    nlt = nb // LANES
+    width = nb // 2
+    nlt = width // LANES
     steps = ngrp // inner
     ts = nlt + 1
     gs = rows + 1
@@ -116,25 +117,25 @@
     later = lambda i: jnp.maximum(i - nblk, 0)
     return pl.pallas_call(
         kern,
-        out_shape=jax.ShapeDtypeStruct((nc, nel, nse * nb), jnp.bfloat16),
+        out_shape=jax.ShapeDtypeStruct((nc, nel, nse * width), jnp.bfloat16),
         grid_spec=pltpu.PrefetchScalarGridSpec(
             num_scalar_prefetch=2,
             grid=(nblk + steps,),
             in_specs=[
                 pl.BlockSpec((inner, 1, rows), lambda i, c, s: (later(i), 0, 0)),
                 pl.BlockSpec((inner, nc, rows), lambda i, c, s: (later(i), 0, 0)),
-                pl.BlockSpec((1, blk, nb), lambda i, c, s: (jnp.minimum(i, nblk - 1), 0, 0)),
-                pl.BlockSpec((HW, nb), lambda i, c, s: (0, 0)),
-                pl.BlockSpec((HW, nb), lambda i, c, s: (0, 0)),
+                pl.BlockSpec((1, blk, width), lambda i, c, s: (jnp.minimum(i, nblk - 1), 0, part)),
+                pl.BlockSpec((HW, width), lambda i, c, s: (0, part)),
+                pl.BlockSpec((HW, width), lambda i, c, s: (0, part)),
             ],
-            out_specs=pl.BlockSpec((nc, SUB * inner, nse * nb), lambda i, c, s: (0, later(i), 0)),
+            out_specs=pl.BlockSpec((nc, SUB * inner, nse * width), lambda i, c, s: (0, later(i), 0)),
             scratch_shapes=[
                 pltpu.VMEM(((nblk * blk + 2 * HW) * ts, LANES), jnp.float32),
             ] + [pltpu.VMEM((gs * nlt, LANES), jnp.float32)] * 4,
         ),
-        compiler_params=pltpu.CompilerParams(dimension_semantics=("arbitrary",), vmem_limit_bytes=60 << 20),
-        cost_estimate=pl.CostEstimate(flops=30 * 10**9, bytes_accessed=120 << 20, transcendentals=0),
-        name="combine",
+        compiler_params=pltpu.CompilerParams(dimension_semantics=("arbitrary",), vmem_limit_bytes=40 << 20),
+        cost_estimate=pl.CostEstimate(flops=15 * 10**9, bytes_accessed=60 << 20, transcendentals=0),
+        name=f"combine_{part}",
     )(conn, se, grow, smat, recovery, head, tail)
 
 
@@ -252,7 +253,7 @@
     )(idx.reshape(-1), src)
 
 
-def product_near_kernel(w_ref, near_hbm, o_ref, bt, near, sem, *, tper, nh, npair, parts):
+def product_near_kernel(w0_ref, w1_ref, near_hbm, o_ref, bt, near, sem, *, tper, nh, npair, parts):
     per = LANES // tper
     nk = bt.shape[0] // parts
 
@@ -281,11 +282,15 @@
 
         lax.fori_loop(0, nk // step_rows, arrange, 0)
 
-    o_ref[...] = jnp.dot(w_ref[...], bt[...], preferred_element_type=jnp.float32).astype(jnp.bfloat16)
+    k = w0_ref.shape[1]
+    res = jnp.dot(w0_ref[...], bt[:k], preferred_element_type=jnp.float32)
+    res = res + jnp.dot(w1_ref[...], bt[k:], preferred_element_type=jnp.float32)
+    o_ref[...] = res.astype(jnp.bfloat16)
 
 
 def product_near(w, near, ngroup, tper):
-    m, k = w.shape
+    m, k = w[0].shape
+    k = 2 * k
     nrow, nk, _ = near.shape
     nh = tper * nrow // LANES
     npair = ngroup // 2
@@ -295,7 +300,7 @@
         functools.partial(product_near_kernel, tper=tper, nh=nh, npair=npair, parts=k // nk),
         out_shape=jax.ShapeDtypeStruct((m, cols), jnp.bfloat16),
         grid=(m // mb,),
-        in_specs=[pl.BlockSpec((mb, k), lambda i: (i, 0)), pl.BlockSpec(memory_space=pl.ANY)],
+        in_specs=[pl.BlockSpec((mb, k // 2), lambda i: (i, 0))] * 2 + [pl.BlockSpec(memory_space=pl.ANY)],
         out_specs=pl.BlockSpec((mb, cols), lambda i: (i, 0)),
         scratch_shapes=[
             pltpu.VMEM((k, cols), jnp.bfloat16),
@@ -307,10 +312,10 @@
         ),
         cost_estimate=pl.CostEstimate(flops=2 * m * k * cols, bytes_accessed=40 << 20, transcendentals=0),
         name="product_near",
-    )(w, near)
-
-
-def product_far_kernel(where, w_ref, near_ref, *refs, ngroup, nh, half):
+    )(*w, near)
+
+
+def product_far_kernel(where, w0_ref, w1_ref, near_ref, *refs, ngroup, nh, half):
     mine = refs[:ngroup]
     theirs = refs[ngroup:2 * ngroup]
     o_ref, bt, sem = refs[2 * ngroup:]
@@ -332,7 +337,8 @@
         for c in copies:
             c.wait()
 
-    res = jnp.dot(w_ref[...], bt[...], preferred_element_type=jnp.float32)
+    res = jnp.dot(w0_ref[...], bt[:rows], preferred_element_type=jnp.float32)
+    res = res + jnp.dot(w1_ref[...], bt[rows:], preferred_element_type=jnp.float32)
     slot = (lax.broadcasted_iota(jnp.int32, (res.shape[0], LANES), 1) // half) % 2
     for s in range(ngroup):
         far = res[:, s * LANES:(s + 1) * LANES]
@@ -348,7 +354,8 @@
 
 
 def product_far(where, w, near, mine, theirs, half, snap):
-    m, k = w.shape
+    m, k = w[0].shape
+    k = 2 * k
     ngroup = len(mine)
     cols = near.shape[1]
     mb = 512
@@ -358,7 +365,8 @@
         grid_spec=pltpu.PrefetchScalarGridSpec(
             num_scalar_prefetch=1,
             grid=(m // mb,),
-            in_specs=[pl.BlockSpec((mb, k), lambda i, c: (i, 0)), pl.BlockSpec((mb, cols), lambda i, c: (i, 0))]
+            in_specs=[pl.BlockSpec((mb, k // 2), lambda i, c: (i, 0))] * 2
+            + [pl.BlockSpec((mb, cols), lambda i, c: (i, 0))]
             + [pl.BlockSpec(memory_space=pl.ANY)] * (2 * ngroup),
             out_specs=pl.BlockSpec((mb, snap), lambda i, c: (i, 0)),
             scratch_shapes=[
@@ -371,7 +379,7 @@
         ),
         cost_estimate=pl.CostEstimate(flops=2 * m * k * cols, bytes_accessed=40 << 20, transcendentals=0),
         name="product_far",
-    )(where, w, near, *mine, *theirs)
+    )(where, *w, near, *mine, *theirs)
 
 
 def body(snapshots, bnd_index, recovery, block_se, connect, stress_mat):
@@ -409,29 +417,31 @@
     flat = conn.reshape(-1)
     where = jnp.stack([group, core]).astype(jnp.int32)
 
-    own_idx = lax.dynamic_slice_in_dim(bnd_index, group * nse, nse, 0).reshape(-1)
+    parted = bnd_index.reshape(ngroup, nse, 2, nb // 2).transpose(0, 2, 1, 3)
     rows = nse * nb // 2
-    far_idx = jnp.stack([
-        lax.dynamic_slice_in_dim(
-            lax.dynamic_slice_in_dim(bnd_index, (group ^ s) * nse, nse, 0).reshape(-1), core * rows, rows, 0
-        )
-        for s in range(ngroup)
-    ]).reshape(-1)
-
-    own_idx, far_idx, flat, conn, smat, se_all, head, tail, where = lax.optimization_barrier(
-        (own_idx, far_idx, flat, conn, smat, se_all, head, tail, where)
+    own_idx = lax.dynamic_index_in_dim(parted, group, 0, keepdims=False).reshape(-1)
+    mid = lax.dynamic_index_in_dim(parted, core, 1, keepdims=False).reshape(ngroup, rows)
+    far_idx = jnp.concatenate([
+        lax.dynamic_index_in_dim(mid, group ^ s, 0, keepdims=False) for s in range(ngroup)
+    ])
+
+    own_idx, far_idx, flat, conn, smat, where = lax.optimization_barrier(
+        (own_idx, far_idx, flat, conn, smat, where)
     )
-    near = lax.all_gather(pick_near(own_idx, along_group), "row", axis=0, tiled=False)
+    picked = pick_near(own_idx, along_group)
+    picked, flat, far_idx = lax.optimization_barrier((picked, flat, far_idx))
+    near = lax.all_gather(picked, "row", axis=0, tiled=False)
+    w0 = combine(flat, se_all, conn, smat, recovery, head, tail, nse, 0)
+    w0, far_idx = lax.optimization_barrier((w0, far_idx))
     per = LANES // tper
     order = [per * h + j for j in range(per) for h in range(nrow // per)]
     far = pick_far(far_idx.reshape(ngroup, rows), along_row, order)
     mine = [far[0]] + [lax.ppermute(far[s], "group", swap(s)) for s in range(1, ngroup)]
-
     flat, mine[0] = lax.optimization_barrier((flat, mine[0]))
-    w = combine(flat, se_all, conn, smat, recovery, head, tail, nse)
-    *mine, w = lax.optimization_barrier((*mine, w))
+    w1 = combine(flat, se_all, conn, smat, recovery, head, tail, nse, 1)
+    *mine, w1 = lax.optimization_barrier((*mine, w1))
     theirs = [lax.ppermute(x, "row", other) for x in mine]
-    w = w.reshape(nc * nel, nse * nb)
+    w = [x.reshape(nc * nel, -1) for x in (w0, w1)]
     out = product_near(w, near, ngroup, tper)
     out = product_far(where, w, out, mine, theirs, half, snap)
     return out.reshape(nc, nel, snap).transpose(1, 0, 2)

time: 173 us -> 198 us (1.14)
  Pallas kernels: 106 us -> 133 us
  waiting for transfers between devices: 18.9 us -> 9.74 us
  local copies, waits for them, and re-layouts: 12.8 us -> 21.1 us
    pallas_call x1 -> x2, Pallas kernels: 38.6 us -> 65.8 us  [combine(): pl.pallas_call(kern, out_shape=jax.ShapeDtypeStruct((nc, nel, nse * width...]
    ppermute x1, waiting for transfers between devices: 17.1 us -> 2.76 us  [body(): tail_se = lax.ppermute(block_se[:1], 'row', down)]
    unnamed x22 -> x19, local copies, waits for them, and re-layouts: 3.47 us -> 11.8 us
    ppermute x3, waiting for transfers between devices: 1.73 us -> 6.79 us  [body(): lax.ppermute(bottom, 'group', swap(s))]
  transfers between devices with their start and end apart: 16 -> 16, of which waited for: 2 -> 4; matrix products, arithmetic and copies ran while one was open for 6% -> 5% of each run, Pallas kernels for 48% -> 56%
where the time goes in v4:
time: 198 us; the launch traced here: 197 us
  Pallas kernels  133 us (67%)
  local copies, waits for them, and re-layouts  21.1 us (11%)
  starting transfers between devices  16.5 us (8%)
  between operations  13.7 us (7%)
  waiting for transfers between devices  9.74 us (5%)
  other arithmetic  2.56 us (1%)
    pallas_call x2, Pallas kernels, combine(): pl.pallas_call(kern, out_shape=jax.ShapeDtypeStruct((nc, nel, nse * width...  65.8 us
    pallas_call x1, Pallas kernels, product_near(): pl.pallas_call(functools.partial(product_near_kernel, tper=tper, nh=nh, n...  23.8 us
    pallas_call x1, Pallas kernels, product_far(): pl.pallas_call(functools.partial(product_far_kernel, ngroup=ngroup, nh=sn...  23 us
    pallas_call x1, Pallas kernels, pick_far(): pl.pallas_call(functools.partial(pick_far_kernel, nout=nout, order=order,...  12.1 us
    unnamed x19, local copies, waits for them, and re-layouts  11.8 us
    pallas_call x1, Pallas kernels, pick_near(): pl.pallas_call(functools.partial(pick_near_kernel, nsrc=len(srcs), half=h...  8.38 us
    ppermute x3, waiting for transfers between devices, body(): lax.ppermute(bottom, 'group', swap(s))  6.79 us
  transfers between devices with their start and end apart: 16, of which 4 were waited for; matrix products, arithmetic and copies ran while one was open for 5% of the time, Pallas kernels for 56%

profile of v4, /device:TPU:11, one launch (start us, length us, event | category | flops | bytes accessed | tf_op | source)
XLA Modules:
  0.0 196.6 jit_solution(13889490106632509456)
XLA Ops:
  6.5 1.8 fusion
  8.3 0.0 all-gather.5.cloned.1.call-update
  8.3 0.0 all-gather.7.cloned.1.call-start
  8.4 1.3 collective-permute-start.2
  9.7 0.2 collective-permute-start.1
  9.9 1.2 collective-permute-start
  11.1 0.9 reshape.34
  12.0 0.1 dynamic-slice_reduce_fusion
  12.2 0.9 copy.10
  13.1 0.2 copy.12
  13.3 0.3 copy.11
  13.6 0.4 reshape_reshape.3.conn
  14.0 1.3 copy.13
  15.3 0.5 copy.14
  15.8 0.6 pad_add_fusion.1.where
  16.4 0.2 collective-permute-done.2.refs_3_
  16.6 6.6 %collective-permute-done.1.refs_2_ = bf16[16,8192]{1,0:T(8,128)(2,1)S(1)} collective-permute-done((bf16[16,8192]{1,0:T(8,128)(2,1)S(1)}, bf16[16,8192]{1,0:T(8,128)(2,1)S(1)}, u32[]{:S(2)}, u32[]{:S(2)}) %collective-permute-start.1) | collective-permute-done | bytes 262176 | tf_op jit(solution)/shard_map/ppermute | solution.py:402
  23.2 8.4 %pick_near.1 = bf16[2048,128]{1,0:T(8,128)(2,1)} custom-call(s32[4096]{0:T(1024)S(1)} %bitcast.35, bf16[16,8192]{1,0:T(8,128)(2,1)S(1)} %get-tuple-element.52.refs_0_, bf16[16,8192]{1,0:T(8,128)(2,1)S(1)} %collective-permute-done.refs_1_, bf16[16,8192]{1,0:T(8,128)(2,1)S(1)} %collective-permute-done.1.refs_2_, ...), custom_call_target="tpu_custom_call" | custom-call | tf_op jit(solution)/shard_map/pick_near/pallas_call | solution.py:181
  31.6 0.0 all-gather.7.cloned.1.call-update
  31.6 1.3 slice_bitcast_fusion
  32.9 2.5 %collective-permute-start.6 = (bf16[256,1024]{1,0:T(8,128)(2,1)S(1)}, bf16[256,1024]{1,0:T(8,128)(2,1)S(1)}, u32[]{:S(2)}, u32[]{:S(2)}) collective-permute-start(bf16[256,1024]{1,0:T(8,128)(2,1)S(1)} %get-tuple-element.49), channel_id=1, source_target_pairs={{1,0},{2,1},{3,2},{4,3},{5,4},{6,5},{7,6},{9,8},{10,9},{11,10},{12... | collective-permute-start | bytes 1572872 | tf_op jit(solution)/shard_map/ppermute | solution.py:408
  35.4 3.1 %collective-permute-start.5 = (bf16[256,1024]{1,0:T(8,128)(2,1)S(1)}, bf16[256,1024]{1,0:T(8,128)(2,1)S(1)}, u32[]{:S(2)}, u32[]{:S(2)}) collective-permute-start(bf16[256,1024]{1,0:T(8,128)(2,1)S(1)} %get-tuple-element.50), channel_id=1, source_target_pairs={{0,1},{1,2},{2,3},{3,4},{4,5},{5,6},{6,7},{8,9},{9,10},{10,11},{11... | collective-permute-start | bytes 1572872 | tf_op jit(solution)/shard_map/ppermute | solution.py:407
  38.5 1.3 fusion.1
  39.8 2.4 %collective-permute-start.3 = (s32[1]{0:T(128)}, s32[1]{0:T(128)}, u32[]{:S(2)}, u32[]{:S(2)}) collective-permute-start(s32[1]{0:T(128)} %get-tuple-element.57), channel_id=1, source_target_pairs={{0,1},{1,2},{2,3},{3,4},{4,5},{5,6},{6,7},{8,9},{9,10},{10,11},{11... | collective-permute-start | bytes 20 | tf_op jit(solution)/shard_map/ppermute | solution.py:409
  42.2 1.9 collective-permute-start.4
  44.2 0.1 copy.15.grow_ref
  44.2 0.3 copy.16.s_ref
  44.5 0.1 collective-permute-done.3
  44.6 2.8 %collective-permute-done.4 = s32[1]{0:T(128)} collective-permute-done((s32[1]{0:T(128)}, s32[1]{0:T(128)}, u32[]{:S(2)}, u32[]{:S(2)}) %collective-permute-start.4) | collective-permute-done | bytes 36 | tf_op jit(solution)/shard_map/ppermute | solution.py:410
  47.4 2.0 pad_add_fusion.2.se
  49.4 32.8 %combine_0.1 = bf16[6,512,2048]{2,1,0:T(8,128)(2,1)S(1)} custom-call(s32[12288]{0:T(1024)S(1)} %reshape_reshape.3.conn, s32[18]{0:T(128)S(1)} %pad_add_fusion.2.se, s32[64,1,192]{2,1,0:T(1,128)S(1)} %copy.15.grow_ref, bf16[64,6,192]{2,1,0:T(8,128)(2,1)S(1)} %copy.16.s_ref, bf16[16,512,1024]{2,1,0:T(8,128)(2,1)} %rec_ref.3, ...), custom_call_target="tpu_custom_call" | custom-call | flops 15000000512 | bytes 62914560 | tf_op jit(solution)/shard_map/combine_0/pallas_call | solution.py:118
  82.2 4.5 %copy-done.2 = bf16[6,512,2048]{2,1,0:T(8,128)(2,1)} copy-done((bf16[6,512,2048]{2,1,0:T(8,128)(2,1)}, bf16[6,512,2048]{2,1,0:T(8,128)(2,1)S(1)}, u32[]{:S(2)}) %copy-start.2) | copy-done | bytes 12582936
  86.7 1.6 copy-done
  88.3 12.1 %pick_far.1 = (bf16[2048,128]{1,0:T(8,128)(2,1)S(1)}, bf16[2048,128]{1,0:T(8,128)(2,1)S(1)}, bf16[2048,128]{1,0:T(8,128)(2,1)S(1)}, bf16[2048,128]{1,0:T(8,128)(2,1)S(1)}) custom-call(s32[8192]{0:T(1024)S(1)} %pad_add_fusion.idx, bf16[8,16,8192]{2,1,0:T(8,128)(2,1)S(1)} %bitcast.34), custom_call_target="tpu_custom_call" | custom-call | tf_op jit(solution)/shard_map/pick_far/pallas_call | solution.py:237
  100.4 0.3 collective-permute-start.7
  100.8 1.2 collective-permute-start.8
  101.9 1.2 collective-permute-start.9
  103.2 32.9 %combine_1.1 = bf16[6,512,2048]{2,1,0:T(8,128)(2,1)S(1)} custom-call(s32[12288]{0:T(1024)S(1)} %reshape_reshape.3.conn, s32[18]{0:T(128)S(1)} %pad_add_fusion.2.se, s32[64,1,192]{2,1,0:T(1,128)S(1)} %copy.15.grow_ref, bf16[64,6,192]{2,1,0:T(8,128)(2,1)S(1)} %copy.16.s_ref, bf16[16,512,1024]{2,1,0:T(8,128)(2,1)} %rec_ref.3, ...), custom_call_target="tpu_custom_call" | custom-call | flops 15000000512 | bytes 62914560 | tf_op jit(solution)/shard_map/combine_1/pallas_call | solution.py:118
  136.1 4.5 %copy-done.3 = bf16[6,512,2048]{2,1,0:T(8,128)(2,1)} copy-done((bf16[6,512,2048]{2,1,0:T(8,128)(2,1)}, bf16[6,512,2048]{2,1,0:T(8,128)(2,1)S(1)}, u32[]{:S(2)}) %copy-start.3) | copy-done | bytes 12582936
  140.6 0.1 collective-permute-start.10
  140.7 0.5 collective-permute-start.11
  141.2 0.1 collective-permute-start.12
  141.3 0.4 collective-permute-start.13
  141.7 23.8 %product_near.1.near_ref = bf16[3072,512]{1,0:T(8,128)(2,1)} custom-call(bf16[3072,2048]{1,0:T(8,128)(2,1)} %bitcast.36, bf16[3072,2048]{1,0:T(8,128)(2,1)} %bitcast.38, bf16[8,2048,128]{2,1,0:T(8,128)(2,1)} %bitcast.54), custom_call_target="tpu_custom_call" | custom-call | flops 12884901888 | bytes 41943040 | tf_op jit(solution)/shard_map/product_near/pallas_call | solution.py:299
  165.6 0.8 copy-done.5
  166.4 0.2 copy-done.6
  166.6 0.1 copy-done.7
  166.7 23.0 %product_far.1 = bf16[3072,1024]{1,0:T(8,128)(2,1)} custom-call(s32[2]{0:T(128)} %pad_add_fusion.1.where, bf16[3072,2048]{1,0:T(8,128)(2,1)} %bitcast.37, bf16[3072,2048]{1,0:T(8,128)(2,1)} %bitcast.39, bf16[3072,512]{1,0:T(8,128)(2,1)} %product_near.1.near_ref, bf16[2048,128]{1,0:T(8,128)(2,1)} %copy-done.1, bf16[2048,128]{1,0:T(8,128)(2,1)} %copy-done.4, ...), custom_call_target="tpu_custom_call" | custom-call | flops 12884901888 | bytes 41943040 | tf_op jit(solution)/shard_map/product_far/pallas_call | solution.py:362
  (29 shorter events, 0.1 us)
Async XLA Ops:
  6.5 80.2 %all-gather.5.cloned.1.call-start = ((), (), s32[]{:S(2)}) async-start(), calls=%async_computation | async-start | bytes 2359296 | tf_op jit(solution)/shard_map/all_gather | solution.py:401
  8.3 133.4 %all-gather.7.cloned.1.call-start = ((), (), s32[]{:S(2)}) async-start(), calls=%async_computation.1 | async-start | bytes 4718592 | tf_op jit(solution)/shard_map/all_gather | solution.py:433
  8.4 8.2 %collective-permute-start.2 = (bf16[16,8192]{1,0:T(8,128)(2,1)S(1)}, bf16[16,8192]{1,0:T(8,128)(2,1)S(1)}, u32[]{:S(2)}, u32[]{:S(2)}) collective-permute-start(bf16[16,8192]{1,0:T(8,128)(2,1)S(1)} %get-tuple-element.52.refs_0_), channel_id=1, source_target_pairs={{0,24},{8,16},{16,8},{24,0},{1,25},{9,17},{17,9},{25,1},{2,26},{10... | collective-permute-start | bytes 786440 | tf_op jit(solution)/shard_map/ppermute | solution.py:402
  9.7 13.5 %collective-permute-start.1 = (bf16[16,8192]{1,0:T(8,128)(2,1)S(1)}, bf16[16,8192]{1,0:T(8,128)(2,1)S(1)}, u32[]{:S(2)}, u32[]{:S(2)}) collective-permute-start(bf16[16,8192]{1,0:T(8,128)(2,1)S(1)} %get-tuple-element.52.refs_0_), channel_id=1, source_target_pairs={{0,16},{8,24},{16,0},{24,8},{1,17},{9,25},{17,1},{25,9},{2,18},{10... | collective-permute-start | bytes 786440 | tf_op jit(solution)/shard_map/ppermute | solution.py:402
  9.9 13.3 %collective-permute-start = (bf16[16,8192]{1,0:T(8,128)(2,1)S(1)}, bf16[16,8192]{1,0:T(8,128)(2,1)S(1)}, u32[]{:S(2)}, u32[]{:S(2)}) collective-permute-start(bf16[16,8192]{1,0:T(8,128)(2,1)S(1)} %get-tuple-element.52.refs_0_), channel_id=1, source_target_pairs={{0,8},{8,0},{16,24},{24,16},{1,9},{9,1},{17,25},{25,17},{2,10},{10... | collective-permute-start | bytes 786440 | tf_op jit(solution)/shard_map/ppermute | solution.py:402
  32.9 16.5 %collective-permute-start.6 = (bf16[256,1024]{1,0:T(8,128)(2,1)S(1)}, bf16[256,1024]{1,0:T(8,128)(2,1)S(1)}, u32[]{:S(2)}, u32[]{:S(2)}) collective-permute-start(bf16[256,1024]{1,0:T(8,128)(2,1)S(1)} %get-tuple-element.49), channel_id=1, source_target_pairs={{1,0},{2,1},{3,2},{4,3},{5,4},{6,5},{7,6},{9,8},{10,9},{11,10},{12... | collective-permute-start | bytes 1572872 | tf_op jit(solution)/shard_map/ppermute | solution.py:408
  35.4 14.0 %collective-permute-start.5 = (bf16[256,1024]{1,0:T(8,128)(2,1)S(1)}, bf16[256,1024]{1,0:T(8,128)(2,1)S(1)}, u32[]{:S(2)}, u32[]{:S(2)}) collective-permute-start(bf16[256,1024]{1,0:T(8,128)(2,1)S(1)} %get-tuple-element.50), channel_id=1, source_target_pairs={{0,1},{1,2},{2,3},{3,4},{4,5},{5,6},{6,7},{8,9},{9,10},{10,11},{11... | collective-permute-start | bytes 1572872 | tf_op jit(solution)/shard_map/ppermute | solution.py:407
  39.8 4.8 %collective-permute-start.3 = (s32[1]{0:T(128)}, s32[1]{0:T(128)}, u32[]{:S(2)}, u32[]{:S(2)}) collective-permute-start(s32[1]{0:T(128)} %get-tuple-element.57), channel_id=1, source_target_pairs={{0,1},{1,2},{2,3},{3,4},{4,5},{5,6},{6,7},{8,9},{9,10},{10,11},{11... | collective-permute-start | bytes 20 | tf_op jit(solution)/shard_map/ppermute | solution.py:409
  42.2 5.2 %collective-permute-start.4 = (s32[1]{0:T(128)}, s32[1]{0:T(128)}, u32[]{:S(2)}, u32[]{:S(2)}) collective-permute-start(s32[1]{0:T(128)} %get-tuple-element.58), channel_id=1, source_target_pairs={{1,0},{2,1},{3,2},{4,3},{5,4},{6,5},{7,6},{9,8},{10,9},{11,10},{12... | collective-permute-start | bytes 20 | tf_op jit(solution)/shard_map/ppermute | solution.py:410
  82.2 4.5 %copy-start.2 = (bf16[6,512,2048]{2,1,0:T(8,128)(2,1)}, bf16[6,512,2048]{2,1,0:T(8,128)(2,1)S(1)}, u32[]{:S(2)}) copy-start(bf16[6,512,2048]{2,1,0:T(8,128)(2,1)S(1)} %combine_0.1) | copy-start | bytes 37748740
  86.7 1.6 copy-start
  100.4 40.2 %copy-start.1 = (bf16[2048,128]{1,0:T(8,128)(2,1)}, bf16[2048,128]{1,0:T(8,128)(2,1)S(1)}, u32[]{:S(2)}) copy-start(bf16[2048,128]{1,0:T(8,128)(2,1)S(1)} %get-tuple-element.45.refs_0_) | copy-start | bytes 1572868
  100.4 40.2 %collective-permute-start.7 = (bf16[2048,128]{1,0:T(8,128)(2,1)S(1)}, bf16[2048,128]{1,0:T(8,128)(2,1)S(1)}, u32[]{:S(2)}, u32[]{:S(2)}) collective-permute-start(bf16[2048,128]{1,0:T(8,128)(2,1)S(1)} %get-tuple-element.39), channel_id=1, source_target_pairs={{0,8},{8,0},{16,24},{24,16},{1,9},{9,1},{17,25},{25,17},{2,10},{10... | collective-permute-start | bytes 1572872 | tf_op jit(solution)/shard_map/ppermute | solution.py:439
  100.8 39.8 %collective-permute-start.8 = (bf16[2048,128]{1,0:T(8,128)(2,1)S(1)}, bf16[2048,128]{1,0:T(8,128)(2,1)}, u32[]{:S(2)}, u32[]{:S(2)}) collective-permute-start(bf16[2048,128]{1,0:T(8,128)(2,1)S(1)} %get-tuple-element.40), channel_id=1, source_target_pairs={{0,16},{8,24},{16,0},{24,8},{1,17},{9,25},{17,1},{25,9},{2,18},{10... | collective-permute-start | bytes 1572872 | tf_op jit(solution)/shard_map/ppermute | solution.py:439
  101.9 38.7 %collective-permute-start.9 = (bf16[2048,128]{1,0:T(8,128)(2,1)S(1)}, bf16[2048,128]{1,0:T(8,128)(2,1)}, u32[]{:S(2)}, u32[]{:S(2)}) collective-permute-start(bf16[2048,128]{1,0:T(8,128)(2,1)S(1)} %get-tuple-element.41), channel_id=1, source_target_pairs={{0,24},{8,16},{16,8},{24,0},{1,25},{9,17},{17,9},{25,1},{2,26},{10... | collective-permute-start | bytes 1572872 | tf_op jit(solution)/shard_map/ppermute | solution.py:439
  136.1 4.5 %copy-start.3 = (bf16[6,512,2048]{2,1,0:T(8,128)(2,1)}, bf16[6,512,2048]{2,1,0:T(8,128)(2,1)S(1)}, u32[]{:S(2)}) copy-start(bf16[6,512,2048]{2,1,0:T(8,128)(2,1)S(1)} %combine_1.1) | copy-start | bytes 37748740
  140.6 24.9 %copy-start.4 = (bf16[2048,128]{1,0:T(8,128)(2,1)}, bf16[2048,128]{1,0:T(8,128)(2,1)S(1)}, u32[]{:S(2)}) copy-start(bf16[2048,128]{1,0:T(8,128)(2,1)S(1)} %collective-permute-done.7.refs_1_) | copy-start | bytes 1572868
  140.6 24.9 %collective-permute-start.10 = (bf16[2048,128]{1,0:T(8,128)(2,1)S(1)}, bf16[2048,128]{1,0:T(8,128)(2,1)S(1)}, u32[]{:S(2)}, u32[]{:S(2)}) collective-permute-start(bf16[2048,128]{1,0:T(8,128)(2,1)S(1)} %get-tuple-element.45.refs_0_), channel_id=1, source_target_pairs={{0,1},{1,0},{2,3},{3,2},{4,5},{5,4},{6,7},{7,6},{8,9},{9,8},{10,11... | collective-permute-start | bytes 1572872 | tf_op jit(solution)/shard_map/ppermute | solution.py:443
  140.7 24.9 %collective-permute-start.11 = (bf16[2048,128]{1,0:T(8,128)(2,1)S(1)}, bf16[2048,128]{1,0:T(8,128)(2,1)S(1)}, u32[]{:S(2)}, u32[]{:S(2)}) collective-permute-start(bf16[2048,128]{1,0:T(8,128)(2,1)S(1)} %collective-permute-done.7.refs_1_), channel_id=1, source_target_pairs={{0,1},{1,0},{2,3},{3,2},{4,5},{5,4},{6,7},{7,6},{8,9},{9,8},{10,11... | collective-permute-start | bytes 1572872 | tf_op jit(solution)/shard_map/ppermute | solution.py:443
  141.2 24.4 %collective-permute-start.12 = (bf16[2048,128]{1,0:T(8,128)(2,1)}, bf16[2048,128]{1,0:T(8,128)(2,1)S(1)}, u32[]{:S(2)}, u32[]{:S(2)}) collective-permute-start(bf16[2048,128]{1,0:T(8,128)(2,1)} %collective-permute-done.8.refs_2_), channel_id=1, source_target_pairs={{0,1},{1,0},{2,3},{3,2},{4,5},{5,4},{6,7},{7,6},{8,9},{9,8},{10,11... | collective-permute-start | bytes 1572872 | tf_op jit(solution)/shard_map/ppermute | solution.py:443
  141.3 24.3 %collective-permute-start.13 = (bf16[2048,128]{1,0:T(8,128)(2,1)}, bf16[2048,128]{1,0:T(8,128)(2,1)}, u32[]{:S(2)}, u32[]{:S(2)}) collective-permute-start(bf16[2048,128]{1,0:T(8,128)(2,1)} %collective-permute-done.9.refs_3_), channel_id=1, source_target_pairs={{0,1},{1,0},{2,3},{3,2},{4,5},{5,4},{6,7},{7,6},{8,9},{9,8},{10,11... | collective-permute-start | bytes 1572872 | tf_op jit(solution)/shard_map/ppermute | solution.py:443
  165.5 0.9 copy-start.5
  165.6 1.0 copy-start.6
  165.6 1.2 copy-start.7
Sparse Core Ops, SparseCore 0:
  9.0 30.6 all-gather.4
  41.2 45.1 all-gather.6

commit v5 on v2

--- a/solution.py
+++ b/solution.py
@@ -12,13 +12,16 @@
 LANES = 128
 
 
-def combine_kernel(conn, se, grow_ref, s_ref, rec_ref, head_ref, tail_ref, w_ref, tbl, g0, g1,
-    *, nfill, blk, nlt, nse, nc, ndof, inner, ts, gs,
+def combine_kernel(
+    conn, se, grow_ref, s_ref, rec_hbm, head_ref, tail_ref, w_ref, tbl, buf, sem, g0, g1, g2, g3,
+    *, nfill, blk, nlt, nse, nc, ndof, inner, ts, gs, nbuf
 ):
     step = pl.program_id(0)
     rows = SUB * ndof
-    out_rows = SUB * nc
     steps = pl.num_programs(0) - nfill
+
+    def fetch(b):
+        return pltpu.make_async_copy(rec_hbm.at[b], buf.at[b % nbuf], sem.at[b % nbuf])
 
     def fill(src, base, count):
         def one(i, carry):
@@ -27,68 +30,88 @@
                 part = src[pl.ds(at, 16), j * LANES:(j + 1) * LANES].astype(jnp.float32)
                 tbl[pl.ds((base + at) * ts + j, 16, stride=ts), :] = part
             return carry
-        lax.fori_loop(0, count // 16, one, 0, unroll=2)
-
-    def gather(group, dst):
+
+        lax.fori_loop(0, count // 16, one, 0, unroll=4)
+
+    def gather(group, dst, lo=0, hi=rows):
         first = group * rows
-        for q in range(rows):
-            dst[pl.ds(q, nlt, stride=gs), :] = tbl[pl.ds(conn[first + q] * ts, nlt), :]
-
-    def matmul(i, src):
-        own = (
-            lax.broadcasted_iota(jnp.int32, (SUB, rows), 1) % SUB
-            == lax.broadcasted_iota(jnp.int32, (SUB, rows), 0)
-        )
+        for q in range(lo, hi):
+            dst[pl.ds(q, nlt, stride=gs), :] = tbl[pl.ds(conn[first + q], nlt), :]
+
+    own = (
+        lax.broadcasted_iota(jnp.int32, (SUB, rows), 1) % SUB
+        == lax.broadcasted_iota(jnp.int32, (SUB, rows), 0)
+    )
+
+    def left(i):
         where = (grow_ref[i] + (blk - HW)) // blk
         tag = jnp.zeros((1, rows), jnp.int32)
         for b in range(nfill + 2):
             tag = jnp.where(where == b, se[b], tag)
         tag = jnp.where(own, jnp.broadcast_to(tag, (SUB, rows)), -1)
+        smat = s_ref[i].astype(jnp.float32)
         parts = []
-        smat = s_ref[i].astype(jnp.float32)
         for s in range(nse):
             hit = tag == s
             for c in range(nc):
                 parts.append(jnp.where(hit, jnp.broadcast_to(smat[c:c + 1], (SUB, rows)), 0.0))
-        lhs = jnp.concatenate(parts, axis=0).astype(jnp.bfloat16)
-        at = pl.multiple_of(i * SUB, SUB)
+        return jnp.concatenate(parts, axis=0).astype(jnp.bfloat16)
+
+    def matmul(i, srcs, nxt, dsts):
+        lhs = [left(i), left(i + 1)]
+        at = pl.multiple_of(i * SUB, 2 * SUB)
         for j in range(0, nlt, 2):
-            rhs = jnp.concatenate(
-                [src[(j + d) * gs:(j + d) * gs + rows, :].astype(jnp.bfloat16) for d in range(2)], axis=1)
-            res = jnp.dot(lhs, rhs, preferred_element_type=jnp.float32).astype(jnp.bfloat16)
+            res = []
+            for t in range(2):
+                src = srcs[t]
+                rhs = jnp.concatenate(
+                    [src[(j + d) * gs:(j + d) * gs + rows, :].astype(jnp.bfloat16) for d in range(2)], axis=1
+                )
+                res.append(jnp.dot(lhs[t], rhs, preferred_element_type=jnp.float32))
+                gather(nxt + t, dsts[t], rows * j // nlt, rows * (j + 2) // nlt)
             for s in range(nse):
                 col = (s * nlt + j) * LANES
                 for c in range(nc):
-                    w_ref[c, pl.ds(at, SUB), col:col + 2 * LANES] = res[(s * nc + c) * SUB:(s * nc + c + 1) * SUB]
-
-    @pl.when(step < nfill)
-    def _():
-        fill(rec_ref.at[0], HW + step * blk, blk)
+                    r0 = (s * nc + c) * SUB
+                    both = jnp.concatenate([r[r0:r0 + SUB] for r in res], axis=0)
+                    w_ref[c, pl.ds(at, 2 * SUB), col:col + 2 * LANES] = both.astype(jnp.bfloat16)
 
     @pl.when(step == 0)
     def _():
+        for b in range(nbuf):
+            fetch(b).start()
         fill(head_ref, 0, HW)
         fill(tail_ref, HW + nfill * blk, HW)
 
+    @pl.when(step < nfill)
+    def _():
+        fetch(step).wait()
+        fill(buf.at[step % nbuf], HW + step * blk, blk)
+
+        @pl.when(step + nbuf < nfill)
+        def _():
+            fetch(step + nbuf).start()
+
     @pl.when(step >= nfill)
     def _():
         base = (step - nfill) * inner
-        last = steps * inner - 1
+        last = steps * inner - 2
 
         @pl.when(step == nfill)
         def _():
             gather(0, g0)
-
-        def two(i, carry):
-            n = base + 2 * i
-            gather(n + 1, g1)
-            matmul(2 * i, g0)
-            gather(jnp.minimum(n + 2, last), g0)
-            matmul(2 * i + 1, g1)
+            gather(1, g1)
+
+        def four(i, carry):
+            n = base + 4 * i
+            matmul(4 * i, (g0, g1), n + 2, (g2, g3))
+            matmul(4 * i + 2, (g2, g3), jnp.minimum(n + 4, last), (g0, g1))
             return carry
-        lax.fori_loop(0, inner // 2, two, 0)
-
-def combine(conn, se, grow, smat, recovery, head, tail, nse, inner=4):
+
+        lax.fori_loop(0, inner // 4, four, 0)
+
+
+def combine(conn, se, grow, smat, recovery, head, tail, nse, inner=4, nbuf=6):
     nblk, blk, nb = recovery.shape
     ngrp, _, rows = grow.shape
     nel = ngrp * SUB
@@ -99,7 +122,8 @@
     ts = nlt + 1
     gs = rows + 1
     kern = functools.partial(
-        combine_kernel, nfill=nblk, blk=blk, nlt=nlt, nse=nse, nc=nc, ndof=ndof, inner=inner, ts=ts, gs=gs
+        combine_kernel, nfill=nblk, blk=blk, nlt=nlt, nse=nse, nc=nc, ndof=ndof, inner=inner, ts=ts, gs=gs,
+        nbuf=nbuf,
     )
     later = lambda i: jnp.maximum(i - nblk, 0)
     return pl.pallas_call(
@@ -111,18 +135,19 @@
             in_specs=[
                 pl.BlockSpec((inner, 1, rows), lambda i, c, s: (later(i), 0, 0)),
                 pl.BlockSpec((inner, nc, rows), lambda i, c, s: (later(i), 0, 0)),
-                pl.BlockSpec((1, blk, nb), lambda i, c, s: (jnp.minimum(i, nblk - 1), 0, 0)),
+                pl.BlockSpec(memory_space=pl.ANY),
                 pl.BlockSpec((HW, nb), lambda i, c, s: (0, 0)),
                 pl.BlockSpec((HW, nb), lambda i, c, s: (0, 0)),
             ],
             out_specs=pl.BlockSpec((nc, SUB * inner, nse * nb), lambda i, c, s: (0, later(i), 0)),
             scratch_shapes=[
                 pltpu.VMEM(((nblk * blk + 2 * HW) * ts, LANES), jnp.float32),
-                pltpu.VMEM((gs * nlt, LANES), jnp.float32),
-                pltpu.VMEM((gs * nlt, LANES), jnp.float32),
-            ],
+                pltpu.VMEM((nbuf, blk, nb), jnp.bfloat16),
+                pltpu.SemaphoreType.DMA((nbuf,)),
+            ] + [pltpu.VMEM((gs * nlt, LANES), jnp.float32)] * 4,
         ),
         compiler_params=pltpu.CompilerParams(dimension_semantics=("arbitrary",), vmem_limit_bytes=60 << 20),
+        cost_estimate=pl.CostEstimate(flops=30 * 10**9, bytes_accessed=120 << 20, transcendentals=0),
         name="combine",
     )(conn, se, grow, smat, recovery, head, tail)
 
@@ -268,7 +293,7 @@
         for c in copies:
             c.start()
         last.wait()
-        step_rows = min(nk, 256)
+        step_rows = min(nk, 128)
         lane = lax.broadcasted_iota(jnp.int32, (step_rows, LANES), 1) // tper
 
         def arrange(i, carry):
@@ -353,22 +378,6 @@
     along_row = lax.all_gather(top, "row", axis=0, tiled=False)
     along_group = [bottom] + [lax.ppermute(bottom, "group", swap(s)) for s in range(1, ngroup)]
 
-    own_idx = lax.dynamic_slice_in_dim(bnd_index, group * nse, nse, 0).reshape(-1)
-    near = lax.all_gather(pick_near(own_idx, along_group), "row", axis=0, tiled=False)
-
-    rows = nse * nb // 2
-    far_idx = jnp.stack([
-        lax.dynamic_slice_in_dim(
-            lax.dynamic_slice_in_dim(bnd_index, (group ^ s) * nse, nse, 0).reshape(-1), core * rows, rows, 0
-        )
-        for s in range(ngroup)
-    ])
-    per = LANES // tper
-    order = [per * h + j for j in range(per) for h in range(nrow // per)]
-    far = pick_far(far_idx, along_row, order)
-    mine = [far[0]] + [lax.ppermute(far[s], "group", swap(s)) for s in range(1, ngroup)]
-    theirs = [lax.ppermute(x, "row", other) for x in mine]
-
     ends = nrow - 1
     up = [(i, i + 1) for i in range(ends)]
     down = [(i + 1, i) for i in range(ends)]
@@ -382,10 +391,31 @@
     conn = connect.T.reshape(ndof, ngrp, SUB).transpose(1, 0, 2).reshape(ngrp, 1, ndof * SUB)
     smat = stress_mat.transpose(1, 2, 0).reshape(nc, ndof, ngrp, SUB).transpose(2, 0, 1, 3)
     smat = smat.reshape(ngrp, nc, ndof * SUB)
-    flat, far0 = lax.optimization_barrier((conn.reshape(-1), far[0]))
-    mine[0] = far0
+    flat = conn.reshape(-1) * (nb // LANES + 1)
+    where = jnp.stack([group, core]).astype(jnp.int32)
+
+    rows = nse * nb // 2
+    parted = bnd_index.reshape(ngroup, 2, rows)
+    own_idx = lax.dynamic_index_in_dim(parted, group, 0, keepdims=False).reshape(-1)
+    mid = lax.dynamic_index_in_dim(parted, core, 1, keepdims=False)
+    far_idx = jnp.concatenate([
+        lax.dynamic_index_in_dim(mid, group ^ s, 0, keepdims=False) for s in range(ngroup)
+    ])
+
+    own_idx, far_idx, flat, conn, smat, where = lax.optimization_barrier(
+        (own_idx, far_idx, flat, conn, smat, where)
+    )
+    picked = pick_near(own_idx, along_group)
+    picked, far_idx = lax.optimization_barrier((picked, far_idx))
+    near = lax.all_gather(picked, "row", axis=0, tiled=False)
+    per = LANES // tper
+    order = [per * h + j for j in range(per) for h in range(nrow // per)]
+    far = pick_far(far_idx.reshape(ngroup, rows), along_row, order)
+    mine = [far[0]] + [lax.ppermute(far[s], "group", swap(s)) for s in range(1, ngroup)]
+    flat, mine[0] = lax.optimization_barrier((flat, mine[0]))
     w = combine(flat, se_all, conn, smat, recovery, head, tail, nse)
-    where = jnp.stack([group, core]).astype(jnp.int32)
+    *mine, w = lax.optimization_barrier((*mine, w))
+    theirs = [lax.ppermute(x, "row", other) for x in mine]
     out = product(where, w.reshape(nc * nel, nse * nb), mine, theirs, near, tper, snap)
     return out.reshape(nc, nel, snap).transpose(1, 0, 2)
 

time: 179 us -> 151 us (0.84)
  starting transfers between devices: 26.5 us -> 16.5 us
  Pallas kernels: 101 us -> 91.2 us
  waiting for transfers between devices: 18.6 us -> 11 us
    pallas_call x1, Pallas kernels: 40.9 us -> 30.3 us  [combine(): pl.pallas_call(kern, out_shape=jax.ShapeDtypeStruct((nc, nel, nse * nb),...]
    ppermute x4, starting transfers between devices: 9.52 us -> 1.09 us  [body(): theirs = [lax.ppermute(x, 'row', other) for x in mine]]
    ppermute x3, waiting for transfers between devices: 11.2 us -> 6.35 us  [body(): lax.ppermute(bottom, 'group', swap(s))]
    all_gather x1, waiting for transfers between devices: 3.29 us -> 0.01 us  [body(): along_row = lax.all_gather(top, 'row', axis=0, tiled=False)]
    ppermute x4, waiting for transfers between devices: 0.01 us -> 3.14 us  [body(): theirs = [lax.ppermute(x, 'row', other) for x in mine]]
  transfers between devices with their start and end apart: 16 -> 16, of which waited for: 6 -> 5; matrix products, arithmetic and copies ran while one was open for 8% -> 9% of each run, Pallas kernels for 35% -> 34%
where the time goes in v5:
time: 151 us; the launch traced here: 150 us
  Pallas kernels  91.2 us (60%)
  starting transfers between devices  16.5 us (11%)
  local copies, waits for them, and re-layouts  14.5 us (10%)
  between operations  13.6 us (9%)
  waiting for transfers between devices  11 us (7%)
  other arithmetic  3.16 us (2%)
    pallas_call x1, Pallas kernels, product(): pl.pallas_call(functools.partial(product_kernel, ngroup=ngroup, nrow=nrow...  40.5 us
    pallas_call x1, Pallas kernels, combine(): pl.pallas_call(kern, out_shape=jax.ShapeDtypeStruct((nc, nel, nse * nb),...  30.3 us
    pallas_call x1, Pallas kernels, pick_far(): pl.pallas_call(functools.partial(pick_far_kernel, nout=nout, order=order,...  12.1 us
    pallas_call x1, Pallas kernels, pick_near(): pl.pallas_call(functools.partial(pick_near_kernel, nsrc=len(srcs), half=h...  8.38 us
    ppermute x3, waiting for transfers between devices, body(): lax.ppermute(bottom, 'group', swap(s))  6.35 us
    ppermute x4, waiting for transfers between devices, body(): theirs = [lax.ppermute(x, 'row', other) for x in mine]  3.14 us
    ppermute x1, starting transfers between devices, body(): head = lax.ppermute(recovery[nblk - 1, blk - HW:], 'row', up)  3.1 us
  transfers between devices with their start and end apart: 16, of which 5 were waited for; matrix products, arithmetic and copies ran while one was open for 9% of the time, Pallas kernels for 34%

profile of v5, /device:TPU:11, one launch (start us, length us, event | category | flops | bytes accessed | tf_op | source)
XLA Modules:
  0.0 149.9 jit_solution(6369183763346170258)
XLA Ops:
  6.5 1.8 %fusion = (bf16[16,8192]{1,0:T(8,128)(2,1)}, bf16[16,8192]{1,0:T(8,128)(2,1)S(1)}) fusion(bf16[32,8192]{1,0:T(8,128)(2,1)} %param.6), kind=kLoop, calls=%fused_computation.11 | loop fusion | bytes 1048576 | tf_op jit(solution)/shard_map/slice | solution.py:376
  8.3 0.0 all-gather.5.cloned.1.call-update
  8.3 0.0 all-gather.7.cloned.1.call-start
  8.4 1.3 collective-permute-start.2
  9.7 0.2 collective-permute-start.1
  9.9 1.2 collective-permute-start
  11.1 0.9 reshape.35
  12.0 0.9 copy.16
  12.9 0.2 copy.17
  13.2 0.3 copy.18
  13.5 0.9 mul.11.conn
  14.4 1.3 copy.19
  15.7 0.5 copy.20
  16.3 0.6 pad_add_fusion.1.where
  16.8 0.0 collective-permute-done.2.refs_3_
  16.9 6.3 %collective-permute-done.1.refs_2_ = bf16[16,8192]{1,0:T(8,128)(2,1)S(1)} collective-permute-done((bf16[16,8192]{1,0:T(8,128)(2,1)S(1)}, bf16[16,8192]{1,0:T(8,128)(2,1)S(1)}, u32[]{:S(2)}, u32[]{:S(2)}) %collective-permute-start.1) | collective-permute-done | bytes 262176 | tf_op jit(solution)/shard_map/ppermute | solution.py:379
  23.2 0.0 collective-permute-done.refs_1_
  23.2 8.4 %pick_near.1 = bf16[2048,128]{1,0:T(8,128)(2,1)} custom-call(s32[4096]{0:T(1024)S(1)} %bitcast.31, bf16[16,8192]{1,0:T(8,128)(2,1)S(1)} %get-tuple-element.46.refs_0_, bf16[16,8192]{1,0:T(8,128)(2,1)S(1)} %collective-permute-done.refs_1_, bf16[16,8192]{1,0:T(8,128)(2,1)S(1)} %collective-permute-done.1.refs_2_, ...), custom_call_target="tpu_custom_call" | custom-call | tf_op jit(solution)/shard_map/pick_near/pallas_call | solution.py:194
  31.6 0.0 all-gather.7.cloned.1.call-update
  31.6 2.2 %slice_bitcast_fusion = (bf16[256,1024]{1,0:T(8,128)(2,1)}, bf16[256,1024]{1,0:T(8,128)(2,1)}) fusion(bf16[16,512,1024]{2,1,0:T(8,128)(2,1)} %rec_hbm.1), kind=kLoop, calls=%fused_computation | loop fusion | bytes 2097152 | tf_op jit(solution)/shard_map/squeeze | solution.py:385
  33.9 2.5 %collective-permute-start.9 = (bf16[256,1024]{1,0:T(8,128)(2,1)}, bf16[256,1024]{1,0:T(8,128)(2,1)}, u32[]{:S(2)}, u32[]{:S(2)}) collective-permute-start(bf16[256,1024]{1,0:T(8,128)(2,1)} %get-tuple-element.43), channel_id=1, source_target_pairs={{1,0},{2,1},{3,2},{4,3},{5,4},{6,5},{7,6},{9,8},{10,9},{11,10},{12... | collective-permute-start | bytes 1572872 | tf_op jit(solution)/shard_map/ppermute | solution.py:385
  36.4 3.1 %collective-permute-start.8 = (bf16[256,1024]{1,0:T(8,128)(2,1)}, bf16[256,1024]{1,0:T(8,128)(2,1)}, u32[]{:S(2)}, u32[]{:S(2)}) collective-permute-start(bf16[256,1024]{1,0:T(8,128)(2,1)} %get-tuple-element.44), channel_id=1, source_target_pairs={{0,1},{1,2},{2,3},{3,4},{4,5},{5,6},{6,7},{8,9},{9,10},{10,11},{11... | collective-permute-start | bytes 1572872 | tf_op jit(solution)/shard_map/ppermute | solution.py:384
  39.5 1.3 fusion.1
  40.8 2.4 %collective-permute-start.6 = (s32[1]{0:T(128)}, s32[1]{0:T(128)}, u32[]{:S(2)}, u32[]{:S(2)}) collective-permute-start(s32[1]{0:T(128)} %get-tuple-element.51), channel_id=1, source_target_pairs={{0,1},{1,2},{2,3},{3,4},{4,5},{5,6},{6,7},{8,9},{9,10},{10,11},{11... | collective-permute-start | bytes 20 | tf_op jit(solution)/shard_map/ppermute | solution.py:386
  43.2 1.9 %collective-permute-start.7 = (s32[1]{0:T(128)}, s32[1]{0:T(128)}, u32[]{:S(2)}, u32[]{:S(2)}) collective-permute-start(s32[1]{0:T(128)} %get-tuple-element.52), channel_id=1, source_target_pairs={{1,0},{2,1},{3,2},{4,3},{5,4},{6,5},{7,6},{9,8},{10,9},{11,10},{12... | collective-permute-start | bytes 20 | tf_op jit(solution)/shard_map/ppermute | solution.py:387
  45.1 0.7 copy.21.grow_ref
  45.8 1.0 copy.22.s_ref
  46.8 0.0 collective-permute-done.6
  46.8 1.4 collective-permute-done.7
  48.2 2.6 %pad_add_fusion.2.se = s32[18]{0:T(128)} fusion(s32[1]{0:T(128)} %collective-permute-done.7, s32[16]{0:T(128)} %param.9, s32[1]{0:T(128)} %collective-permute-done.6), kind=kLoop, calls=%fused_computation.10 | loop fusion | flops 36 | bytes 144 | tf_op jit(solution)/shard_map/concatenate | solution.py:388
  50.8 1.6 %copy-done = bf16[128,8192]{1,0:T(8,128)(2,1)S(1)} copy-done((bf16[128,8192]{1,0:T(8,128)(2,1)S(1)}, bf16[128,8192]{1,0:T(8,128)(2,1)}, u32[]{:S(2)}) %copy-start) | copy-done | bytes 2097176
  52.4 12.1 %pick_far.1 = (bf16[2048,128]{1,0:T(8,128)(2,1)S(1)}, bf16[2048,128]{1,0:T(8,128)(2,1)S(1)}, bf16[2048,128]{1,0:T(8,128)(2,1)S(1)}, bf16[2048,128]{1,0:T(8,128)(2,1)S(1)}) custom-call(s32[8192]{0:T(1024)S(1)} %pad_add_fusion.idx, bf16[8,16,8192]{2,1,0:T(8,128)(2,1)S(1)} %bitcast.30), custom_call_target="tpu_custom_call" | custom-call | tf_op jit(solution)/shard_map/pick_far/pallas_call | solution.py:250
  64.5 0.3 collective-permute-start.3
  64.8 1.1 collective-permute-start.4
  65.9 1.3 collective-permute-start.5
  67.2 0.0 collective-permute-done.9.tail_ref
  67.2 30.3 %combine.1 = bf16[6,512,4096]{2,1,0:T(8,128)(2,1)} custom-call(s32[12288]{0:T(1024)} %mul.11.conn, s32[18]{0:T(128)} %pad_add_fusion.2.se, s32[64,1,192]{2,1,0:T(1,128)} %copy.21.grow_ref, bf16[64,6,192]{2,1,0:T(8,128)(2,1)} %copy.22.s_ref, bf16[16,512,1024]{2,1,0:T(8,128)(2,1)} %rec_hbm.1, bf16[256,1024]{1,0:T(8,128)(2,1)} %collective-permute-done.8.head_ref, ...), custom_call_target="tpu_custom_call" | custom-call | flops 30000001024 | bytes 125829120 | tf_op jit(solution)/shard_map/combine/pallas_call | solution.py:129
  97.5 0.0 collective-permute-done.3.refs_1_
  97.5 0.3 collective-permute-start.10
  97.8 0.3 collective-permute-start.11
  98.1 0.2 collective-permute-start.12
  98.3 0.3 collective-permute-start.13
  98.6 0.9 collective-permute-done.10.refs_4_
  99.5 1.5 collective-permute-done.11.refs_5_
  101.0 0.7 collective-permute-done.12.refs_6_
  101.8 0.8 copy-done.7
  102.6 0.0 collective-permute-done.13.refs_7_
  102.6 40.5 %product.1 = bf16[3072,1024]{1,0:T(8,128)(2,1)} custom-call(s32[2]{0:T(128)} %pad_add_fusion.1.where, bf16[3072,4096]{1,0:T(8,128)(2,1)} %bitcast.32, bf16[2048,128]{1,0:T(8,128)(2,1)} %copy-done.1, bf16[2048,128]{1,0:T(8,128)(2,1)} %copy-done.2, bf16[2048,128]{1,0:T(8,128)(2,1)} %copy-done.3, bf16[2048,128]{1,0:T(8,128)(2,1)} %copy-done.4, ...), custom_call_target="tpu_custom_call" | custom-call | tf_op jit(solution)/shard_map/product/pallas_call | solution.py:338
  (25 shorter events, 0.1 us)
Async XLA Ops:
  6.5 44.2 %all-gather.5.cloned.1.call-start = ((), (), s32[]{:S(2)}) async-start(), calls=%async_computation | async-start | bytes 2359296 | tf_op jit(solution)/shard_map/all_gather | solution.py:378
  8.3 94.2 %all-gather.7.cloned.1.call-start = ((), (), s32[]{:S(2)}) async-start(), calls=%async_computation.1 | async-start | bytes 4718592 | tf_op jit(solution)/shard_map/all_gather | solution.py:410
  8.4 8.5 %collective-permute-start.2 = (bf16[16,8192]{1,0:T(8,128)(2,1)S(1)}, bf16[16,8192]{1,0:T(8,128)(2,1)S(1)}, u32[]{:S(2)}, u32[]{:S(2)}) collective-permute-start(bf16[16,8192]{1,0:T(8,128)(2,1)S(1)} %get-tuple-element.46.refs_0_), channel_id=1, source_target_pairs={{0,24},{8,16},{16,8},{24,0},{1,25},{9,17},{17,9},{25,1},{2,26},{10... | collective-permute-start | bytes 786440 | tf_op jit(solution)/shard_map/ppermute | solution.py:379
  9.7 13.5 %collective-permute-start.1 = (bf16[16,8192]{1,0:T(8,128)(2,1)S(1)}, bf16[16,8192]{1,0:T(8,128)(2,1)S(1)}, u32[]{:S(2)}, u32[]{:S(2)}) collective-permute-start(bf16[16,8192]{1,0:T(8,128)(2,1)S(1)} %get-tuple-element.46.refs_0_), channel_id=1, source_target_pairs={{0,16},{8,24},{16,0},{24,8},{1,17},{9,25},{17,1},{25,9},{2,18},{10... | collective-permute-start | bytes 786440 | tf_op jit(solution)/shard_map/ppermute | solution.py:379
  9.9 13.3 %collective-permute-start = (bf16[16,8192]{1,0:T(8,128)(2,1)S(1)}, bf16[16,8192]{1,0:T(8,128)(2,1)S(1)}, u32[]{:S(2)}, u32[]{:S(2)}) collective-permute-start(bf16[16,8192]{1,0:T(8,128)(2,1)S(1)} %get-tuple-element.46.refs_0_), channel_id=1, source_target_pairs={{0,8},{8,0},{16,24},{24,16},{1,9},{9,1},{17,25},{25,17},{2,10},{10... | collective-permute-start | bytes 786440 | tf_op jit(solution)/shard_map/ppermute | solution.py:379
  33.9 33.3 %collective-permute-start.9 = (bf16[256,1024]{1,0:T(8,128)(2,1)}, bf16[256,1024]{1,0:T(8,128)(2,1)}, u32[]{:S(2)}, u32[]{:S(2)}) collective-permute-start(bf16[256,1024]{1,0:T(8,128)(2,1)} %get-tuple-element.43), channel_id=1, source_target_pairs={{1,0},{2,1},{3,2},{4,3},{5,4},{6,5},{7,6},{9,8},{10,9},{11,10},{12... | collective-permute-start | bytes 1572872 | tf_op jit(solution)/shard_map/ppermute | solution.py:385
  36.4 30.8 %collective-permute-start.8 = (bf16[256,1024]{1,0:T(8,128)(2,1)}, bf16[256,1024]{1,0:T(8,128)(2,1)}, u32[]{:S(2)}, u32[]{:S(2)}) collective-permute-start(bf16[256,1024]{1,0:T(8,128)(2,1)} %get-tuple-element.44), channel_id=1, source_target_pairs={{0,1},{1,2},{2,3},{3,4},{4,5},{5,6},{6,7},{8,9},{9,10},{10,11},{11... | collective-permute-start | bytes 1572872 | tf_op jit(solution)/shard_map/ppermute | solution.py:384
  40.8 6.0 %collective-permute-start.6 = (s32[1]{0:T(128)}, s32[1]{0:T(128)}, u32[]{:S(2)}, u32[]{:S(2)}) collective-permute-start(s32[1]{0:T(128)} %get-tuple-element.51), channel_id=1, source_target_pairs={{0,1},{1,2},{2,3},{3,4},{4,5},{5,6},{6,7},{8,9},{9,10},{10,11},{11... | collective-permute-start | bytes 20 | tf_op jit(solution)/shard_map/ppermute | solution.py:386
  43.2 5.0 %collective-permute-start.7 = (s32[1]{0:T(128)}, s32[1]{0:T(128)}, u32[]{:S(2)}, u32[]{:S(2)}) collective-permute-start(s32[1]{0:T(128)} %get-tuple-element.52), channel_id=1, source_target_pairs={{1,0},{2,1},{3,2},{4,3},{5,4},{6,5},{7,6},{9,8},{10,9},{11,10},{12... | collective-permute-start | bytes 20 | tf_op jit(solution)/shard_map/ppermute | solution.py:387
  50.8 1.6 %copy-start = (bf16[128,8192]{1,0:T(8,128)(2,1)S(1)}, bf16[128,8192]{1,0:T(8,128)(2,1)}, u32[]{:S(2)}) copy-start(bf16[128,8192]{1,0:T(8,128)(2,1)} %all-gather.5.cloned.1.call-done) | copy-start | bytes 6291460
  64.5 33.0 %copy-start.1 = (bf16[2048,128]{1,0:T(8,128)(2,1)}, bf16[2048,128]{1,0:T(8,128)(2,1)S(1)}, u32[]{:S(2)}) copy-start(bf16[2048,128]{1,0:T(8,128)(2,1)S(1)} %get-tuple-element.38.refs_0_) | copy-start | bytes 1572868
  64.5 33.0 %collective-permute-start.3 = (bf16[2048,128]{1,0:T(8,128)(2,1)S(1)}, bf16[2048,128]{1,0:T(8,128)(2,1)S(1)}, u32[]{:S(2)}, u32[]{:S(2)}) collective-permute-start(bf16[2048,128]{1,0:T(8,128)(2,1)S(1)} %get-tuple-element.31), channel_id=1, source_target_pairs={{0,8},{8,0},{16,24},{24,16},{1,9},{9,1},{17,25},{25,17},{2,10},{10... | collective-permute-start | bytes 1572872 | tf_op jit(solution)/shard_map/ppermute | solution.py:414
  64.8 32.7 %collective-permute-start.4 = (bf16[2048,128]{1,0:T(8,128)(2,1)S(1)}, bf16[2048,128]{1,0:T(8,128)(2,1)S(1)}, u32[]{:S(2)}, u32[]{:S(2)}) collective-permute-start(bf16[2048,128]{1,0:T(8,128)(2,1)S(1)} %get-tuple-element.32), channel_id=1, source_target_pairs={{0,16},{8,24},{16,0},{24,8},{1,17},{9,25},{17,1},{25,9},{2,18},{10... | collective-permute-start | bytes 1572872 | tf_op jit(solution)/shard_map/ppermute | solution.py:414
  65.9 31.6 %collective-permute-start.5 = (bf16[2048,128]{1,0:T(8,128)(2,1)S(1)}, bf16[2048,128]{1,0:T(8,128)(2,1)S(1)}, u32[]{:S(2)}, u32[]{:S(2)}) collective-permute-start(bf16[2048,128]{1,0:T(8,128)(2,1)S(1)} %get-tuple-element.33), channel_id=1, source_target_pairs={{0,24},{8,16},{16,8},{24,0},{1,25},{9,17},{17,9},{25,1},{2,26},{10... | collective-permute-start | bytes 1572872 | tf_op jit(solution)/shard_map/ppermute | solution.py:414
  97.5 5.1 %copy-start.2 = (bf16[2048,128]{1,0:T(8,128)(2,1)}, bf16[2048,128]{1,0:T(8,128)(2,1)S(1)}, u32[]{:S(2)}) copy-start(bf16[2048,128]{1,0:T(8,128)(2,1)S(1)} %collective-permute-done.3.refs_1_) | copy-start | bytes 1572868
  97.5 5.1 %copy-start.3 = (bf16[2048,128]{1,0:T(8,128)(2,1)}, bf16[2048,128]{1,0:T(8,128)(2,1)S(1)}, u32[]{:S(2)}) copy-start(bf16[2048,128]{1,0:T(8,128)(2,1)S(1)} %collective-permute-done.4.refs_2_) | copy-start | bytes 1572868
  97.5 5.1 %copy-start.4 = (bf16[2048,128]{1,0:T(8,128)(2,1)}, bf16[2048,128]{1,0:T(8,128)(2,1)S(1)}, u32[]{:S(2)}) copy-start(bf16[2048,128]{1,0:T(8,128)(2,1)S(1)} %collective-permute-done.5.refs_3_) | copy-start | bytes 1572868
  97.5 2.0 %collective-permute-start.10 = (bf16[2048,128]{1,0:T(8,128)(2,1)S(1)}, bf16[2048,128]{1,0:T(8,128)(2,1)S(1)}, u32[]{:S(2)}, u32[]{:S(2)}) collective-permute-start(bf16[2048,128]{1,0:T(8,128)(2,1)S(1)} %get-tuple-element.38.refs_0_), channel_id=1, source_target_pairs={{0,1},{1,0},{2,3},{3,2},{4,5},{5,4},{6,7},{7,6},{8,9},{9,8},{10,11... | collective-permute-start | bytes 1572872 | tf_op jit(solution)/shard_map/ppermute | solution.py:418
  97.8 3.2 %collective-permute-start.11 = (bf16[2048,128]{1,0:T(8,128)(2,1)S(1)}, bf16[2048,128]{1,0:T(8,128)(2,1)S(1)}, u32[]{:S(2)}, u32[]{:S(2)}) collective-permute-start(bf16[2048,128]{1,0:T(8,128)(2,1)S(1)} %collective-permute-done.3.refs_1_), channel_id=1, source_target_pairs={{0,1},{1,0},{2,3},{3,2},{4,5},{5,4},{6,7},{7,6},{8,9},{9,8},{10,11... | collective-permute-start | bytes 1572872 | tf_op jit(solution)/shard_map/ppermute | solution.py:418
  98.1 3.6 %collective-permute-start.12 = (bf16[2048,128]{1,0:T(8,128)(2,1)S(1)}, bf16[2048,128]{1,0:T(8,128)(2,1)S(1)}, u32[]{:S(2)}, u32[]{:S(2)}) collective-permute-start(bf16[2048,128]{1,0:T(8,128)(2,1)S(1)} %collective-permute-done.4.refs_2_), channel_id=1, source_target_pairs={{0,1},{1,0},{2,3},{3,2},{4,5},{5,4},{6,7},{7,6},{8,9},{9,8},{10,11... | collective-permute-start | bytes 1572872 | tf_op jit(solution)/shard_map/ppermute | solution.py:418
  98.3 4.3 %collective-permute-start.13 = (bf16[2048,128]{1,0:T(8,128)(2,1)S(1)}, bf16[2048,128]{1,0:T(8,128)(2,1)}, u32[]{:S(2)}, u32[]{:S(2)}) collective-permute-start(bf16[2048,128]{1,0:T(8,128)(2,1)S(1)} %collective-permute-done.5.refs_3_), channel_id=1, source_target_pairs={{0,1},{1,0},{2,3},{3,2},{4,5},{5,4},{6,7},{7,6},{8,9},{9,8},{10,11... | collective-permute-start | bytes 1572872 | tf_op jit(solution)/shard_map/ppermute | solution.py:418
  99.5 3.1 %copy-start.5 = (bf16[2048,128]{1,0:T(8,128)(2,1)}, bf16[2048,128]{1,0:T(8,128)(2,1)S(1)}, u32[]{:S(2)}) copy-start(bf16[2048,128]{1,0:T(8,128)(2,1)S(1)} %collective-permute-done.10.refs_4_) | copy-start | bytes 1572868
  101.0 1.6 %copy-start.6 = (bf16[2048,128]{1,0:T(8,128)(2,1)}, bf16[2048,128]{1,0:T(8,128)(2,1)S(1)}, u32[]{:S(2)}) copy-start(bf16[2048,128]{1,0:T(8,128)(2,1)S(1)} %collective-permute-done.11.refs_5_) | copy-start | bytes 1572868
  101.8 0.8 copy-start.7
Sparse Core Ops, SparseCore 0:
  9.0 30.7 all-gather.4
  41.3 46.0 all-gather.6

commit v6 on v5

--- a/solution.py
+++ b/solution.py
@@ -43,22 +43,28 @@
         == lax.broadcasted_iota(jnp.int32, (SUB, rows), 0)
     )
 
+    def halo_tag(ref):
+        wide = -(-rows // LANES) * LANES
+        return ref[HW:HW + 16, :wide].astype(jnp.float32)[:1, :rows].astype(jnp.int32)
+
+    head_tag = halo_tag(head_ref)
+    tail_tag = halo_tag(tail_ref)
+
     def left(i):
-        where = (grow_ref[i] + (blk - HW)) // blk
-        tag = jnp.zeros((1, rows), jnp.int32)
-        for b in range(nfill + 2):
-            tag = jnp.where(where == b, se[b], tag)
+        where = (grow_ref[pl.ds(i, 1), :] + (blk - HW)) // blk
+        tag = jnp.where(where == 0, head_tag, tail_tag)
+        for b in range(nfill):
+            tag = jnp.where(where == b + 1, se[b], tag)
         tag = jnp.where(own, jnp.broadcast_to(tag, (SUB, rows)), -1)
-        smat = s_ref[i].astype(jnp.float32)
         parts = []
         for s in range(nse):
             hit = tag == s
             for c in range(nc):
-                parts.append(jnp.where(hit, jnp.broadcast_to(smat[c:c + 1], (SUB, rows)), 0.0))
+                parts.append(jnp.where(hit, jnp.broadcast_to(s_ref[c, pl.ds(i, 1), :], (SUB, rows)), 0.0))
         return jnp.concatenate(parts, axis=0).astype(jnp.bfloat16)
 
-    def matmul(i, srcs, nxt, dsts):
-        lhs = [left(i), left(i + 1)]
+    def matmul(first, i, srcs, nxt, dsts):
+        lhs = [left(first + i), left(first + i + 1)]
         at = pl.multiple_of(i * SUB, 2 * SUB)
         for j in range(0, nlt, 2):
             res = []
@@ -104,8 +110,8 @@
 
         def four(i, carry):
             n = base + 4 * i
-            matmul(4 * i, (g0, g1), n + 2, (g2, g3))
-            matmul(4 * i + 2, (g2, g3), jnp.minimum(n + 4, last), (g0, g1))
+            matmul(base, 4 * i, (g0, g1), n + 2, (g2, g3))
+            matmul(base, 4 * i + 2, (g2, g3), jnp.minimum(n + 4, last), (g0, g1))
             return carry
 
         lax.fori_loop(0, inner // 4, four, 0)
@@ -113,10 +119,10 @@
 
 def combine(conn, se, grow, smat, recovery, head, tail, nse, inner=4, nbuf=6):
     nblk, blk, nb = recovery.shape
-    ngrp, _, rows = grow.shape
+    ngrp, rows = grow.shape
     nel = ngrp * SUB
     ndof = rows // SUB
-    nc = smat.shape[1]
+    nc = smat.shape[0]
     nlt = nb // LANES
     steps = ngrp // inner
     ts = nlt + 1
@@ -133,11 +139,11 @@
             num_scalar_prefetch=2,
             grid=(nblk + steps,),
             in_specs=[
-                pl.BlockSpec((inner, 1, rows), lambda i, c, s: (later(i), 0, 0)),
-                pl.BlockSpec((inner, nc, rows), lambda i, c, s: (later(i), 0, 0)),
+                pl.BlockSpec((ngrp, rows), lambda i, c, s: (0, 0)),
+                pl.BlockSpec((nc, ngrp, rows), lambda i, c, s: (0, 0, 0)),
                 pl.BlockSpec(memory_space=pl.ANY),
-                pl.BlockSpec((HW, nb), lambda i, c, s: (0, 0)),
-                pl.BlockSpec((HW, nb), lambda i, c, s: (0, 0)),
+                pl.BlockSpec((HW + 16, nb), lambda i, c, s: (0, 0)),
+                pl.BlockSpec((HW + 16, nb), lambda i, c, s: (0, 0)),
             ],
             out_specs=pl.BlockSpec((nc, SUB * inner, nse * nb), lambda i, c, s: (0, later(i), 0)),
             scratch_shapes=[
@@ -164,8 +170,8 @@
     def _():
         def one(i, carry):
             at = pl.multiple_of(i * LANES, LANES)
-            rows = jnp.concatenate([s[:, pl.ds(at, LANES)].astype(jnp.float32) for s in srcs] * parts, axis=0)
-            tbl[pl.ds(at, LANES), :] = rows.T
+            rows = jnp.concatenate([s[:, pl.ds(at, LANES)] for s in srcs] * parts, axis=0)
+            tbl[pl.ds(at, LANES), :] = rows.T.astype(jnp.float32)
             return carry
 
         lax.fori_loop(0, nd // LANES, one, 0, unroll=2)
@@ -219,8 +225,8 @@
     def _():
         def one(i, carry):
             at = pl.multiple_of(i * LANES, LANES)
-            rows = jnp.concatenate([src[r, :, pl.ds(at, LANES)].astype(jnp.float32) for r in order], axis=0)
-            tbl[pl.ds(at, LANES), :] = rows.T
+            rows = jnp.concatenate([src[r, :, pl.ds(at, LANES)] for r in order], axis=0)
+            tbl[pl.ds(at, LANES), :] = rows.T.astype(jnp.float32)
             return carry
 
         lax.fori_loop(0, nd // LANES, one, 0, unroll=2)
@@ -266,25 +272,55 @@
     )(idx.reshape(-1), src)
 
 
-def product_kernel(
-    where, w_ref, *refs, ngroup, nrow, tper, half, parts
-):
+def arrange_kernel(near, o_ref, *, nh, per, npair, parts, tper):
+    step_rows = near.shape[1]
+    lane = lax.broadcasted_iota(jnp.int32, (step_rows, LANES), 1) // tper
+    for h in range(nh):
+        got = [near[h * per + j].astype(jnp.float32) for j in range(per)]
+        for p in range(npair):
+            for kp in range(parts):
+                tile = None
+                for j in range(per):
+                    shift = (tper * j - (kp * (LANES // parts) + tper * p)) % LANES
+                    moved = pltpu.roll(got[j], shift, 1) if shift else got[j]
+                    tile = moved if tile is None else jnp.where(lane == j, moved, tile)
+                col = (h * npair + p) * LANES
+                o_ref[kp, :, col:col + LANES] = tile.astype(jnp.bfloat16)
+
+
+def arrange(near, ngroup, tper, k):
+    nrow, nk, _ = near.shape
+    nh = tper * nrow // LANES
+    npair = ngroup // 2
+    parts = k // nk
+    cols = nh * npair * LANES
+    step_rows = min(nk, 256)
+    out = pl.pallas_call(
+        functools.partial(arrange_kernel, nh=nh, per=LANES // tper, npair=npair, parts=parts, tper=tper),
+        out_shape=jax.ShapeDtypeStruct((parts, nk, cols), jnp.bfloat16),
+        grid=(nk // step_rows,),
+        in_specs=[pl.BlockSpec((nrow, step_rows, LANES), lambda i: (0, i, 0))],
+        out_specs=pl.BlockSpec((parts, step_rows, cols), lambda i: (0, i, 0)),
+        compiler_params=pltpu.CompilerParams(
+            dimension_semantics=("arbitrary",), vmem_limit_bytes=40 << 20
+        ),
+        name="arrange",
+    )(near)
+    return out.reshape(k, cols)
+
+
+def product_kernel(where, w_ref, *refs, ngroup, nh, half):
     mine = refs[:ngroup]
     theirs = refs[ngroup:2 * ngroup]
-    near_hbm, o_ref, bt, near, sem = refs[2 * ngroup:]
+    near_hbm, o_ref, bt, sem = refs[2 * ngroup:]
     group = where[0]
     core = where[1]
-    nh = tper * nrow // LANES
-    per = LANES // tper
-    npair = ngroup * half // tper
+    npair = ngroup // 2
     rows = bt.shape[0] // 2
-    nk = bt.shape[0] // parts
 
     @pl.when(pl.program_id(0) == 0)
     def _():
-        last = pltpu.make_async_copy(near_hbm, near, sem.at[2 * ngroup])
-        last.start()
-        copies = []
+        copies = [pltpu.make_async_copy(near_hbm, bt.at[:, ngroup * LANES:], sem.at[2 * ngroup])]
         for s in range(ngroup):
             cols = slice(s * LANES, (s + 1) * LANES)
             for d, ref in ((0, mine[s]), (1, theirs[s])):
@@ -292,26 +328,6 @@
                 copies.append(pltpu.make_async_copy(ref, bt.at[pl.ds(at, rows), cols], sem.at[2 * s + d]))
         for c in copies:
             c.start()
-        last.wait()
-        step_rows = min(nk, 128)
-        lane = lax.broadcasted_iota(jnp.int32, (step_rows, LANES), 1) // tper
-
-        def arrange(i, carry):
-            at = pl.multiple_of(i * step_rows, step_rows)
-            for h in range(nh):
-                got = [near[h * per + j, pl.ds(at, step_rows), :].astype(jnp.float32) for j in range(per)]
-                for p in range(npair):
-                    for kp in range(parts):
-                        tile = None
-                        for j in range(per):
-                            shift = (tper * j - (kp * (LANES // parts) + tper * p)) % LANES
-                            moved = pltpu.roll(got[j], shift, 1) if shift else got[j]
-                            tile = moved if tile is None else jnp.where(lane == j, moved, tile)
-                        col = (ngroup + h * npair + p) * LANES
-                        bt[pl.ds(kp * nk + at, step_rows), col:col + LANES] = tile.astype(jnp.bfloat16)
-            return carry
-
-        lax.fori_loop(0, nk // step_rows, arrange, 0)
         for c in copies:
             c.wait()
 
@@ -330,15 +346,12 @@
             o_ref[:, pl.ds(col, LANES)] = tile
 
 
-def product(where, w, mine, theirs, near, tper, snap):
+def product(where, w, mine, theirs, near, half, snap):
     m, k = w.shape
     ngroup = len(mine)
-    nrow, nk, _ = near.shape
-    mb = 256
+    mb = 384
     return pl.pallas_call(
-        functools.partial(
-            product_kernel, ngroup=ngroup, nrow=nrow, tper=tper, half=tper // 2, parts=k // nk
-        ),
+        functools.partial(product_kernel, ngroup=ngroup, nh=snap // (ngroup * LANES), half=half),
         out_shape=jax.ShapeDtypeStruct((m, snap), jnp.bfloat16),
         grid_spec=pltpu.PrefetchScalarGridSpec(
             num_scalar_prefetch=1,
@@ -348,7 +361,6 @@
             out_specs=pl.BlockSpec((mb, snap), lambda i, c: (i, 0)),
             scratch_shapes=[
                 pltpu.VMEM((k, snap), jnp.bfloat16),
-                pltpu.VMEM(near.shape, jnp.bfloat16),
                 pltpu.SemaphoreType.DMA((2 * ngroup + 1,)),
             ],
         ),
@@ -381,16 +393,17 @@
     ends = nrow - 1
     up = [(i, i + 1) for i in range(ends)]
     down = [(i + 1, i) for i in range(ends)]
-    head = lax.ppermute(recovery[nblk - 1, blk - HW:], "row", up)
-    tail = lax.ppermute(recovery[0, :HW], "row", down)
-    head_se = lax.ppermute(block_se[-1:], "row", up)
-    tail_se = lax.ppermute(block_se[:1], "row", down)
-    se_all = jnp.concatenate([head_se, block_se, tail_se])
+
+    def with_se(part, se):
+        return jnp.concatenate([part, jnp.full((16, nb), se.astype(part.dtype))])
+
+    last_rows = with_se(recovery[nblk - 1, blk - HW:], block_se[nblk - 1])
+    first_rows = with_se(recovery[0, :HW], block_se[0])
 
     ngrp = nel // SUB
-    conn = connect.T.reshape(ndof, ngrp, SUB).transpose(1, 0, 2).reshape(ngrp, 1, ndof * SUB)
-    smat = stress_mat.transpose(1, 2, 0).reshape(nc, ndof, ngrp, SUB).transpose(2, 0, 1, 3)
-    smat = smat.reshape(ngrp, nc, ndof * SUB)
+    conn = connect.T.reshape(ndof, ngrp, SUB).transpose(1, 0, 2).reshape(ngrp, ndof * SUB)
+    smat = stress_mat.transpose(1, 2, 0).astype(jnp.float32).reshape(nc, ndof, ngrp, SUB)
+    smat = smat.transpose(0, 2, 1, 3).reshape(nc, ngrp, ndof * SUB)
     flat = conn.reshape(-1) * (nb // LANES + 1)
     where = jnp.stack([group, core]).astype(jnp.int32)
 
@@ -402,21 +415,25 @@
         lax.dynamic_index_in_dim(mid, group ^ s, 0, keepdims=False) for s in range(ngroup)
     ])
 
-    own_idx, far_idx, flat, conn, smat, where = lax.optimization_barrier(
-        (own_idx, far_idx, flat, conn, smat, where)
+    own_idx, far_idx, flat, conn, smat, where, last_rows, first_rows = lax.optimization_barrier(
+        (own_idx, far_idx, flat, conn, smat, where, last_rows, first_rows)
     )
     picked = pick_near(own_idx, along_group)
     picked, far_idx = lax.optimization_barrier((picked, far_idx))
     near = lax.all_gather(picked, "row", axis=0, tiled=False)
+    head = lax.ppermute(last_rows, "row", up)
+    tail = lax.ppermute(first_rows, "row", down)
     per = LANES // tper
     order = [per * h + j for j in range(per) for h in range(nrow // per)]
     far = pick_far(far_idx.reshape(ngroup, rows), along_row, order)
     mine = [far[0]] + [lax.ppermute(far[s], "group", swap(s)) for s in range(1, ngroup)]
     flat, mine[0] = lax.optimization_barrier((flat, mine[0]))
-    w = combine(flat, se_all, conn, smat, recovery, head, tail, nse)
+    w = combine(flat, block_se, conn, smat, recovery, head, tail, nse)
     *mine, w = lax.optimization_barrier((*mine, w))
     theirs = [lax.ppermute(x, "row", other) for x in mine]
-    out = product(where, w.reshape(nc * nel, nse * nb), mine, theirs, near, tper, snap)
+    near, w = lax.optimization_barrier((near, w))
+    near = arrange(near, ngroup, tper, nse * nb)
+    out = product(where, w.reshape(nc * nel, nse * nb), mine, theirs, near, half, snap)
     return out.reshape(nc, nel, snap).transpose(1, 0, 2)
 
 

time: 151 us -> 144 us (0.954)
  waiting for transfers between devices: 11 us -> 0.07 us
  local copies, waits for them, and re-layouts: 14.5 us -> 21.1 us
  starting transfers between devices: 16.5 us -> 14 us
    ppermute x3, waiting for transfers between devices: 6.35 us -> 0.01 us  [body(): lax.ppermute(bottom, 'group', swap(s))]
    unnamed x18 -> x20, local copies, waits for them, and re-layouts: 2.43 us -> 7.04 us
    concatenate x0 -> x2, local copies, waits for them, and re-layouts: none -> 3.47 us  [with_se(): return jnp.concatenate([part, jnp.full((16, nb), se.astype(part.dtype))])]
    ppermute x4 -> x2, starting transfers between devices: 9.91 us -> 6.54 us  [the longest x1 4.61 us: body(): head = lax.ppermute(last_rows, 'row', up)]
    ppermute x4, waiting for transfers between devices: 3.14 us -> 0.01 us  [body(): theirs = [lax.ppermute(x, 'row', other) for x in mine]]
    concatenate x1 -> x0, other arithmetic: 2.55 us -> none  [body(): se_all = jnp.concatenate([head_se, block_se, tail_se])]
    transpose x2 -> x0, local copies, waits for them, and re-layouts: 1.81 us -> none  [body(): stress_mat.transpose(1, 2, 0).reshape(nc, ndof, ngrp, SUB)]
    pallas_call x1 -> x2, Pallas kernels: 40.5 us -> 41.2 us  [the longest x1 36.6 us: product(): pl.pallas_call(functools.partial(product_kernel, ngroup=ngroup, nh=snap /...]
  transfers between devices with their start and end apart: 16 -> 14, of which waited for: 5 -> 0; matrix products, arithmetic and copies ran while one was open for 9% -> 10% of each run, Pallas kernels for 34% -> 38%
where the time goes in v6:
time: 144 us; the launch traced here: 141 us
  Pallas kernels  90.3 us (63%)
  local copies, waits for them, and re-layouts  21.1 us (15%)
  starting transfers between devices  14 us (10%)
  between operations  13.7 us (10%)
  other arithmetic  2.24 us (2%)
    pallas_call x1, Pallas kernels, product(): pl.pallas_call(functools.partial(product_kernel, ngroup=ngroup, nh=snap /...  36.6 us
    pallas_call x1, Pallas kernels, combine(): pl.pallas_call(kern, out_shape=jax.ShapeDtypeStruct((nc, nel, nse * nb),...  30.5 us
    pallas_call x1, Pallas kernels, pick_far(): pl.pallas_call(functools.partial(pick_far_kernel, nout=nout, order=order,...  11.1 us
    pallas_call x1, Pallas kernels, pick_near(): pl.pallas_call(functools.partial(pick_near_kernel, nsrc=len(srcs), half=h...  7.42 us
    unnamed x20, local copies, waits for them, and re-layouts  7.04 us
    pallas_call x1, Pallas kernels, arrange(): pl.pallas_call(functools.partial(arrange_kernel, nh=nh, per=LANES // tper...  4.66 us
    ppermute x1, starting transfers between devices, body(): head = lax.ppermute(last_rows, 'row', up)  4.61 us
    concatenate x2, local copies, waits for them, and re-layouts, with_se(): return jnp.concatenate([part, jnp.full((16, nb), se.astype(part.dtype))])  3.47 us
  transfers between devices with their start and end apart: 14, of which 0 were waited for; matrix products, arithmetic and copies ran while one was open for 10% of the time, Pallas kernels for 38%

profile of v6, /device:TPU:11, one launch (start us, length us, event | category | flops | bytes accessed | tf_op | source)
XLA Modules:
  0.0 141.4 jit_solution(490812159006482451)
XLA Ops:
  6.5 1.8 %fusion = (bf16[16,8192]{1,0:T(8,128)(2,1)}, bf16[16,8192]{1,0:T(8,128)(2,1)S(1)}) fusion(bf16[32,8192]{1,0:T(8,128)(2,1)} %param.6), kind=kLoop, calls=%fused_computation.11 | loop fusion | bytes 1048576 | tf_op jit(solution)/shard_map/slice | solution.py:388
  8.3 0.0 all-gather.7.cloned.1.call-update
  8.3 0.0 all-gather.5.cloned.1.call-start
  8.4 1.3 collective-permute-start.2
  9.6 0.2 collective-permute-start.1
  9.9 1.2 collective-permute-start
  11.1 0.7 convert.8
  11.7 0.9 reshape.44
  12.6 0.9 copy.16
  13.6 0.2 copy.17
  13.8 0.9 convert_bitcast_fusion
  14.7 2.3 %slice_bitcast_fusion = (bf16[256,1024]{1,0:T(8,128)(2,1)}, bf16[256,1024]{1,0:T(8,128)(2,1)}) fusion(bf16[16,512,1024]{2,1,0:T(8,128)(2,1)} %rec_hbm.1), kind=kLoop, calls=%fused_computation | loop fusion | bytes 2097152 | tf_op jit(solution)/shard_map/squeeze | solution.py:401
  17.0 0.7 fusion.1
  17.7 0.3 copy.18
  18.0 0.9 mul.11.conn
  18.9 0.5 copy.19
  19.4 0.5 copy.20
  19.9 1.7 %concatenate.11 = bf16[272,1024]{1,0:T(8,128)(2,1)S(1)} pad(bf16[256,1024]{1,0:T(8,128)(2,1)} %get-tuple-element.51, bf16[]{:T(256)} %bitcast.17), padding=0_16x0_0 | pad | bytes 1081346 | tf_op jit(solution)/shard_map/concatenate | solution.py:398
  21.6 1.8 %concatenate.10 = bf16[272,1024]{1,0:T(8,128)(2,1)S(1)} pad(bf16[256,1024]{1,0:T(8,128)(2,1)} %get-tuple-element.52, bf16[]{:T(256)} %bitcast.15), padding=0_16x0_0 | pad | bytes 1081346 | tf_op jit(solution)/shard_map/concatenate | solution.py:398
  23.4 0.6 pad_add_fusion.1.where
  24.1 0.0 collective-permute-done.refs_1_
  24.1 7.4 %pick_near.1 = bf16[2048,128]{1,0:T(8,128)(2,1)} custom-call(s32[4096]{0:T(1024)S(1)} %bitcast.37, bf16[16,8192]{1,0:T(8,128)(2,1)S(1)} %get-tuple-element.54.refs_0_, bf16[16,8192]{1,0:T(8,128)(2,1)S(1)} %collective-permute-done.refs_1_, bf16[16,8192]{1,0:T(8,128)(2,1)S(1)} %collective-permute-done.1.refs_2_, ...), custom_call_target="tpu_custom_call" | custom-call | tf_op jit(solution)/shard_map/pick_near/pallas_call | solution.py:200
  31.5 0.0 all-gather.5.cloned.1.call-update
  31.5 4.6 %collective-permute-start.6 = (bf16[272,1024]{1,0:T(8,128)(2,1)S(1)}, bf16[272,1024]{1,0:T(8,128)(2,1)}, u32[]{:S(2)}, u32[]{:S(2)}) collective-permute-start(bf16[272,1024]{1,0:T(8,128)(2,1)S(1)} %concatenate.10), channel_id=1, source_target_pairs={{0,1},{1,2},{2,3},{3,4},{4,5},{5,6},{6,7},{8,9},{9,10},{10,11},{11... | collective-permute-start | bytes 1671176 | tf_op jit(solution)/shard_map/ppermute | solution.py:424
  36.1 1.9 %collective-permute-start.7 = (bf16[272,1024]{1,0:T(8,128)(2,1)S(1)}, bf16[272,1024]{1,0:T(8,128)(2,1)}, u32[]{:S(2)}, u32[]{:S(2)}) collective-permute-start(bf16[272,1024]{1,0:T(8,128)(2,1)S(1)} %concatenate.11), channel_id=1, source_target_pairs={{1,0},{2,1},{3,2},{4,3},{5,4},{6,5},{7,6},{9,8},{10,9},{11,10},{12... | collective-permute-start | bytes 1671176 | tf_op jit(solution)/shard_map/ppermute | solution.py:425
  38.1 0.7 copy.21.grow_ref
  38.8 1.0 copy.22.s_ref
  39.8 1.6 %copy-done.2 = bf16[128,8192]{1,0:T(8,128)(2,1)S(1)} copy-done((bf16[128,8192]{1,0:T(8,128)(2,1)S(1)}, bf16[128,8192]{1,0:T(8,128)(2,1)}, u32[]{:S(2)}) %copy-start.2) | copy-done | bytes 2097176
  41.4 11.1 %pick_far.1 = (bf16[2048,128]{1,0:T(8,128)(2,1)S(1)}, bf16[2048,128]{1,0:T(8,128)(2,1)S(1)}, bf16[2048,128]{1,0:T(8,128)(2,1)S(1)}, bf16[2048,128]{1,0:T(8,128)(2,1)S(1)}) custom-call(s32[8192]{0:T(1024)S(1)} %pad_add_fusion.idx, bf16[8,16,8192]{2,1,0:T(8,128)(2,1)S(1)} %bitcast.36), custom_call_target="tpu_custom_call" | custom-call | tf_op jit(solution)/shard_map/pick_far/pallas_call | solution.py:256
  52.5 0.3 collective-permute-start.3
  52.8 1.2 collective-permute-start.4
  54.1 1.1 collective-permute-start.5
  55.2 0.0 collective-permute-done.6.head_ref
  55.2 0.0 collective-permute-done.7.tail_ref
  55.2 30.5 %combine.1 = bf16[6,512,4096]{2,1,0:T(8,128)(2,1)} custom-call(s32[12288]{0:T(1024)} %mul.11.conn, s32[16]{0:T(128)} %se.1, s32[64,192]{1,0:T(8,128)} %copy.21.grow_ref, f32[6,64,192]{2,1,0:T(8,128)} %copy.22.s_ref, bf16[16,512,1024]{2,1,0:T(8,128)(2,1)} %rec_hbm.1, bf16[272,1024]{1,0:T(8,128)(2,1)} %collective-permute-done.6.head_ref, ...), custom_call_target="tpu_custom_call" | custom-call | flops 30000001024 | bytes 125829120 | tf_op jit(solution)/shard_map/combine/pallas_call | solution.py:135
  85.7 0.0 collective-permute-done.4.refs_2_
  85.8 1.5 %collective-permute-start.8 = (bf16[2048,128]{1,0:T(8,128)(2,1)S(1)}, bf16[2048,128]{1,0:T(8,128)(2,1)S(1)}, u32[]{:S(2)}, u32[]{:S(2)}) collective-permute-start(bf16[2048,128]{1,0:T(8,128)(2,1)S(1)} %get-tuple-element.46.refs_0_), channel_id=1, source_target_pairs={{0,1},{1,0},{2,3},{3,2},{4,5},{5,4},{6,7},{7,6},{8,9},{9,8},{10,11... | collective-permute-start | bytes 1572872 | tf_op jit(solution)/shard_map/ppermute | solution.py:433
  87.2 0.1 collective-permute-start.9
  87.3 0.4 collective-permute-start.10
  87.7 0.1 collective-permute-start.11
  87.8 2.2 %copy-done.1 = bf16[16384,128]{1,0:T(8,128)(2,1)S(1)} copy-done((bf16[16384,128]{1,0:T(8,128)(2,1)S(1)}, bf16[16384,128]{1,0:T(8,128)(2,1)}, u32[]{:S(2)}) %copy-start.1) | copy-done | bytes 4194328
  90.0 4.7 %arrange.1 = bf16[2,2048,512]{2,1,0:T(8,128)(2,1)S(1)} custom-call(bf16[8,2048,128]{2,1,0:T(8,128)(2,1)S(1)} %bitcast.35), custom_call_target="tpu_custom_call" | custom-call | tf_op jit(solution)/shard_map/arrange/pallas_call | solution.py:298
  94.7 2.0 %copy-done = bf16[2,2048,512]{2,1,0:T(8,128)(2,1)} copy-done((bf16[2,2048,512]{2,1,0:T(8,128)(2,1)}, bf16[2,2048,512]{2,1,0:T(8,128)(2,1)S(1)}, u32[]{:S(2)}) %copy-start) | copy-done | bytes 4194328
  96.7 0.7 copy-done.5
  97.5 0.2 copy-done.6
  97.6 0.2 copy-done.7
  97.8 0.1 copy-done.8
  98.0 36.6 %product.1 = bf16[3072,1024]{1,0:T(8,128)(2,1)} custom-call(s32[2]{0:T(128)} %pad_add_fusion.1.where, bf16[3072,4096]{1,0:T(8,128)(2,1)} %bitcast.38, bf16[2048,128]{1,0:T(8,128)(2,1)} %copy-done.3, bf16[2048,128]{1,0:T(8,128)(2,1)} %copy-done.4, bf16[2048,128]{1,0:T(8,128)(2,1)} %collective-permute-done.4.refs_2_, ...), custom_call_target="tpu_custom_call" | custom-call | tf_op jit(solution)/shard_map/product/pallas_call | solution.py:353
  (27 shorter events, 0.1 us)
Async XLA Ops:
  6.5 33.2 %all-gather.7.cloned.1.call-start = ((), (), s32[]{:S(2)}) async-start(), calls=%async_computation.1 | async-start | bytes 2359296 | tf_op jit(solution)/shard_map/all_gather | solution.py:390
  8.3 79.5 %all-gather.5.cloned.1.call-start = ((), (), s32[]{:S(2)}) async-start(), calls=%async_computation | async-start | bytes 4718592 | tf_op jit(solution)/shard_map/all_gather | solution.py:423
  8.4 15.7 %collective-permute-start.2 = (bf16[16,8192]{1,0:T(8,128)(2,1)S(1)}, bf16[16,8192]{1,0:T(8,128)(2,1)S(1)}, u32[]{:S(2)}, u32[]{:S(2)}) collective-permute-start(bf16[16,8192]{1,0:T(8,128)(2,1)S(1)} %get-tuple-element.54.refs_0_), channel_id=1, source_target_pairs={{0,24},{8,16},{16,8},{24,0},{1,25},{9,17},{17,9},{25,1},{2,26},{10... | collective-permute-start | bytes 786440 | tf_op jit(solution)/shard_map/ppermute | solution.py:391
  9.6 14.4 %collective-permute-start.1 = (bf16[16,8192]{1,0:T(8,128)(2,1)S(1)}, bf16[16,8192]{1,0:T(8,128)(2,1)S(1)}, u32[]{:S(2)}, u32[]{:S(2)}) collective-permute-start(bf16[16,8192]{1,0:T(8,128)(2,1)S(1)} %get-tuple-element.54.refs_0_), channel_id=1, source_target_pairs={{0,16},{8,24},{16,0},{24,8},{1,17},{9,25},{17,1},{25,9},{2,18},{10... | collective-permute-start | bytes 786440 | tf_op jit(solution)/shard_map/ppermute | solution.py:391
  9.9 14.2 %collective-permute-start = (bf16[16,8192]{1,0:T(8,128)(2,1)S(1)}, bf16[16,8192]{1,0:T(8,128)(2,1)S(1)}, u32[]{:S(2)}, u32[]{:S(2)}) collective-permute-start(bf16[16,8192]{1,0:T(8,128)(2,1)S(1)} %get-tuple-element.54.refs_0_), channel_id=1, source_target_pairs={{0,8},{8,0},{16,24},{24,16},{1,9},{9,1},{17,25},{25,17},{2,10},{10... | collective-permute-start | bytes 786440 | tf_op jit(solution)/shard_map/ppermute | solution.py:391
  31.5 23.7 %collective-permute-start.6 = (bf16[272,1024]{1,0:T(8,128)(2,1)S(1)}, bf16[272,1024]{1,0:T(8,128)(2,1)}, u32[]{:S(2)}, u32[]{:S(2)}) collective-permute-start(bf16[272,1024]{1,0:T(8,128)(2,1)S(1)} %concatenate.10), channel_id=1, source_target_pairs={{0,1},{1,2},{2,3},{3,4},{4,5},{5,6},{6,7},{8,9},{9,10},{10,11},{11... | collective-permute-start | bytes 1671176 | tf_op jit(solution)/shard_map/ppermute | solution.py:424
  36.1 19.1 %collective-permute-start.7 = (bf16[272,1024]{1,0:T(8,128)(2,1)S(1)}, bf16[272,1024]{1,0:T(8,128)(2,1)}, u32[]{:S(2)}, u32[]{:S(2)}) collective-permute-start(bf16[272,1024]{1,0:T(8,128)(2,1)S(1)} %concatenate.11), channel_id=1, source_target_pairs={{1,0},{2,1},{3,2},{4,3},{5,4},{6,5},{7,6},{9,8},{10,9},{11,10},{12... | collective-permute-start | bytes 1671176 | tf_op jit(solution)/shard_map/ppermute | solution.py:425
  39.8 1.6 %copy-start.2 = (bf16[128,8192]{1,0:T(8,128)(2,1)S(1)}, bf16[128,8192]{1,0:T(8,128)(2,1)}, u32[]{:S(2)}) copy-start(bf16[128,8192]{1,0:T(8,128)(2,1)} %all-gather.7.cloned.1.call-done) | copy-start | bytes 6291460
  52.5 33.3 %copy-start.3 = (bf16[2048,128]{1,0:T(8,128)(2,1)}, bf16[2048,128]{1,0:T(8,128)(2,1)S(1)}, u32[]{:S(2)}) copy-start(bf16[2048,128]{1,0:T(8,128)(2,1)S(1)} %get-tuple-element.46.refs_0_) | copy-start | bytes 1572868
  52.5 33.2 %collective-permute-start.3 = (bf16[2048,128]{1,0:T(8,128)(2,1)S(1)}, bf16[2048,128]{1,0:T(8,128)(2,1)S(1)}, u32[]{:S(2)}, u32[]{:S(2)}) collective-permute-start(bf16[2048,128]{1,0:T(8,128)(2,1)S(1)} %get-tuple-element.36), channel_id=1, source_target_pairs={{0,8},{8,0},{16,24},{24,16},{1,9},{9,1},{17,25},{25,17},{2,10},{10... | collective-permute-start | bytes 1572872 | tf_op jit(solution)/shard_map/ppermute | solution.py:429
  52.8 32.9 %collective-permute-start.4 = (bf16[2048,128]{1,0:T(8,128)(2,1)S(1)}, bf16[2048,128]{1,0:T(8,128)(2,1)}, u32[]{:S(2)}, u32[]{:S(2)}) collective-permute-start(bf16[2048,128]{1,0:T(8,128)(2,1)S(1)} %get-tuple-element.37), channel_id=1, source_target_pairs={{0,16},{8,24},{16,0},{24,8},{1,17},{9,25},{17,1},{25,9},{2,18},{10... | collective-permute-start | bytes 1572872 | tf_op jit(solution)/shard_map/ppermute | solution.py:429
  54.1 31.7 %collective-permute-start.5 = (bf16[2048,128]{1,0:T(8,128)(2,1)S(1)}, bf16[2048,128]{1,0:T(8,128)(2,1)}, u32[]{:S(2)}, u32[]{:S(2)}) collective-permute-start(bf16[2048,128]{1,0:T(8,128)(2,1)S(1)} %get-tuple-element.38), channel_id=1, source_target_pairs={{0,24},{8,16},{16,8},{24,0},{1,25},{9,17},{17,9},{25,1},{2,26},{10... | collective-permute-start | bytes 1572872 | tf_op jit(solution)/shard_map/ppermute | solution.py:429
  85.7 11.0 %copy-start.4 = (bf16[2048,128]{1,0:T(8,128)(2,1)}, bf16[2048,128]{1,0:T(8,128)(2,1)S(1)}, u32[]{:S(2)}) copy-start(bf16[2048,128]{1,0:T(8,128)(2,1)S(1)} %collective-permute-done.3.refs_1_) | copy-start | bytes 1572868
  85.8 10.9 %collective-permute-start.8 = (bf16[2048,128]{1,0:T(8,128)(2,1)S(1)}, bf16[2048,128]{1,0:T(8,128)(2,1)S(1)}, u32[]{:S(2)}, u32[]{:S(2)}) collective-permute-start(bf16[2048,128]{1,0:T(8,128)(2,1)S(1)} %get-tuple-element.46.refs_0_), channel_id=1, source_target_pairs={{0,1},{1,0},{2,3},{3,2},{4,5},{5,4},{6,7},{7,6},{8,9},{9,8},{10,11... | collective-permute-start | bytes 1572872 | tf_op jit(solution)/shard_map/ppermute | solution.py:433
  87.2 9.4 %collective-permute-start.9 = (bf16[2048,128]{1,0:T(8,128)(2,1)S(1)}, bf16[2048,128]{1,0:T(8,128)(2,1)S(1)}, u32[]{:S(2)}, u32[]{:S(2)}) collective-permute-start(bf16[2048,128]{1,0:T(8,128)(2,1)S(1)} %collective-permute-done.3.refs_1_), channel_id=1, source_target_pairs={{0,1},{1,0},{2,3},{3,2},{4,5},{5,4},{6,7},{7,6},{8,9},{9,8},{10,11... | collective-permute-start | bytes 1572872 | tf_op jit(solution)/shard_map/ppermute | solution.py:433
  87.3 9.4 %collective-permute-start.10 = (bf16[2048,128]{1,0:T(8,128)(2,1)}, bf16[2048,128]{1,0:T(8,128)(2,1)S(1)}, u32[]{:S(2)}, u32[]{:S(2)}) collective-permute-start(bf16[2048,128]{1,0:T(8,128)(2,1)} %collective-permute-done.4.refs_2_), channel_id=1, source_target_pairs={{0,1},{1,0},{2,3},{3,2},{4,5},{5,4},{6,7},{7,6},{8,9},{9,8},{10,11... | collective-permute-start | bytes 1572872 | tf_op jit(solution)/shard_map/ppermute | solution.py:433
  87.7 9.0 %collective-permute-start.11 = (bf16[2048,128]{1,0:T(8,128)(2,1)}, bf16[2048,128]{1,0:T(8,128)(2,1)S(1)}, u32[]{:S(2)}, u32[]{:S(2)}) collective-permute-start(bf16[2048,128]{1,0:T(8,128)(2,1)} %collective-permute-done.5.refs_3_), channel_id=1, source_target_pairs={{0,1},{1,0},{2,3},{3,2},{4,5},{5,4},{6,7},{7,6},{8,9},{9,8},{10,11... | collective-permute-start | bytes 1572872 | tf_op jit(solution)/shard_map/ppermute | solution.py:433
  87.8 2.2 %copy-start.1 = (bf16[16384,128]{1,0:T(8,128)(2,1)S(1)}, bf16[16384,128]{1,0:T(8,128)(2,1)}, u32[]{:S(2)}) copy-start(bf16[16384,128]{1,0:T(8,128)(2,1)} %all-gather.5.cloned.1.call-done) | copy-start | bytes 12582916
  94.7 2.0 %copy-start = (bf16[2,2048,512]{2,1,0:T(8,128)(2,1)}, bf16[2,2048,512]{2,1,0:T(8,128)(2,1)S(1)}, u32[]{:S(2)}) copy-start(bf16[2,2048,512]{2,1,0:T(8,128)(2,1)S(1)} %arrange.1) | copy-start | bytes 12582916
  96.7 0.8 copy-start.5
  96.7 1.0 copy-start.6
  96.7 1.1 copy-start.7
  96.7 1.3 copy-start.8
Sparse Core Ops, SparseCore 0:
  9.0 30.6 all-gather.6
  41.2 45.1 all-gather.4

commit v7 on v6

--- a/solution.py
+++ b/solution.py
@@ -215,14 +215,22 @@
     )(idx, *srcs)
 
 
-def pick_far_kernel(idx, src, *refs, nout, order, half, chunk, per_out):
-    outs = refs[:nout]
-    tbl, buf = refs[nout:]
+def pick_far_kernel(idx, slots, *refs, nsrc, order, chunk):
+    srcs = refs[:nsrc]
+    o_ref, src, tbl, buf, sem = refs[nsrc:]
     step = pl.program_id(0)
     nd = tbl.shape[0]
 
     @pl.when(step == 0)
     def _():
+        copies = [
+            pltpu.make_async_copy(ref, src.at[slots[i]], sem.at[i]) for i, ref in enumerate(srcs)
+        ]
+        for copy in copies:
+            copy.start()
+        for copy in copies:
+            copy.wait()
+
         def one(i, carry):
             at = pl.multiple_of(i * LANES, LANES)
             rows = jnp.concatenate([src[r, :, pl.ds(at, LANES)] for r in order], axis=0)
@@ -238,45 +246,56 @@
         return carry
 
     lax.fori_loop(0, chunk // 64, some, 0)
-    for s in range(nout):
-        @pl.when(step // per_out == s)
-        def _():
-            outs[s][...] = buf[...].astype(jnp.bfloat16)
-
-
-def pick_far(idx, src, order):
-    nrow, half, nd = src.shape
-    nout, n = idx.shape
+    o_ref[...] = buf[...].astype(jnp.bfloat16)
+
+
+def pick_far(idx, slots, srcs, order):
+    nrow = len(srcs)
+    half, nd = srcs[0].shape
+    n = idx.shape[0]
     chunk = min(n, 1024)
-    per_out = n // chunk
-
-    def place(s):
-        return lambda i, c: (jnp.clip(i - s * per_out, 0, per_out - 1), 0)
-
     return pl.pallas_call(
-        functools.partial(
-            pick_far_kernel, nout=nout, order=order, half=half, chunk=chunk, per_out=per_out
-        ),
-        out_shape=[jax.ShapeDtypeStruct((n, LANES), jnp.bfloat16) for _ in range(nout)],
+        functools.partial(pick_far_kernel, nsrc=nrow, order=order, chunk=chunk),
+        out_shape=jax.ShapeDtypeStruct((n, LANES), jnp.bfloat16),
         grid_spec=pltpu.PrefetchScalarGridSpec(
-            num_scalar_prefetch=1,
-            grid=(nout * per_out,),
-            in_specs=[pl.BlockSpec((nrow, half, nd), lambda i, c: (0, 0, 0))],
-            out_specs=[pl.BlockSpec((chunk, LANES), place(s)) for s in range(nout)],
-            scratch_shapes=[pltpu.VMEM((nd, LANES), jnp.float32), pltpu.VMEM((chunk, LANES), jnp.float32)],
+            num_scalar_prefetch=2,
+            grid=(n // chunk,),
+            in_specs=[pl.BlockSpec(memory_space=pl.ANY)] * nrow,
+            out_specs=pl.BlockSpec((chunk, LANES), lambda i, c, d: (i, 0)),
+            scratch_shapes=[
+                pltpu.VMEM((nrow, half, nd), jnp.bfloat16),
+                pltpu.VMEM((nd, LANES), jnp.float32),
+                pltpu.VMEM((chunk, LANES), jnp.float32),
+                pltpu.SemaphoreType.DMA((nrow,)),
+            ],
         ),
         compiler_params=pltpu.CompilerParams(
             dimension_semantics=("arbitrary",), vmem_limit_bytes=40 << 20
         ),
         name="pick_far",
-    )(idx.reshape(-1), src)
-
-
-def arrange_kernel(near, o_ref, *, nh, per, npair, parts, tper):
-    step_rows = near.shape[1]
+    )(idx, slots, *srcs)
+
+
+def arrange_kernel(slots, *refs, nsrc, nh, per, npair, parts, tper):
+    srcs = refs[:nsrc]
+    o_ref, near, sem = refs[nsrc:]
+    step_rows = o_ref.shape[1]
+    step = pl.program_id(0)
+
+    @pl.when(step == 0)
+    def _():
+        copies = [
+            pltpu.make_async_copy(ref, near.at[slots[i]], sem.at[i]) for i, ref in enumerate(srcs)
+        ]
+        for copy in copies:
+            copy.start()
+        for copy in copies:
+            copy.wait()
+
     lane = lax.broadcasted_iota(jnp.int32, (step_rows, LANES), 1) // tper
+    at = pl.multiple_of(step * step_rows, step_rows)
     for h in range(nh):
-        got = [near[h * per + j].astype(jnp.float32) for j in range(per)]
+        got = [near[h * per + j, pl.ds(at, step_rows), :].astype(jnp.float32) for j in range(per)]
         for p in range(npair):
             for kp in range(parts):
                 tile = None
@@ -288,31 +307,38 @@
                 o_ref[kp, :, col:col + LANES] = tile.astype(jnp.bfloat16)
 
 
-def arrange(near, ngroup, tper, k):
-    nrow, nk, _ = near.shape
+def arrange(slots, srcs, ngroup, tper, k):
+    nrow = len(srcs)
+    nk = srcs[0].shape[0]
     nh = tper * nrow // LANES
     npair = ngroup // 2
     parts = k // nk
     cols = nh * npair * LANES
     step_rows = min(nk, 256)
     out = pl.pallas_call(
-        functools.partial(arrange_kernel, nh=nh, per=LANES // tper, npair=npair, parts=parts, tper=tper),
+        functools.partial(
+            arrange_kernel, nsrc=nrow, nh=nh, per=LANES // tper, npair=npair, parts=parts, tper=tper
+        ),
         out_shape=jax.ShapeDtypeStruct((parts, nk, cols), jnp.bfloat16),
-        grid=(nk // step_rows,),
-        in_specs=[pl.BlockSpec((nrow, step_rows, LANES), lambda i: (0, i, 0))],
-        out_specs=pl.BlockSpec((parts, step_rows, cols), lambda i: (0, i, 0)),
+        grid_spec=pltpu.PrefetchScalarGridSpec(
+            num_scalar_prefetch=1,
+            grid=(nk // step_rows,),
+            in_specs=[pl.BlockSpec(memory_space=pl.ANY)] * nrow,
+            out_specs=pl.BlockSpec((parts, step_rows, cols), lambda i, c: (0, i, 0)),
+            scratch_shapes=[
+                pltpu.VMEM((nrow, nk, LANES), jnp.bfloat16),
+                pltpu.SemaphoreType.DMA((nrow,)),
+            ],
+        ),
         compiler_params=pltpu.CompilerParams(
             dimension_semantics=("arbitrary",), vmem_limit_bytes=40 << 20
         ),
         name="arrange",
-    )(near)
+    )(slots, *srcs)
     return out.reshape(k, cols)
 
 
-def product_kernel(where, w_ref, *refs, ngroup, nh, half):
-    mine = refs[:ngroup]
-    theirs = refs[ngroup:2 * ngroup]
-    near_hbm, o_ref, bt, sem = refs[2 * ngroup:]
+def product_kernel(where, w_ref, mine, theirs, near_hbm, o_ref, bt, sem, *, ngroup, nh, half):
     group = where[0]
     core = where[1]
     npair = ngroup // 2
@@ -323,9 +349,11 @@
         copies = [pltpu.make_async_copy(near_hbm, bt.at[:, ngroup * LANES:], sem.at[2 * ngroup])]
         for s in range(ngroup):
             cols = slice(s * LANES, (s + 1) * LANES)
-            for d, ref in ((0, mine[s]), (1, theirs[s])):
+            for d, ref in ((0, mine), (1, theirs)):
                 at = pl.multiple_of(jnp.where(core == d, 0, 1) * rows, rows)
-                copies.append(pltpu.make_async_copy(ref, bt.at[pl.ds(at, rows), cols], sem.at[2 * s + d]))
+                copies.append(
+                    pltpu.make_async_copy(ref.at[group ^ s], bt.at[pl.ds(at, rows), cols], sem.at[2 * s + d])
+                )
         for c in copies:
             c.start()
         for c in copies:
@@ -348,7 +376,7 @@
 
 def product(where, w, mine, theirs, near, half, snap):
     m, k = w.shape
-    ngroup = len(mine)
+    ngroup = mine.shape[0]
     mb = 384
     return pl.pallas_call(
         functools.partial(product_kernel, ngroup=ngroup, nh=snap // (ngroup * LANES), half=half),
@@ -357,7 +385,7 @@
             num_scalar_prefetch=1,
             grid=(m // mb,),
             in_specs=[pl.BlockSpec((mb, k), lambda i, c: (i, 0))]
-            + [pl.BlockSpec(memory_space=pl.ANY)] * (2 * ngroup + 1),
+            + [pl.BlockSpec(memory_space=pl.ANY)] * 3,
             out_specs=pl.BlockSpec((mb, snap), lambda i, c: (i, 0)),
             scratch_shapes=[
                 pltpu.VMEM((k, snap), jnp.bfloat16),
@@ -368,7 +396,7 @@
             dimension_semantics=("arbitrary",), vmem_limit_bytes=56 << 20
         ),
         name="product",
-    )(where, w, *mine, *theirs, near)
+    )(where, w, mine, theirs, near)
 
 
 def body(snapshots, bnd_index, recovery, block_se, connect, stress_mat):
@@ -387,7 +415,12 @@
 
     top = snapshots[:half]
     bottom = snapshots[half:]
-    along_row = lax.all_gather(top, "row", axis=0, tiled=False)
+    row = lax.axis_index("row")
+    nz = nrow // 2
+    along = lambda s: [(i, (i + 2 * s) % nrow) for i in range(nrow)]
+    to_other = lambda x: lax.ppermute(x, "row", other)
+    tops = [top] + [lax.ppermute(top, "row", along(s)) for s in range(1, nz)]
+    top_other = to_other(top)
     along_group = [bottom] + [lax.ppermute(bottom, "group", swap(s)) for s in range(1, ngroup)]
 
     ends = nrow - 1
@@ -406,33 +439,35 @@
     smat = smat.transpose(0, 2, 1, 3).reshape(nc, ngrp, ndof * SUB)
     flat = conn.reshape(-1) * (nb // LANES + 1)
     where = jnp.stack([group, core]).astype(jnp.int32)
+    sender = (row - 2 * jnp.arange(nz, dtype=jnp.int32)) % nrow
+    slots = jnp.concatenate([sender, sender ^ 1]).astype(jnp.int32)
 
     rows = nse * nb // 2
     parted = bnd_index.reshape(ngroup, 2, rows)
     own_idx = lax.dynamic_index_in_dim(parted, group, 0, keepdims=False).reshape(-1)
-    mid = lax.dynamic_index_in_dim(parted, core, 1, keepdims=False)
-    far_idx = jnp.concatenate([
-        lax.dynamic_index_in_dim(mid, group ^ s, 0, keepdims=False) for s in range(ngroup)
-    ])
-
-    own_idx, far_idx, flat, conn, smat, where, last_rows, first_rows = lax.optimization_barrier(
-        (own_idx, far_idx, flat, conn, smat, where, last_rows, first_rows)
+    far_idx = lax.dynamic_index_in_dim(parted, core, 1, keepdims=False).reshape(-1)
+
+    own_idx, far_idx, flat, conn, smat, where, slots, last_rows, first_rows = lax.optimization_barrier(
+        (own_idx, far_idx, flat, conn, smat, where, slots, last_rows, first_rows)
     )
     picked = pick_near(own_idx, along_group)
-    picked, far_idx = lax.optimization_barrier((picked, far_idx))
-    near = lax.all_gather(picked, "row", axis=0, tiled=False)
+    picked, far_idx, last_rows, first_rows, *tops = lax.optimization_barrier(
+        (picked, far_idx, last_rows, first_rows, *tops)
+    )
     head = lax.ppermute(last_rows, "row", up)
     tail = lax.ppermute(first_rows, "row", down)
+    nears = [picked] + [lax.ppermute(picked, "row", along(s)) for s in range(1, nz)]
+    tops = tops + [top_other] + [to_other(x) for x in tops[1:]]
     per = LANES // tper
     order = [per * h + j for j in range(per) for h in range(nrow // per)]
-    far = pick_far(far_idx.reshape(ngroup, rows), along_row, order)
-    mine = [far[0]] + [lax.ppermute(far[s], "group", swap(s)) for s in range(1, ngroup)]
-    flat, mine[0] = lax.optimization_barrier((flat, mine[0]))
+    far = pick_far(far_idx, slots, tops, order)
+    mine = lax.all_to_all(far.reshape(ngroup, rows, LANES), "group", split_axis=0, concat_axis=0, tiled=True)
+    flat, far = lax.optimization_barrier((flat, far))
     w = combine(flat, block_se, conn, smat, recovery, head, tail, nse)
-    *mine, w = lax.optimization_barrier((*mine, w))
-    theirs = [lax.ppermute(x, "row", other) for x in mine]
-    near, w = lax.optimization_barrier((near, w))
-    near = arrange(near, ngroup, tper, nse * nb)
+    mine, nears, w = lax.optimization_barrier((mine, nears, w))
+    nears = nears + [to_other(x) for x in nears]
+    theirs = to_other(mine)
+    near = arrange(slots, nears, ngroup, tper, nse * nb)
     out = product(where, w.reshape(nc * nel, nse * nb), mine, theirs, near, half, snap)
     return out.reshape(nc, nel, snap).transpose(1, 0, 2)
 

time: 144 us -> 156 us (1.083); the launches traced: 141 us -> 156 us
  between operations: 13.7 us -> 0.21 us
  starting transfers between devices: 14 us -> 26.3 us
  local copies, waits for them, and re-layouts: 21.1 us -> 28 us
  waiting for transfers between devices: 0.07 us -> 6.46 us
    ppermute x7 -> x15, starting transfers between devices: 4.75 us -> 12.7 us  [the longest x9 5.05 us: body(): to_other = lambda x: lax.ppermute(x, 'row', other)]
    ppermute x7 -> x15, waiting for transfers between devices: 0.02 us -> 6.44 us  [the longest x9 6.42 us: body(): to_other = lambda x: lax.ppermute(x, 'row', other)]
    all_to_all x0 -> x1, starting transfers between devices: none -> 4.69 us  [body(): lax.all_to_all(far.reshape(ngroup, rows, LANES), 'group', split_axis=0, c...]
    reshape x2, local copies, waits for them, and re-layouts: 0.99 us -> 5.32 us  [body(): smat = smat.transpose(0, 2, 1, 3).reshape(nc, ngrp, ndof * SUB)]
    unnamed x20 -> x26, local copies, waits for them, and re-layouts: 7.04 us -> 8.28 us
  transfers between devices with their start and end apart: 14 -> 21, of which waited for: 0 -> 5; matrix products, arithmetic and copies ran while one was open for 10% -> 14% of each run, Pallas kernels for 38% -> 35%
where the time goes in v7:
time: 156 us
  Pallas kernels  90.8 us (58%)
  local copies, waits for them, and re-layouts  28 us (18%)
  starting transfers between devices  26.3 us (17%)
  waiting for transfers between devices  6.46 us (4%)
  other arithmetic  3.72 us (2%)
    pallas_call x1, Pallas kernels, product(): pl.pallas_call(functools.partial(product_kernel, ngroup=ngroup, nh=snap /...  36.6 us
    pallas_call x1, Pallas kernels, combine(): pl.pallas_call(kern, out_shape=jax.ShapeDtypeStruct((nc, nel, nse * nb),...  30.4 us
    pallas_call x1, Pallas kernels, pick_far(): pl.pallas_call(functools.partial(pick_far_kernel, nsrc=nrow, order=order,...  11.9 us
    unnamed x26, local copies, waits for them, and re-layouts  8.28 us
    pallas_call x1, Pallas kernels, pick_near(): pl.pallas_call(functools.partial(pick_near_kernel, nsrc=len(srcs), half=h...  6.68 us
    ppermute x9, waiting for transfers between devices, body(): to_other = lambda x: lax.ppermute(x, 'row', other)  6.42 us
    reshape x2, local copies, waits for them, and re-layouts, body(): smat = smat.transpose(0, 2, 1, 3).reshape(nc, ngrp, ndof * SUB)  5.32 us
    pallas_call x1, Pallas kernels, arrange(): pl.pallas_call(functools.partial(arrange_kernel, nsrc=nrow, nh=nh, per=LA...  5.21 us
  transfers between devices with their start and end apart: 21, of which 5 were waited for; matrix products, arithmetic and copies ran while one was open for 14% of the time, Pallas kernels for 35%

profile of v7, /device:TPU:11, one launch (start us, length us, event | category | flops | bytes accessed | tf_op | source)
XLA Modules:
  0.0 155.5 jit_solution(13033757047352483507)
XLA Ops:
  0.0 1.1 fusion.1
  1.1 1.3 collective-permute-start.2
  2.6 1.2 collective-permute-start
  4.0 2.3 %collective-permute-start.4 = (bf16[16,8192]{1,0:T(8,128)(2,1)S(1)}, bf16[16,8192]{1,0:T(8,128)(2,1)S(1)}, u32[]{:S(2)}, u32[]{:S(2)}) collective-permute-start(bf16[16,8192]{1,0:T(8,128)(2,1)S(1)} %get-tuple-element.36.refs_0_), channel_id=1, source_target_pairs={{0,4},{1,5},{2,6},{3,7},{4,0},{5,1},{6,2},{7,3},{8,12},{9,13},{10,... | collective-permute-start | bytes 786440 | tf_op jit(solution)/shard_map/ppermute | solution.py:422
  6.3 0.7 convert.8
  6.9 0.6 fusion.2
  7.5 0.9 reshape.43
  8.4 0.9 copy.16
  9.6 0.7 bitcast_multiply_fusion
  10.2 1.6 %convert_bitcast_fusion = f32[6,24,512]{2,1,0:T(8,128)} fusion(bf16[512,6,24]{0,2,1:T(8,128)(2,1)} %param.11), kind=kLoop, calls=%fused_computation.2 | loop fusion | flops 73728 | bytes 442368 | tf_op jit(solution)/shard_map/reshape | solution.py:439
  11.9 0.7 pad_add_fusion.where
  12.5 2.1 %slice_bitcast_fusion = (bf16[256,1024]{1,0:T(8,128)(2,1)}, bf16[256,1024]{1,0:T(8,128)(2,1)S(1)}) fusion(bf16[16,512,1024]{2,1,0:T(8,128)(2,1)} %rec_hbm.1), kind=kLoop, calls=%fused_computation | loop fusion | bytes 2097152 | tf_op jit(solution)/shard_map/squeeze | solution.py:434
  14.6 2.2 %collective-permute-start.3 = (bf16[16,8192]{1,0:T(8,128)(2,1)S(1)}, bf16[16,8192]{1,0:T(8,128)(2,1)S(1)}, u32[]{:S(2)}, u32[]{:S(2)}) collective-permute-start(bf16[16,8192]{1,0:T(8,128)(2,1)S(1)} %get-tuple-element.36.refs_0_), channel_id=1, source_target_pairs={{0,2},{1,3},{2,4},{3,5},{4,6},{5,7},{6,0},{7,1},{8,10},{9,11},{10,... | collective-permute-start | bytes 786440 | tf_op jit(solution)/shard_map/ppermute | solution.py:422
  16.9 1.2 copy.18
  18.1 0.9 mul.14.conn
  19.1 2.6 %copy.19 = f32[6,24,512]{1,2,0:T(8,128)} copy(f32[6,24,512]{2,1,0:T(8,128)} %convert_bitcast_fusion) | data formatting | bytes 589824 | tf_op jit(solution)/shard_map/reshape | solution.py:439
  21.7 2.7 %copy.20 = f32[6,64,24,8]{1,3,2,0:T(8,128)} copy(f32[6,64,24,8]{2,3,1,0:T(8,128)} %bitcast.34) | data formatting | bytes 589824 | tf_op jit(solution)/shard_map/reshape | solution.py:439
  24.4 1.4 concatenate.11
  25.8 1.5 concatenate.10
  27.3 0.9 constant_dynamic-slice_fusion
  28.2 6.7 %pick_near.1.refs_0_ = bf16[2048,128]{1,0:T(8,128)(2,1)S(1)} custom-call(s32[4096]{0:T(1024)S(1)} %bitcast.32, bf16[16,8192]{1,0:T(8,128)(2,1)S(1)} %get-tuple-element.56.refs_0_, bf16[16,8192]{1,0:T(8,128)(2,1)S(1)} %collective-permute-done.refs_1_, bf16[16,8192]{1,0:T(8,128)(2,1)S(1)} %collective-permute-done.1.refs_2_, ...), custom_call_target="tpu_custom_call" | custom-call | tf_op jit(solution)/shard_map/pick_near/pallas_call | solution.py:200
  34.9 3.9 %collective-permute-start.13 = (bf16[272,1024]{1,0:T(8,128)(2,1)}, bf16[272,1024]{1,0:T(8,128)(2,1)}, u32[]{:S(2)}, u32[]{:S(2)}) collective-permute-start(bf16[272,1024]{1,0:T(8,128)(2,1)} %concatenate.10), channel_id=1, source_target_pairs={{0,1},{1,2},{2,3},{3,4},{4,5},{5,6},{6,7},{8,9},{9,10},{10,11},{11... | collective-permute-start | bytes 1671176 | tf_op jit(solution)/shard_map/ppermute | solution.py:457
  38.8 2.3 %collective-permute-start.14 = (bf16[272,1024]{1,0:T(8,128)(2,1)}, bf16[272,1024]{1,0:T(8,128)(2,1)}, u32[]{:S(2)}, u32[]{:S(2)}) collective-permute-start(bf16[272,1024]{1,0:T(8,128)(2,1)} %concatenate.11), channel_id=1, source_target_pairs={{1,0},{2,1},{3,2},{4,3},{5,4},{6,5},{7,6},{9,8},{10,9},{11,10},{12... | collective-permute-start | bytes 1671176 | tf_op jit(solution)/shard_map/ppermute | solution.py:458
  41.1 1.8 %collective-permute-start.6 = (bf16[16,8192]{1,0:T(8,128)(2,1)S(1)}, bf16[16,8192]{1,0:T(8,128)(2,1)S(1)}, u32[]{:S(2)}, u32[]{:S(2)}) collective-permute-start(bf16[16,8192]{1,0:T(8,128)(2,1)S(1)} %get-tuple-element.36.refs_0_), channel_id=1, source_target_pairs={{0,1},{1,0},{2,3},{3,2},{4,5},{5,4},{6,7},{7,6},{8,9},{9,8},{10,11... | collective-permute-start | bytes 786440 | tf_op jit(solution)/shard_map/ppermute | solution.py:421
  43.4 0.7 collective-permute-done.6.refs_4_
  44.4 0.7 copy.21.grow_ref
  45.1 2.1 %copy.22.s_ref = f32[6,64,192]{2,1,0:T(8,128)} copy(f32[6,64,192]{1,2,0:T(8,128)} %bitcast.35) | data formatting | bytes 589824 | tf_op jit(solution)/shard_map/optimization_barrier | solution.py:450
  47.2 0.7 copy-done.1
  48.3 0.7 copy-done.3
  49.0 0.6 collective-permute-start.11
  49.6 0.7 copy-done.5
  50.3 2.0 %collective-permute-start.10 = (bf16[2048,128]{1,0:T(8,128)(2,1)S(1)}, bf16[2048,128]{1,0:T(8,128)(2,1)S(1)}, u32[]{:S(2)}, u32[]{:S(2)}) collective-permute-start(bf16[2048,128]{1,0:T(8,128)(2,1)S(1)} %pick_near.1.refs_0_), channel_id=1, source_target_pairs={{0,2},{1,3},{2,4},{3,5},{4,6},{5,7},{6,0},{7,1},{8,10},{9,11},{10,... | collective-permute-start | bytes 1572872 | tf_op jit(solution)/shard_map/ppermute | solution.py:459
  52.3 0.9 copy-done.2
  53.3 0.9 copy-done.4
  54.2 0.9 copy-done.6
  55.2 11.9 %pick_far.1 = bf16[8192,128]{1,0:T(8,128)(2,1)} custom-call(s32[8192]{0:T(1024)S(1)} %bitcast.31, s32[8]{0:T(128)S(1)} %pad_add_fusion.1.slots, bf16[16,8192]{1,0:T(8,128)(2,1)S(1)} %get-tuple-element.36.refs_0_, bf16[16,8192]{1,0:T(8,128)(2,1)S(1)} %collective-permute-done.3.refs_1_, bf16[16,8192]{1,0:T(8,128)(2,1)S(1)} %collective-permute-done.4.refs_2_, ...), custom_call_target="tpu_custom_call" | custom-call | tf_op jit(solution)/shard_map/pick_far/pallas_call | solution.py:257
  67.1 4.7 %all-to-all-start = ((bf16[4,2048,128]{2,1,0:T(8,128)(2,1)}), bf16[4,2048,128]{2,1,0:T(8,128)(2,1)}, u32[]{:S(2)}, u32[]{:S(2)}) async-start(bf16[4,2048,128]{2,1,0:T(8,128)(2,1)} %bitcast.15), calls=%async_computation | async-start | bytes 4194304 | tf_op jit(solution)/shard_map/all_to_all | solution.py:464
  71.8 30.4 %combine.1 = bf16[6,512,4096]{2,1,0:T(8,128)(2,1)} custom-call(s32[12288]{0:T(1024)} %mul.14.conn, s32[16]{0:T(128)} %se.1, s32[64,192]{1,0:T(8,128)} %copy.21.grow_ref, f32[6,64,192]{2,1,0:T(8,128)} %copy.22.s_ref, bf16[16,512,1024]{2,1,0:T(8,128)(2,1)} %rec_hbm.1, bf16[272,1024]{1,0:T(8,128)(2,1)} %collective-permute-done.13.head_ref, ...), custom_call_target="tpu_custom_call" | custom-call | flops 30000001024 | bytes 125829120 | tf_op jit(solution)/shard_map/combine/pallas_call | solution.py:135
  102.3 1.4 collective-permute-start.15
  103.7 0.4 collective-permute-start.17
  104.6 3.4 %collective-permute-done.16.refs_4_ = bf16[2048,128]{1,0:T(8,128)(2,1)S(1)} collective-permute-done((bf16[2048,128]{1,0:T(8,128)(2,1)S(1)}, bf16[2048,128]{1,0:T(8,128)(2,1)S(1)}, u32[]{:S(2)}, u32[]{:S(2)}) %collective-permute-start.16) | collective-permute-done | bytes 524320 | tf_op jit(solution)/shard_map/ppermute | solution.py:421
  108.0 0.7 collective-permute-done.17.refs_5_
  108.8 0.9 collective-permute-done.18.refs_6_
  109.6 0.7 collective-permute-done.19.refs_7_
  110.4 5.2 %arrange.1 = bf16[2,2048,512]{2,1,0:T(8,128)(2,1)S(1)} custom-call(s32[8]{0:T(128)S(1)} %pad_add_fusion.1.slots, bf16[2048,128]{1,0:T(8,128)(2,1)S(1)} %pick_near.1.refs_0_, bf16[2048,128]{1,0:T(8,128)(2,1)S(1)} %collective-permute-done.10.refs_1_, bf16[2048,128]{1,0:T(8,128)(2,1)S(1)} %collective-permute-done.11.refs_2_, ...), custom_call_target="tpu_custom_call" | custom-call | tf_op jit(solution)/shard_map/arrange/pallas_call | solution.py:318
  115.6 2.0 %copy-done = bf16[2,2048,512]{2,1,0:T(8,128)(2,1)} copy-done((bf16[2,2048,512]{2,1,0:T(8,128)(2,1)}, bf16[2,2048,512]{2,1,0:T(8,128)(2,1)S(1)}, u32[]{:S(2)}) %copy-start) | copy-done | bytes 4194328
  117.6 1.3 copy-done.8
  118.9 36.6 %product.1 = bf16[3072,1024]{1,0:T(8,128)(2,1)} custom-call(s32[2]{0:T(128)} %pad_add_fusion.where, bf16[3072,4096]{1,0:T(8,128)(2,1)} %bitcast.33, bf16[4,2048,128]{2,1,0:T(8,128)(2,1)} %all-to-all-done.mine, bf16[4,2048,128]{2,1,0:T(8,128)(2,1)} %copy-done.8, bf16[4096,512]{1,0:T(8,128)(2,1)} %bitcast.30), custom_call_target="tpu_custom_call" | custom-call | tf_op jit(solution)/shard_map/product/pallas_call | solution.py:381
  (46 shorter events, 2.5 us)
Async XLA Ops:
  1.1 13.6 %collective-permute-start.2 = (bf16[16,8192]{1,0:T(8,128)(2,1)S(1)}, bf16[16,8192]{1,0:T(8,128)(2,1)S(1)}, u32[]{:S(2)}, u32[]{:S(2)}) collective-permute-start(bf16[16,8192]{1,0:T(8,128)(2,1)S(1)} %get-tuple-element.56.refs_0_), channel_id=1, source_target_pairs={{0,24},{8,16},{16,8},{24,0},{1,25},{9,17},{17,9},{25,1},{2,26},{10... | collective-permute-start | bytes 786440 | tf_op jit(solution)/shard_map/ppermute | solution.py:424
  2.3 25.8 %collective-permute-start.1 = (bf16[16,8192]{1,0:T(8,128)(2,1)S(1)}, bf16[16,8192]{1,0:T(8,128)(2,1)S(1)}, u32[]{:S(2)}, u32[]{:S(2)}) collective-permute-start(bf16[16,8192]{1,0:T(8,128)(2,1)S(1)} %get-tuple-element.56.refs_0_), channel_id=1, source_target_pairs={{0,16},{8,24},{16,0},{24,8},{1,17},{9,25},{17,1},{25,9},{2,18},{10... | collective-permute-start | bytes 786440 | tf_op jit(solution)/shard_map/ppermute | solution.py:424
  2.6 25.6 %collective-permute-start = (bf16[16,8192]{1,0:T(8,128)(2,1)S(1)}, bf16[16,8192]{1,0:T(8,128)(2,1)S(1)}, u32[]{:S(2)}, u32[]{:S(2)}) collective-permute-start(bf16[16,8192]{1,0:T(8,128)(2,1)S(1)} %get-tuple-element.56.refs_0_), channel_id=1, source_target_pairs={{0,8},{8,0},{16,24},{24,16},{1,9},{9,1},{17,25},{25,17},{2,10},{10... | collective-permute-start | bytes 786440 | tf_op jit(solution)/shard_map/ppermute | solution.py:424
  3.8 31.1 %collective-permute-start.5 = (bf16[16,8192]{1,0:T(8,128)(2,1)S(1)}, bf16[16,8192]{1,0:T(8,128)(2,1)S(1)}, u32[]{:S(2)}, u32[]{:S(2)}) collective-permute-start(bf16[16,8192]{1,0:T(8,128)(2,1)S(1)} %get-tuple-element.36.refs_0_), channel_id=1, source_target_pairs={{0,6},{1,7},{2,0},{3,1},{4,2},{5,3},{6,4},{7,5},{8,14},{9,15},{10,... | collective-permute-start | bytes 786440 | tf_op jit(solution)/shard_map/ppermute | solution.py:422
  4.0 30.9 %collective-permute-start.4 = (bf16[16,8192]{1,0:T(8,128)(2,1)S(1)}, bf16[16,8192]{1,0:T(8,128)(2,1)S(1)}, u32[]{:S(2)}, u32[]{:S(2)}) collective-permute-start(bf16[16,8192]{1,0:T(8,128)(2,1)S(1)} %get-tuple-element.36.refs_0_), channel_id=1, source_target_pairs={{0,4},{1,5},{2,6},{3,7},{4,0},{5,1},{6,2},{7,3},{8,12},{9,13},{10,... | collective-permute-start | bytes 786440 | tf_op jit(solution)/shard_map/ppermute | solution.py:422
  8.4 4.1 %copy-start.11 = (s32[4,2,2048]{2,1,0:T(2,128)}, s32[4,2,2048]{2,1,0:T(2,128)S(1)}, u32[]{:S(2)}) copy-start(s32[4,2,2048]{2,1,0:T(2,128)S(1)} %reshape.43) | copy-start | bytes 196612
  9.5 3.0 %copy-start.9 = (s32[24,64,8]{1,2,0:T(8,128)}, s32[24,64,8]{1,2,0:T(8,128)S(1)}, u32[]{:S(2)}) copy-start(s32[24,64,8]{1,2,0:T(8,128)S(1)} %copy.17) | copy-start | bytes 147460
  14.6 20.3 %collective-permute-start.3 = (bf16[16,8192]{1,0:T(8,128)(2,1)S(1)}, bf16[16,8192]{1,0:T(8,128)(2,1)S(1)}, u32[]{:S(2)}, u32[]{:S(2)}) collective-permute-start(bf16[16,8192]{1,0:T(8,128)(2,1)S(1)} %get-tuple-element.36.refs_0_), channel_id=1, source_target_pairs={{0,2},{1,3},{2,4},{3,5},{4,6},{5,7},{6,0},{7,1},{8,10},{9,11},{10,... | collective-permute-start | bytes 786440 | tf_op jit(solution)/shard_map/ppermute | solution.py:422
  19.0 5.3 %copy-start.7 = (bf16[256,1024]{1,0:T(8,128)(2,1)S(1)}, bf16[256,1024]{1,0:T(8,128)(2,1)}, u32[]{:S(2)}) copy-start(bf16[256,1024]{1,0:T(8,128)(2,1)} %get-tuple-element.53) | copy-start | bytes 1572868
  19.1 25.4 %copy-start.10 = (s32[24,64,8]{1,2,0:T(8,128)S(1)}, s32[24,64,8]{1,2,0:T(8,128)}, u32[]{:S(2)}) copy-start(s32[24,64,8]{1,2,0:T(8,128)} %copy-done.9) | copy-start | bytes 147460
  34.9 36.9 %collective-permute-start.13 = (bf16[272,1024]{1,0:T(8,128)(2,1)}, bf16[272,1024]{1,0:T(8,128)(2,1)}, u32[]{:S(2)}, u32[]{:S(2)}) collective-permute-start(bf16[272,1024]{1,0:T(8,128)(2,1)} %concatenate.10), channel_id=1, source_target_pairs={{0,1},{1,2},{2,3},{3,4},{4,5},{5,6},{6,7},{8,9},{9,10},{10,11},{11... | collective-permute-start | bytes 1671176 | tf_op jit(solution)/shard_map/ppermute | solution.py:457
  38.8 33.0 %collective-permute-start.14 = (bf16[272,1024]{1,0:T(8,128)(2,1)}, bf16[272,1024]{1,0:T(8,128)(2,1)}, u32[]{:S(2)}, u32[]{:S(2)}) collective-permute-start(bf16[272,1024]{1,0:T(8,128)(2,1)} %concatenate.11), channel_id=1, source_target_pairs={{1,0},{2,1},{3,2},{4,3},{5,4},{6,5},{7,6},{9,8},{10,9},{11,10},{12... | collective-permute-start | bytes 1671176 | tf_op jit(solution)/shard_map/ppermute | solution.py:458
  41.1 3.0 %collective-permute-start.6 = (bf16[16,8192]{1,0:T(8,128)(2,1)S(1)}, bf16[16,8192]{1,0:T(8,128)(2,1)S(1)}, u32[]{:S(2)}, u32[]{:S(2)}) collective-permute-start(bf16[16,8192]{1,0:T(8,128)(2,1)S(1)} %get-tuple-element.36.refs_0_), channel_id=1, source_target_pairs={{0,1},{1,0},{2,3},{3,2},{4,5},{5,4},{6,7},{7,6},{8,9},{9,8},{10,11... | collective-permute-start | bytes 786440 | tf_op jit(solution)/shard_map/ppermute | solution.py:421
  42.9 4.3 %collective-permute-start.7 = (bf16[16,8192]{1,0:T(8,128)(2,1)S(1)}, bf16[16,8192]{1,0:T(8,128)(2,1)S(1)}, u32[]{:S(2)}, u32[]{:S(2)}) collective-permute-start(bf16[16,8192]{1,0:T(8,128)(2,1)S(1)} %collective-permute-done.3.refs_1_), channel_id=1, source_target_pairs={{0,1},{1,0},{2,3},{3,2},{4,5},{5,4},{6,7},{7,6},{8,9},{9,8},{10,11... | collective-permute-start | bytes 786440 | tf_op jit(solution)/shard_map/ppermute | solution.py:421
  43.0 5.3 %collective-permute-start.8 = (bf16[16,8192]{1,0:T(8,128)(2,1)S(1)}, bf16[16,8192]{1,0:T(8,128)(2,1)S(1)}, u32[]{:S(2)}, u32[]{:S(2)}) collective-permute-start(bf16[16,8192]{1,0:T(8,128)(2,1)S(1)} %collective-permute-done.4.refs_2_), channel_id=1, source_target_pairs={{0,1},{1,0},{2,3},{3,2},{4,5},{5,4},{6,7},{7,6},{8,9},{9,8},{10,11... | collective-permute-start | bytes 786440 | tf_op jit(solution)/shard_map/ppermute | solution.py:421
  44.1 5.5 %collective-permute-start.9 = (bf16[16,8192]{1,0:T(8,128)(2,1)S(1)}, bf16[16,8192]{1,0:T(8,128)(2,1)S(1)}, u32[]{:S(2)}, u32[]{:S(2)}) collective-permute-start(bf16[16,8192]{1,0:T(8,128)(2,1)S(1)} %collective-permute-done.5.refs_3_), channel_id=1, source_target_pairs={{0,1},{1,0},{2,3},{3,2},{4,5},{5,4},{6,7},{7,6},{8,9},{9,8},{10,11... | collective-permute-start | bytes 786440 | tf_op jit(solution)/shard_map/ppermute | solution.py:421
  47.2 0.7 copy-start.1
  47.9 54.3 %collective-permute-start.12 = (bf16[2048,128]{1,0:T(8,128)(2,1)S(1)}, bf16[2048,128]{1,0:T(8,128)(2,1)S(1)}, u32[]{:S(2)}, u32[]{:S(2)}) collective-permute-start(bf16[2048,128]{1,0:T(8,128)(2,1)S(1)} %pick_near.1.refs_0_), channel_id=1, source_target_pairs={{0,6},{1,7},{2,0},{3,1},{4,2},{5,3},{6,4},{7,5},{8,14},{9,15},{10,... | collective-permute-start | bytes 1572872 | tf_op jit(solution)/shard_map/ppermute | solution.py:459
  48.3 0.7 copy-start.3
  49.0 53.3 %collective-permute-start.11 = (bf16[2048,128]{1,0:T(8,128)(2,1)S(1)}, bf16[2048,128]{1,0:T(8,128)(2,1)S(1)}, u32[]{:S(2)}, u32[]{:S(2)}) collective-permute-start(bf16[2048,128]{1,0:T(8,128)(2,1)S(1)} %pick_near.1.refs_0_), channel_id=1, source_target_pairs={{0,4},{1,5},{2,6},{3,7},{4,0},{5,1},{6,2},{7,3},{8,12},{9,13},{10,... | collective-permute-start | bytes 1572872 | tf_op jit(solution)/shard_map/ppermute | solution.py:459
  49.6 0.7 copy-start.5
  50.3 52.0 %collective-permute-start.10 = (bf16[2048,128]{1,0:T(8,128)(2,1)S(1)}, bf16[2048,128]{1,0:T(8,128)(2,1)S(1)}, u32[]{:S(2)}, u32[]{:S(2)}) collective-permute-start(bf16[2048,128]{1,0:T(8,128)(2,1)S(1)} %pick_near.1.refs_0_), channel_id=1, source_target_pairs={{0,2},{1,3},{2,4},{3,5},{4,6},{5,7},{6,0},{7,1},{8,10},{9,11},{10,... | collective-permute-start | bytes 1572872 | tf_op jit(solution)/shard_map/ppermute | solution.py:459
  52.3 0.9 copy-start.2
  53.3 0.9 copy-start.4
  54.2 0.9 copy-start.6
  67.1 35.2 %all-to-all-start = ((bf16[4,2048,128]{2,1,0:T(8,128)(2,1)}), bf16[4,2048,128]{2,1,0:T(8,128)(2,1)}, u32[]{:S(2)}, u32[]{:S(2)}) async-start(bf16[4,2048,128]{2,1,0:T(8,128)(2,1)} %bitcast.15), calls=%async_computation | async-start | bytes 4194304 | tf_op jit(solution)/shard_map/all_to_all | solution.py:464
  102.3 15.4 %collective-permute-start.15 = (bf16[4,2048,128]{2,1,0:T(8,128)(2,1)}, bf16[4,2048,128]{2,1,0:T(8,128)(2,1)S(1)}, u32[]{:S(2)}, u32[]{:S(2)}) collective-permute-start(bf16[4,2048,128]{2,1,0:T(8,128)(2,1)} %all-to-all-done.mine), channel_id=1, source_target_pairs={{0,1},{1,0},{2,3},{3,2},{4,5},{5,4},{6,7},{7,6},{8,9},{9,8},{10,11... | collective-permute-start | bytes 6291464 | tf_op jit(solution)/shard_map/ppermute | solution.py:421
  103.6 4.4 %collective-permute-start.16 = (bf16[2048,128]{1,0:T(8,128)(2,1)S(1)}, bf16[2048,128]{1,0:T(8,128)(2,1)S(1)}, u32[]{:S(2)}, u32[]{:S(2)}) collective-permute-start(bf16[2048,128]{1,0:T(8,128)(2,1)S(1)} %pick_near.1.refs_0_), channel_id=1, source_target_pairs={{0,1},{1,0},{2,3},{3,2},{4,5},{5,4},{6,7},{7,6},{8,9},{9,8},{10,11... | collective-permute-start | bytes 1572872 | tf_op jit(solution)/shard_map/ppermute | solution.py:421
  103.7 5.1 %collective-permute-start.17 = (bf16[2048,128]{1,0:T(8,128)(2,1)S(1)}, bf16[2048,128]{1,0:T(8,128)(2,1)S(1)}, u32[]{:S(2)}, u32[]{:S(2)}) collective-permute-start(bf16[2048,128]{1,0:T(8,128)(2,1)S(1)} %collective-permute-done.10.refs_1_), channel_id=1, source_target_pairs={{0,1},{1,0},{2,3},{3,2},{4,5},{5,4},{6,7},{7,6},{8,9},{9,8},{10,11... | collective-permute-start | bytes 1572872 | tf_op jit(solution)/shard_map/ppermute | solution.py:421
  104.1 5.5 %collective-permute-start.18 = (bf16[2048,128]{1,0:T(8,128)(2,1)S(1)}, bf16[2048,128]{1,0:T(8,128)(2,1)S(1)}, u32[]{:S(2)}, u32[]{:S(2)}) collective-permute-start(bf16[2048,128]{1,0:T(8,128)(2,1)S(1)} %collective-permute-done.11.refs_2_), channel_id=1, source_target_pairs={{0,1},{1,0},{2,3},{3,2},{4,5},{5,4},{6,7},{7,6},{8,9},{9,8},{10,11... | collective-permute-start | bytes 1572872 | tf_op jit(solution)/shard_map/ppermute | solution.py:421
  104.2 6.2 %collective-permute-start.19 = (bf16[2048,128]{1,0:T(8,128)(2,1)S(1)}, bf16[2048,128]{1,0:T(8,128)(2,1)S(1)}, u32[]{:S(2)}, u32[]{:S(2)}) collective-permute-start(bf16[2048,128]{1,0:T(8,128)(2,1)S(1)} %collective-permute-done.12.refs_3_), channel_id=1, source_target_pairs={{0,1},{1,0},{2,3},{3,2},{4,5},{5,4},{6,7},{7,6},{8,9},{9,8},{10,11... | collective-permute-start | bytes 1572872 | tf_op jit(solution)/shard_map/ppermute | solution.py:421
  115.6 2.0 %copy-start = (bf16[2,2048,512]{2,1,0:T(8,128)(2,1)}, bf16[2,2048,512]{2,1,0:T(8,128)(2,1)S(1)}, u32[]{:S(2)}) copy-start(bf16[2,2048,512]{2,1,0:T(8,128)(2,1)S(1)} %arrange.1) | copy-start | bytes 12582916
  117.6 1.3 copy-start.8

commit v8 on v7

--- a/solution.py
+++ b/solution.py
@@ -43,12 +43,12 @@
         == lax.broadcasted_iota(jnp.int32, (SUB, rows), 0)
     )
 
-    def halo_tag(ref):
+    def halo_tag(ref, at):
         wide = -(-rows // LANES) * LANES
-        return ref[HW:HW + 16, :wide].astype(jnp.float32)[:1, :rows].astype(jnp.int32)
-
-    head_tag = halo_tag(head_ref)
-    tail_tag = halo_tag(tail_ref)
+        return ref[at:at + 16, :wide].astype(jnp.float32)[:1, :rows].astype(jnp.int32)
+
+    head_tag = halo_tag(head_ref, 0)
+    tail_tag = halo_tag(tail_ref, HW)
 
     def left(i):
         where = (grow_ref[pl.ds(i, 1), :] + (blk - HW)) // blk
@@ -86,7 +86,7 @@
     def _():
         for b in range(nbuf):
             fetch(b).start()
-        fill(head_ref, 0, HW)
+        fill(head_ref.at[pl.ds(16, HW)], 0, HW)
         fill(tail_ref, HW + nfill * blk, HW)
 
     @pl.when(step < nfill)
@@ -260,7 +260,7 @@
         grid_spec=pltpu.PrefetchScalarGridSpec(
             num_scalar_prefetch=2,
             grid=(n // chunk,),
-            in_specs=[pl.BlockSpec(memory_space=pl.ANY)] * nrow,
+            in_specs=[pl.BlockSpec(memory_space=pltpu.VMEM)] * nrow,
             out_specs=pl.BlockSpec((chunk, LANES), lambda i, c, d: (i, 0)),
             scratch_shapes=[
                 pltpu.VMEM((nrow, half, nd), jnp.bfloat16),
@@ -323,7 +323,7 @@
         grid_spec=pltpu.PrefetchScalarGridSpec(
             num_scalar_prefetch=1,
             grid=(nk // step_rows,),
-            in_specs=[pl.BlockSpec(memory_space=pl.ANY)] * nrow,
+            in_specs=[pl.BlockSpec(memory_space=pltpu.VMEM)] * nrow,
             out_specs=pl.BlockSpec((parts, step_rows, cols), lambda i, c: (0, i, 0)),
             scratch_shapes=[
                 pltpu.VMEM((nrow, nk, LANES), jnp.bfloat16),
@@ -385,7 +385,7 @@
             num_scalar_prefetch=1,
             grid=(m // mb,),
             in_specs=[pl.BlockSpec((mb, k), lambda i, c: (i, 0))]
-            + [pl.BlockSpec(memory_space=pl.ANY)] * 3,
+            + [pl.BlockSpec(memory_space=pltpu.VMEM)] * 3,
             out_specs=pl.BlockSpec((mb, snap), lambda i, c: (i, 0)),
             scratch_shapes=[
                 pltpu.VMEM((k, snap), jnp.bfloat16),
@@ -393,7 +393,7 @@
             ],
         ),
         compiler_params=pltpu.CompilerParams(
-            dimension_semantics=("arbitrary",), vmem_limit_bytes=56 << 20
+            dimension_semantics=("arbitrary",), vmem_limit_bytes=36 << 20
         ),
         name="product",
     )(where, w, mine, theirs, near)
@@ -427,16 +427,15 @@
     up = [(i, i + 1) for i in range(ends)]
     down = [(i + 1, i) for i in range(ends)]
 
-    def with_se(part, se):
-        return jnp.concatenate([part, jnp.full((16, nb), se.astype(part.dtype))])
-
-    last_rows = with_se(recovery[nblk - 1, blk - HW:], block_se[nblk - 1])
-    first_rows = with_se(recovery[0, :HW], block_se[0])
+    def with_se(part, se, first):
+        row_id = lax.broadcasted_iota(jnp.int32, part.shape, 0) - first
+        return jnp.where((row_id >= 0) & (row_id < 16), se.astype(part.dtype), part)
+
+    last_rows = with_se(recovery[nblk - 1, blk - HW - 16:], block_se[nblk - 1], 0)
+    first_rows = with_se(recovery[0, :HW + 16], block_se[0], HW)
 
     ngrp = nel // SUB
     conn = connect.T.reshape(ndof, ngrp, SUB).transpose(1, 0, 2).reshape(ngrp, ndof * SUB)
-    smat = stress_mat.transpose(1, 2, 0).astype(jnp.float32).reshape(nc, ndof, ngrp, SUB)
-    smat = smat.transpose(0, 2, 1, 3).reshape(nc, ngrp, ndof * SUB)
     flat = conn.reshape(-1) * (nb // LANES + 1)
     where = jnp.stack([group, core]).astype(jnp.int32)
     sender = (row - 2 * jnp.arange(nz, dtype=jnp.int32)) % nrow
@@ -447,13 +446,16 @@
     own_idx = lax.dynamic_index_in_dim(parted, group, 0, keepdims=False).reshape(-1)
     far_idx = lax.dynamic_index_in_dim(parted, core, 1, keepdims=False).reshape(-1)
 
-    own_idx, far_idx, flat, conn, smat, where, slots, last_rows, first_rows = lax.optimization_barrier(
-        (own_idx, far_idx, flat, conn, smat, where, slots, last_rows, first_rows)
+    own_idx, far_idx, flat, conn, where, slots = lax.optimization_barrier(
+        (own_idx, far_idx, flat, conn, where, slots)
     )
     picked = pick_near(own_idx, along_group)
-    picked, far_idx, last_rows, first_rows, *tops = lax.optimization_barrier(
-        (picked, far_idx, last_rows, first_rows, *tops)
+    picked, far_idx, last_rows, first_rows, stress_mat, *tops = lax.optimization_barrier(
+        (picked, far_idx, last_rows, first_rows, stress_mat, *tops)
     )
+    near_other = to_other(picked)
+    smat = stress_mat.transpose(1, 2, 0).astype(jnp.float32).reshape(nc, ndof, ngrp, SUB)
+    smat = smat.transpose(0, 2, 1, 3).reshape(nc, ngrp, ndof * SUB)
     head = lax.ppermute(last_rows, "row", up)
     tail = lax.ppermute(first_rows, "row", down)
     nears = [picked] + [lax.ppermute(picked, "row", along(s)) for s in range(1, nz)]
@@ -465,7 +467,8 @@
     flat, far = lax.optimization_barrier((flat, far))
     w = combine(flat, block_se, conn, smat, recovery, head, tail, nse)
     mine, nears, w = lax.optimization_barrier((mine, nears, w))
-    nears = nears + [to_other(x) for x in nears]
+    nears = nears + [near_other] + [to_other(x) for x in nears[1:]]
+    mine, nears = lax.optimization_barrier((mine, nears))
     theirs = to_other(mine)
     near = arrange(slots, nears, ngroup, tper, nse * nb)
     out = product(where, w.reshape(nc * nel, nse * nb), mine, theirs, near, half, snap)

time: 156 us -> 143 us (0.917); the launches traced: 156 us -> 140 us
  local copies, waits for them, and re-layouts: 28 us -> 12.1 us
  waiting for transfers between devices: 6.46 us -> 8.77 us
  starting transfers between devices: 26.3 us -> 24.2 us
    unnamed x26 -> x4, local copies, waits for them, and re-layouts: 8.28 us -> 0.02 us
    ppermute x3, waiting for transfers between devices: 0.01 us -> 4.72 us  [body(): tops = [top] + [lax.ppermute(top, 'row', along(s)) for s in range(1, nz)]]
    select_n x0 -> x1, other arithmetic: none -> 3.69 us  [with_se(): return jnp.where((row_id >= 0) & (row_id < 16), se.astype(part.dtype), part)]
    concatenate x2 -> x0, local copies, waits for them, and re-layouts: 2.89 us -> none  [with_se(): return jnp.concatenate([part, jnp.full((16, nb), se.astype(part.dtype))])]
    ppermute x9, waiting for transfers between devices: 6.42 us -> 4.03 us  [body(): to_other = lambda x: lax.ppermute(x, 'row', other)]
    optimization_barrier x2 -> x1, local copies, waits for them, and re-layouts: 2.8 us -> 0.7 us  [body(): lax.optimization_barrier((own_idx, far_idx, flat, conn, where, slots))]
    squeeze x1 -> x0, local copies, waits for them, and re-layouts: 2.09 us -> none  [body(): first_rows = with_se(recovery[0, :HW], block_se[0])]
    pallas_call x1, Pallas kernels: 36.6 us -> 34.6 us  [product(): pl.pallas_call(functools.partial(product_kernel, ngroup=ngroup, nh=snap /...]
  transfers between devices with their start and end apart: 21 -> 21, of which waited for: 5 -> 5; matrix products, arithmetic and copies ran while one was open for 14% -> 11% of each run, Pallas kernels for 35% -> 40%
where the time goes in v8:
time: 143 us; the launch traced here: 140 us
  Pallas kernels  90.2 us (63%)
  starting transfers between devices  24.2 us (17%)
  local copies, waits for them, and re-layouts  12.1 us (8%)
  waiting for transfers between devices  8.77 us (6%)
  other arithmetic  4.55 us (3%)
    pallas_call x1, Pallas kernels, product(): pl.pallas_call(functools.partial(product_kernel, ngroup=ngroup, nh=snap /...  34.6 us
    pallas_call x1, Pallas kernels, combine(): pl.pallas_call(kern, out_shape=jax.ShapeDtypeStruct((nc, nel, nse * nb),...  30.4 us
    pallas_call x1, Pallas kernels, pick_far(): pl.pallas_call(functools.partial(pick_far_kernel, nsrc=nrow, order=order,...  11.9 us
    pallas_call x1, Pallas kernels, pick_near(): pl.pallas_call(functools.partial(pick_near_kernel, nsrc=len(srcs), half=h...  6.68 us
    pallas_call x1, Pallas kernels, arrange(): pl.pallas_call(functools.partial(arrange_kernel, nsrc=nrow, nh=nh, per=LA...  6.6 us
    reshape x3, local copies, waits for them, and re-layouts, body(): smat = smat.transpose(0, 2, 1, 3).reshape(nc, ngrp, ndof * SUB)  6.4 us
    ppermute x1, starting transfers between devices, body(): head = lax.ppermute(last_rows, 'row', up)  5.27 us
    ppermute x3, waiting for transfers between devices, body(): tops = [top] + [lax.ppermute(top, 'row', along(s)) for s in range(1, nz)]  4.72 us
  transfers between devices with their start and end apart: 21, of which 5 were waited for; matrix products, arithmetic and copies ran while one was open for 11% of the time, Pallas kernels for 40%

profile of v8, /device:TPU:11, one launch (start us, length us, event | category | flops | bytes accessed | tf_op | source)
XLA Modules:
  0.0 140.1 jit_solution(11228052166235023684)
XLA Ops:
  0.0 1.1 fusion.4
  1.1 1.3 collective-permute-start.2
  2.4 0.2 collective-permute-start.1
  2.6 1.2 collective-permute-start
  3.8 0.2 collective-permute-start.5
  4.0 2.3 %collective-permute-start.4 = (bf16[16,8192]{1,0:T(8,128)(2,1)S(1)}, bf16[16,8192]{1,0:T(8,128)(2,1)S(1)}, u32[]{:S(2)}, u32[]{:S(2)}) collective-permute-start(bf16[16,8192]{1,0:T(8,128)(2,1)S(1)} %get-tuple-element.41.refs_0_), channel_id=1, source_target_pairs={{0,4},{1,5},{2,6},{3,7},{4,0},{5,1},{6,2},{7,3},{8,12},{9,13},{10,... | collective-permute-start | bytes 786440 | tf_op jit(solution)/shard_map/ppermute | solution.py:422
  6.3 0.9 reshape.42
  7.3 0.9 copy.16
  8.2 0.2 copy.17
  8.4 0.1 pad_add_fusion.where
  8.5 0.1 pad_add_fusion.1.slots
  8.5 0.7 convert.8
  9.2 0.3 copy.18
  9.5 0.9 mul.14.conn
  10.5 0.6 fusion.5
  11.1 2.2 %collective-permute-start.3 = (bf16[16,8192]{1,0:T(8,128)(2,1)S(1)}, bf16[16,8192]{1,0:T(8,128)(2,1)S(1)}, u32[]{:S(2)}, u32[]{:S(2)}) collective-permute-start(bf16[16,8192]{1,0:T(8,128)(2,1)S(1)} %get-tuple-element.41.refs_0_), channel_id=1, source_target_pairs={{0,2},{1,3},{2,4},{3,5},{4,6},{5,7},{6,0},{7,1},{8,10},{9,11},{10,... | collective-permute-start | bytes 786440 | tf_op jit(solution)/shard_map/ppermute | solution.py:422
  13.3 3.7 %bitcast_select_fusion = (bf16[272,1024]{1,0:T(8,128)(2,1)}, bf16[272,1024]{1,0:T(8,128)(2,1)}) fusion(bf16[16,512,1024]{2,1,0:T(8,128)(2,1)} %rec_hbm.1, pred[272]{0:T(512)(128)(4,1)S(1)} %get-tuple-element.76, bf16[]{:T(256)} %bitcast.9, bf16[]{:T(256)} %bitcast.7, pred[272]{0:T(512)(128)(4,1)S(1)} %get-tuple-element.75), kind=kLoop, calls=%fused_computation | loop fusion | flops 557056 | bytes 2228772 | tf_op jit(solution)/shard_map/jit(_where)/select_n | solution.py:432
  17.0 6.7 %pick_near.1.refs_0_ = bf16[2048,128]{1,0:T(8,128)(2,1)S(1)} custom-call(s32[4096]{0:T(1024)S(1)} %bitcast.32, bf16[16,8192]{1,0:T(8,128)(2,1)S(1)} %get-tuple-element.70.refs_0_, bf16[16,8192]{1,0:T(8,128)(2,1)S(1)} %collective-permute-done.refs_1_, bf16[16,8192]{1,0:T(8,128)(2,1)S(1)} %collective-permute-done.1.refs_2_, ...), custom_call_target="tpu_custom_call" | custom-call | tf_op jit(solution)/shard_map/pick_near/pallas_call | solution.py:200
  23.7 0.0 collective-permute-done.4.refs_2_
  23.7 4.7 %collective-permute-done.3.refs_1_ = bf16[16,8192]{1,0:T(8,128)(2,1)S(1)} collective-permute-done((bf16[16,8192]{1,0:T(8,128)(2,1)S(1)}, bf16[16,8192]{1,0:T(8,128)(2,1)S(1)}, u32[]{:S(2)}, u32[]{:S(2)}) %collective-permute-start.3) | collective-permute-done | bytes 262176 | tf_op jit(solution)/shard_map/ppermute | solution.py:422
  28.4 5.3 %collective-permute-start.13 = (bf16[272,1024]{1,0:T(8,128)(2,1)}, bf16[272,1024]{1,0:T(8,128)(2,1)}, u32[]{:S(2)}, u32[]{:S(2)}) collective-permute-start(bf16[272,1024]{1,0:T(8,128)(2,1)} %get-tuple-element.50), channel_id=1, source_target_pairs={{0,1},{1,2},{2,3},{3,4},{4,5},{5,6},{6,7},{8,9},{9,10},{10,11},{11... | collective-permute-start | bytes 1671176 | tf_op jit(solution)/shard_map/ppermute | solution.py:459
  33.7 1.9 %collective-permute-start.14 = (bf16[272,1024]{1,0:T(8,128)(2,1)}, bf16[272,1024]{1,0:T(8,128)(2,1)}, u32[]{:S(2)}, u32[]{:S(2)}) collective-permute-start(bf16[272,1024]{1,0:T(8,128)(2,1)} %get-tuple-element.51), channel_id=1, source_target_pairs={{1,0},{2,1},{3,2},{4,3},{5,4},{6,5},{7,6},{9,8},{10,9},{11,10},{12... | collective-permute-start | bytes 1671176 | tf_op jit(solution)/shard_map/ppermute | solution.py:460
  35.6 0.1 collective-permute-start.6
  35.7 0.5 collective-permute-start.7
  36.2 0.1 collective-permute-start.8
  36.3 1.3 collective-permute-done.6.refs_4_
  37.6 0.4 collective-permute-start.9
  37.9 0.7 copy.21.grow_ref
  38.7 1.6 %copy.19 = f32[6,24,512]{1,2,0:T(8,128)} copy(f32[6,24,512]{2,1,0:T(8,128)S(1)} %convert_bitcast_fusion) | data formatting | bytes 589824 | tf_op jit(solution)/shard_map/reshape | solution.py:458
  40.3 2.7 %copy.20 = f32[6,64,24,8]{1,3,2,0:T(8,128)} copy(f32[6,64,24,8]{2,3,1,0:T(8,128)} %bitcast.34) | data formatting | bytes 589824 | tf_op jit(solution)/shard_map/reshape | solution.py:458
  43.0 2.1 %copy.22.s_ref = f32[6,64,192]{2,1,0:T(8,128)} copy(f32[6,64,192]{1,2,0:T(8,128)} %bitcast.35) | data formatting | bytes 589824 | tf_op jit(solution)/shard_map/reshape | solution.py:458
  45.1 0.1 collective-permute-start.15
  45.2 0.0 collective-permute-done.8.refs_6_
  45.2 0.0 collective-permute-start.12
  45.2 0.0 collective-permute-done.9.refs_7_
  45.2 2.3 %collective-permute-start.11 = (bf16[2048,128]{1,0:T(8,128)(2,1)S(1)}, bf16[2048,128]{1,0:T(8,128)(2,1)}, u32[]{:S(2)}, u32[]{:S(2)}) collective-permute-start(bf16[2048,128]{1,0:T(8,128)(2,1)S(1)} %pick_near.1.refs_0_), channel_id=1, source_target_pairs={{0,4},{1,5},{2,6},{3,7},{4,0},{5,1},{6,2},{7,3},{8,12},{9,13},{10,... | collective-permute-start | bytes 1572872 | tf_op jit(solution)/shard_map/ppermute | solution.py:461
  47.6 11.9 %pick_far.1 = bf16[8192,128]{1,0:T(8,128)(2,1)} custom-call(s32[8192]{0:T(1024)S(1)} %bitcast.31, s32[8]{0:T(128)S(1)} %pad_add_fusion.1.slots, bf16[16,8192]{1,0:T(8,128)(2,1)S(1)} %get-tuple-element.41.refs_0_, bf16[16,8192]{1,0:T(8,128)(2,1)S(1)} %collective-permute-done.3.refs_1_, bf16[16,8192]{1,0:T(8,128)(2,1)S(1)} %collective-permute-done.4.refs_2_, ...), custom_call_target="tpu_custom_call" | custom-call | tf_op jit(solution)/shard_map/pick_far/pallas_call | solution.py:257
  59.5 3.8 %all-to-all-start = ((bf16[4,2048,128]{2,1,0:T(8,128)(2,1)}), bf16[4,2048,128]{2,1,0:T(8,128)(2,1)S(1)}, u32[]{:S(2)}, u32[]{:S(2)}) async-start(bf16[4,2048,128]{2,1,0:T(8,128)(2,1)} %bitcast.11), calls=%async_computation | async-start | bytes 4194304 | tf_op jit(solution)/shard_map/all_to_all | solution.py:466
  63.3 30.4 %combine.1 = bf16[6,512,4096]{2,1,0:T(8,128)(2,1)} custom-call(s32[12288]{0:T(1024)} %mul.14.conn, s32[16]{0:T(128)} %se.1, s32[64,192]{1,0:T(8,128)} %copy.21.grow_ref, f32[6,64,192]{2,1,0:T(8,128)} %copy.22.s_ref, bf16[16,512,1024]{2,1,0:T(8,128)(2,1)} %rec_hbm.1, bf16[272,1024]{1,0:T(8,128)(2,1)} %collective-permute-done.13.head_ref, ...), custom_call_target="tpu_custom_call" | custom-call | flops 30000001024 | bytes 125829120 | tf_op jit(solution)/shard_map/combine/pallas_call | solution.py:135
  93.8 1.4 %collective-permute-start.16 = (bf16[2048,128]{1,0:T(8,128)(2,1)}, bf16[2048,128]{1,0:T(8,128)(2,1)S(1)}, u32[]{:S(2)}, u32[]{:S(2)}) collective-permute-start(bf16[2048,128]{1,0:T(8,128)(2,1)} %collective-permute-done.10.refs_1_), channel_id=1, source_target_pairs={{0,1},{1,0},{2,3},{3,2},{4,5},{5,4},{6,7},{7,6},{8,9},{9,8},{10,11... | collective-permute-start | bytes 1572872 | tf_op jit(solution)/shard_map/ppermute | solution.py:421
  95.2 0.1 collective-permute-start.17
  95.3 0.4 collective-permute-start.18
  95.7 1.2 collective-permute-done.16.refs_5_
  96.9 0.7 collective-permute-done.17.refs_6_
  97.7 0.7 collective-permute-done.18.refs_7_
  98.4 0.4 collective-permute-start.19
  98.8 6.6 %arrange.1 = bf16[2,2048,512]{2,1,0:T(8,128)(2,1)S(1)} custom-call(s32[8]{0:T(128)S(1)} %pad_add_fusion.1.slots, bf16[2048,128]{1,0:T(8,128)(2,1)S(1)} %pick_near.1.refs_0_, bf16[2048,128]{1,0:T(8,128)(2,1)} %collective-permute-done.10.refs_1_, bf16[2048,128]{1,0:T(8,128)(2,1)} %collective-permute-done.11.refs_2_, ...), custom_call_target="tpu_custom_call" | custom-call | tf_op jit(solution)/shard_map/arrange/pallas_call | solution.py:318
  105.4 34.6 %product.1 = bf16[3072,1024]{1,0:T(8,128)(2,1)} custom-call(s32[2]{0:T(128)S(1)} %pad_add_fusion.where, bf16[3072,4096]{1,0:T(8,128)(2,1)} %bitcast.33, bf16[4,2048,128]{2,1,0:T(8,128)(2,1)S(1)} %all-to-all-done.mine, bf16[4,2048,128]{2,1,0:T(8,128)(2,1)S(1)} %collective-permute-done.19.theirs, bf16[4096,512]{1,0:T(8,128)(2,1)S(1)} %bitcast.30), custom_call_target="tpu_custom_call" | custom-call | tf_op jit(solution)/shard_map/product/pallas_call | solution.py:381
  (23 shorter events, 0.1 us)
Async XLA Ops:
  0.0 38.6 %copy-start = (bf16[512,6,24]{0,2,1:T(8,128)(2,1)S(1)}, bf16[512,6,24]{0,2,1:T(8,128)(2,1)}, u32[]{:S(2)}) copy-start(bf16[512,6,24]{0,2,1:T(8,128)(2,1)} %param.11) | copy-start | bytes 442372
  1.1 10.0 %collective-permute-start.2 = (bf16[16,8192]{1,0:T(8,128)(2,1)S(1)}, bf16[16,8192]{1,0:T(8,128)(2,1)S(1)}, u32[]{:S(2)}, u32[]{:S(2)}) collective-permute-start(bf16[16,8192]{1,0:T(8,128)(2,1)S(1)} %get-tuple-element.70.refs_0_), channel_id=1, source_target_pairs={{0,24},{8,16},{16,8},{24,0},{1,25},{9,17},{17,9},{25,1},{2,26},{10... | collective-permute-start | bytes 786440 | tf_op jit(solution)/shard_map/ppermute | solution.py:424
  2.4 14.6 %collective-permute-start.1 = (bf16[16,8192]{1,0:T(8,128)(2,1)S(1)}, bf16[16,8192]{1,0:T(8,128)(2,1)S(1)}, u32[]{:S(2)}, u32[]{:S(2)}) collective-permute-start(bf16[16,8192]{1,0:T(8,128)(2,1)S(1)} %get-tuple-element.70.refs_0_), channel_id=1, source_target_pairs={{0,16},{8,24},{16,0},{24,8},{1,17},{9,25},{17,1},{25,9},{2,18},{10... | collective-permute-start | bytes 786440 | tf_op jit(solution)/shard_map/ppermute | solution.py:424
  2.6 14.4 %collective-permute-start = (bf16[16,8192]{1,0:T(8,128)(2,1)S(1)}, bf16[16,8192]{1,0:T(8,128)(2,1)S(1)}, u32[]{:S(2)}, u32[]{:S(2)}) collective-permute-start(bf16[16,8192]{1,0:T(8,128)(2,1)S(1)} %get-tuple-element.70.refs_0_), channel_id=1, source_target_pairs={{0,8},{8,0},{16,24},{24,16},{1,9},{9,1},{17,25},{25,17},{2,10},{10... | collective-permute-start | bytes 786440 | tf_op jit(solution)/shard_map/ppermute | solution.py:424
  3.8 19.9 %collective-permute-start.5 = (bf16[16,8192]{1,0:T(8,128)(2,1)S(1)}, bf16[16,8192]{1,0:T(8,128)(2,1)S(1)}, u32[]{:S(2)}, u32[]{:S(2)}) collective-permute-start(bf16[16,8192]{1,0:T(8,128)(2,1)S(1)} %get-tuple-element.41.refs_0_), channel_id=1, source_target_pairs={{0,6},{1,7},{2,0},{3,1},{4,2},{5,3},{6,4},{7,5},{8,14},{9,15},{10,... | collective-permute-start | bytes 786440 | tf_op jit(solution)/shard_map/ppermute | solution.py:422
  4.0 19.7 %collective-permute-start.4 = (bf16[16,8192]{1,0:T(8,128)(2,1)S(1)}, bf16[16,8192]{1,0:T(8,128)(2,1)S(1)}, u32[]{:S(2)}, u32[]{:S(2)}) collective-permute-start(bf16[16,8192]{1,0:T(8,128)(2,1)S(1)} %get-tuple-element.41.refs_0_), channel_id=1, source_target_pairs={{0,4},{1,5},{2,6},{3,7},{4,0},{5,1},{6,2},{7,3},{8,12},{9,13},{10,... | collective-permute-start | bytes 786440 | tf_op jit(solution)/shard_map/ppermute | solution.py:422
  11.1 17.3 %collective-permute-start.3 = (bf16[16,8192]{1,0:T(8,128)(2,1)S(1)}, bf16[16,8192]{1,0:T(8,128)(2,1)S(1)}, u32[]{:S(2)}, u32[]{:S(2)}) collective-permute-start(bf16[16,8192]{1,0:T(8,128)(2,1)S(1)} %get-tuple-element.41.refs_0_), channel_id=1, source_target_pairs={{0,2},{1,3},{2,4},{3,5},{4,6},{5,7},{6,0},{7,1},{8,10},{9,11},{10,... | collective-permute-start | bytes 786440 | tf_op jit(solution)/shard_map/ppermute | solution.py:422
  28.4 34.9 %collective-permute-start.13 = (bf16[272,1024]{1,0:T(8,128)(2,1)}, bf16[272,1024]{1,0:T(8,128)(2,1)}, u32[]{:S(2)}, u32[]{:S(2)}) collective-permute-start(bf16[272,1024]{1,0:T(8,128)(2,1)} %get-tuple-element.50), channel_id=1, source_target_pairs={{0,1},{1,2},{2,3},{3,4},{4,5},{5,6},{6,7},{8,9},{9,10},{10,11},{11... | collective-permute-start | bytes 1671176 | tf_op jit(solution)/shard_map/ppermute | solution.py:459
  33.7 29.6 %collective-permute-start.14 = (bf16[272,1024]{1,0:T(8,128)(2,1)}, bf16[272,1024]{1,0:T(8,128)(2,1)}, u32[]{:S(2)}, u32[]{:S(2)}) collective-permute-start(bf16[272,1024]{1,0:T(8,128)(2,1)} %get-tuple-element.51), channel_id=1, source_target_pairs={{1,0},{2,1},{3,2},{4,3},{5,4},{6,5},{7,6},{9,8},{10,9},{11,10},{12... | collective-permute-start | bytes 1671176 | tf_op jit(solution)/shard_map/ppermute | solution.py:460
  35.6 1.9 %collective-permute-start.6 = (bf16[16,8192]{1,0:T(8,128)(2,1)S(1)}, bf16[16,8192]{1,0:T(8,128)(2,1)S(1)}, u32[]{:S(2)}, u32[]{:S(2)}) collective-permute-start(bf16[16,8192]{1,0:T(8,128)(2,1)S(1)} %get-tuple-element.41.refs_0_), channel_id=1, source_target_pairs={{0,1},{1,0},{2,3},{3,2},{4,5},{5,4},{6,7},{7,6},{8,9},{9,8},{10,11... | collective-permute-start | bytes 786440 | tf_op jit(solution)/shard_map/ppermute | solution.py:421
  35.7 9.4 %collective-permute-start.7 = (bf16[16,8192]{1,0:T(8,128)(2,1)S(1)}, bf16[16,8192]{1,0:T(8,128)(2,1)S(1)}, u32[]{:S(2)}, u32[]{:S(2)}) collective-permute-start(bf16[16,8192]{1,0:T(8,128)(2,1)S(1)} %collective-permute-done.3.refs_1_), channel_id=1, source_target_pairs={{0,1},{1,0},{2,3},{3,2},{4,5},{5,4},{6,7},{7,6},{8,9},{9,8},{10,11... | collective-permute-start | bytes 786440 | tf_op jit(solution)/shard_map/ppermute | solution.py:421
  36.2 9.0 %collective-permute-start.8 = (bf16[16,8192]{1,0:T(8,128)(2,1)S(1)}, bf16[16,8192]{1,0:T(8,128)(2,1)S(1)}, u32[]{:S(2)}, u32[]{:S(2)}) collective-permute-start(bf16[16,8192]{1,0:T(8,128)(2,1)S(1)} %collective-permute-done.4.refs_2_), channel_id=1, source_target_pairs={{0,1},{1,0},{2,3},{3,2},{4,5},{5,4},{6,7},{7,6},{8,9},{9,8},{10,11... | collective-permute-start | bytes 786440 | tf_op jit(solution)/shard_map/ppermute | solution.py:421
  37.6 7.7 %collective-permute-start.9 = (bf16[16,8192]{1,0:T(8,128)(2,1)S(1)}, bf16[16,8192]{1,0:T(8,128)(2,1)S(1)}, u32[]{:S(2)}, u32[]{:S(2)}) collective-permute-start(bf16[16,8192]{1,0:T(8,128)(2,1)S(1)} %collective-permute-done.5.refs_3_), channel_id=1, source_target_pairs={{0,1},{1,0},{2,3},{3,2},{4,5},{5,4},{6,7},{7,6},{8,9},{9,8},{10,11... | collective-permute-start | bytes 786440 | tf_op jit(solution)/shard_map/ppermute | solution.py:421
  45.1 50.6 %collective-permute-start.15 = (bf16[2048,128]{1,0:T(8,128)(2,1)S(1)}, bf16[2048,128]{1,0:T(8,128)(2,1)S(1)}, u32[]{:S(2)}, u32[]{:S(2)}) collective-permute-start(bf16[2048,128]{1,0:T(8,128)(2,1)S(1)} %pick_near.1.refs_0_), channel_id=1, source_target_pairs={{0,1},{1,0},{2,3},{3,2},{4,5},{5,4},{6,7},{7,6},{8,9},{9,8},{10,11... | collective-permute-start | bytes 1572872 | tf_op jit(solution)/shard_map/ppermute | solution.py:421
  45.2 48.5 %collective-permute-start.12 = (bf16[2048,128]{1,0:T(8,128)(2,1)S(1)}, bf16[2048,128]{1,0:T(8,128)(2,1)}, u32[]{:S(2)}, u32[]{:S(2)}) collective-permute-start(bf16[2048,128]{1,0:T(8,128)(2,1)S(1)} %pick_near.1.refs_0_), channel_id=1, source_target_pairs={{0,6},{1,7},{2,0},{3,1},{4,2},{5,3},{6,4},{7,5},{8,14},{9,15},{10,... | collective-permute-start | bytes 1572872 | tf_op jit(solution)/shard_map/ppermute | solution.py:461
  45.2 48.5 %collective-permute-start.11 = (bf16[2048,128]{1,0:T(8,128)(2,1)S(1)}, bf16[2048,128]{1,0:T(8,128)(2,1)}, u32[]{:S(2)}, u32[]{:S(2)}) collective-permute-start(bf16[2048,128]{1,0:T(8,128)(2,1)S(1)} %pick_near.1.refs_0_), channel_id=1, source_target_pairs={{0,4},{1,5},{2,6},{3,7},{4,0},{5,1},{6,2},{7,3},{8,12},{9,13},{10,... | collective-permute-start | bytes 1572872 | tf_op jit(solution)/shard_map/ppermute | solution.py:461
  59.5 34.3 %all-to-all-start = ((bf16[4,2048,128]{2,1,0:T(8,128)(2,1)}), bf16[4,2048,128]{2,1,0:T(8,128)(2,1)S(1)}, u32[]{:S(2)}, u32[]{:S(2)}) async-start(bf16[4,2048,128]{2,1,0:T(8,128)(2,1)} %bitcast.11), calls=%async_computation | async-start | bytes 4194304 | tf_op jit(solution)/shard_map/all_to_all | solution.py:466
  63.3 30.4 %collective-permute-start.10 = (bf16[2048,128]{1,0:T(8,128)(2,1)S(1)}, bf16[2048,128]{1,0:T(8,128)(2,1)}, u32[]{:S(2)}, u32[]{:S(2)}) collective-permute-start(bf16[2048,128]{1,0:T(8,128)(2,1)S(1)} %pick_near.1.refs_0_), channel_id=1, source_target_pairs={{0,2},{1,3},{2,4},{3,5},{4,6},{5,7},{6,0},{7,1},{8,10},{9,11},{10,... | collective-permute-start | bytes 1572872 | tf_op jit(solution)/shard_map/ppermute | solution.py:461
  93.8 3.2 %collective-permute-start.16 = (bf16[2048,128]{1,0:T(8,128)(2,1)}, bf16[2048,128]{1,0:T(8,128)(2,1)S(1)}, u32[]{:S(2)}, u32[]{:S(2)}) collective-permute-start(bf16[2048,128]{1,0:T(8,128)(2,1)} %collective-permute-done.10.refs_1_), channel_id=1, source_target_pairs={{0,1},{1,0},{2,3},{3,2},{4,5},{5,4},{6,7},{7,6},{8,9},{9,8},{10,11... | collective-permute-start | bytes 1572872 | tf_op jit(solution)/shard_map/ppermute | solution.py:421
  95.2 2.5 %collective-permute-start.17 = (bf16[2048,128]{1,0:T(8,128)(2,1)}, bf16[2048,128]{1,0:T(8,128)(2,1)S(1)}, u32[]{:S(2)}, u32[]{:S(2)}) collective-permute-start(bf16[2048,128]{1,0:T(8,128)(2,1)} %collective-permute-done.11.refs_2_), channel_id=1, source_target_pairs={{0,1},{1,0},{2,3},{3,2},{4,5},{5,4},{6,7},{7,6},{8,9},{9,8},{10,11... | collective-permute-start | bytes 1572872 | tf_op jit(solution)/shard_map/ppermute | solution.py:421
  95.3 3.2 %collective-permute-start.18 = (bf16[2048,128]{1,0:T(8,128)(2,1)}, bf16[2048,128]{1,0:T(8,128)(2,1)S(1)}, u32[]{:S(2)}, u32[]{:S(2)}) collective-permute-start(bf16[2048,128]{1,0:T(8,128)(2,1)} %collective-permute-done.12.refs_3_), channel_id=1, source_target_pairs={{0,1},{1,0},{2,3},{3,2},{4,5},{5,4},{6,7},{7,6},{8,9},{9,8},{10,11... | collective-permute-start | bytes 1572872 | tf_op jit(solution)/shard_map/ppermute | solution.py:421
  98.4 7.0 %collective-permute-start.19 = (bf16[4,2048,128]{2,1,0:T(8,128)(2,1)S(1)}, bf16[4,2048,128]{2,1,0:T(8,128)(2,1)S(1)}, u32[]{:S(2)}, u32[]{:S(2)}) collective-permute-start(bf16[4,2048,128]{2,1,0:T(8,128)(2,1)S(1)} %all-to-all-done.mine), channel_id=1, source_target_pairs={{0,1},{1,0},{2,3},{3,2},{4,5},{5,4},{6,7},{7,6},{8,9},{9,8},{10,11... | collective-permute-start | bytes 6291464 | tf_op jit(solution)/shard_map/ppermute | solution.py:421

commit v9 on v8

--- a/solution.py
+++ b/solution.py
@@ -158,10 +158,7 @@
     )(conn, se, grow, smat, recovery, head, tail)
 
 
-def pick_near_kernel(idx, *refs, nsrc, half, parts, chunk):
-    srcs = refs[:nsrc]
-    o_ref, tbl = refs[nsrc:nsrc + 2]
-    bufs = refs[nsrc + 2:]
+def pick_near_kernel(idx, src, o_ref, tbl, *bufs, parts, chunk):
     step = pl.program_id(0)
     nd = tbl.shape[0]
     total = chunk * pl.num_programs(0)
@@ -170,7 +167,7 @@
     def _():
         def one(i, carry):
             at = pl.multiple_of(i * LANES, LANES)
-            rows = jnp.concatenate([s[:, pl.ds(at, LANES)] for s in srcs] * parts, axis=0)
+            rows = jnp.concatenate([src[g, :, pl.ds(at, LANES)] for g in range(src.shape[0])] * parts, axis=0)
             tbl[pl.ds(at, LANES), :] = rows.T.astype(jnp.float32)
             return carry
 
@@ -192,18 +189,18 @@
     o_ref[...] = out.astype(jnp.bfloat16)
 
 
-def pick_near(idx, srcs):
-    half, nd = srcs[0].shape
-    parts = LANES // (half * len(srcs))
+def pick_near(idx, src):
+    ngroup, half, nd = src.shape
+    parts = LANES // (half * ngroup)
     n = idx.shape[0] // parts
     chunk = min(n, 1024)
     return pl.pallas_call(
-        functools.partial(pick_near_kernel, nsrc=len(srcs), half=half, parts=parts, chunk=chunk),
+        functools.partial(pick_near_kernel, parts=parts, chunk=chunk),
         out_shape=jax.ShapeDtypeStruct((n, LANES), jnp.bfloat16),
         grid_spec=pltpu.PrefetchScalarGridSpec(
             num_scalar_prefetch=1,
             grid=(n // chunk,),
-            in_specs=[pl.BlockSpec((half, nd), lambda i, c: (0, 0)) for _ in srcs],
+            in_specs=[pl.BlockSpec((ngroup, half, nd), lambda i, c: (0, 0, 0))],
             out_specs=pl.BlockSpec((chunk, LANES), lambda i, c: (i, 0)),
             scratch_shapes=[pltpu.VMEM((nd, LANES), jnp.float32)]
             + [pltpu.VMEM((chunk, LANES), jnp.float32) for _ in range(parts)],
@@ -212,7 +209,7 @@
             dimension_semantics=("arbitrary",), vmem_limit_bytes=40 << 20
         ),
         name="pick_near",
-    )(idx, *srcs)
+    )(idx, src)
 
 
 def pick_far_kernel(idx, slots, *refs, nsrc, order, chunk):
@@ -338,9 +335,7 @@
     return out.reshape(k, cols)
 
 
-def product_kernel(where, w_ref, mine, theirs, near_hbm, o_ref, bt, sem, *, ngroup, nh, half):
-    group = where[0]
-    core = where[1]
+def product_kernel(core, w_ref, mine, theirs, near_hbm, o_ref, bt, sem, *, ngroup, nh, half):
     npair = ngroup // 2
     rows = bt.shape[0] // 2
 
@@ -350,9 +345,9 @@
         for s in range(ngroup):
             cols = slice(s * LANES, (s + 1) * LANES)
             for d, ref in ((0, mine), (1, theirs)):
-                at = pl.multiple_of(jnp.where(core == d, 0, 1) * rows, rows)
+                at = pl.multiple_of(jnp.where(core[0] == d, 0, 1) * rows, rows)
                 copies.append(
-                    pltpu.make_async_copy(ref.at[group ^ s], bt.at[pl.ds(at, rows), cols], sem.at[2 * s + d])
+                    pltpu.make_async_copy(ref.at[s], bt.at[pl.ds(at, rows), cols], sem.at[2 * s + d])
                 )
         for c in copies:
             c.start()
@@ -370,8 +365,8 @@
             if s % 2 == 0:
                 second = pltpu.roll(second, half, 1)
             tile = jnp.where(slot == 0, first, second).astype(jnp.bfloat16)
-            col = pl.multiple_of(((group ^ s) * nh + h) * LANES, LANES)
-            o_ref[:, pl.ds(col, LANES)] = tile
+            col = (s * nh + h) * LANES
+            o_ref[:, col:col + LANES] = tile
 
 
 def product(where, w, mine, theirs, near, half, snap):
@@ -410,7 +405,6 @@
     snap = tper * ngroup * nrow
     group = lax.axis_index("group")
     core = lax.axis_index("row") % 2
-    swap = lambda s: [(i, i ^ s) for i in range(ngroup)]
     other = [(i, i ^ 1) for i in range(nrow)]
 
     top = snapshots[:half]
@@ -421,7 +415,9 @@
     to_other = lambda x: lax.ppermute(x, "row", other)
     tops = [top] + [lax.ppermute(top, "row", along(s)) for s in range(1, nz)]
     top_other = to_other(top)
-    along_group = [bottom] + [lax.ppermute(bottom, "group", swap(s)) for s in range(1, ngroup)]
+    along_group = lax.all_to_all(
+        jnp.broadcast_to(bottom, (ngroup, *bottom.shape)), "group", split_axis=0, concat_axis=0, tiled=True
+    )
 
     ends = nrow - 1
     up = [(i, i + 1) for i in range(ends)]
@@ -436,8 +432,10 @@
 
     ngrp = nel // SUB
     conn = connect.T.reshape(ndof, ngrp, SUB).transpose(1, 0, 2).reshape(ngrp, ndof * SUB)
+    smat = stress_mat.transpose(1, 2, 0).astype(jnp.float32).reshape(nc, ndof, ngrp, SUB)
+    smat = smat.transpose(0, 2, 1, 3).reshape(nc, ngrp, ndof * SUB)
     flat = conn.reshape(-1) * (nb // LANES + 1)
-    where = jnp.stack([group, core]).astype(jnp.int32)
+    where = core.reshape(1).astype(jnp.int32)
     sender = (row - 2 * jnp.arange(nz, dtype=jnp.int32)) % nrow
     slots = jnp.concatenate([sender, sender ^ 1]).astype(jnp.int32)
 
@@ -446,16 +444,14 @@
     own_idx = lax.dynamic_index_in_dim(parted, group, 0, keepdims=False).reshape(-1)
     far_idx = lax.dynamic_index_in_dim(parted, core, 1, keepdims=False).reshape(-1)
 
-    own_idx, far_idx, flat, conn, where, slots = lax.optimization_barrier(
-        (own_idx, far_idx, flat, conn, where, slots)
+    own_idx, far_idx, flat, conn, smat, where, slots, last_rows, first_rows = lax.optimization_barrier(
+        (own_idx, far_idx, flat, conn, smat, where, slots, last_rows, first_rows)
     )
     picked = pick_near(own_idx, along_group)
-    picked, far_idx, last_rows, first_rows, stress_mat, *tops = lax.optimization_barrier(
-        (picked, far_idx, last_rows, first_rows, stress_mat, *tops)
+    picked, far_idx, last_rows, first_rows, *tops = lax.optimization_barrier(
+        (picked, far_idx, last_rows, first_rows, *tops)
     )
     near_other = to_other(picked)
-    smat = stress_mat.transpose(1, 2, 0).astype(jnp.float32).reshape(nc, ndof, ngrp, SUB)
-    smat = smat.transpose(0, 2, 1, 3).reshape(nc, ngrp, ndof * SUB)
     head = lax.ppermute(last_rows, "row", up)
     tail = lax.ppermute(first_rows, "row", down)
     nears = [picked] + [lax.ppermute(picked, "row", along(s)) for s in range(1, nz)]

time: 143 us -> 136 us (0.951); the launches traced: 140 us -> 136 us
  waiting for transfers between devices: 8.77 us -> 4.48 us
  starting transfers between devices: 24.2 us -> 27.4 us
  Pallas kernels: 90.2 us -> 88.3 us
    ppermute x3, waiting for transfers between devices: 4.72 us -> 0.01 us  [body(): tops = [top] + [lax.ppermute(top, 'row', along(s)) for s in range(1, nz)]]
    all_to_all x0 -> x1, starting transfers between devices: none -> 3.74 us  [body(): lax.all_to_all(jnp.broadcast_to(bottom, (ngroup, *bottom.shape)), 'group'...]
    ppermute x3 -> x0, starting transfers between devices: 2.71 us -> none  [body(): lax.ppermute(bottom, 'group', swap(s))]
    reshape x3 -> x2, local copies, waits for them, and re-layouts: 6.4 us -> 4.31 us  [body(): smat = smat.transpose(0, 2, 1, 3).reshape(nc, ngrp, ndof * SUB)]
    optimization_barrier x1 -> x2, local copies, waits for them, and re-layouts: 0.7 us -> 2.77 us  [body(): lax.optimization_barrier((own_idx, far_idx, flat, conn, smat, where, slot...]
    pallas_call x1, Pallas kernels: 34.6 us -> 32.8 us  [product(): pl.pallas_call(functools.partial(product_kernel, ngroup=ngroup, nh=snap /...]
    ppermute x9, starting transfers between devices: 3.45 us -> 5.28 us  [body(): to_other = lambda x: lax.ppermute(x, 'row', other)]
  transfers between devices with their start and end apart: 21 -> 19, of which waited for: 5 -> 5; matrix products, arithmetic and copies ran while one was open for 11% -> 10% of each run, Pallas kernels for 40% -> 41%
where the time goes in v9:
time: 136 us
  Pallas kernels  88.3 us (65%)
  starting transfers between devices  27.4 us (20%)
  local copies, waits for them, and re-layouts  11.5 us (8%)
  waiting for transfers between devices  4.48 us (3%)
  other arithmetic  3.84 us (3%)
    pallas_call x1, Pallas kernels, product(): pl.pallas_call(functools.partial(product_kernel, ngroup=ngroup, nh=snap /...  32.8 us
    pallas_call x1, Pallas kernels, combine(): pl.pallas_call(kern, out_shape=jax.ShapeDtypeStruct((nc, nel, nse * nb),...  30.3 us
    pallas_call x1, Pallas kernels, pick_far(): pl.pallas_call(functools.partial(pick_far_kernel, nsrc=nrow, order=order,...  11.9 us
    pallas_call x1, Pallas kernels, pick_near(): pl.pallas_call(functools.partial(pick_near_kernel, parts=parts, chunk=chu...  6.68 us
    pallas_call x1, Pallas kernels, arrange(): pl.pallas_call(functools.partial(arrange_kernel, nsrc=nrow, nh=nh, per=LA...  6.6 us
    ppermute x9, starting transfers between devices, body(): to_other = lambda x: lax.ppermute(x, 'row', other)  5.28 us
    ppermute x3, starting transfers between devices, body(): tops = [top] + [lax.ppermute(top, 'row', along(s)) for s in range(1, nz)]  4.73 us
    ppermute x1, starting transfers between devices, body(): head = lax.ppermute(last_rows, 'row', up)  4.47 us
  transfers between devices with their start and end apart: 19, of which 5 were waited for; matrix products, arithmetic and copies ran while one was open for 10% of the time, Pallas kernels for 41%

profile of v9, /device:TPU:11, one launch (start us, length us, event | category | flops | bytes accessed | tf_op | source)
XLA Modules:
  0.0 135.9 jit_solution(11803639558861977707)
XLA Ops:
  0.0 1.1 fusion.4
  1.1 0.2 collective-permute-start.2
  1.4 2.3 %collective-permute-start.1 = (bf16[16,8192]{1,0:T(8,128)(2,1)S(1)}, bf16[16,8192]{1,0:T(8,128)(2,1)S(1)}, u32[]{:S(2)}, u32[]{:S(2)}) collective-permute-start(bf16[16,8192]{1,0:T(8,128)(2,1)S(1)} %get-tuple-element.45.refs_0_), channel_id=1, source_target_pairs={{0,4},{1,5},{2,6},{3,7},{4,0},{5,1},{6,2},{7,3},{8,12},{9,13},{10,... | collective-permute-start | bytes 786440 | tf_op jit(solution)/shard_map/ppermute | solution.py:416
  3.7 2.2 %collective-permute-start = (bf16[16,8192]{1,0:T(8,128)(2,1)S(1)}, bf16[16,8192]{1,0:T(8,128)(2,1)S(1)}, u32[]{:S(2)}, u32[]{:S(2)}) collective-permute-start(bf16[16,8192]{1,0:T(8,128)(2,1)S(1)} %get-tuple-element.45.refs_0_), channel_id=1, source_target_pairs={{0,2},{1,3},{2,4},{3,5},{4,6},{5,7},{6,0},{7,1},{8,10},{9,11},{10,... | collective-permute-start | bytes 786440 | tf_op jit(solution)/shard_map/ppermute | solution.py:416
  5.9 1.1 broadcast_in_dim.12
  6.9 3.7 %all-to-all-start = ((bf16[4,16,8192]{2,1,0:T(8,128)(2,1)}), bf16[4,16,8192]{2,1,0:T(8,128)(2,1)S(1)}, u32[]{:S(2)}, u32[]{:S(2)}) async-start(bf16[4,16,8192]{2,1,0:T(8,128)(2,1)} %broadcast_in_dim.12), calls=%async_computation | async-start | bytes 2097152 | tf_op jit(solution)/shard_map/all_to_all | solution.py:418
  10.8 0.1 copy.16
  10.9 0.2 copy.17
  11.1 0.3 copy.18
  11.5 0.9 mul.14.conn
  12.4 1.6 %copy.19 = f32[6,24,512]{1,2,0:T(8,128)} copy(f32[6,24,512]{2,1,0:T(8,128)S(1)} %convert_bitcast_fusion) | data formatting | bytes 589824 | tf_op jit(solution)/shard_map/reshape | solution.py:436
  14.0 2.7 %copy.20 = f32[6,64,24,8]{1,3,2,0:T(8,128)} copy(f32[6,64,24,8]{2,3,1,0:T(8,128)} %bitcast.33) | data formatting | bytes 589824 | tf_op jit(solution)/shard_map/reshape | solution.py:436
  16.7 0.1 pad_add_fusion.slots
  16.8 0.7 fusion.5
  17.5 3.7 %bitcast_select_fusion = (bf16[272,1024]{1,0:T(8,128)(2,1)}, bf16[272,1024]{1,0:T(8,128)(2,1)}) fusion(bf16[16,512,1024]{2,1,0:T(8,128)(2,1)} %rec_hbm.1, pred[272]{0:T(512)(128)(4,1)S(1)} %get-tuple-element.80, bf16[]{:T(256)} %bitcast.12, bf16[]{:T(256)} %bitcast.10, pred[272]{0:T(512)(128)(4,1)S(1)} %get-tuple-element.79), kind=kLoop, calls=%fused_computation | loop fusion | flops 557056 | bytes 2228772 | tf_op jit(solution)/shard_map/jit(_where)/select_n | solution.py:428
  21.2 1.1 all-to-all-done.src
  22.3 6.7 %pick_near.1.refs_0_ = bf16[2048,128]{1,0:T(8,128)(2,1)S(1)} custom-call(s32[4096]{0:T(1024)S(1)} %bitcast.31, bf16[4,16,8192]{2,1,0:T(8,128)(2,1)S(1)} %all-to-all-done.src), custom_call_target="tpu_custom_call" | custom-call | tf_op jit(solution)/shard_map/pick_near/pallas_call | solution.py:197
  28.9 0.0 collective-permute-done.2.refs_3_
  29.0 0.0 collective-permute-done.1.refs_2_
  29.0 4.5 %collective-permute-start.10 = (bf16[272,1024]{1,0:T(8,128)(2,1)}, bf16[272,1024]{1,0:T(8,128)(2,1)}, u32[]{:S(2)}, u32[]{:S(2)}) collective-permute-start(bf16[272,1024]{1,0:T(8,128)(2,1)} %get-tuple-element.54), channel_id=1, source_target_pairs={{0,1},{1,2},{2,3},{3,4},{4,5},{5,6},{6,7},{8,9},{9,10},{10,11},{11... | collective-permute-start | bytes 1671176 | tf_op jit(solution)/shard_map/ppermute | solution.py:455
  33.4 2.0 %collective-permute-start.11 = (bf16[272,1024]{1,0:T(8,128)(2,1)}, bf16[272,1024]{1,0:T(8,128)(2,1)}, u32[]{:S(2)}, u32[]{:S(2)}) collective-permute-start(bf16[272,1024]{1,0:T(8,128)(2,1)} %get-tuple-element.55), channel_id=1, source_target_pairs={{1,0},{2,1},{3,2},{4,3},{5,4},{6,5},{7,6},{9,8},{10,9},{11,10},{12... | collective-permute-start | bytes 1671176 | tf_op jit(solution)/shard_map/ppermute | solution.py:456
  35.5 1.8 %collective-permute-start.3 = (bf16[16,8192]{1,0:T(8,128)(2,1)S(1)}, bf16[16,8192]{1,0:T(8,128)(2,1)S(1)}, u32[]{:S(2)}, u32[]{:S(2)}) collective-permute-start(bf16[16,8192]{1,0:T(8,128)(2,1)S(1)} %get-tuple-element.45.refs_0_), channel_id=1, source_target_pairs={{0,1},{1,0},{2,3},{3,2},{4,5},{5,4},{6,7},{7,6},{8,9},{9,8},{10,11... | collective-permute-start | bytes 786440 | tf_op jit(solution)/shard_map/ppermute | solution.py:415
  37.3 0.1 collective-permute-start.4
  37.4 0.4 collective-permute-start.5
  37.8 0.7 collective-permute-done.3.refs_4_
  38.5 0.4 collective-permute-start.6
  38.8 0.7 copy.21.grow_ref
  39.5 2.1 %copy.22.s_ref = f32[6,64,192]{2,1,0:T(8,128)} copy(f32[6,64,192]{1,2,0:T(8,128)} %bitcast.34) | data formatting | bytes 589824 | tf_op jit(solution)/shard_map/optimization_barrier | solution.py:447
  41.6 0.0 collective-permute-done.4.refs_5_
  41.6 0.1 collective-permute-start.12
  41.7 0.3 collective-permute-start.9
  42.1 0.0 collective-permute-done.6.refs_7_
  42.1 0.9 collective-permute-start.8
  43.0 11.9 %pick_far.1 = bf16[8192,128]{1,0:T(8,128)(2,1)} custom-call(s32[8192]{0:T(1024)S(1)} %bitcast.30, s32[8]{0:T(128)S(1)} %pad_add_fusion.slots, bf16[16,8192]{1,0:T(8,128)(2,1)S(1)} %get-tuple-element.45.refs_0_, bf16[16,8192]{1,0:T(8,128)(2,1)S(1)} %collective-permute-done.refs_1_, bf16[16,8192]{1,0:T(8,128)(2,1)S(1)} %collective-permute-done.1.refs_2_, ...), custom_call_target="tpu_custom_call" | custom-call | tf_op jit(solution)/shard_map/pick_far/pallas_call | solution.py:254
  54.9 3.9 %all-to-all-start.1 = ((bf16[4,2048,128]{2,1,0:T(8,128)(2,1)}), bf16[4,2048,128]{2,1,0:T(8,128)(2,1)S(1)}, u32[]{:S(2)}, u32[]{:S(2)}) async-start(bf16[4,2048,128]{2,1,0:T(8,128)(2,1)} %bitcast.14), calls=%async_computation.1 | async-start | bytes 4194304 | tf_op jit(solution)/shard_map/all_to_all | solution.py:462
  58.8 0.0 collective-permute-done.10.head_ref
  58.8 2.0 %collective-permute-start.7 = (bf16[2048,128]{1,0:T(8,128)(2,1)S(1)}, bf16[2048,128]{1,0:T(8,128)(2,1)}, u32[]{:S(2)}, u32[]{:S(2)}) collective-permute-start(bf16[2048,128]{1,0:T(8,128)(2,1)S(1)} %pick_near.1.refs_0_), channel_id=1, source_target_pairs={{0,2},{1,3},{2,4},{3,5},{4,6},{5,7},{6,0},{7,1},{8,10},{9,11},{10,... | collective-permute-start | bytes 1572872 | tf_op jit(solution)/shard_map/ppermute | solution.py:457
  60.9 30.3 %combine.1 = bf16[6,512,4096]{2,1,0:T(8,128)(2,1)} custom-call(s32[12288]{0:T(1024)} %mul.14.conn, s32[16]{0:T(128)} %se.1, s32[64,192]{1,0:T(8,128)} %copy.21.grow_ref, f32[6,64,192]{2,1,0:T(8,128)} %copy.22.s_ref, bf16[16,512,1024]{2,1,0:T(8,128)(2,1)} %rec_hbm.1, bf16[272,1024]{1,0:T(8,128)(2,1)} %collective-permute-done.10.head_ref, ...), custom_call_target="tpu_custom_call" | custom-call | flops 30000001024 | bytes 125829120 | tf_op jit(solution)/shard_map/combine/pallas_call | solution.py:135
  91.2 0.0 collective-permute-done.9.refs_3_
  91.3 1.6 %collective-permute-start.13 = (bf16[2048,128]{1,0:T(8,128)(2,1)}, bf16[2048,128]{1,0:T(8,128)(2,1)S(1)}, u32[]{:S(2)}, u32[]{:S(2)}) collective-permute-start(bf16[2048,128]{1,0:T(8,128)(2,1)} %collective-permute-done.7.refs_1_), channel_id=1, source_target_pairs={{0,1},{1,0},{2,3},{3,2},{4,5},{5,4},{6,7},{7,6},{8,9},{9,8},{10,11... | collective-permute-start | bytes 1572872 | tf_op jit(solution)/shard_map/ppermute | solution.py:415
  92.8 0.1 collective-permute-start.14
  92.9 0.4 collective-permute-start.15
  93.3 1.2 collective-permute-done.13.refs_5_
  94.6 0.7 collective-permute-done.14.refs_6_
  95.3 0.7 collective-permute-done.15.refs_7_
  96.1 0.4 collective-permute-start.16
  96.5 6.6 %arrange.1 = bf16[2,2048,512]{2,1,0:T(8,128)(2,1)S(1)} custom-call(s32[8]{0:T(128)S(1)} %pad_add_fusion.slots, bf16[2048,128]{1,0:T(8,128)(2,1)S(1)} %pick_near.1.refs_0_, bf16[2048,128]{1,0:T(8,128)(2,1)} %collective-permute-done.7.refs_1_, bf16[2048,128]{1,0:T(8,128)(2,1)} %collective-permute-done.8.refs_2_, ...), custom_call_target="tpu_custom_call" | custom-call | tf_op jit(solution)/shard_map/arrange/pallas_call | solution.py:315
  103.1 32.8 %product.1 = bf16[3072,1024]{1,0:T(8,128)(2,1)} custom-call(s32[1]{0:T(128)} %bitcast.9.core, bf16[3072,4096]{1,0:T(8,128)(2,1)} %bitcast.32, bf16[4,2048,128]{2,1,0:T(8,128)(2,1)S(1)} %all-to-all-done.1.mine, bf16[4,2048,128]{2,1,0:T(8,128)(2,1)S(1)} %collective-permute-done.16.theirs, bf16[4096,512]{1,0:T(8,128)(2,1)S(1)} %bitcast.29), custom_call_target="tpu_custom_call" | custom-call | tf_op jit(solution)/shard_map/product/pallas_call | solution.py:376
  (25 shorter events, 0.2 us)
Async XLA Ops:
  0.0 10.7 %copy-start.3 = (s32[16]{0:T(128)S(1)}, s32[16]{0:T(128)}, u32[]{:S(2)}) copy-start(s32[16]{0:T(128)} %se.1) | copy-start | bytes 196
  0.0 10.7 %copy-start.1 = (s32[16,1024]{1,0:T(8,128)S(1)}, s32[16,1024]{1,0:T(8,128)}, u32[]{:S(2)}) copy-start(s32[16,1024]{1,0:T(8,128)} %param.7) | copy-start | bytes 196612
  0.0 10.8 %copy-start.2 = (s32[512,24]{0,1:T(8,128)S(1)}, s32[512,24]{0,1:T(8,128)}, u32[]{:S(2)}) copy-start(s32[512,24]{0,1:T(8,128)} %param.10) | copy-start | bytes 147460
  0.0 11.1 %copy-start = (bf16[512,6,24]{0,2,1:T(8,128)(2,1)S(1)}, bf16[512,6,24]{0,2,1:T(8,128)(2,1)}, u32[]{:S(2)}) copy-start(bf16[512,6,24]{0,2,1:T(8,128)(2,1)} %param.11) | copy-start | bytes 442372
  1.1 27.8 %collective-permute-start.2 = (bf16[16,8192]{1,0:T(8,128)(2,1)S(1)}, bf16[16,8192]{1,0:T(8,128)(2,1)S(1)}, u32[]{:S(2)}, u32[]{:S(2)}) collective-permute-start(bf16[16,8192]{1,0:T(8,128)(2,1)S(1)} %get-tuple-element.45.refs_0_), channel_id=1, source_target_pairs={{0,6},{1,7},{2,0},{3,1},{4,2},{5,3},{6,4},{7,5},{8,14},{9,15},{10,... | collective-permute-start | bytes 786440 | tf_op jit(solution)/shard_map/ppermute | solution.py:416
  1.4 27.6 %collective-permute-start.1 = (bf16[16,8192]{1,0:T(8,128)(2,1)S(1)}, bf16[16,8192]{1,0:T(8,128)(2,1)S(1)}, u32[]{:S(2)}, u32[]{:S(2)}) collective-permute-start(bf16[16,8192]{1,0:T(8,128)(2,1)S(1)} %get-tuple-element.45.refs_0_), channel_id=1, source_target_pairs={{0,4},{1,5},{2,6},{3,7},{4,0},{5,1},{6,2},{7,3},{8,12},{9,13},{10,... | collective-permute-start | bytes 786440 | tf_op jit(solution)/shard_map/ppermute | solution.py:416
  3.7 25.3 %collective-permute-start = (bf16[16,8192]{1,0:T(8,128)(2,1)S(1)}, bf16[16,8192]{1,0:T(8,128)(2,1)S(1)}, u32[]{:S(2)}, u32[]{:S(2)}) collective-permute-start(bf16[16,8192]{1,0:T(8,128)(2,1)S(1)} %get-tuple-element.45.refs_0_), channel_id=1, source_target_pairs={{0,2},{1,3},{2,4},{3,5},{4,6},{5,7},{6,0},{7,1},{8,10},{9,11},{10,... | collective-permute-start | bytes 786440 | tf_op jit(solution)/shard_map/ppermute | solution.py:416
  6.9 15.3 %all-to-all-start = ((bf16[4,16,8192]{2,1,0:T(8,128)(2,1)}), bf16[4,16,8192]{2,1,0:T(8,128)(2,1)S(1)}, u32[]{:S(2)}, u32[]{:S(2)}) async-start(bf16[4,16,8192]{2,1,0:T(8,128)(2,1)} %broadcast_in_dim.12), calls=%async_computation | async-start | bytes 2097152 | tf_op jit(solution)/shard_map/all_to_all | solution.py:418
  29.0 29.9 %collective-permute-start.10 = (bf16[272,1024]{1,0:T(8,128)(2,1)}, bf16[272,1024]{1,0:T(8,128)(2,1)}, u32[]{:S(2)}, u32[]{:S(2)}) collective-permute-start(bf16[272,1024]{1,0:T(8,128)(2,1)} %get-tuple-element.54), channel_id=1, source_target_pairs={{0,1},{1,2},{2,3},{3,4},{4,5},{5,6},{6,7},{8,9},{9,10},{10,11},{11... | collective-permute-start | bytes 1671176 | tf_op jit(solution)/shard_map/ppermute | solution.py:455
  33.4 27.4 %collective-permute-start.11 = (bf16[272,1024]{1,0:T(8,128)(2,1)}, bf16[272,1024]{1,0:T(8,128)(2,1)}, u32[]{:S(2)}, u32[]{:S(2)}) collective-permute-start(bf16[272,1024]{1,0:T(8,128)(2,1)} %get-tuple-element.55), channel_id=1, source_target_pairs={{1,0},{2,1},{3,2},{4,3},{5,4},{6,5},{7,6},{9,8},{10,9},{11,10},{12... | collective-permute-start | bytes 1671176 | tf_op jit(solution)/shard_map/ppermute | solution.py:456
  35.5 3.0 %collective-permute-start.3 = (bf16[16,8192]{1,0:T(8,128)(2,1)S(1)}, bf16[16,8192]{1,0:T(8,128)(2,1)S(1)}, u32[]{:S(2)}, u32[]{:S(2)}) collective-permute-start(bf16[16,8192]{1,0:T(8,128)(2,1)S(1)} %get-tuple-element.45.refs_0_), channel_id=1, source_target_pairs={{0,1},{1,0},{2,3},{3,2},{4,5},{5,4},{6,7},{7,6},{8,9},{9,8},{10,11... | collective-permute-start | bytes 786440 | tf_op jit(solution)/shard_map/ppermute | solution.py:415
  37.3 4.3 %collective-permute-start.4 = (bf16[16,8192]{1,0:T(8,128)(2,1)S(1)}, bf16[16,8192]{1,0:T(8,128)(2,1)S(1)}, u32[]{:S(2)}, u32[]{:S(2)}) collective-permute-start(bf16[16,8192]{1,0:T(8,128)(2,1)S(1)} %collective-permute-done.refs_1_), channel_id=1, source_target_pairs={{0,1},{1,0},{2,3},{3,2},{4,5},{5,4},{6,7},{7,6},{8,9},{9,8},{10,11... | collective-permute-start | bytes 786440 | tf_op jit(solution)/shard_map/ppermute | solution.py:415
  37.4 4.4 %collective-permute-start.5 = (bf16[16,8192]{1,0:T(8,128)(2,1)S(1)}, bf16[16,8192]{1,0:T(8,128)(2,1)S(1)}, u32[]{:S(2)}, u32[]{:S(2)}) collective-permute-start(bf16[16,8192]{1,0:T(8,128)(2,1)S(1)} %collective-permute-done.1.refs_2_), channel_id=1, source_target_pairs={{0,1},{1,0},{2,3},{3,2},{4,5},{5,4},{6,7},{7,6},{8,9},{9,8},{10,11... | collective-permute-start | bytes 786440 | tf_op jit(solution)/shard_map/ppermute | solution.py:415
  38.5 3.6 %collective-permute-start.6 = (bf16[16,8192]{1,0:T(8,128)(2,1)S(1)}, bf16[16,8192]{1,0:T(8,128)(2,1)S(1)}, u32[]{:S(2)}, u32[]{:S(2)}) collective-permute-start(bf16[16,8192]{1,0:T(8,128)(2,1)S(1)} %collective-permute-done.2.refs_3_), channel_id=1, source_target_pairs={{0,1},{1,0},{2,3},{3,2},{4,5},{5,4},{6,7},{7,6},{8,9},{9,8},{10,11... | collective-permute-start | bytes 786440 | tf_op jit(solution)/shard_map/ppermute | solution.py:415
  41.6 51.7 %collective-permute-start.12 = (bf16[2048,128]{1,0:T(8,128)(2,1)S(1)}, bf16[2048,128]{1,0:T(8,128)(2,1)S(1)}, u32[]{:S(2)}, u32[]{:S(2)}) collective-permute-start(bf16[2048,128]{1,0:T(8,128)(2,1)S(1)} %pick_near.1.refs_0_), channel_id=1, source_target_pairs={{0,1},{1,0},{2,3},{3,2},{4,5},{5,4},{6,7},{7,6},{8,9},{9,8},{10,11... | collective-permute-start | bytes 1572872 | tf_op jit(solution)/shard_map/ppermute | solution.py:415
  41.7 49.5 %collective-permute-start.9 = (bf16[2048,128]{1,0:T(8,128)(2,1)S(1)}, bf16[2048,128]{1,0:T(8,128)(2,1)}, u32[]{:S(2)}, u32[]{:S(2)}) collective-permute-start(bf16[2048,128]{1,0:T(8,128)(2,1)S(1)} %pick_near.1.refs_0_), channel_id=1, source_target_pairs={{0,6},{1,7},{2,0},{3,1},{4,2},{5,3},{6,4},{7,5},{8,14},{9,15},{10,... | collective-permute-start | bytes 1572872 | tf_op jit(solution)/shard_map/ppermute | solution.py:457
  42.1 49.2 %collective-permute-start.8 = (bf16[2048,128]{1,0:T(8,128)(2,1)S(1)}, bf16[2048,128]{1,0:T(8,128)(2,1)}, u32[]{:S(2)}, u32[]{:S(2)}) collective-permute-start(bf16[2048,128]{1,0:T(8,128)(2,1)S(1)} %pick_near.1.refs_0_), channel_id=1, source_target_pairs={{0,4},{1,5},{2,6},{3,7},{4,0},{5,1},{6,2},{7,3},{8,12},{9,13},{10,... | collective-permute-start | bytes 1572872 | tf_op jit(solution)/shard_map/ppermute | solution.py:457
  54.9 36.3 %all-to-all-start.1 = ((bf16[4,2048,128]{2,1,0:T(8,128)(2,1)}), bf16[4,2048,128]{2,1,0:T(8,128)(2,1)S(1)}, u32[]{:S(2)}, u32[]{:S(2)}) async-start(bf16[4,2048,128]{2,1,0:T(8,128)(2,1)} %bitcast.14), calls=%async_computation.1 | async-start | bytes 4194304 | tf_op jit(solution)/shard_map/all_to_all | solution.py:462
  58.8 32.4 %collective-permute-start.7 = (bf16[2048,128]{1,0:T(8,128)(2,1)S(1)}, bf16[2048,128]{1,0:T(8,128)(2,1)}, u32[]{:S(2)}, u32[]{:S(2)}) collective-permute-start(bf16[2048,128]{1,0:T(8,128)(2,1)S(1)} %pick_near.1.refs_0_), channel_id=1, source_target_pairs={{0,2},{1,3},{2,4},{3,5},{4,6},{5,7},{6,0},{7,1},{8,10},{9,11},{10,... | collective-permute-start | bytes 1572872 | tf_op jit(solution)/shard_map/ppermute | solution.py:457
  91.3 3.3 %collective-permute-start.13 = (bf16[2048,128]{1,0:T(8,128)(2,1)}, bf16[2048,128]{1,0:T(8,128)(2,1)S(1)}, u32[]{:S(2)}, u32[]{:S(2)}) collective-permute-start(bf16[2048,128]{1,0:T(8,128)(2,1)} %collective-permute-done.7.refs_1_), channel_id=1, source_target_pairs={{0,1},{1,0},{2,3},{3,2},{4,5},{5,4},{6,7},{7,6},{8,9},{9,8},{10,11... | collective-permute-start | bytes 1572872 | tf_op jit(solution)/shard_map/ppermute | solution.py:415
  92.8 2.5 %collective-permute-start.14 = (bf16[2048,128]{1,0:T(8,128)(2,1)}, bf16[2048,128]{1,0:T(8,128)(2,1)S(1)}, u32[]{:S(2)}, u32[]{:S(2)}) collective-permute-start(bf16[2048,128]{1,0:T(8,128)(2,1)} %collective-permute-done.8.refs_2_), channel_id=1, source_target_pairs={{0,1},{1,0},{2,3},{3,2},{4,5},{5,4},{6,7},{7,6},{8,9},{9,8},{10,11... | collective-permute-start | bytes 1572872 | tf_op jit(solution)/shard_map/ppermute | solution.py:415
  92.9 3.2 %collective-permute-start.15 = (bf16[2048,128]{1,0:T(8,128)(2,1)}, bf16[2048,128]{1,0:T(8,128)(2,1)S(1)}, u32[]{:S(2)}, u32[]{:S(2)}) collective-permute-start(bf16[2048,128]{1,0:T(8,128)(2,1)} %collective-permute-done.9.refs_3_), channel_id=1, source_target_pairs={{0,1},{1,0},{2,3},{3,2},{4,5},{5,4},{6,7},{7,6},{8,9},{9,8},{10,11... | collective-permute-start | bytes 1572872 | tf_op jit(solution)/shard_map/ppermute | solution.py:415
  96.1 7.0 %collective-permute-start.16 = (bf16[4,2048,128]{2,1,0:T(8,128)(2,1)S(1)}, bf16[4,2048,128]{2,1,0:T(8,128)(2,1)S(1)}, u32[]{:S(2)}, u32[]{:S(2)}) collective-permute-start(bf16[4,2048,128]{2,1,0:T(8,128)(2,1)S(1)} %all-to-all-done.1.mine), channel_id=1, source_target_pairs={{0,1},{1,0},{2,3},{3,2},{4,5},{5,4},{6,7},{7,6},{8,9},{9,8},{10,11... | collective-permute-start | bytes 6291464 | tf_op jit(solution)/shard_map/ppermute | solution.py:415

commit v10 on v9

--- a/solution.py
+++ b/solution.py
@@ -158,7 +158,7 @@
     )(conn, se, grow, smat, recovery, head, tail)
 
 
-def pick_near_kernel(idx, src, o_ref, tbl, *bufs, parts, chunk):
+def pick_near_kernel(idx, src, grow_hbm, smat_hbm, o_ref, tbl, *bufs, parts, chunk):
     step = pl.program_id(0)
     nd = tbl.shape[0]
     total = chunk * pl.num_programs(0)
@@ -189,7 +189,7 @@
     o_ref[...] = out.astype(jnp.bfloat16)
 
 
-def pick_near(idx, src):
+def pick_near(idx, src, grow, smat):
     ngroup, half, nd = src.shape
     parts = LANES // (half * ngroup)
     n = idx.shape[0] // parts
@@ -200,7 +200,11 @@
         grid_spec=pltpu.PrefetchScalarGridSpec(
             num_scalar_prefetch=1,
             grid=(n // chunk,),
-            in_specs=[pl.BlockSpec((ngroup, half, nd), lambda i, c: (0, 0, 0))],
+            in_specs=[
+                pl.BlockSpec((ngroup, half, nd), lambda i, c: (0, 0, 0)),
+                pl.BlockSpec(memory_space=pl.ANY),
+                pl.BlockSpec(memory_space=pl.ANY),
+            ],
             out_specs=pl.BlockSpec((chunk, LANES), lambda i, c: (i, 0)),
             scratch_shapes=[pltpu.VMEM((nd, LANES), jnp.float32)]
             + [pltpu.VMEM((chunk, LANES), jnp.float32) for _ in range(parts)],
@@ -209,7 +213,7 @@
             dimension_semantics=("arbitrary",), vmem_limit_bytes=40 << 20
         ),
         name="pick_near",
-    )(idx, src)
+    )(idx, src, grow, smat)
 
 
 def pick_far_kernel(idx, slots, *refs, nsrc, order, chunk):
@@ -279,14 +283,25 @@
     step_rows = o_ref.shape[1]
     step = pl.program_id(0)
 
+    cut = near.shape[1] // 2
+
+    def copies(part):
+        where = pl.ds(part * cut, cut)
+        return [
+            pltpu.make_async_copy(ref.at[where], near.at[slots[i], where], sem.at[part, i])
+            for i, ref in enumerate(srcs)
+        ]
+
     @pl.when(step == 0)
     def _():
-        copies = [
-            pltpu.make_async_copy(ref, near.at[slots[i]], sem.at[i]) for i, ref in enumerate(srcs)
-        ]
-        for copy in copies:
+        for copy in copies(0) + copies(1):
             copy.start()
-        for copy in copies:
+        for copy in copies(0):
+            copy.wait()
+
+    @pl.when(step * step_rows == cut)
+    def _():
+        for copy in copies(1):
             copy.wait()
 
     lane = lax.broadcasted_iota(jnp.int32, (step_rows, LANES), 1) // tper
@@ -311,7 +326,7 @@
     npair = ngroup // 2
     parts = k // nk
     cols = nh * npair * LANES
-    step_rows = min(nk, 256)
+    step_rows = min(nk // 2, 256)
     out = pl.pallas_call(
         functools.partial(
             arrange_kernel, nsrc=nrow, nh=nh, per=LANES // tper, npair=npair, parts=parts, tper=tper
@@ -324,7 +339,7 @@
             out_specs=pl.BlockSpec((parts, step_rows, cols), lambda i, c: (0, i, 0)),
             scratch_shapes=[
                 pltpu.VMEM((nrow, nk, LANES), jnp.bfloat16),
-                pltpu.SemaphoreType.DMA((nrow,)),
+                pltpu.SemaphoreType.DMA((2, nrow)),
             ],
         ),
         compiler_params=pltpu.CompilerParams(
@@ -335,22 +350,26 @@
     return out.reshape(k, cols)
 
 
-def product_kernel(core, w_ref, mine, theirs, near_hbm, o_ref, bt, sem, *, ngroup, nh, half):
+def product_kernel(core, w_ref, mine, theirs, near, o_ref, bt, sem, *, ngroup, nh, half):
     npair = ngroup // 2
     rows = bt.shape[0] // 2
 
+    copies = []
+    for s in range(ngroup):
+        cols = slice(s * LANES, (s + 1) * LANES)
+        for d, ref in ((0, mine), (1, theirs)):
+            at = pl.multiple_of(jnp.where(core[0] == d, 0, 1) * rows, rows)
+            copies.append(pltpu.make_async_copy(ref.at[s], bt.at[pl.ds(at, rows), cols], sem.at[2 * s + d]))
+
     @pl.when(pl.program_id(0) == 0)
     def _():
-        copies = [pltpu.make_async_copy(near_hbm, bt.at[:, ngroup * LANES:], sem.at[2 * ngroup])]
-        for s in range(ngroup):
-            cols = slice(s * LANES, (s + 1) * LANES)
-            for d, ref in ((0, mine), (1, theirs)):
-                at = pl.multiple_of(jnp.where(core[0] == d, 0, 1) * rows, rows)
-                copies.append(
-                    pltpu.make_async_copy(ref.at[s], bt.at[pl.ds(at, rows), cols], sem.at[2 * s + d])
-                )
         for c in copies:
             c.start()
+
+    res_near = jnp.dot(w_ref[...], near[...], preferred_element_type=jnp.float32)
+
+    @pl.when(pl.program_id(0) == 0)
+    def _():
         for c in copies:
             c.wait()
 
@@ -360,8 +379,8 @@
         far = res[:, s * LANES:(s + 1) * LANES]
         for h in range(nh):
             first = pltpu.roll(far, LANES - half * h, 1) if h else far
-            at = (ngroup + h * npair + s // 2) * LANES
-            second = res[:, at:at + LANES]
+            at = (h * npair + s // 2) * LANES
+            second = res_near[:, at:at + LANES]
             if s % 2 == 0:
                 second = pltpu.roll(second, half, 1)
             tile = jnp.where(slot == 0, first, second).astype(jnp.bfloat16)
@@ -383,8 +402,8 @@
             + [pl.BlockSpec(memory_space=pltpu.VMEM)] * 3,
             out_specs=pl.BlockSpec((mb, snap), lambda i, c: (i, 0)),
             scratch_shapes=[
-                pltpu.VMEM((k, snap), jnp.bfloat16),
-                pltpu.SemaphoreType.DMA((2 * ngroup + 1,)),
+                pltpu.VMEM((k, ngroup * LANES), jnp.bfloat16),
+                pltpu.SemaphoreType.DMA((2 * ngroup,)),
             ],
         ),
         compiler_params=pltpu.CompilerParams(
@@ -447,7 +466,7 @@
     own_idx, far_idx, flat, conn, smat, where, slots, last_rows, first_rows = lax.optimization_barrier(
         (own_idx, far_idx, flat, conn, smat, where, slots, last_rows, first_rows)
     )
-    picked = pick_near(own_idx, along_group)
+    picked = pick_near(own_idx, along_group, conn, smat)
     picked, far_idx, last_rows, first_rows, *tops = lax.optimization_barrier(
         (picked, far_idx, last_rows, first_rows, *tops)
     )

time: 136 us -> 137 us (level); the launches traced: 136 us -> 135 us
  no operation moved by 1% of the time
where the time goes in v10:
time: 137 us; the launch traced here: 135 us
  Pallas kernels  89.3 us (65%)
  starting transfers between devices  26.3 us (19%)
  local copies, waits for them, and re-layouts  11.5 us (8%)
  waiting for transfers between devices  3.88 us (3%)
  other arithmetic  3.77 us (3%)
    pallas_call x1, Pallas kernels, product(): pl.pallas_call(functools.partial(product_kernel, ngroup=ngroup, nh=snap /...  33.5 us
    pallas_call x1, Pallas kernels, combine(): pl.pallas_call(kern, out_shape=jax.ShapeDtypeStruct((nc, nel, nse * nb),...  30.3 us
    pallas_call x1, Pallas kernels, pick_far(): pl.pallas_call(functools.partial(pick_far_kernel, nsrc=nrow, order=order,...  11.9 us
    pallas_call x1, Pallas kernels, arrange(): pl.pallas_call(functools.partial(arrange_kernel, nsrc=nrow, nh=nh, per=LA...  6.75 us
    pallas_call x1, Pallas kernels, pick_near(): pl.pallas_call(functools.partial(pick_near_kernel, parts=parts, chunk=chu...  6.68 us
    ppermute x9, starting transfers between devices, body(): to_other = lambda x: lax.ppermute(x, 'row', other)  5.47 us
    ppermute x3, starting transfers between devices, body(): tops = [top] + [lax.ppermute(top, 'row', along(s)) for s in range(1, nz)]  4.73 us
    reshape x2, local copies, waits for them, and re-layouts, body(): smat = smat.transpose(0, 2, 1, 3).reshape(nc, ngrp, ndof * SUB)  4.29 us
  transfers between devices with their start and end apart: 19, of which 5 were waited for; matrix products, arithmetic and copies ran while one was open for 10% of the time, Pallas kernels for 41%

profile of v10, /device:TPU:11, one launch (start us, length us, event | category | flops | bytes accessed | tf_op | source)
XLA Modules:
  0.0 135.0 jit_solution(10034776092020849189)
XLA Ops:
  0.0 1.1 fusion.4
  1.1 0.2 collective-permute-start.2
  1.4 2.3 %collective-permute-start.1 = (bf16[16,8192]{1,0:T(8,128)(2,1)S(1)}, bf16[16,8192]{1,0:T(8,128)(2,1)S(1)}, u32[]{:S(2)}, u32[]{:S(2)}) collective-permute-start(bf16[16,8192]{1,0:T(8,128)(2,1)S(1)} %get-tuple-element.47.refs_0_), channel_id=1, source_target_pairs={{0,4},{1,5},{2,6},{3,7},{4,0},{5,1},{6,2},{7,3},{8,12},{9,13},{10,... | collective-permute-start | bytes 786440 | tf_op jit(solution)/shard_map/ppermute | solution.py:435
  3.7 2.2 %collective-permute-start = (bf16[16,8192]{1,0:T(8,128)(2,1)S(1)}, bf16[16,8192]{1,0:T(8,128)(2,1)S(1)}, u32[]{:S(2)}, u32[]{:S(2)}) collective-permute-start(bf16[16,8192]{1,0:T(8,128)(2,1)S(1)} %get-tuple-element.47.refs_0_), channel_id=1, source_target_pairs={{0,2},{1,3},{2,4},{3,5},{4,6},{5,7},{6,0},{7,1},{8,10},{9,11},{10,... | collective-permute-start | bytes 786440 | tf_op jit(solution)/shard_map/ppermute | solution.py:435
  5.9 1.0 broadcast_in_dim.12
  6.9 3.7 %all-to-all-start = ((bf16[4,16,8192]{2,1,0:T(8,128)(2,1)}), bf16[4,16,8192]{2,1,0:T(8,128)(2,1)S(1)}, u32[]{:S(2)}, u32[]{:S(2)}) async-start(bf16[4,16,8192]{2,1,0:T(8,128)(2,1)} %broadcast_in_dim.12), calls=%async_computation | async-start | bytes 2097152 | tf_op jit(solution)/shard_map/all_to_all | solution.py:437
  10.8 0.1 copy.18
  10.9 0.2 copy.19
  11.1 0.3 copy.20
  11.4 0.9 mul.14.conn
  12.4 1.6 %copy.21 = f32[6,24,512]{1,2,0:T(8,128)} copy(f32[6,24,512]{2,1,0:T(8,128)S(1)} %convert_bitcast_fusion) | data formatting | bytes 589824 | tf_op jit(solution)/shard_map/reshape | solution.py:455
  14.0 2.7 %copy.22 = f32[6,64,24,8]{1,3,2,0:T(8,128)} copy(f32[6,64,24,8]{2,3,1,0:T(8,128)} %bitcast.33) | data formatting | bytes 589824 | tf_op jit(solution)/shard_map/reshape | solution.py:455
  16.7 0.1 pad_add_fusion.slots
  16.8 0.6 fusion.5
  17.4 0.6 constant_dynamic-slice_fusion
  18.1 3.6 %bitcast_select_fusion = (bf16[272,1024]{1,0:T(8,128)(2,1)}, bf16[272,1024]{1,0:T(8,128)(2,1)}) fusion(bf16[16,512,1024]{2,1,0:T(8,128)(2,1)} %rec_hbm.1, pred[272]{0:T(512)(128)(4,1)S(1)} %get-tuple-element.80, bf16[]{:T(256)} %bitcast.12, bf16[]{:T(256)} %bitcast.10, pred[272]{0:T(512)(128)(4,1)S(1)} %get-tuple-element.79), kind=kLoop, calls=%fused_computation | loop fusion | flops 557056 | bytes 2228772 | tf_op jit(solution)/shard_map/jit(_where)/select_n | solution.py:447
  21.7 0.1 copy.23.grow_hbm.grow_ref
  21.8 1.3 copy.24.smat_hbm.s_ref
  23.1 6.7 %pick_near.1.refs_0_ = bf16[2048,128]{1,0:T(8,128)(2,1)S(1)} custom-call(s32[4096]{0:T(1024)S(1)} %bitcast.31, bf16[4,16,8192]{2,1,0:T(8,128)(2,1)S(1)} %all-to-all-done.src, s32[64,192]{1,0:T(8,128)S(1)} %copy.23.grow_hbm.grow_ref, f32[6,64,192]{2,1,0:T(8,128)S(1)} %copy.24.smat_hbm.s_ref), custom_call_target="tpu_custom_call" | custom-call | tf_op jit(solution)/shard_map/pick_near/pallas_call | solution.py:197
  29.9 0.0 collective-permute-done.refs_1_
  29.9 3.6 %collective-permute-start.10 = (bf16[272,1024]{1,0:T(8,128)(2,1)}, bf16[272,1024]{1,0:T(8,128)(2,1)}, u32[]{:S(2)}, u32[]{:S(2)}) collective-permute-start(bf16[272,1024]{1,0:T(8,128)(2,1)} %get-tuple-element.54), channel_id=1, source_target_pairs={{0,1},{1,2},{2,3},{3,4},{4,5},{5,6},{6,7},{8,9},{9,10},{10,11},{11... | collective-permute-start | bytes 1671176 | tf_op jit(solution)/shard_map/ppermute | solution.py:474
  33.4 2.3 %collective-permute-start.11 = (bf16[272,1024]{1,0:T(8,128)(2,1)}, bf16[272,1024]{1,0:T(8,128)(2,1)}, u32[]{:S(2)}, u32[]{:S(2)}) collective-permute-start(bf16[272,1024]{1,0:T(8,128)(2,1)} %get-tuple-element.55), channel_id=1, source_target_pairs={{1,0},{2,1},{3,2},{4,3},{5,4},{6,5},{7,6},{9,8},{10,9},{11,10},{12... | collective-permute-start | bytes 1671176 | tf_op jit(solution)/shard_map/ppermute | solution.py:475
  35.7 1.8 %collective-permute-start.3 = (bf16[16,8192]{1,0:T(8,128)(2,1)S(1)}, bf16[16,8192]{1,0:T(8,128)(2,1)S(1)}, u32[]{:S(2)}, u32[]{:S(2)}) collective-permute-start(bf16[16,8192]{1,0:T(8,128)(2,1)S(1)} %get-tuple-element.47.refs_0_), channel_id=1, source_target_pairs={{0,1},{1,0},{2,3},{3,2},{4,5},{5,4},{6,7},{7,6},{8,9},{9,8},{10,11... | collective-permute-start | bytes 786440 | tf_op jit(solution)/shard_map/ppermute | solution.py:434
  37.5 0.1 collective-permute-start.4
  37.6 0.4 collective-permute-start.5
  38.0 0.7 collective-permute-done.3.refs_4_
  38.7 0.4 collective-permute-start.6
  39.1 0.4 collective-permute-start.12
  39.4 0.0 collective-permute-done.5.refs_6_
  39.5 0.3 collective-permute-start.9
  39.8 0.5 collective-permute-done.6.refs_7_
  40.2 0.6 collective-permute-start.8
  40.9 0.8 copy-done.2
  41.6 11.9 %pick_far.1 = bf16[8192,128]{1,0:T(8,128)(2,1)} custom-call(s32[8192]{0:T(1024)S(1)} %bitcast.30, s32[8]{0:T(128)S(1)} %pad_add_fusion.slots, bf16[16,8192]{1,0:T(8,128)(2,1)S(1)} %get-tuple-element.47.refs_0_, bf16[16,8192]{1,0:T(8,128)(2,1)S(1)} %collective-permute-done.refs_1_, bf16[16,8192]{1,0:T(8,128)(2,1)S(1)} %collective-permute-done.1.refs_2_, ...), custom_call_target="tpu_custom_call" | custom-call | tf_op jit(solution)/shard_map/pick_far/pallas_call | solution.py:258
  53.6 3.9 %all-to-all-start.1 = ((bf16[4,2048,128]{2,1,0:T(8,128)(2,1)}), bf16[4,2048,128]{2,1,0:T(8,128)(2,1)S(1)}, u32[]{:S(2)}, u32[]{:S(2)}) async-start(bf16[4,2048,128]{2,1,0:T(8,128)(2,1)} %bitcast.14), calls=%async_computation.1 | async-start | bytes 4194304 | tf_op jit(solution)/shard_map/all_to_all | solution.py:481
  57.5 0.0 collective-permute-done.10.head_ref
  57.5 1.6 %collective-permute-start.7 = (bf16[2048,128]{1,0:T(8,128)(2,1)S(1)}, bf16[2048,128]{1,0:T(8,128)(2,1)}, u32[]{:S(2)}, u32[]{:S(2)}) collective-permute-start(bf16[2048,128]{1,0:T(8,128)(2,1)S(1)} %pick_near.1.refs_0_), channel_id=1, source_target_pairs={{0,2},{1,3},{2,4},{3,5},{4,6},{5,7},{6,0},{7,1},{8,10},{9,11},{10,... | collective-permute-start | bytes 1572872 | tf_op jit(solution)/shard_map/ppermute | solution.py:476
  59.1 30.3 %combine.1 = bf16[6,512,4096]{2,1,0:T(8,128)(2,1)} custom-call(s32[12288]{0:T(1024)} %mul.14.conn, s32[16]{0:T(128)} %se.1, s32[64,192]{1,0:T(8,128)} %copy-done.1, f32[6,64,192]{2,1,0:T(8,128)} %copy-done, bf16[16,512,1024]{2,1,0:T(8,128)(2,1)} %rec_hbm.1, bf16[272,1024]{1,0:T(8,128)(2,1)} %collective-permute-done.10.head_ref, ...), custom_call_target="tpu_custom_call" | custom-call | flops 30000001024 | bytes 125829120 | tf_op jit(solution)/shard_map/combine/pallas_call | solution.py:135
  89.4 0.0 collective-permute-done.8.refs_2_
  89.5 1.5 %collective-permute-start.13 = (bf16[2048,128]{1,0:T(8,128)(2,1)}, bf16[2048,128]{1,0:T(8,128)(2,1)S(1)}, u32[]{:S(2)}, u32[]{:S(2)}) collective-permute-start(bf16[2048,128]{1,0:T(8,128)(2,1)} %collective-permute-done.7.refs_1_), channel_id=1, source_target_pairs={{0,1},{1,0},{2,3},{3,2},{4,5},{5,4},{6,7},{7,6},{8,9},{9,8},{10,11... | collective-permute-start | bytes 1572872 | tf_op jit(solution)/shard_map/ppermute | solution.py:434
  91.0 0.1 collective-permute-start.14
  91.1 0.4 collective-permute-start.15
  91.5 1.2 collective-permute-done.13.refs_5_
  92.8 0.7 collective-permute-done.14.refs_6_
  93.5 0.7 collective-permute-done.15.refs_7_
  94.3 0.4 collective-permute-start.16
  94.6 6.8 %arrange.1 = bf16[2,2048,512]{2,1,0:T(8,128)(2,1)S(1)} custom-call(s32[8]{0:T(128)S(1)} %pad_add_fusion.slots, bf16[2048,128]{1,0:T(8,128)(2,1)S(1)} %pick_near.1.refs_0_, bf16[2048,128]{1,0:T(8,128)(2,1)} %collective-permute-done.7.refs_1_, bf16[2048,128]{1,0:T(8,128)(2,1)} %collective-permute-done.8.refs_2_, ...), custom_call_target="tpu_custom_call" | custom-call | tf_op jit(solution)/shard_map/arrange/pallas_call | solution.py:330
  101.4 33.5 %product.1 = bf16[3072,1024]{1,0:T(8,128)(2,1)} custom-call(s32[1]{0:T(128)} %bitcast.9.core, bf16[3072,4096]{1,0:T(8,128)(2,1)} %bitcast.32, bf16[4,2048,128]{2,1,0:T(8,128)(2,1)S(1)} %all-to-all-done.1.mine, bf16[4,2048,128]{2,1,0:T(8,128)(2,1)S(1)} %collective-permute-done.16.theirs, bf16[4096,512]{1,0:T(8,128)(2,1)S(1)} %bitcast.29), custom_call_target="tpu_custom_call" | custom-call | tf_op jit(solution)/shard_map/product/pallas_call | solution.py:395
  (31 shorter events, 0.2 us)
Async XLA Ops:
  0.0 10.7 %copy-start.6 = (s32[16]{0:T(128)S(1)}, s32[16]{0:T(128)}, u32[]{:S(2)}) copy-start(s32[16]{0:T(128)} %se.1) | copy-start | bytes 196
  0.0 10.7 %copy-start.4 = (s32[16,1024]{1,0:T(8,128)S(1)}, s32[16,1024]{1,0:T(8,128)}, u32[]{:S(2)}) copy-start(s32[16,1024]{1,0:T(8,128)} %param.7) | copy-start | bytes 196612
  0.0 10.8 %copy-start.5 = (s32[512,24]{0,1:T(8,128)S(1)}, s32[512,24]{0,1:T(8,128)}, u32[]{:S(2)}) copy-start(s32[512,24]{0,1:T(8,128)} %param.10) | copy-start | bytes 147460
  0.0 11.1 %copy-start.3 = (bf16[512,6,24]{0,2,1:T(8,128)(2,1)S(1)}, bf16[512,6,24]{0,2,1:T(8,128)(2,1)}, u32[]{:S(2)}) copy-start(bf16[512,6,24]{0,2,1:T(8,128)(2,1)} %param.11) | copy-start | bytes 442372
  1.1 28.7 %collective-permute-start.2 = (bf16[16,8192]{1,0:T(8,128)(2,1)S(1)}, bf16[16,8192]{1,0:T(8,128)(2,1)S(1)}, u32[]{:S(2)}, u32[]{:S(2)}) collective-permute-start(bf16[16,8192]{1,0:T(8,128)(2,1)S(1)} %get-tuple-element.47.refs_0_), channel_id=1, source_target_pairs={{0,6},{1,7},{2,0},{3,1},{4,2},{5,3},{6,4},{7,5},{8,14},{9,15},{10,... | collective-permute-start | bytes 786440 | tf_op jit(solution)/shard_map/ppermute | solution.py:435
  1.4 28.5 %collective-permute-start.1 = (bf16[16,8192]{1,0:T(8,128)(2,1)S(1)}, bf16[16,8192]{1,0:T(8,128)(2,1)S(1)}, u32[]{:S(2)}, u32[]{:S(2)}) collective-permute-start(bf16[16,8192]{1,0:T(8,128)(2,1)S(1)} %get-tuple-element.47.refs_0_), channel_id=1, source_target_pairs={{0,4},{1,5},{2,6},{3,7},{4,0},{5,1},{6,2},{7,3},{8,12},{9,13},{10,... | collective-permute-start | bytes 786440 | tf_op jit(solution)/shard_map/ppermute | solution.py:435
  3.7 26.2 %collective-permute-start = (bf16[16,8192]{1,0:T(8,128)(2,1)S(1)}, bf16[16,8192]{1,0:T(8,128)(2,1)S(1)}, u32[]{:S(2)}, u32[]{:S(2)}) collective-permute-start(bf16[16,8192]{1,0:T(8,128)(2,1)S(1)} %get-tuple-element.47.refs_0_), channel_id=1, source_target_pairs={{0,2},{1,3},{2,4},{3,5},{4,6},{5,7},{6,0},{7,1},{8,10},{9,11},{10,... | collective-permute-start | bytes 786440 | tf_op jit(solution)/shard_map/ppermute | solution.py:435
  6.9 16.2 %all-to-all-start = ((bf16[4,16,8192]{2,1,0:T(8,128)(2,1)}), bf16[4,16,8192]{2,1,0:T(8,128)(2,1)S(1)}, u32[]{:S(2)}, u32[]{:S(2)}) async-start(bf16[4,16,8192]{2,1,0:T(8,128)(2,1)} %broadcast_in_dim.12), calls=%async_computation | async-start | bytes 2097152 | tf_op jit(solution)/shard_map/all_to_all | solution.py:437
  21.8 17.3 %copy-start.1 = (s32[64,192]{1,0:T(8,128)}, s32[64,192]{1,0:T(8,128)S(1)}, u32[]{:S(2)}) copy-start(s32[64,192]{1,0:T(8,128)S(1)} %copy.23.grow_hbm.grow_ref) | copy-start | bytes 147460
  23.1 30.5 %copy-start = (f32[6,64,192]{2,1,0:T(8,128)}, f32[6,64,192]{2,1,0:T(8,128)S(1)}, u32[]{:S(2)}) copy-start(f32[6,64,192]{2,1,0:T(8,128)S(1)} %copy.24.smat_hbm.s_ref) | copy-start | bytes 884740
  29.9 27.6 %collective-permute-start.10 = (bf16[272,1024]{1,0:T(8,128)(2,1)}, bf16[272,1024]{1,0:T(8,128)(2,1)}, u32[]{:S(2)}, u32[]{:S(2)}) collective-permute-start(bf16[272,1024]{1,0:T(8,128)(2,1)} %get-tuple-element.54), channel_id=1, source_target_pairs={{0,1},{1,2},{2,3},{3,4},{4,5},{5,6},{6,7},{8,9},{9,10},{10,11},{11... | collective-permute-start | bytes 1671176 | tf_op jit(solution)/shard_map/ppermute | solution.py:474
  33.4 25.7 %collective-permute-start.11 = (bf16[272,1024]{1,0:T(8,128)(2,1)}, bf16[272,1024]{1,0:T(8,128)(2,1)}, u32[]{:S(2)}, u32[]{:S(2)}) collective-permute-start(bf16[272,1024]{1,0:T(8,128)(2,1)} %get-tuple-element.55), channel_id=1, source_target_pairs={{1,0},{2,1},{3,2},{4,3},{5,4},{6,5},{7,6},{9,8},{10,9},{11,10},{12... | collective-permute-start | bytes 1671176 | tf_op jit(solution)/shard_map/ppermute | solution.py:475
  35.7 3.0 %collective-permute-start.3 = (bf16[16,8192]{1,0:T(8,128)(2,1)S(1)}, bf16[16,8192]{1,0:T(8,128)(2,1)S(1)}, u32[]{:S(2)}, u32[]{:S(2)}) collective-permute-start(bf16[16,8192]{1,0:T(8,128)(2,1)S(1)} %get-tuple-element.47.refs_0_), channel_id=1, source_target_pairs={{0,1},{1,0},{2,3},{3,2},{4,5},{5,4},{6,7},{7,6},{8,9},{9,8},{10,11... | collective-permute-start | bytes 786440 | tf_op jit(solution)/shard_map/ppermute | solution.py:434
  37.5 1.5 %collective-permute-start.4 = (bf16[16,8192]{1,0:T(8,128)(2,1)S(1)}, bf16[16,8192]{1,0:T(8,128)(2,1)S(1)}, u32[]{:S(2)}, u32[]{:S(2)}) collective-permute-start(bf16[16,8192]{1,0:T(8,128)(2,1)S(1)} %collective-permute-done.refs_1_), channel_id=1, source_target_pairs={{0,1},{1,0},{2,3},{3,2},{4,5},{5,4},{6,7},{7,6},{8,9},{9,8},{10,11... | collective-permute-start | bytes 786440 | tf_op jit(solution)/shard_map/ppermute | solution.py:434
  37.6 1.8 %collective-permute-start.5 = (bf16[16,8192]{1,0:T(8,128)(2,1)S(1)}, bf16[16,8192]{1,0:T(8,128)(2,1)S(1)}, u32[]{:S(2)}, u32[]{:S(2)}) collective-permute-start(bf16[16,8192]{1,0:T(8,128)(2,1)S(1)} %collective-permute-done.1.refs_2_), channel_id=1, source_target_pairs={{0,1},{1,0},{2,3},{3,2},{4,5},{5,4},{6,7},{7,6},{8,9},{9,8},{10,11... | collective-permute-start | bytes 786440 | tf_op jit(solution)/shard_map/ppermute | solution.py:434
  38.7 1.5 %collective-permute-start.6 = (bf16[16,8192]{1,0:T(8,128)(2,1)S(1)}, bf16[16,8192]{1,0:T(8,128)(2,1)S(1)}, u32[]{:S(2)}, u32[]{:S(2)}) collective-permute-start(bf16[16,8192]{1,0:T(8,128)(2,1)S(1)} %collective-permute-done.2.refs_3_), channel_id=1, source_target_pairs={{0,1},{1,0},{2,3},{3,2},{4,5},{5,4},{6,7},{7,6},{8,9},{9,8},{10,11... | collective-permute-start | bytes 786440 | tf_op jit(solution)/shard_map/ppermute | solution.py:434
  39.1 52.4 %collective-permute-start.12 = (bf16[2048,128]{1,0:T(8,128)(2,1)S(1)}, bf16[2048,128]{1,0:T(8,128)(2,1)S(1)}, u32[]{:S(2)}, u32[]{:S(2)}) collective-permute-start(bf16[2048,128]{1,0:T(8,128)(2,1)S(1)} %pick_near.1.refs_0_), channel_id=1, source_target_pairs={{0,1},{1,0},{2,3},{3,2},{4,5},{5,4},{6,7},{7,6},{8,9},{9,8},{10,11... | collective-permute-start | bytes 1572872 | tf_op jit(solution)/shard_map/ppermute | solution.py:434
  39.5 50.0 %collective-permute-start.9 = (bf16[2048,128]{1,0:T(8,128)(2,1)S(1)}, bf16[2048,128]{1,0:T(8,128)(2,1)}, u32[]{:S(2)}, u32[]{:S(2)}) collective-permute-start(bf16[2048,128]{1,0:T(8,128)(2,1)S(1)} %pick_near.1.refs_0_), channel_id=1, source_target_pairs={{0,6},{1,7},{2,0},{3,1},{4,2},{5,3},{6,4},{7,5},{8,14},{9,15},{10,... | collective-permute-start | bytes 1572872 | tf_op jit(solution)/shard_map/ppermute | solution.py:476
  40.2 49.2 %collective-permute-start.8 = (bf16[2048,128]{1,0:T(8,128)(2,1)S(1)}, bf16[2048,128]{1,0:T(8,128)(2,1)}, u32[]{:S(2)}, u32[]{:S(2)}) collective-permute-start(bf16[2048,128]{1,0:T(8,128)(2,1)S(1)} %pick_near.1.refs_0_), channel_id=1, source_target_pairs={{0,4},{1,5},{2,6},{3,7},{4,0},{5,1},{6,2},{7,3},{8,12},{9,13},{10,... | collective-permute-start | bytes 1572872 | tf_op jit(solution)/shard_map/ppermute | solution.py:476
  40.9 0.8 copy-start.2
  53.6 35.9 %all-to-all-start.1 = ((bf16[4,2048,128]{2,1,0:T(8,128)(2,1)}), bf16[4,2048,128]{2,1,0:T(8,128)(2,1)S(1)}, u32[]{:S(2)}, u32[]{:S(2)}) async-start(bf16[4,2048,128]{2,1,0:T(8,128)(2,1)} %bitcast.14), calls=%async_computation.1 | async-start | bytes 4194304 | tf_op jit(solution)/shard_map/all_to_all | solution.py:481
  57.5 32.0 %collective-permute-start.7 = (bf16[2048,128]{1,0:T(8,128)(2,1)S(1)}, bf16[2048,128]{1,0:T(8,128)(2,1)}, u32[]{:S(2)}, u32[]{:S(2)}) collective-permute-start(bf16[2048,128]{1,0:T(8,128)(2,1)S(1)} %pick_near.1.refs_0_), channel_id=1, source_target_pairs={{0,2},{1,3},{2,4},{3,5},{4,6},{5,7},{6,0},{7,1},{8,10},{9,11},{10,... | collective-permute-start | bytes 1572872 | tf_op jit(solution)/shard_map/ppermute | solution.py:476
  89.5 3.3 %collective-permute-start.13 = (bf16[2048,128]{1,0:T(8,128)(2,1)}, bf16[2048,128]{1,0:T(8,128)(2,1)S(1)}, u32[]{:S(2)}, u32[]{:S(2)}) collective-permute-start(bf16[2048,128]{1,0:T(8,128)(2,1)} %collective-permute-done.7.refs_1_), channel_id=1, source_target_pairs={{0,1},{1,0},{2,3},{3,2},{4,5},{5,4},{6,7},{7,6},{8,9},{9,8},{10,11... | collective-permute-start | bytes 1572872 | tf_op jit(solution)/shard_map/ppermute | solution.py:434
  91.0 2.5 %collective-permute-start.14 = (bf16[2048,128]{1,0:T(8,128)(2,1)}, bf16[2048,128]{1,0:T(8,128)(2,1)S(1)}, u32[]{:S(2)}, u32[]{:S(2)}) collective-permute-start(bf16[2048,128]{1,0:T(8,128)(2,1)} %collective-permute-done.8.refs_2_), channel_id=1, source_target_pairs={{0,1},{1,0},{2,3},{3,2},{4,5},{5,4},{6,7},{7,6},{8,9},{9,8},{10,11... | collective-permute-start | bytes 1572872 | tf_op jit(solution)/shard_map/ppermute | solution.py:434
  91.1 3.2 %collective-permute-start.15 = (bf16[2048,128]{1,0:T(8,128)(2,1)}, bf16[2048,128]{1,0:T(8,128)(2,1)S(1)}, u32[]{:S(2)}, u32[]{:S(2)}) collective-permute-start(bf16[2048,128]{1,0:T(8,128)(2,1)} %collective-permute-done.9.refs_3_), channel_id=1, source_target_pairs={{0,1},{1,0},{2,3},{3,2},{4,5},{5,4},{6,7},{7,6},{8,9},{9,8},{10,11... | collective-permute-start | bytes 1572872 | tf_op jit(solution)/shard_map/ppermute | solution.py:434
  94.3 7.1 %collective-permute-start.16 = (bf16[4,2048,128]{2,1,0:T(8,128)(2,1)S(1)}, bf16[4,2048,128]{2,1,0:T(8,128)(2,1)S(1)}, u32[]{:S(2)}, u32[]{:S(2)}) collective-permute-start(bf16[4,2048,128]{2,1,0:T(8,128)(2,1)S(1)} %all-to-all-done.1.mine), channel_id=1, source_target_pairs={{0,1},{1,0},{2,3},{3,2},{4,5},{5,4},{6,7},{7,6},{8,9},{9,8},{10,11... | collective-permute-start | bytes 6291464 | tf_op jit(solution)/shard_map/ppermute | solution.py:434

commit v11 on v10

--- a/solution.py
+++ b/solution.py
@@ -391,7 +391,7 @@
 def product(where, w, mine, theirs, near, half, snap):
     m, k = w.shape
     ngroup = mine.shape[0]
-    mb = 384
+    mb = 512
     return pl.pallas_call(
         functools.partial(product_kernel, ngroup=ngroup, nh=snap // (ngroup * LANES), half=half),
         out_shape=jax.ShapeDtypeStruct((m, snap), jnp.bfloat16),

time: 137 us -> 136 us (level)
  transfers between devices with their start and end apart: 19 -> 19, of which waited for: 5 -> 5; matrix products, arithmetic and copies ran while one was open for 10% -> 10% of each run, Pallas kernels for 41% -> 42%
where the time goes in v11:
time: 136 us; the launch traced here: 134 us
  Pallas kernels  88.5 us (65%)
  starting transfers between devices  26.3 us (19%)
  local copies, waits for them, and re-layouts  11.5 us (8%)
  waiting for transfers between devices  3.88 us (3%)
  other arithmetic  3.77 us (3%)
    pallas_call x1, Pallas kernels, product(): pl.pallas_call(functools.partial(product_kernel, ngroup=ngroup, nh=snap /...  32.8 us
    pallas_call x1, Pallas kernels, combine(): pl.pallas_call(kern, out_shape=jax.ShapeDtypeStruct((nc, nel, nse * nb),...  30.3 us
    pallas_call x1, Pallas kernels, pick_far(): pl.pallas_call(functools.partial(pick_far_kernel, nsrc=nrow, order=order,...  11.9 us
    pallas_call x1, Pallas kernels, arrange(): pl.pallas_call(functools.partial(arrange_kernel, nsrc=nrow, nh=nh, per=LA...  6.75 us
    pallas_call x1, Pallas kernels, pick_near(): pl.pallas_call(functools.partial(pick_near_kernel, parts=parts, chunk=chu...  6.68 us
    ppermute x9, starting transfers between devices, body(): to_other = lambda x: lax.ppermute(x, 'row', other)  5.47 us
    ppermute x3, starting transfers between devices, body(): tops = [top] + [lax.ppermute(top, 'row', along(s)) for s in range(1, nz)]  4.73 us
    reshape x2, local copies, waits for them, and re-layouts, body(): smat = smat.transpose(0, 2, 1, 3).reshape(nc, ngrp, ndof * SUB)  4.29 us
  transfers between devices with their start and end apart: 19, of which 5 were waited for; matrix products, arithmetic and copies ran while one was open for 10% of the time, Pallas kernels for 42%

profile of v11, /device:TPU:11, one launch (start us, length us, event | category | flops | bytes accessed | tf_op | source)
XLA Modules:
  0.0 134.2 jit_solution(7815655940269994171)
XLA Ops:
  0.0 1.1 fusion.4
  1.1 0.2 collective-permute-start.2
  1.4 2.3 %collective-permute-start.1 = (bf16[16,8192]{1,0:T(8,128)(2,1)S(1)}, bf16[16,8192]{1,0:T(8,128)(2,1)S(1)}, u32[]{:S(2)}, u32[]{:S(2)}) collective-permute-start(bf16[16,8192]{1,0:T(8,128)(2,1)S(1)} %get-tuple-element.47.refs_0_), channel_id=1, source_target_pairs={{0,4},{1,5},{2,6},{3,7},{4,0},{5,1},{6,2},{7,3},{8,12},{9,13},{10,... | collective-permute-start | bytes 786440 | tf_op jit(solution)/shard_map/ppermute | solution.py:435
  3.7 2.2 %collective-permute-start = (bf16[16,8192]{1,0:T(8,128)(2,1)S(1)}, bf16[16,8192]{1,0:T(8,128)(2,1)S(1)}, u32[]{:S(2)}, u32[]{:S(2)}) collective-permute-start(bf16[16,8192]{1,0:T(8,128)(2,1)S(1)} %get-tuple-element.47.refs_0_), channel_id=1, source_target_pairs={{0,2},{1,3},{2,4},{3,5},{4,6},{5,7},{6,0},{7,1},{8,10},{9,11},{10,... | collective-permute-start | bytes 786440 | tf_op jit(solution)/shard_map/ppermute | solution.py:435
  5.9 1.0 broadcast_in_dim.12
  6.9 3.7 %all-to-all-start = ((bf16[4,16,8192]{2,1,0:T(8,128)(2,1)}), bf16[4,16,8192]{2,1,0:T(8,128)(2,1)S(1)}, u32[]{:S(2)}, u32[]{:S(2)}) async-start(bf16[4,16,8192]{2,1,0:T(8,128)(2,1)} %broadcast_in_dim.12), calls=%async_computation | async-start | bytes 2097152 | tf_op jit(solution)/shard_map/all_to_all | solution.py:437
  10.8 0.1 copy.18
  10.9 0.2 copy.19
  11.1 0.3 copy.20
  11.4 0.9 mul.14.conn
  12.4 1.6 %copy.21 = f32[6,24,512]{1,2,0:T(8,128)} copy(f32[6,24,512]{2,1,0:T(8,128)S(1)} %convert_bitcast_fusion) | data formatting | bytes 589824 | tf_op jit(solution)/shard_map/reshape | solution.py:455
  14.0 2.7 %copy.22 = f32[6,64,24,8]{1,3,2,0:T(8,128)} copy(f32[6,64,24,8]{2,3,1,0:T(8,128)} %bitcast.33) | data formatting | bytes 589824 | tf_op jit(solution)/shard_map/reshape | solution.py:455
  16.7 0.1 pad_add_fusion.slots
  16.8 0.6 fusion.5
  17.4 0.6 constant_dynamic-slice_fusion
  18.1 3.6 %bitcast_select_fusion = (bf16[272,1024]{1,0:T(8,128)(2,1)}, bf16[272,1024]{1,0:T(8,128)(2,1)}) fusion(bf16[16,512,1024]{2,1,0:T(8,128)(2,1)} %rec_hbm.1, pred[272]{0:T(512)(128)(4,1)S(1)} %get-tuple-element.80, bf16[]{:T(256)} %bitcast.12, bf16[]{:T(256)} %bitcast.10, pred[272]{0:T(512)(128)(4,1)S(1)} %get-tuple-element.79), kind=kLoop, calls=%fused_computation | loop fusion | flops 557056 | bytes 2228772 | tf_op jit(solution)/shard_map/jit(_where)/select_n | solution.py:447
  21.7 0.1 copy.23.grow_hbm.grow_ref
  21.8 1.3 copy.24.smat_hbm.s_ref
  23.1 6.7 %pick_near.1.refs_0_ = bf16[2048,128]{1,0:T(8,128)(2,1)S(1)} custom-call(s32[4096]{0:T(1024)S(1)} %bitcast.31, bf16[4,16,8192]{2,1,0:T(8,128)(2,1)S(1)} %all-to-all-done.src, s32[64,192]{1,0:T(8,128)S(1)} %copy.23.grow_hbm.grow_ref, f32[6,64,192]{2,1,0:T(8,128)S(1)} %copy.24.smat_hbm.s_ref), custom_call_target="tpu_custom_call" | custom-call | tf_op jit(solution)/shard_map/pick_near/pallas_call | solution.py:197
  29.8 0.0 collective-permute-done.2.refs_3_
  29.9 0.0 collective-permute-done.refs_1_
  29.9 3.6 %collective-permute-start.10 = (bf16[272,1024]{1,0:T(8,128)(2,1)}, bf16[272,1024]{1,0:T(8,128)(2,1)}, u32[]{:S(2)}, u32[]{:S(2)}) collective-permute-start(bf16[272,1024]{1,0:T(8,128)(2,1)} %get-tuple-element.54), channel_id=1, source_target_pairs={{0,1},{1,2},{2,3},{3,4},{4,5},{5,6},{6,7},{8,9},{9,10},{10,11},{11... | collective-permute-start | bytes 1671176 | tf_op jit(solution)/shard_map/ppermute | solution.py:474
  33.4 2.3 %collective-permute-start.11 = (bf16[272,1024]{1,0:T(8,128)(2,1)}, bf16[272,1024]{1,0:T(8,128)(2,1)}, u32[]{:S(2)}, u32[]{:S(2)}) collective-permute-start(bf16[272,1024]{1,0:T(8,128)(2,1)} %get-tuple-element.55), channel_id=1, source_target_pairs={{1,0},{2,1},{3,2},{4,3},{5,4},{6,5},{7,6},{9,8},{10,9},{11,10},{12... | collective-permute-start | bytes 1671176 | tf_op jit(solution)/shard_map/ppermute | solution.py:475
  35.7 1.8 %collective-permute-start.3 = (bf16[16,8192]{1,0:T(8,128)(2,1)S(1)}, bf16[16,8192]{1,0:T(8,128)(2,1)S(1)}, u32[]{:S(2)}, u32[]{:S(2)}) collective-permute-start(bf16[16,8192]{1,0:T(8,128)(2,1)S(1)} %get-tuple-element.47.refs_0_), channel_id=1, source_target_pairs={{0,1},{1,0},{2,3},{3,2},{4,5},{5,4},{6,7},{7,6},{8,9},{9,8},{10,11... | collective-permute-start | bytes 786440 | tf_op jit(solution)/shard_map/ppermute | solution.py:434
  37.5 0.1 collective-permute-start.4
  37.6 0.4 collective-permute-start.5
  38.0 0.7 collective-permute-done.3.refs_4_
  38.7 0.4 collective-permute-start.6
  39.1 0.4 collective-permute-start.12
  39.4 0.0 collective-permute-done.5.refs_6_
  39.5 0.3 collective-permute-start.9
  39.8 0.5 collective-permute-done.6.refs_7_
  40.2 0.6 collective-permute-start.8
  40.9 0.8 copy-done.2
  41.6 11.9 %pick_far.1 = bf16[8192,128]{1,0:T(8,128)(2,1)} custom-call(s32[8192]{0:T(1024)S(1)} %bitcast.30, s32[8]{0:T(128)S(1)} %pad_add_fusion.slots, bf16[16,8192]{1,0:T(8,128)(2,1)S(1)} %get-tuple-element.47.refs_0_, bf16[16,8192]{1,0:T(8,128)(2,1)S(1)} %collective-permute-done.refs_1_, bf16[16,8192]{1,0:T(8,128)(2,1)S(1)} %collective-permute-done.1.refs_2_, ...), custom_call_target="tpu_custom_call" | custom-call | tf_op jit(solution)/shard_map/pick_far/pallas_call | solution.py:258
  53.6 3.9 %all-to-all-start.1 = ((bf16[4,2048,128]{2,1,0:T(8,128)(2,1)}), bf16[4,2048,128]{2,1,0:T(8,128)(2,1)S(1)}, u32[]{:S(2)}, u32[]{:S(2)}) async-start(bf16[4,2048,128]{2,1,0:T(8,128)(2,1)} %bitcast.14), calls=%async_computation.1 | async-start | bytes 4194304 | tf_op jit(solution)/shard_map/all_to_all | solution.py:481
  57.5 0.0 collective-permute-done.10.head_ref
  57.5 1.6 %collective-permute-start.7 = (bf16[2048,128]{1,0:T(8,128)(2,1)S(1)}, bf16[2048,128]{1,0:T(8,128)(2,1)}, u32[]{:S(2)}, u32[]{:S(2)}) collective-permute-start(bf16[2048,128]{1,0:T(8,128)(2,1)S(1)} %pick_near.1.refs_0_), channel_id=1, source_target_pairs={{0,2},{1,3},{2,4},{3,5},{4,6},{5,7},{6,0},{7,1},{8,10},{9,11},{10,... | collective-permute-start | bytes 1572872 | tf_op jit(solution)/shard_map/ppermute | solution.py:476
  59.1 30.3 %combine.1 = bf16[6,512,4096]{2,1,0:T(8,128)(2,1)} custom-call(s32[12288]{0:T(1024)} %mul.14.conn, s32[16]{0:T(128)} %se.1, s32[64,192]{1,0:T(8,128)} %copy-done.1, f32[6,64,192]{2,1,0:T(8,128)} %copy-done, bf16[16,512,1024]{2,1,0:T(8,128)(2,1)} %rec_hbm.1, bf16[272,1024]{1,0:T(8,128)(2,1)} %collective-permute-done.10.head_ref, ...), custom_call_target="tpu_custom_call" | custom-call | flops 30000001024 | bytes 125829120 | tf_op jit(solution)/shard_map/combine/pallas_call | solution.py:135
  89.5 1.5 %collective-permute-start.13 = (bf16[2048,128]{1,0:T(8,128)(2,1)}, bf16[2048,128]{1,0:T(8,128)(2,1)S(1)}, u32[]{:S(2)}, u32[]{:S(2)}) collective-permute-start(bf16[2048,128]{1,0:T(8,128)(2,1)} %collective-permute-done.7.refs_1_), channel_id=1, source_target_pairs={{0,1},{1,0},{2,3},{3,2},{4,5},{5,4},{6,7},{7,6},{8,9},{9,8},{10,11... | collective-permute-start | bytes 1572872 | tf_op jit(solution)/shard_map/ppermute | solution.py:434
  91.0 0.1 collective-permute-start.14
  91.1 0.4 collective-permute-start.15
  91.5 1.2 collective-permute-done.13.refs_5_
  92.8 0.7 collective-permute-done.14.refs_6_
  93.5 0.7 collective-permute-done.15.refs_7_
  94.3 0.4 collective-permute-start.16
  94.6 6.8 %arrange.1 = bf16[2,2048,512]{2,1,0:T(8,128)(2,1)S(1)} custom-call(s32[8]{0:T(128)S(1)} %pad_add_fusion.slots, bf16[2048,128]{1,0:T(8,128)(2,1)S(1)} %pick_near.1.refs_0_, bf16[2048,128]{1,0:T(8,128)(2,1)} %collective-permute-done.7.refs_1_, bf16[2048,128]{1,0:T(8,128)(2,1)} %collective-permute-done.8.refs_2_, ...), custom_call_target="tpu_custom_call" | custom-call | tf_op jit(solution)/shard_map/arrange/pallas_call | solution.py:330
  101.4 32.8 %product.1 = bf16[3072,1024]{1,0:T(8,128)(2,1)} custom-call(s32[1]{0:T(128)} %bitcast.9.core, bf16[3072,4096]{1,0:T(8,128)(2,1)} %bitcast.32, bf16[4,2048,128]{2,1,0:T(8,128)(2,1)S(1)} %all-to-all-done.1.mine, bf16[4,2048,128]{2,1,0:T(8,128)(2,1)S(1)} %collective-permute-done.16.theirs, bf16[4096,512]{1,0:T(8,128)(2,1)S(1)} %bitcast.29), custom_call_target="tpu_custom_call" | custom-call | tf_op jit(solution)/shard_map/product/pallas_call | solution.py:395
  (31 shorter events, 0.2 us)
Async XLA Ops:
  0.0 10.7 %copy-start.6 = (s32[16]{0:T(128)S(1)}, s32[16]{0:T(128)}, u32[]{:S(2)}) copy-start(s32[16]{0:T(128)} %se.1) | copy-start | bytes 196
  0.0 10.7 %copy-start.4 = (s32[16,1024]{1,0:T(8,128)S(1)}, s32[16,1024]{1,0:T(8,128)}, u32[]{:S(2)}) copy-start(s32[16,1024]{1,0:T(8,128)} %param.7) | copy-start | bytes 196612
  0.0 10.8 %copy-start.5 = (s32[512,24]{0,1:T(8,128)S(1)}, s32[512,24]{0,1:T(8,128)}, u32[]{:S(2)}) copy-start(s32[512,24]{0,1:T(8,128)} %param.10) | copy-start | bytes 147460
  0.0 11.1 %copy-start.3 = (bf16[512,6,24]{0,2,1:T(8,128)(2,1)S(1)}, bf16[512,6,24]{0,2,1:T(8,128)(2,1)}, u32[]{:S(2)}) copy-start(bf16[512,6,24]{0,2,1:T(8,128)(2,1)} %param.11) | copy-start | bytes 442372
  1.1 28.7 %collective-permute-start.2 = (bf16[16,8192]{1,0:T(8,128)(2,1)S(1)}, bf16[16,8192]{1,0:T(8,128)(2,1)S(1)}, u32[]{:S(2)}, u32[]{:S(2)}) collective-permute-start(bf16[16,8192]{1,0:T(8,128)(2,1)S(1)} %get-tuple-element.47.refs_0_), channel_id=1, source_target_pairs={{0,6},{1,7},{2,0},{3,1},{4,2},{5,3},{6,4},{7,5},{8,14},{9,15},{10,... | collective-permute-start | bytes 786440 | tf_op jit(solution)/shard_map/ppermute | solution.py:435
  1.4 28.5 %collective-permute-start.1 = (bf16[16,8192]{1,0:T(8,128)(2,1)S(1)}, bf16[16,8192]{1,0:T(8,128)(2,1)S(1)}, u32[]{:S(2)}, u32[]{:S(2)}) collective-permute-start(bf16[16,8192]{1,0:T(8,128)(2,1)S(1)} %get-tuple-element.47.refs_0_), channel_id=1, source_target_pairs={{0,4},{1,5},{2,6},{3,7},{4,0},{5,1},{6,2},{7,3},{8,12},{9,13},{10,... | collective-permute-start | bytes 786440 | tf_op jit(solution)/shard_map/ppermute | solution.py:435
  3.7 26.2 %collective-permute-start = (bf16[16,8192]{1,0:T(8,128)(2,1)S(1)}, bf16[16,8192]{1,0:T(8,128)(2,1)S(1)}, u32[]{:S(2)}, u32[]{:S(2)}) collective-permute-start(bf16[16,8192]{1,0:T(8,128)(2,1)S(1)} %get-tuple-element.47.refs_0_), channel_id=1, source_target_pairs={{0,2},{1,3},{2,4},{3,5},{4,6},{5,7},{6,0},{7,1},{8,10},{9,11},{10,... | collective-permute-start | bytes 786440 | tf_op jit(solution)/shard_map/ppermute | solution.py:435
  6.9 16.2 %all-to-all-start = ((bf16[4,16,8192]{2,1,0:T(8,128)(2,1)}), bf16[4,16,8192]{2,1,0:T(8,128)(2,1)S(1)}, u32[]{:S(2)}, u32[]{:S(2)}) async-start(bf16[4,16,8192]{2,1,0:T(8,128)(2,1)} %broadcast_in_dim.12), calls=%async_computation | async-start | bytes 2097152 | tf_op jit(solution)/shard_map/all_to_all | solution.py:437
  21.8 17.3 %copy-start.1 = (s32[64,192]{1,0:T(8,128)}, s32[64,192]{1,0:T(8,128)S(1)}, u32[]{:S(2)}) copy-start(s32[64,192]{1,0:T(8,128)S(1)} %copy.23.grow_hbm.grow_ref) | copy-start | bytes 147460
  23.1 30.5 %copy-start = (f32[6,64,192]{2,1,0:T(8,128)}, f32[6,64,192]{2,1,0:T(8,128)S(1)}, u32[]{:S(2)}) copy-start(f32[6,64,192]{2,1,0:T(8,128)S(1)} %copy.24.smat_hbm.s_ref) | copy-start | bytes 884740
  29.9 27.6 %collective-permute-start.10 = (bf16[272,1024]{1,0:T(8,128)(2,1)}, bf16[272,1024]{1,0:T(8,128)(2,1)}, u32[]{:S(2)}, u32[]{:S(2)}) collective-permute-start(bf16[272,1024]{1,0:T(8,128)(2,1)} %get-tuple-element.54), channel_id=1, source_target_pairs={{0,1},{1,2},{2,3},{3,4},{4,5},{5,6},{6,7},{8,9},{9,10},{10,11},{11... | collective-permute-start | bytes 1671176 | tf_op jit(solution)/shard_map/ppermute | solution.py:474
  33.4 25.7 %collective-permute-start.11 = (bf16[272,1024]{1,0:T(8,128)(2,1)}, bf16[272,1024]{1,0:T(8,128)(2,1)}, u32[]{:S(2)}, u32[]{:S(2)}) collective-permute-start(bf16[272,1024]{1,0:T(8,128)(2,1)} %get-tuple-element.55), channel_id=1, source_target_pairs={{1,0},{2,1},{3,2},{4,3},{5,4},{6,5},{7,6},{9,8},{10,9},{11,10},{12... | collective-permute-start | bytes 1671176 | tf_op jit(solution)/shard_map/ppermute | solution.py:475
  35.7 3.0 %collective-permute-start.3 = (bf16[16,8192]{1,0:T(8,128)(2,1)S(1)}, bf16[16,8192]{1,0:T(8,128)(2,1)S(1)}, u32[]{:S(2)}, u32[]{:S(2)}) collective-permute-start(bf16[16,8192]{1,0:T(8,128)(2,1)S(1)} %get-tuple-element.47.refs_0_), channel_id=1, source_target_pairs={{0,1},{1,0},{2,3},{3,2},{4,5},{5,4},{6,7},{7,6},{8,9},{9,8},{10,11... | collective-permute-start | bytes 786440 | tf_op jit(solution)/shard_map/ppermute | solution.py:434
  37.5 1.5 %collective-permute-start.4 = (bf16[16,8192]{1,0:T(8,128)(2,1)S(1)}, bf16[16,8192]{1,0:T(8,128)(2,1)S(1)}, u32[]{:S(2)}, u32[]{:S(2)}) collective-permute-start(bf16[16,8192]{1,0:T(8,128)(2,1)S(1)} %collective-permute-done.refs_1_), channel_id=1, source_target_pairs={{0,1},{1,0},{2,3},{3,2},{4,5},{5,4},{6,7},{7,6},{8,9},{9,8},{10,11... | collective-permute-start | bytes 786440 | tf_op jit(solution)/shard_map/ppermute | solution.py:434
  37.6 1.8 %collective-permute-start.5 = (bf16[16,8192]{1,0:T(8,128)(2,1)S(1)}, bf16[16,8192]{1,0:T(8,128)(2,1)S(1)}, u32[]{:S(2)}, u32[]{:S(2)}) collective-permute-start(bf16[16,8192]{1,0:T(8,128)(2,1)S(1)} %collective-permute-done.1.refs_2_), channel_id=1, source_target_pairs={{0,1},{1,0},{2,3},{3,2},{4,5},{5,4},{6,7},{7,6},{8,9},{9,8},{10,11... | collective-permute-start | bytes 786440 | tf_op jit(solution)/shard_map/ppermute | solution.py:434
  38.7 1.5 %collective-permute-start.6 = (bf16[16,8192]{1,0:T(8,128)(2,1)S(1)}, bf16[16,8192]{1,0:T(8,128)(2,1)S(1)}, u32[]{:S(2)}, u32[]{:S(2)}) collective-permute-start(bf16[16,8192]{1,0:T(8,128)(2,1)S(1)} %collective-permute-done.2.refs_3_), channel_id=1, source_target_pairs={{0,1},{1,0},{2,3},{3,2},{4,5},{5,4},{6,7},{7,6},{8,9},{9,8},{10,11... | collective-permute-start | bytes 786440 | tf_op jit(solution)/shard_map/ppermute | solution.py:434
  39.1 52.4 %collective-permute-start.12 = (bf16[2048,128]{1,0:T(8,128)(2,1)S(1)}, bf16[2048,128]{1,0:T(8,128)(2,1)S(1)}, u32[]{:S(2)}, u32[]{:S(2)}) collective-permute-start(bf16[2048,128]{1,0:T(8,128)(2,1)S(1)} %pick_near.1.refs_0_), channel_id=1, source_target_pairs={{0,1},{1,0},{2,3},{3,2},{4,5},{5,4},{6,7},{7,6},{8,9},{9,8},{10,11... | collective-permute-start | bytes 1572872 | tf_op jit(solution)/shard_map/ppermute | solution.py:434
  39.5 50.0 %collective-permute-start.9 = (bf16[2048,128]{1,0:T(8,128)(2,1)S(1)}, bf16[2048,128]{1,0:T(8,128)(2,1)}, u32[]{:S(2)}, u32[]{:S(2)}) collective-permute-start(bf16[2048,128]{1,0:T(8,128)(2,1)S(1)} %pick_near.1.refs_0_), channel_id=1, source_target_pairs={{0,6},{1,7},{2,0},{3,1},{4,2},{5,3},{6,4},{7,5},{8,14},{9,15},{10,... | collective-permute-start | bytes 1572872 | tf_op jit(solution)/shard_map/ppermute | solution.py:476
  40.2 49.2 %collective-permute-start.8 = (bf16[2048,128]{1,0:T(8,128)(2,1)S(1)}, bf16[2048,128]{1,0:T(8,128)(2,1)}, u32[]{:S(2)}, u32[]{:S(2)}) collective-permute-start(bf16[2048,128]{1,0:T(8,128)(2,1)S(1)} %pick_near.1.refs_0_), channel_id=1, source_target_pairs={{0,4},{1,5},{2,6},{3,7},{4,0},{5,1},{6,2},{7,3},{8,12},{9,13},{10,... | collective-permute-start | bytes 1572872 | tf_op jit(solution)/shard_map/ppermute | solution.py:476
  40.9 0.8 copy-start.2
  53.6 35.9 %all-to-all-start.1 = ((bf16[4,2048,128]{2,1,0:T(8,128)(2,1)}), bf16[4,2048,128]{2,1,0:T(8,128)(2,1)S(1)}, u32[]{:S(2)}, u32[]{:S(2)}) async-start(bf16[4,2048,128]{2,1,0:T(8,128)(2,1)} %bitcast.14), calls=%async_computation.1 | async-start | bytes 4194304 | tf_op jit(solution)/shard_map/all_to_all | solution.py:481
  57.5 31.9 %collective-permute-start.7 = (bf16[2048,128]{1,0:T(8,128)(2,1)S(1)}, bf16[2048,128]{1,0:T(8,128)(2,1)}, u32[]{:S(2)}, u32[]{:S(2)}) collective-permute-start(bf16[2048,128]{1,0:T(8,128)(2,1)S(1)} %pick_near.1.refs_0_), channel_id=1, source_target_pairs={{0,2},{1,3},{2,4},{3,5},{4,6},{5,7},{6,0},{7,1},{8,10},{9,11},{10,... | collective-permute-start | bytes 1572872 | tf_op jit(solution)/shard_map/ppermute | solution.py:476
  89.5 3.3 %collective-permute-start.13 = (bf16[2048,128]{1,0:T(8,128)(2,1)}, bf16[2048,128]{1,0:T(8,128)(2,1)S(1)}, u32[]{:S(2)}, u32[]{:S(2)}) collective-permute-start(bf16[2048,128]{1,0:T(8,128)(2,1)} %collective-permute-done.7.refs_1_), channel_id=1, source_target_pairs={{0,1},{1,0},{2,3},{3,2},{4,5},{5,4},{6,7},{7,6},{8,9},{9,8},{10,11... | collective-permute-start | bytes 1572872 | tf_op jit(solution)/shard_map/ppermute | solution.py:434
  91.0 2.5 %collective-permute-start.14 = (bf16[2048,128]{1,0:T(8,128)(2,1)}, bf16[2048,128]{1,0:T(8,128)(2,1)S(1)}, u32[]{:S(2)}, u32[]{:S(2)}) collective-permute-start(bf16[2048,128]{1,0:T(8,128)(2,1)} %collective-permute-done.8.refs_2_), channel_id=1, source_target_pairs={{0,1},{1,0},{2,3},{3,2},{4,5},{5,4},{6,7},{7,6},{8,9},{9,8},{10,11... | collective-permute-start | bytes 1572872 | tf_op jit(solution)/shard_map/ppermute | solution.py:434
  91.1 3.2 %collective-permute-start.15 = (bf16[2048,128]{1,0:T(8,128)(2,1)}, bf16[2048,128]{1,0:T(8,128)(2,1)S(1)}, u32[]{:S(2)}, u32[]{:S(2)}) collective-permute-start(bf16[2048,128]{1,0:T(8,128)(2,1)} %collective-permute-done.9.refs_3_), channel_id=1, source_target_pairs={{0,1},{1,0},{2,3},{3,2},{4,5},{5,4},{6,7},{7,6},{8,9},{9,8},{10,11... | collective-permute-start | bytes 1572872 | tf_op jit(solution)/shard_map/ppermute | solution.py:434
  94.3 7.1 %collective-permute-start.16 = (bf16[4,2048,128]{2,1,0:T(8,128)(2,1)S(1)}, bf16[4,2048,128]{2,1,0:T(8,128)(2,1)S(1)}, u32[]{:S(2)}, u32[]{:S(2)}) collective-permute-start(bf16[4,2048,128]{2,1,0:T(8,128)(2,1)S(1)} %all-to-all-done.1.mine), channel_id=1, source_target_pairs={{0,1},{1,0},{2,3},{3,2},{4,5},{5,4},{6,7},{7,6},{8,9},{9,8},{10,11... | collective-permute-start | bytes 6291464 | tf_op jit(solution)/shard_map/ppermute | solution.py:434

commit v12 on v11

--- a/solution.py
+++ b/solution.py
@@ -326,7 +326,7 @@
     npair = ngroup // 2
     parts = k // nk
     cols = nh * npair * LANES
-    step_rows = min(nk // 2, 256)
+    step_rows = min(nk // 2, 512)
     out = pl.pallas_call(
         functools.partial(
             arrange_kernel, nsrc=nrow, nh=nh, per=LANES // tper, npair=npair, parts=parts, tper=tper

time: 136 us -> 136 us (level)
  transfers between devices with their start and end apart: 19 -> 19, of which waited for: 5 -> 5; matrix products, arithmetic and copies ran while one was open for 10% -> 10% of each run, Pallas kernels for 42% -> 41%
where the time goes in v12:
time: 136 us; the launch traced here: 134 us
  Pallas kernels  88.2 us (65%)
  starting transfers between devices  26.3 us (19%)
  local copies, waits for them, and re-layouts  11.5 us (8%)
  waiting for transfers between devices  3.88 us (3%)
  other arithmetic  3.77 us (3%)
    pallas_call x1, Pallas kernels, product(): pl.pallas_call(functools.partial(product_kernel, ngroup=ngroup, nh=snap /...  32.8 us
    pallas_call x1, Pallas kernels, combine(): pl.pallas_call(kern, out_shape=jax.ShapeDtypeStruct((nc, nel, nse * nb),...  30.3 us
    pallas_call x1, Pallas kernels, pick_far(): pl.pallas_call(functools.partial(pick_far_kernel, nsrc=nrow, order=order,...  11.9 us
    pallas_call x1, Pallas kernels, pick_near(): pl.pallas_call(functools.partial(pick_near_kernel, parts=parts, chunk=chu...  6.68 us
    pallas_call x1, Pallas kernels, arrange(): pl.pallas_call(functools.partial(arrange_kernel, nsrc=nrow, nh=nh, per=LA...  6.49 us
    ppermute x9, starting transfers between devices, body(): to_other = lambda x: lax.ppermute(x, 'row', other)  5.53 us
    ppermute x3, starting transfers between devices, body(): tops = [top] + [lax.ppermute(top, 'row', along(s)) for s in range(1, nz)]  4.73 us
    reshape x2, local copies, waits for them, and re-layouts, body(): smat = smat.transpose(0, 2, 1, 3).reshape(nc, ngrp, ndof * SUB)  4.29 us
  transfers between devices with their start and end apart: 19, of which 5 were waited for; matrix products, arithmetic and copies ran while one was open for 10% of the time, Pallas kernels for 41%

profile of v12, /device:TPU:11, one launch (start us, length us, event | category | flops | bytes accessed | tf_op | source)
XLA Modules:
  0.0 134.0 jit_solution(11979007816492658273)
XLA Ops:
  0.0 1.1 fusion.4
  1.1 0.2 collective-permute-start.2
  1.4 2.3 %collective-permute-start.1 = (bf16[16,8192]{1,0:T(8,128)(2,1)S(1)}, bf16[16,8192]{1,0:T(8,128)(2,1)S(1)}, u32[]{:S(2)}, u32[]{:S(2)}) collective-permute-start(bf16[16,8192]{1,0:T(8,128)(2,1)S(1)} %get-tuple-element.47.refs_0_), channel_id=1, source_target_pairs={{0,4},{1,5},{2,6},{3,7},{4,0},{5,1},{6,2},{7,3},{8,12},{9,13},{10,... | collective-permute-start | bytes 786440 | tf_op jit(solution)/shard_map/ppermute | solution.py:435
  3.7 2.2 %collective-permute-start = (bf16[16,8192]{1,0:T(8,128)(2,1)S(1)}, bf16[16,8192]{1,0:T(8,128)(2,1)S(1)}, u32[]{:S(2)}, u32[]{:S(2)}) collective-permute-start(bf16[16,8192]{1,0:T(8,128)(2,1)S(1)} %get-tuple-element.47.refs_0_), channel_id=1, source_target_pairs={{0,2},{1,3},{2,4},{3,5},{4,6},{5,7},{6,0},{7,1},{8,10},{9,11},{10,... | collective-permute-start | bytes 786440 | tf_op jit(solution)/shard_map/ppermute | solution.py:435
  5.9 1.0 broadcast_in_dim.12
  6.9 3.7 %all-to-all-start = ((bf16[4,16,8192]{2,1,0:T(8,128)(2,1)}), bf16[4,16,8192]{2,1,0:T(8,128)(2,1)S(1)}, u32[]{:S(2)}, u32[]{:S(2)}) async-start(bf16[4,16,8192]{2,1,0:T(8,128)(2,1)} %broadcast_in_dim.12), calls=%async_computation | async-start | bytes 2097152 | tf_op jit(solution)/shard_map/all_to_all | solution.py:437
  10.8 0.1 copy.18
  10.9 0.2 copy.19
  11.1 0.3 copy.20
  11.4 0.9 mul.14.conn
  12.4 1.6 %copy.21 = f32[6,24,512]{1,2,0:T(8,128)} copy(f32[6,24,512]{2,1,0:T(8,128)S(1)} %convert_bitcast_fusion) | data formatting | bytes 589824 | tf_op jit(solution)/shard_map/reshape | solution.py:455
  14.0 2.7 %copy.22 = f32[6,64,24,8]{1,3,2,0:T(8,128)} copy(f32[6,64,24,8]{2,3,1,0:T(8,128)} %bitcast.33) | data formatting | bytes 589824 | tf_op jit(solution)/shard_map/reshape | solution.py:455
  16.7 0.1 pad_add_fusion.slots
  16.8 0.6 fusion.5
  17.4 0.6 constant_dynamic-slice_fusion
  18.1 3.6 %bitcast_select_fusion = (bf16[272,1024]{1,0:T(8,128)(2,1)}, bf16[272,1024]{1,0:T(8,128)(2,1)}) fusion(bf16[16,512,1024]{2,1,0:T(8,128)(2,1)} %rec_hbm.1, pred[272]{0:T(512)(128)(4,1)S(1)} %get-tuple-element.80, bf16[]{:T(256)} %bitcast.12, bf16[]{:T(256)} %bitcast.10, pred[272]{0:T(512)(128)(4,1)S(1)} %get-tuple-element.79), kind=kLoop, calls=%fused_computation | loop fusion | flops 557056 | bytes 2228772 | tf_op jit(solution)/shard_map/jit(_where)/select_n | solution.py:447
  21.7 0.1 copy.23.grow_hbm.grow_ref
  21.8 1.3 copy.24.smat_hbm.s_ref
  23.1 0.0 all-to-all-done.src
  23.1 6.7 %pick_near.1.refs_0_ = bf16[2048,128]{1,0:T(8,128)(2,1)S(1)} custom-call(s32[4096]{0:T(1024)S(1)} %bitcast.31, bf16[4,16,8192]{2,1,0:T(8,128)(2,1)S(1)} %all-to-all-done.src, s32[64,192]{1,0:T(8,128)S(1)} %copy.23.grow_hbm.grow_ref, f32[6,64,192]{2,1,0:T(8,128)S(1)} %copy.24.smat_hbm.s_ref), custom_call_target="tpu_custom_call" | custom-call | tf_op jit(solution)/shard_map/pick_near/pallas_call | solution.py:197
  29.8 0.0 collective-permute-done.2.refs_3_
  29.8 0.0 collective-permute-done.1.refs_2_
  29.9 3.6 %collective-permute-start.10 = (bf16[272,1024]{1,0:T(8,128)(2,1)}, bf16[272,1024]{1,0:T(8,128)(2,1)}, u32[]{:S(2)}, u32[]{:S(2)}) collective-permute-start(bf16[272,1024]{1,0:T(8,128)(2,1)} %get-tuple-element.54), channel_id=1, source_target_pairs={{0,1},{1,2},{2,3},{3,4},{4,5},{5,6},{6,7},{8,9},{9,10},{10,11},{11... | collective-permute-start | bytes 1671176 | tf_op jit(solution)/shard_map/ppermute | solution.py:474
  33.4 2.3 %collective-permute-start.11 = (bf16[272,1024]{1,0:T(8,128)(2,1)}, bf16[272,1024]{1,0:T(8,128)(2,1)}, u32[]{:S(2)}, u32[]{:S(2)}) collective-permute-start(bf16[272,1024]{1,0:T(8,128)(2,1)} %get-tuple-element.55), channel_id=1, source_target_pairs={{1,0},{2,1},{3,2},{4,3},{5,4},{6,5},{7,6},{9,8},{10,9},{11,10},{12... | collective-permute-start | bytes 1671176 | tf_op jit(solution)/shard_map/ppermute | solution.py:475
  35.7 1.8 %collective-permute-start.3 = (bf16[16,8192]{1,0:T(8,128)(2,1)S(1)}, bf16[16,8192]{1,0:T(8,128)(2,1)S(1)}, u32[]{:S(2)}, u32[]{:S(2)}) collective-permute-start(bf16[16,8192]{1,0:T(8,128)(2,1)S(1)} %get-tuple-element.47.refs_0_), channel_id=1, source_target_pairs={{0,1},{1,0},{2,3},{3,2},{4,5},{5,4},{6,7},{7,6},{8,9},{9,8},{10,11... | collective-permute-start | bytes 786440 | tf_op jit(solution)/shard_map/ppermute | solution.py:434
  37.5 0.1 collective-permute-start.4
  37.6 0.4 collective-permute-start.5
  38.0 0.7 collective-permute-done.3.refs_4_
  38.7 0.4 collective-permute-start.6
  39.1 0.0 collective-permute-done.4.refs_5_
  39.1 0.4 collective-permute-start.12
  39.5 0.3 collective-permute-start.9
  39.8 0.5 collective-permute-done.6.refs_7_
  40.2 0.6 collective-permute-start.8
  40.9 0.8 copy-done.2
  41.6 11.9 %pick_far.1 = bf16[8192,128]{1,0:T(8,128)(2,1)} custom-call(s32[8192]{0:T(1024)S(1)} %bitcast.30, s32[8]{0:T(128)S(1)} %pad_add_fusion.slots, bf16[16,8192]{1,0:T(8,128)(2,1)S(1)} %get-tuple-element.47.refs_0_, bf16[16,8192]{1,0:T(8,128)(2,1)S(1)} %collective-permute-done.refs_1_, bf16[16,8192]{1,0:T(8,128)(2,1)S(1)} %collective-permute-done.1.refs_2_, ...), custom_call_target="tpu_custom_call" | custom-call | tf_op jit(solution)/shard_map/pick_far/pallas_call | solution.py:258
  53.6 3.9 %all-to-all-start.1 = ((bf16[4,2048,128]{2,1,0:T(8,128)(2,1)}), bf16[4,2048,128]{2,1,0:T(8,128)(2,1)S(1)}, u32[]{:S(2)}, u32[]{:S(2)}) async-start(bf16[4,2048,128]{2,1,0:T(8,128)(2,1)} %bitcast.14), calls=%async_computation.1 | async-start | bytes 4194304 | tf_op jit(solution)/shard_map/all_to_all | solution.py:481
  57.5 1.6 %collective-permute-start.7 = (bf16[2048,128]{1,0:T(8,128)(2,1)S(1)}, bf16[2048,128]{1,0:T(8,128)(2,1)}, u32[]{:S(2)}, u32[]{:S(2)}) collective-permute-start(bf16[2048,128]{1,0:T(8,128)(2,1)S(1)} %pick_near.1.refs_0_), channel_id=1, source_target_pairs={{0,2},{1,3},{2,4},{3,5},{4,6},{5,7},{6,0},{7,1},{8,10},{9,11},{10,... | collective-permute-start | bytes 1572872 | tf_op jit(solution)/shard_map/ppermute | solution.py:476
  59.1 30.3 %combine.1 = bf16[6,512,4096]{2,1,0:T(8,128)(2,1)} custom-call(s32[12288]{0:T(1024)} %mul.14.conn, s32[16]{0:T(128)} %se.1, s32[64,192]{1,0:T(8,128)} %copy-done.1, f32[6,64,192]{2,1,0:T(8,128)} %copy-done, bf16[16,512,1024]{2,1,0:T(8,128)(2,1)} %rec_hbm.1, bf16[272,1024]{1,0:T(8,128)(2,1)} %collective-permute-done.10.head_ref, ...), custom_call_target="tpu_custom_call" | custom-call | flops 30000001024 | bytes 125829120 | tf_op jit(solution)/shard_map/combine/pallas_call | solution.py:135
  89.4 1.6 %collective-permute-start.13 = (bf16[2048,128]{1,0:T(8,128)(2,1)}, bf16[2048,128]{1,0:T(8,128)(2,1)S(1)}, u32[]{:S(2)}, u32[]{:S(2)}) collective-permute-start(bf16[2048,128]{1,0:T(8,128)(2,1)} %collective-permute-done.7.refs_1_), channel_id=1, source_target_pairs={{0,1},{1,0},{2,3},{3,2},{4,5},{5,4},{6,7},{7,6},{8,9},{9,8},{10,11... | collective-permute-start | bytes 1572872 | tf_op jit(solution)/shard_map/ppermute | solution.py:434
  91.0 0.1 collective-permute-start.14
  91.1 0.4 collective-permute-start.15
  91.6 1.2 collective-permute-done.13.refs_5_
  92.8 0.7 collective-permute-done.14.refs_6_
  93.5 0.7 collective-permute-done.15.refs_7_
  94.3 0.4 collective-permute-start.16
  94.7 6.5 %arrange.1 = bf16[2,2048,512]{2,1,0:T(8,128)(2,1)S(1)} custom-call(s32[8]{0:T(128)S(1)} %pad_add_fusion.slots, bf16[2048,128]{1,0:T(8,128)(2,1)S(1)} %pick_near.1.refs_0_, bf16[2048,128]{1,0:T(8,128)(2,1)} %collective-permute-done.7.refs_1_, bf16[2048,128]{1,0:T(8,128)(2,1)} %collective-permute-done.8.refs_2_, ...), custom_call_target="tpu_custom_call" | custom-call | tf_op jit(solution)/shard_map/arrange/pallas_call | solution.py:330
  101.2 32.8 %product.1 = bf16[3072,1024]{1,0:T(8,128)(2,1)} custom-call(s32[1]{0:T(128)} %bitcast.9.core, bf16[3072,4096]{1,0:T(8,128)(2,1)} %bitcast.32, bf16[4,2048,128]{2,1,0:T(8,128)(2,1)S(1)} %all-to-all-done.1.mine, bf16[4,2048,128]{2,1,0:T(8,128)(2,1)S(1)} %collective-permute-done.16.theirs, bf16[4096,512]{1,0:T(8,128)(2,1)S(1)} %bitcast.29), custom_call_target="tpu_custom_call" | custom-call | tf_op jit(solution)/shard_map/product/pallas_call | solution.py:395
  (31 shorter events, 0.2 us)
Async XLA Ops:
  0.0 10.7 %copy-start.6 = (s32[16]{0:T(128)S(1)}, s32[16]{0:T(128)}, u32[]{:S(2)}) copy-start(s32[16]{0:T(128)} %se.1) | copy-start | bytes 196
  0.0 10.7 %copy-start.4 = (s32[16,1024]{1,0:T(8,128)S(1)}, s32[16,1024]{1,0:T(8,128)}, u32[]{:S(2)}) copy-start(s32[16,1024]{1,0:T(8,128)} %param.7) | copy-start | bytes 196612
  0.0 10.8 %copy-start.5 = (s32[512,24]{0,1:T(8,128)S(1)}, s32[512,24]{0,1:T(8,128)}, u32[]{:S(2)}) copy-start(s32[512,24]{0,1:T(8,128)} %param.10) | copy-start | bytes 147460
  0.0 11.1 %copy-start.3 = (bf16[512,6,24]{0,2,1:T(8,128)(2,1)S(1)}, bf16[512,6,24]{0,2,1:T(8,128)(2,1)}, u32[]{:S(2)}) copy-start(bf16[512,6,24]{0,2,1:T(8,128)(2,1)} %param.11) | copy-start | bytes 442372
  1.1 28.7 %collective-permute-start.2 = (bf16[16,8192]{1,0:T(8,128)(2,1)S(1)}, bf16[16,8192]{1,0:T(8,128)(2,1)S(1)}, u32[]{:S(2)}, u32[]{:S(2)}) collective-permute-start(bf16[16,8192]{1,0:T(8,128)(2,1)S(1)} %get-tuple-element.47.refs_0_), channel_id=1, source_target_pairs={{0,6},{1,7},{2,0},{3,1},{4,2},{5,3},{6,4},{7,5},{8,14},{9,15},{10,... | collective-permute-start | bytes 786440 | tf_op jit(solution)/shard_map/ppermute | solution.py:435
  1.4 28.5 %collective-permute-start.1 = (bf16[16,8192]{1,0:T(8,128)(2,1)S(1)}, bf16[16,8192]{1,0:T(8,128)(2,1)S(1)}, u32[]{:S(2)}, u32[]{:S(2)}) collective-permute-start(bf16[16,8192]{1,0:T(8,128)(2,1)S(1)} %get-tuple-element.47.refs_0_), channel_id=1, source_target_pairs={{0,4},{1,5},{2,6},{3,7},{4,0},{5,1},{6,2},{7,3},{8,12},{9,13},{10,... | collective-permute-start | bytes 786440 | tf_op jit(solution)/shard_map/ppermute | solution.py:435
  3.7 26.2 %collective-permute-start = (bf16[16,8192]{1,0:T(8,128)(2,1)S(1)}, bf16[16,8192]{1,0:T(8,128)(2,1)S(1)}, u32[]{:S(2)}, u32[]{:S(2)}) collective-permute-start(bf16[16,8192]{1,0:T(8,128)(2,1)S(1)} %get-tuple-element.47.refs_0_), channel_id=1, source_target_pairs={{0,2},{1,3},{2,4},{3,5},{4,6},{5,7},{6,0},{7,1},{8,10},{9,11},{10,... | collective-permute-start | bytes 786440 | tf_op jit(solution)/shard_map/ppermute | solution.py:435
  6.9 16.2 %all-to-all-start = ((bf16[4,16,8192]{2,1,0:T(8,128)(2,1)}), bf16[4,16,8192]{2,1,0:T(8,128)(2,1)S(1)}, u32[]{:S(2)}, u32[]{:S(2)}) async-start(bf16[4,16,8192]{2,1,0:T(8,128)(2,1)} %broadcast_in_dim.12), calls=%async_computation | async-start | bytes 2097152 | tf_op jit(solution)/shard_map/all_to_all | solution.py:437
  21.8 17.3 %copy-start.1 = (s32[64,192]{1,0:T(8,128)}, s32[64,192]{1,0:T(8,128)S(1)}, u32[]{:S(2)}) copy-start(s32[64,192]{1,0:T(8,128)S(1)} %copy.23.grow_hbm.grow_ref) | copy-start | bytes 147460
  23.1 30.5 %copy-start = (f32[6,64,192]{2,1,0:T(8,128)}, f32[6,64,192]{2,1,0:T(8,128)S(1)}, u32[]{:S(2)}) copy-start(f32[6,64,192]{2,1,0:T(8,128)S(1)} %copy.24.smat_hbm.s_ref) | copy-start | bytes 884740
  29.9 27.6 %collective-permute-start.10 = (bf16[272,1024]{1,0:T(8,128)(2,1)}, bf16[272,1024]{1,0:T(8,128)(2,1)}, u32[]{:S(2)}, u32[]{:S(2)}) collective-permute-start(bf16[272,1024]{1,0:T(8,128)(2,1)} %get-tuple-element.54), channel_id=1, source_target_pairs={{0,1},{1,2},{2,3},{3,4},{4,5},{5,6},{6,7},{8,9},{9,10},{10,11},{11... | collective-permute-start | bytes 1671176 | tf_op jit(solution)/shard_map/ppermute | solution.py:474
  33.4 25.7 %collective-permute-start.11 = (bf16[272,1024]{1,0:T(8,128)(2,1)}, bf16[272,1024]{1,0:T(8,128)(2,1)}, u32[]{:S(2)}, u32[]{:S(2)}) collective-permute-start(bf16[272,1024]{1,0:T(8,128)(2,1)} %get-tuple-element.55), channel_id=1, source_target_pairs={{1,0},{2,1},{3,2},{4,3},{5,4},{6,5},{7,6},{9,8},{10,9},{11,10},{12... | collective-permute-start | bytes 1671176 | tf_op jit(solution)/shard_map/ppermute | solution.py:475
  35.7 3.0 %collective-permute-start.3 = (bf16[16,8192]{1,0:T(8,128)(2,1)S(1)}, bf16[16,8192]{1,0:T(8,128)(2,1)S(1)}, u32[]{:S(2)}, u32[]{:S(2)}) collective-permute-start(bf16[16,8192]{1,0:T(8,128)(2,1)S(1)} %get-tuple-element.47.refs_0_), channel_id=1, source_target_pairs={{0,1},{1,0},{2,3},{3,2},{4,5},{5,4},{6,7},{7,6},{8,9},{9,8},{10,11... | collective-permute-start | bytes 786440 | tf_op jit(solution)/shard_map/ppermute | solution.py:434
  37.5 1.5 %collective-permute-start.4 = (bf16[16,8192]{1,0:T(8,128)(2,1)S(1)}, bf16[16,8192]{1,0:T(8,128)(2,1)S(1)}, u32[]{:S(2)}, u32[]{:S(2)}) collective-permute-start(bf16[16,8192]{1,0:T(8,128)(2,1)S(1)} %collective-permute-done.refs_1_), channel_id=1, source_target_pairs={{0,1},{1,0},{2,3},{3,2},{4,5},{5,4},{6,7},{7,6},{8,9},{9,8},{10,11... | collective-permute-start | bytes 786440 | tf_op jit(solution)/shard_map/ppermute | solution.py:434
  37.6 1.8 %collective-permute-start.5 = (bf16[16,8192]{1,0:T(8,128)(2,1)S(1)}, bf16[16,8192]{1,0:T(8,128)(2,1)S(1)}, u32[]{:S(2)}, u32[]{:S(2)}) collective-permute-start(bf16[16,8192]{1,0:T(8,128)(2,1)S(1)} %collective-permute-done.1.refs_2_), channel_id=1, source_target_pairs={{0,1},{1,0},{2,3},{3,2},{4,5},{5,4},{6,7},{7,6},{8,9},{9,8},{10,11... | collective-permute-start | bytes 786440 | tf_op jit(solution)/shard_map/ppermute | solution.py:434
  38.7 1.5 %collective-permute-start.6 = (bf16[16,8192]{1,0:T(8,128)(2,1)S(1)}, bf16[16,8192]{1,0:T(8,128)(2,1)S(1)}, u32[]{:S(2)}, u32[]{:S(2)}) collective-permute-start(bf16[16,8192]{1,0:T(8,128)(2,1)S(1)} %collective-permute-done.2.refs_3_), channel_id=1, source_target_pairs={{0,1},{1,0},{2,3},{3,2},{4,5},{5,4},{6,7},{7,6},{8,9},{9,8},{10,11... | collective-permute-start | bytes 786440 | tf_op jit(solution)/shard_map/ppermute | solution.py:434
  39.1 52.5 %collective-permute-start.12 = (bf16[2048,128]{1,0:T(8,128)(2,1)S(1)}, bf16[2048,128]{1,0:T(8,128)(2,1)S(1)}, u32[]{:S(2)}, u32[]{:S(2)}) collective-permute-start(bf16[2048,128]{1,0:T(8,128)(2,1)S(1)} %pick_near.1.refs_0_), channel_id=1, source_target_pairs={{0,1},{1,0},{2,3},{3,2},{4,5},{5,4},{6,7},{7,6},{8,9},{9,8},{10,11... | collective-permute-start | bytes 1572872 | tf_op jit(solution)/shard_map/ppermute | solution.py:434
  39.5 50.0 %collective-permute-start.9 = (bf16[2048,128]{1,0:T(8,128)(2,1)S(1)}, bf16[2048,128]{1,0:T(8,128)(2,1)}, u32[]{:S(2)}, u32[]{:S(2)}) collective-permute-start(bf16[2048,128]{1,0:T(8,128)(2,1)S(1)} %pick_near.1.refs_0_), channel_id=1, source_target_pairs={{0,6},{1,7},{2,0},{3,1},{4,2},{5,3},{6,4},{7,5},{8,14},{9,15},{10,... | collective-permute-start | bytes 1572872 | tf_op jit(solution)/shard_map/ppermute | solution.py:476
  40.2 49.2 %collective-permute-start.8 = (bf16[2048,128]{1,0:T(8,128)(2,1)S(1)}, bf16[2048,128]{1,0:T(8,128)(2,1)}, u32[]{:S(2)}, u32[]{:S(2)}) collective-permute-start(bf16[2048,128]{1,0:T(8,128)(2,1)S(1)} %pick_near.1.refs_0_), channel_id=1, source_target_pairs={{0,4},{1,5},{2,6},{3,7},{4,0},{5,1},{6,2},{7,3},{8,12},{9,13},{10,... | collective-permute-start | bytes 1572872 | tf_op jit(solution)/shard_map/ppermute | solution.py:476
  40.9 0.8 copy-start.2
  53.6 35.8 %all-to-all-start.1 = ((bf16[4,2048,128]{2,1,0:T(8,128)(2,1)}), bf16[4,2048,128]{2,1,0:T(8,128)(2,1)S(1)}, u32[]{:S(2)}, u32[]{:S(2)}) async-start(bf16[4,2048,128]{2,1,0:T(8,128)(2,1)} %bitcast.14), calls=%async_computation.1 | async-start | bytes 4194304 | tf_op jit(solution)/shard_map/all_to_all | solution.py:481
  57.5 31.9 %collective-permute-start.7 = (bf16[2048,128]{1,0:T(8,128)(2,1)S(1)}, bf16[2048,128]{1,0:T(8,128)(2,1)}, u32[]{:S(2)}, u32[]{:S(2)}) collective-permute-start(bf16[2048,128]{1,0:T(8,128)(2,1)S(1)} %pick_near.1.refs_0_), channel_id=1, source_target_pairs={{0,2},{1,3},{2,4},{3,5},{4,6},{5,7},{6,0},{7,1},{8,10},{9,11},{10,... | collective-permute-start | bytes 1572872 | tf_op jit(solution)/shard_map/ppermute | solution.py:476
  89.4 3.3 %collective-permute-start.13 = (bf16[2048,128]{1,0:T(8,128)(2,1)}, bf16[2048,128]{1,0:T(8,128)(2,1)S(1)}, u32[]{:S(2)}, u32[]{:S(2)}) collective-permute-start(bf16[2048,128]{1,0:T(8,128)(2,1)} %collective-permute-done.7.refs_1_), channel_id=1, source_target_pairs={{0,1},{1,0},{2,3},{3,2},{4,5},{5,4},{6,7},{7,6},{8,9},{9,8},{10,11... | collective-permute-start | bytes 1572872 | tf_op jit(solution)/shard_map/ppermute | solution.py:434
  91.0 2.5 %collective-permute-start.14 = (bf16[2048,128]{1,0:T(8,128)(2,1)}, bf16[2048,128]{1,0:T(8,128)(2,1)S(1)}, u32[]{:S(2)}, u32[]{:S(2)}) collective-permute-start(bf16[2048,128]{1,0:T(8,128)(2,1)} %collective-permute-done.8.refs_2_), channel_id=1, source_target_pairs={{0,1},{1,0},{2,3},{3,2},{4,5},{5,4},{6,7},{7,6},{8,9},{9,8},{10,11... | collective-permute-start | bytes 1572872 | tf_op jit(solution)/shard_map/ppermute | solution.py:434
  91.1 3.2 %collective-permute-start.15 = (bf16[2048,128]{1,0:T(8,128)(2,1)}, bf16[2048,128]{1,0:T(8,128)(2,1)S(1)}, u32[]{:S(2)}, u32[]{:S(2)}) collective-permute-start(bf16[2048,128]{1,0:T(8,128)(2,1)} %collective-permute-done.9.refs_3_), channel_id=1, source_target_pairs={{0,1},{1,0},{2,3},{3,2},{4,5},{5,4},{6,7},{7,6},{8,9},{9,8},{10,11... | collective-permute-start | bytes 1572872 | tf_op jit(solution)/shard_map/ppermute | solution.py:434
  94.3 6.9 %collective-permute-start.16 = (bf16[4,2048,128]{2,1,0:T(8,128)(2,1)S(1)}, bf16[4,2048,128]{2,1,0:T(8,128)(2,1)S(1)}, u32[]{:S(2)}, u32[]{:S(2)}) collective-permute-start(bf16[4,2048,128]{2,1,0:T(8,128)(2,1)S(1)} %all-to-all-done.1.mine), channel_id=1, source_target_pairs={{0,1},{1,0},{2,3},{3,2},{4,5},{5,4},{6,7},{7,6},{8,9},{9,8},{10,11... | collective-permute-start | bytes 6291464 | tf_op jit(solution)/shard_map/ppermute | solution.py:434
